TPU v7x, 32 devices: a whole 2x2x4 slice. The times are simulated.
32 devices in a mesh: node: 8 (over z, x), hid: 4 (over y, core).
Axes of the slice: x: 2, y: 2, z: 4, core: 2. Of those that a mesh axis runs over, the one named last changes fastest.
Arguments:
- node_in: bfloat16 [1280, 6, 512], P('node'), may hold values from -6 to 6
- edge_in: bfloat16 [10240, 512], P('node'), may hold values from -6 to 6
- cotangent: bfloat16 [1280, 6, 512], P(('node', 'hid')), may hold values from -6 to 6
- ocean_mask: int32 [1280], P(('node', 'hid')), may hold values 0 or 1
- present_mask: int32 [1280, 6], P(('node', 'hid')), may hold values 0 or 1
- valid_counts: int32 [6], replicated, may hold values from 640 to 1280
- send_slot: int32 [10240], P('node'), may hold values from 0 to 239, as said below
- recv_local: int32 [10240], P('node'), may hold values from 0 to 159, as said below
- halo_lists: int32 [16, 40], P('node'), may hold values from 0 to 159, as said below
- edge_first: float32 [2, 1536, 512], P(None, 'node', 'hid'), may hold values from -0.15625 to 0.15625
- edge_second: float32 [2, 512, 512], P(None, 'hid', 'node'), may hold values from -0.25 to 0.25
- node_first: float32 [2, 1024, 512], P(None, 'node', 'hid'), may hold values from -0.1875 to 0.1875
- node_second: float32 [2, 512, 512], P(None, 'hid', 'node'), may hold values from -0.25 to 0.25
- edge_first_m: float32 [2, 1536, 512], P(None, 'node', 'hid'), may hold values from -512 to 512
- edge_second_m: float32 [2, 512, 512], P(None, 'hid', 'node'), may hold values from -512 to 512
- node_first_m: float32 [2, 1024, 512], P(None, 'node', 'hid'), may hold values from -640 to 640
- node_second_m: float32 [2, 512, 512], P(None, 'hid', 'node'), may hold values from -640 to 640
- edge_first_v: float32 [2, 1536, 512], P(None, 'node', 'hid'), may hold values from 7372.8 to 30720
- edge_second_v: float32 [2, 512, 512], P(None, 'hid', 'node'), may hold values from 7372.8 to 30720
- node_first_v: float32 [2, 1024, 512], P(None, 'node', 'hid'), may hold values from 11059.2 to 44236.8
- node_second_v: float32 [2, 512, 512], P(None, 'hid', 'node'), may hold values from 11059.2 to 44236.8
- small_params: float32 [2, 8, 512], replicated, may hold values from -1.2 to 1.6
- small_m: float32 [2, 8, 512], replicated, may hold values from -448 to 448
- small_v: float32 [2, 8, 512], replicated, may hold values from 614.4 to 24576
- learn_rate: float32 [1], replicated, may hold values from 0.2 to 0.5
Outputs:
- node_out: bfloat16 [1280, 6, 512], P(('node', 'hid'))
- grad_node: bfloat16 [1280, 6, 512], P(('node', 'hid'))
- grad_edge: bfloat16 [10240, 512], P(('node', 'hid'))
- edge_first_new: float32 [2, 1536, 512], P(None, 'node', 'hid')
- edge_second_new: float32 [2, 512, 512], P(None, 'hid', 'node')
- node_first_new: float32 [2, 1024, 512], P(None, 'node', 'hid')
- node_second_new: float32 [2, 512, 512], P(None, 'hid', 'node')
- edge_first_m_new: float32 [2, 1536, 512], P(None, 'node', 'hid')
- edge_second_m_new: float32 [2, 512, 512], P(None, 'hid', 'node')
- node_first_m_new: float32 [2, 1024, 512], P(None, 'node', 'hid')
- node_second_m_new: float32 [2, 512, 512], P(None, 'hid', 'node')
- edge_first_v_new: float32 [2, 1536, 512], P(None, 'node', 'hid')
- edge_second_v_new: float32 [2, 512, 512], P(None, 'hid', 'node')
- node_first_v_new: float32 [2, 1024, 512], P(None, 'node', 'hid')
- node_second_v_new: float32 [2, 512, 512], P(None, 'hid', 'node')
- edge_first_copy: bfloat16 [2, 1536, 512], P(None, 'node', 'hid')
- edge_second_copy: bfloat16 [2, 512, 512], P(None, 'hid', 'node')
- node_first_copy: bfloat16 [2, 1024, 512], P(None, 'node', 'hid')
- node_second_copy: bfloat16 [2, 512, 512], P(None, 'hid', 'node')
- small_new: float32 [2, 8, 512], replicated
- small_m_new: float32 [2, 8, 512], replicated
- small_v_new: float32 [2, 8, 512], replicated
- norms: float32 [2, 12, 2], replicated
Inputs may be any that keep to these rules, and one draw needn't show every extreme that they name: `recv_local`: within each block of 1280 edges the values never fall, and every one of the block's 160 nodes receives at least one edge. `send_slot`: below 160: a node of the edge's own block; 160 to 199: an entry of the previous block's list; above: an entry of the next block's list. `halo_lists`: row 2b holds 40 different nodes of block b, numbered within the block, read by the previous block; row 2b + 1 those read by the next block.
All inputs are finite; a program needn't handle non-finite values. No bound on the sum of `ocean_mask` or of `present_mask` on one device may be relied on, other than what follows from the above.
Results may differ from a plain program's by a relative error of at most 0.023.
Values may be sent and summed in bfloat16 or wider, within the bound.
No kernel may reach another device: no remote copies, remote signals or barrier semaphores. Data moves between devices by JAX's collectives and lax.ppermute only.
A program may use at most 256 MiB of HBM per device.

v0:
```python
import jax
import jax.numpy as jnp
from jax import lax
from jax.experimental import pallas as pl
from jax.experimental.pallas import tpu as pltpu
from jax.sharding import PartitionSpec as P

LAYERS = 2


NORM_EPS = 1e-05
BETA_FIRST = 0.5
BETA_SECOND = 0.5
ADAM_EPS = 1e-06
WEIGHT_DECAY = 0.01
BF16 = jnp.bfloat16
F32 = jnp.float32
VMEM_BYTES = 56 * 1024 * 1024


def matmul(left, right):
    return lax.dot_general(left, right, (((1,), (0,)), ((), ())), preferred_element_type=F32)


def matmul_nt(left, right):
    return lax.dot_general(left, right, (((1,), (1,)), ((), ())), preferred_element_type=F32)


def matmul_tn(left, right):
    return lax.dot_general(left, right, (((0,), (0,)), ((), ())), preferred_element_type=F32)


def sigmoid(values):
    return 1.0 / (1.0 + jnp.exp(-values))


def silu_slope(values):
    gate = sigmoid(values)
    return gate * (1.0 + values * (1.0 - gate))


def norm_forward(values):
    center = values - jnp.mean(values, axis=-1, keepdims=True)
    spread = jnp.mean(center * center, axis=-1, keepdims=True)
    inverse = lax.rsqrt(spread + NORM_EPS)
    return center * inverse, inverse


def norm_backward(upstream, normed, inverse, gain_row):
    scaled = upstream * gain_row
    return inverse * (
        scaled
        - jnp.mean(scaled, axis=-1, keepdims=True)
        - normed * jnp.mean(scaled * normed, axis=-1, keepdims=True)
    )


def column_sum(values):
    return jnp.sum(values, axis=0, keepdims=True)


def assemble(source, rows, offset, target):
    nodes, hids, _, width = source.shape
    for i in range(nodes):
        for j in range(hids):
            target[i * rows : (i + 1) * rows, j * width : (j + 1) * width] = source[
                i, j, offset : offset + rows, :
            ]


def pack(values, rows, offset, target):
    nodes, hids, _, width = target.shape
    for i in range(nodes):
        for j in range(hids):
            target[i, j, offset : offset + rows, :] = values[
                i * rows : (i + 1) * rows, j * width : (j + 1) * width
            ].astype(target.dtype)


def per_sample(array):
    block = (1,) + array.shape[1:]
    return pl.BlockSpec(block, lambda s: (s,) + (0,) * (len(block) - 1))


def constant(array):
    return pl.BlockSpec(array.shape, lambda s: (0,) * len(array.shape))


def weight_block(array, rows, place):
    nodes, hids, _, width = array.shape
    return pl.BlockSpec((nodes, hids, rows, width), lambda s: (0, 0, place, 0))


def shape_of(shape, dtype):
    return jax.ShapeDtypeStruct(shape, dtype)


def run_kernel(kernel, name, samples, inputs, in_specs, outputs, scratch, flops):
    moved = sum(a.size * a.dtype.itemsize for a in inputs) + sum(
        shape.size * shape.dtype.itemsize for shape, _ in outputs
    )
    return pl.pallas_call(
        kernel,
        name=name,
        grid=(samples,),
        in_specs=in_specs,
        out_specs=[spec for _, spec in outputs],
        out_shape=[shape for shape, _ in outputs],
        scratch_shapes=scratch,
        compiler_params=pltpu.CompilerParams(
            dimension_semantics=("arbitrary",), vmem_limit_bytes=VMEM_BYTES
        ),
        cost_estimate=pl.CostEstimate(flops=flops, bytes_accessed=moved, transcendentals=0),
    )(*inputs)


def sampled(shape, dtype):
    result = shape_of(shape, dtype)
    return (result, per_sample(result))


def shared(shape, dtype):
    result = shape_of(shape, dtype)
    return (result, constant(result))


def edge_forward(first, second, table, edge_low, edge_state, at_both, at_nodes, params, node_total, last):
    samples, table_total, latent = table.shape
    edges = edge_low.shape[1]
    alike = edge_low.shape[0] == 1

    def kernel(w1, w2, table, low, state, both, nodes, params, pre, act, normed, inverse, *rest):
        if last:
            pooled, w1s, w2s, projected = rest
        else:
            new_state, new_low, pooled, w1s, w2s, projected = rest

        @pl.when(pl.program_id(0) == 0)
        def _():
            assemble(w1, w1.shape[2], 0, w1s)
            assemble(w2, w2.shape[2], 0, w2s)

        rows = table[0]
        projected[:table_total] = matmul(rows, w1s[latent : 2 * latent]).astype(BF16)
        projected[table_total:] = matmul(rows[:node_total], w1s[2 * latent :]).astype(BF16)
        hidden = matmul(low[0], w1s[:latent]) + matmul(both[...], projected[...]) + params[0:1]
        pre[0] = hidden.astype(BF16)
        active = (hidden * sigmoid(hidden)).astype(BF16)
        act[0] = active
        output = matmul_nt(active, w2s[...]) + params[1:2]
        scaled, scale = norm_forward(output)
        normed[0] = scaled.astype(BF16)
        inverse[0] = scale
        state_new = state[0] + scaled * params[2:3] + params[3:4]
        low_new = state_new.astype(BF16)
        if not last:
            new_state[0] = state_new
            new_low[0] = low_new
        pooled[0] = matmul(nodes[...], low_new).astype(BF16)

    wide = (samples, edges, latent)
    outputs = [sampled(wide, BF16), sampled(wide, BF16), sampled(wide, BF16), sampled((samples, edges, 1), F32)]
    if not last:
        outputs += [sampled(wide, F32), sampled(wide, BF16)]
    outputs += [sampled((samples, node_total, latent), BF16)]
    of_edges = constant if alike else per_sample
    return run_kernel(
        kernel,
        "edge_forward",
        samples,
        [first[0], second[0], table, edge_low, edge_state, at_both, at_nodes, params],
        [
            weight_block(*first),
            weight_block(*second),
            per_sample(table),
            of_edges(edge_low),
            of_edges(edge_state),
            constant(at_both),
            constant(at_nodes),
            constant(params),
        ],
        outputs,
        [
            pltpu.VMEM((3 * latent, latent), BF16),
            pltpu.VMEM((latent, latent), BF16),
            pltpu.VMEM((at_both.shape[1], latent), BF16),
        ],
        2 * samples * edges * latent * (3 * latent + at_both.shape[1]),
    )


def edge_backward(first, second, pooled_grad, edge_grad, normed, inverse, pre, at_receiver, at_both_t, gain, last, node_total):
    samples, edges, latent = normed.shape
    at_total = at_both_t.shape[0]
    table_total = at_total - node_total

    def kernel(w1, w2, upstream, *rest):
        if not last:
            later, rest = rest[0], rest[1:]
        normed, inverse, pre, receiver, both_t, gain, low, hidden_low, at_rows, partial, returned, grad_out, minor = rest[:13]
        if last:
            w1s, w2s = rest[13:]
        else:
            hidden_sum, w1s, w2s, hidden_acc = rest[13:]
        step = pl.program_id(0)

        @pl.when(step == 0)
        def _():
            assemble(w1, w1.shape[2], 0, w1s)
            assemble(w2, w2.shape[2], 0, w2s)
            minor[...] = jnp.zeros_like(minor)

        grad = matmul(receiver[...], upstream[0])
        if not last:
            grad = grad + later[0]
        scaled = normed[0].astype(F32)
        output_grad = norm_backward(grad, scaled, inverse[0], gain[0:1]).astype(BF16)
        low[0] = output_grad
        act_grad = matmul(output_grad, w2s[...])
        pre_grad = (act_grad * silu_slope(pre[0].astype(F32))).astype(BF16)
        hidden_low[0] = pre_grad
        minor[0:1] += column_sum(pre_grad.astype(F32))
        minor[1:2] += column_sum(output_grad.astype(F32))
        minor[2:3] += column_sum(grad * scaled)
        minor[3:4] += column_sum(grad)
        at_rows[0] = matmul(both_t[...], pre_grad).astype(BF16)
        send = w1s[latent : 2 * latent]
        partial[0] = matmul_nt(at_rows[0, :node_total], send) + matmul_nt(
            at_rows[0, table_total:], w1s[2 * latent :]
        )
        returned[0] = matmul_nt(at_rows[0, node_total:table_total], send).astype(BF16)
        if last:
            grad_out[0] = grad + matmul_nt(pre_grad, w1s[:latent])
        else:

            @pl.when(step == 0)
            def _():
                grad_out[...] = grad
                hidden_acc[...] = pre_grad.astype(F32)

            @pl.when(step > 0)
            def _():
                grad_out[...] += grad
                hidden_acc[...] += pre_grad.astype(F32)

            @pl.when(step == samples - 1)
            def _():
                total = hidden_acc[...].astype(BF16)
                hidden_sum[...] = total
                grad_out[...] += matmul_nt(total, w1s[:latent])

    wide = (samples, edges, latent)
    outputs = [
        sampled(wide, BF16),
        sampled(wide, BF16),
        sampled((samples, at_total, latent), BF16),
        sampled((samples, node_total, latent), F32),
        sampled((samples, table_total - node_total, latent), BF16),
        sampled(wide, F32) if last else shared((edges, latent), F32),
        shared((4, latent), F32),
    ]
    scratch = [pltpu.VMEM((3 * latent, latent), BF16), pltpu.VMEM((latent, latent), BF16)]
    inputs = [first[0], second[0], pooled_grad]
    specs = [weight_block(*first), weight_block(*second), per_sample(pooled_grad)]
    if not last:
        outputs.append(shared((edges, latent), BF16))
        scratch.append(pltpu.VMEM((edges, latent), F32))
        inputs.append(edge_grad)
        specs.append(per_sample(edge_grad))
    inputs += [normed, inverse, pre, at_receiver, at_both_t, gain]
    specs += [
        per_sample(normed),
        per_sample(inverse),
        per_sample(pre),
        constant(at_receiver),
        constant(at_both_t),
        constant(gain),
    ]
    return run_kernel(
        kernel,
        "edge_backward",
        samples,
        inputs,
        specs,
        outputs,
        scratch,
        2 * samples * edges * latent * (2 * latent + 2 * at_total),
    )


def edge_weight_grads(edge_low, table, hidden_low, at_rows, low, act, node_total, nodes, hids, width, packed_before):
    samples, table_total, latent = table.shape
    alike = edge_low.ndim == 2
    first_rows, second_rows = 3 * latent // nodes, latent // nodes
    offset = 0 if packed_before is None else packed_before.shape[2]

    def kernel(edge_low, table, hidden_low, at_rows, low, act, *rest):
        if packed_before is not None:
            before, rest = rest[0], rest[1:]
        packed, first, second = rest
        step = pl.program_id(0)

        @pl.when(step == 0)
        def _():
            first[...] = jnp.zeros_like(first)
            second[...] = jnp.zeros_like(second)
            if packed_before is not None:
                packed[:, :, :offset, :] = before[...]
            if alike:
                first[:latent] = matmul_tn(edge_low[...], hidden_low[...])

        if not alike:
            first[:latent] += matmul_tn(edge_low[0], hidden_low[0])
        first[latent : 2 * latent] += matmul_tn(table[0], at_rows[0, :table_total])
        first[2 * latent :] += matmul_tn(table[0, :node_total], at_rows[0, table_total:])
        second[...] += matmul_tn(low[0], act[0])

        @pl.when(step == samples - 1)
        def _():
            pack(first, first_rows, offset, packed)
            pack(second, second_rows, offset + first_rows, packed)

    of_edges = constant if alike else per_sample
    inputs = [edge_low, table, hidden_low, at_rows, low, act]
    specs = [of_edges(edge_low), per_sample(table), of_edges(hidden_low), per_sample(at_rows), per_sample(low), per_sample(act)]
    if packed_before is not None:
        inputs.append(packed_before)
        specs.append(constant(packed_before))
    return run_kernel(
        kernel,
        "edge_weight_grads",
        samples,
        inputs,
        specs,
        [shared((nodes, hids, offset + first_rows + second_rows, width), BF16)],
        [pltpu.VMEM((3 * latent, latent), F32), pltpu.VMEM((latent, latent), F32)],
        4 * low.size * latent,
    )[0]


def node_pass(weights, table, state, pooled_pair, params, at_halo, target, scaling, mask, node_total):
    samples, _, latent = table.shape
    array, rows, place = weights
    nodes, hids, _, width = array.shape
    second_rows = latent // nodes
    first_rows = rows - second_rows
    last = target is not None

    def kernel(w, table, state, pooled_own, pooled_other, params, *rest):
        if last:
            target, scaling, mask, new_low, upstream, input_grad, packed, minor, w1s, w2s, first, second = rest
        else:
            at_halo, pooled_out, pre, act, normed, inverse, new_state, new_low, halo, w1s, w2s = rest
        step = pl.program_id(0)

        @pl.when(step == 0)
        def _():
            assemble(w, first_rows, 0, w1s)
            assemble(w, second_rows, first_rows, w2s)

        rows_low = table[0, :node_total]
        pooled = (pooled_own[0].astype(F32) + pooled_other[0].astype(F32)).astype(BF16)
        hidden = matmul(rows_low, w1s[:latent]) + matmul(pooled, w1s[latent:]) + params[4:5]
        active = (hidden * sigmoid(hidden)).astype(BF16)
        output = matmul_nt(active, w2s[...]) + params[5:6]
        scaled, scale = norm_forward(output)
        state_new = state[0] + scaled * params[6:7] + params[7:8]
        low_new = state_new.astype(BF16)
        new_low[0] = low_new
        if not last:
            pooled_out[0] = pooled
            pre[0] = hidden.astype(BF16)
            act[0] = active
            normed[0] = scaled.astype(BF16)
            inverse[0] = scale
            new_state[0] = state_new
            halo[0] = matmul(at_halo[...], low_new).astype(BF16)
        else:
            grad = target[0].astype(F32) * scaling[0]
            node_gradients(
                step, samples, grad, scaled, scale, hidden, active, rows_low, pooled, params, mask,
                w1s, w2s, first, second, upstream, input_grad, packed, minor, first_rows, second_rows,
            )

    rows_shape = (samples, node_total, latent)
    inputs = [array, table, state, *pooled_pair, params]
    specs = [weight_block(*weights), per_sample(table), per_sample(state), per_sample(pooled_pair[0]), per_sample(pooled_pair[1]), constant(params)]
    scratch = [pltpu.VMEM((2 * latent, latent), BF16), pltpu.VMEM((latent, latent), BF16)]
    if last:
        inputs += [target, scaling, mask]
        specs += [per_sample(target), per_sample(scaling), constant(mask)]
        outputs = [sampled(rows_shape, BF16), *gradient_outputs(samples, node_total, latent, nodes, hids, rows, width)]
        scratch += [pltpu.VMEM((2 * latent, latent), F32), pltpu.VMEM((latent, latent), F32)]
    else:
        inputs += [at_halo]
        specs += [constant(at_halo)]
        outputs = [
            sampled(rows_shape, BF16),
            sampled(rows_shape, BF16),
            sampled(rows_shape, BF16),
            sampled(rows_shape, BF16),
            sampled((samples, node_total, 1), F32),
            sampled(rows_shape, F32),
            sampled(rows_shape, BF16),
            sampled((samples, at_halo.shape[0], latent), BF16),
        ]
    return run_kernel(kernel, "node_pass", samples, inputs, specs, outputs, scratch, 6 * samples * node_total * latent * latent * (3 if last else 1))


def gradient_outputs(samples, node_total, latent, nodes, hids, rows, width):
    return [
        sampled((samples, node_total, latent), BF16),
        sampled((samples, node_total, latent), F32),
        shared((nodes, hids, rows, width), BF16),
        shared((4, latent), F32),
    ]


def node_gradients(
    step, samples, grad, scaled, scale, hidden, active, rows_low, pooled, params, mask,
    w1s, w2s, first, second, upstream, input_grad, packed, minor, first_rows, second_rows,
):
    latent = w2s.shape[0]

    @pl.when(step == 0)
    def _():
        minor[...] = jnp.zeros_like(minor)
        first[...] = jnp.zeros_like(first)
        second[...] = jnp.zeros_like(second)

    output_grad = norm_backward(grad, scaled, scale, params[6:7]).astype(BF16)
    pre_grad = (matmul(output_grad, w2s[...]) * silu_slope(hidden)).astype(BF16)
    upstream[0] = matmul_nt(pre_grad, w1s[latent:]).astype(BF16)
    input_grad[0] = grad + matmul_nt(pre_grad, w1s[:latent])
    chosen = mask[...] > 0.5
    output_mine = jnp.where(chosen, output_grad.astype(F32), 0.0)
    pre_mine = jnp.where(chosen, pre_grad.astype(F32), 0.0)
    grad_mine = jnp.where(chosen, grad, 0.0)
    minor[0:1] += column_sum(pre_mine)
    minor[1:2] += column_sum(output_mine)
    minor[2:3] += column_sum(grad_mine * scaled)
    minor[3:4] += column_sum(grad_mine)
    pre_mine = pre_mine.astype(BF16)
    first[:latent] += matmul_tn(rows_low, pre_mine)
    first[latent:] += matmul_tn(pooled, pre_mine)
    second[...] += matmul_tn(output_mine.astype(BF16), active)

    @pl.when(step == samples - 1)
    def _():
        pack(first, first_rows, 0, packed)
        pack(second, second_rows, first_rows, packed)


def node_backward(weights, grads, table, pooled, pre, act, normed, inverse, params, mask, node_total):
    samples, _, latent = table.shape
    array, rows, place = weights
    nodes, hids, _, width = array.shape
    second_rows = latent // nodes
    first_rows = rows - second_rows

    def kernel(w, base, own, other, table, pooled, pre, act, normed, inverse, params, mask, upstream, input_grad, packed, minor, w1s, w2s, first, second):
        step = pl.program_id(0)

        @pl.when(step == 0)
        def _():
            assemble(w, first_rows, 0, w1s)
            assemble(w, second_rows, first_rows, w2s)

        grad = base[0] + (own[0] + other[0].astype(F32))
        node_gradients(
            step, samples, grad, normed[0].astype(F32), inverse[0], pre[0].astype(F32), act[0],
            table[0, :node_total], pooled[0], params, mask,
            w1s, w2s, first, second, upstream, input_grad, packed, minor, first_rows, second_rows,
        )

    inputs = [array, *grads, table, pooled, pre, act, normed, inverse, params, mask]
    specs = [weight_block(*weights)] + [per_sample(a) for a in inputs[1:10]] + [constant(params), constant(mask)]
    return run_kernel(
        kernel,
        "node_backward",
        samples,
        inputs,
        specs,
        gradient_outputs(samples, node_total, latent, nodes, hids, rows, width),
        [
            pltpu.VMEM((2 * latent, latent), BF16),
            pltpu.VMEM((latent, latent), BF16),
            pltpu.VMEM((2 * latent, latent), F32),
            pltpu.VMEM((latent, latent), F32),
        ],
        12 * samples * node_total * latent * latent,
    )


def dot(spec, left, right):
    return jnp.einsum(spec, left, right, preferred_element_type=F32)


def swap(values, axis, offset):
    return lax.ppermute(values, axis, [(i, i ^ offset) for i in range(lax.axis_size(axis))])


def bits_of(axis):
    return lax.axis_size(axis).bit_length() - 1


def own_bit(axis, bit):
    return (lax.axis_index(axis) >> bit) & 1


def all_bits():
    return [(axis, bit) for axis in ("node", "hid") for bit in reversed(range(bits_of(axis)))]


def ordered(own, mine, other):
    low = jnp.where(own == 0, mine, other)
    high = jnp.where(own == 0, other, mine)
    return low, high


def double_up(part, axis, bit, place):
    low, high = ordered(own_bit(axis, bit), part, swap(part, axis, 1 << bit))
    return jnp.stack([low, high], axis=place)


def halve_sum(parts, axis, bit, place):
    own = own_bit(axis, bit)
    sent = lax.dynamic_index_in_dim(parts, 1 - own, place, keepdims=False)
    kept = lax.dynamic_index_in_dim(parts, own, place, keepdims=False)
    return kept.astype(F32) + swap(sent.astype(BF16), axis, 1 << bit).astype(F32)


def gather_all(packed):
    present, early = [], None
    for key in all_bits():
        present.append(key)
        packed = double_up(packed, *key, len(present) - 1)
        if len(present) == 2:
            early = packed
    return packed.reshape(lax.axis_size("node"), lax.axis_size("hid"), *packed.shape[-2:]), early


def scatter_all(parts, values=None):
    left = all_bits()
    parts = parts.reshape((2,) * len(left) + parts.shape[2:])
    while left:
        axis, bit = left.pop()
        parts = halve_sum(parts, axis, bit, len(left))
        if values is not None:
            values = values + swap(values, axis, 1 << bit)
            parts, values = lax.optimization_barrier((parts, values))
    return parts, values


def sum_everywhere(values):
    for axis, bit in reversed(all_bits()):
        values = values + swap(values, axis, 1 << bit)
    return values


def to_neighbours(rows, halo_width):
    count = lax.axis_size("node")
    onward = [(i, (i + 1) % count) for i in range(count)]
    back = [(target, source) for source, target in onward]
    from_previous = lax.ppermute(rows[:, halo_width:], "node", onward)
    from_next = lax.ppermute(rows[:, :halo_width], "node", back)
    return jnp.concatenate([from_previous, from_next], axis=1)


def adam_terms(weight, grad, first, second, decay):
    first_new = BETA_FIRST * first + (1.0 - BETA_FIRST) * grad
    second_new = BETA_SECOND * second + (1.0 - BETA_SECOND) * grad * grad
    update = first_new / (jnp.sqrt(second_new) + ADAM_EPS) + decay * weight
    return (first_new, second_new, update)


def pack_shards(first, second):
    return jnp.concatenate([first, second.T], axis=0).astype(BF16)


def adam_terms(weight, grad, first, second, decay):
    first_new = BETA_FIRST * first + (1.0 - BETA_FIRST) * grad
    second_new = BETA_SECOND * second + (1.0 - BETA_SECOND) * grad * grad
    update = first_new / (jnp.sqrt(second_new) + ADAM_EPS) + decay * weight
    return (first_new, second_new, update)


def per_device(
    node_in,
    edge_in,
    cotangent,
    ocean_mask,
    present_mask,
    valid_counts,
    send_slot,
    recv_local,
    halo_lists,
    edge_first,
    edge_second,
    node_first,
    node_second,
    edge_first_m,
    edge_second_m,
    node_first_m,
    node_second_m,
    edge_first_v,
    edge_second_v,
    node_first_v,
    node_second_v,
    small_params,
    small_m,
    small_v,
    learn_rate,
):
    hid_count = lax.axis_size("hid")
    hid_index = lax.axis_index("hid")
    node_total, sample_count, latent = node_in.shape
    edge_part = edge_in.shape[0] // hid_count
    node_part = node_total // hid_count
    halo_width = halo_lists.shape[1]
    table_total = node_total + 2 * halo_width
    sample_half, edge_half = hid_index >> 1, hid_index & 1
    samples = sample_count // 2
    nodes, hids = lax.axis_size("node"), hid_count
    first_rows = edge_first.shape[1]
    second_rows = edge_second.shape[2]
    node_rows = node_first.shape[1] + second_rows
    width = edge_first.shape[2]

    edge_zero, early = gather_all(pack_shards(edge_first[0], edge_second[0]))
    piece, _ = lax.optimization_barrier((pack_shards(node_first[0], node_second[0]), early))
    node_zero, early = gather_all(piece)
    piece = jnp.concatenate(
        [pack_shards(node_first[1], node_second[1]), pack_shards(edge_first[1], edge_second[1])], axis=0
    )
    piece, _ = lax.optimization_barrier((piece, early))
    layer_one, _ = gather_all(piece)
    edge_weights = [
        ((edge_zero, first_rows, 0), (edge_zero, second_rows, first_rows // second_rows)),
        ((layer_one, first_rows, 1), (layer_one, second_rows, 2 * first_rows // second_rows)),
    ]
    node_weights = [(node_zero, node_rows, 0), (layer_one, node_rows, 0)]

    def own_edges(values):
        return lax.dynamic_index_in_dim(
            values.reshape(2, 2, edge_part, *values.shape[1:]), edge_half, 1, keepdims=False
        ).reshape(2 * edge_part, *values.shape[1:])

    def own_nodes(values):
        return lax.dynamic_index_in_dim(
            values.reshape(samples, 2, 2, node_part, latent), edge_half, 2, keepdims=False
        ).reshape(samples, 2 * node_part, latent)

    def own_samples(values):
        return lax.dynamic_slice_in_dim(values, sample_half * samples, samples, 1)

    def to_own_rows(values):
        quarters = jnp.moveaxis(values.reshape(samples, 2, 2, node_part, latent), 0, 3)
        quarters = lax.dynamic_index_in_dim(quarters, edge_half, 1, keepdims=False)
        sent = lax.dynamic_index_in_dim(quarters, 1 - sample_half, 0, keepdims=False)
        kept = lax.dynamic_index_in_dim(quarters, sample_half, 0, keepdims=False)
        return jnp.concatenate(ordered(sample_half, kept, swap(sent, "hid", 2)), axis=1)

    sender = own_edges(send_slot)
    receiver = own_edges(recv_local)
    node_ids, table_ids = jnp.arange(node_total), jnp.arange(table_total)
    at_receiver = (receiver[:, None] == node_ids[None, :]).astype(BF16)
    at_both = jnp.concatenate(
        [(sender[:, None] == table_ids[None, :]).astype(BF16), at_receiver], axis=1
    )
    at_nodes = (node_ids[:, None] == receiver[None, :]).astype(BF16)
    at_both_t = jnp.concatenate(
        [(table_ids[:, None] == sender[None, :]).astype(BF16), at_nodes], axis=0
    )
    at_halo = (halo_lists.reshape(-1)[:, None] == node_ids[None, :]).astype(BF16)
    mask = ((node_ids // node_part) % 2 == edge_half).astype(F32)[:, None]

    valid_mask = (ocean_mask[:, None] * present_mask).astype(BF16)
    masked = cotangent * valid_mask[:, :, None]
    masked, _ = lax.optimization_barrier((masked, edge_zero))
    sent = lax.dynamic_slice_in_dim(masked, (1 - sample_half) * samples, samples, 1)
    masked = jnp.stack(ordered(sample_half, own_samples(masked), swap(sent, "hid", 2)), axis=0)
    masked = double_up(masked, "hid", 0, 1).reshape(node_total, samples, latent)
    scaling = node_total * lax.axis_size("node") / valid_counts.astype(F32)
    scaling = lax.dynamic_slice_in_dim(scaling, sample_half * samples, samples, 0)
    target = jnp.transpose(masked, (1, 0, 2))
    scaling = scaling[:, None, None]

    node_low = jnp.transpose(own_samples(node_in), (1, 0, 2))
    edge_in_own = own_edges(edge_in)
    halo_rows = dot("hn,snl->shl", at_halo, node_low).astype(BF16)
    table_zero = jnp.concatenate([node_low, to_neighbours(halo_rows, halo_width)], axis=1)
    pre_zero, act_zero, normed_zero, inverse_zero, edge_state, edge_low, pooled = edge_forward(
        *edge_weights[0],
        table_zero,
        edge_in_own[None],
        edge_in_own.astype(F32)[None],
        at_both,
        at_nodes,
        small_params[0],
        node_total,
        False,
    )
    (
        pooled_zero,
        node_pre,
        node_act,
        node_normed,
        node_inverse,
        node_state,
        node_low,
        halo_rows,
    ) = node_pass(
        node_weights[0],
        table_zero,
        node_low.astype(F32),
        (pooled, swap(pooled, "hid", 1)),
        small_params[0],
        at_halo,
        None,
        None,
        None,
        node_total,
    )
    table_one = jnp.concatenate([node_low, to_neighbours(halo_rows, halo_width)], axis=1)
    pre_one, act_one, normed_one, inverse_one, pooled = edge_forward(
        *edge_weights[1],
        table_one,
        edge_low,
        edge_state,
        at_both,
        at_nodes,
        small_params[1],
        node_total,
        True,
    )
    node_low, pooled_grad, node_grad, node_packed, node_minor_one = node_pass(
        node_weights[1],
        table_one,
        node_state,
        (pooled, swap(pooled, "hid", 1)),
        small_params[1],
        None,
        target,
        scaling,
        mask,
        node_total,
    )
    node_out = to_own_rows(node_low)

    def from_edges(partial, returned):
        returned = to_neighbours(returned, halo_width)
        return partial + dot("hn,shl->snl", at_halo, returned)

    low, hidden_low, at_rows, partial, returned, edge_grad, edge_minor_one = edge_backward(
        *edge_weights[1],
        pooled_grad,
        None,
        normed_one,
        inverse_one,
        pre_one,
        at_receiver,
        at_both_t,
        small_params[1, 2:3],
        True,
        node_total,
    )
    packed = edge_weight_grads(
        edge_low,
        table_one,
        hidden_low,
        at_rows,
        low,
        act_one,
        node_total,
        nodes,
        hids,
        width,
        node_packed,
    )
    layer_one_grads, _ = scatter_all(packed)
    partial = from_edges(partial, returned)
    pooled_grad, node_grad, node_packed, node_minor_zero = node_backward(
        node_weights[0],
        (node_grad, partial, swap(partial.astype(BF16), "hid", 1)),
        table_zero,
        pooled_zero,
        node_pre,
        node_act,
        node_normed,
        node_inverse,
        small_params[0],
        mask,
        node_total,
    )
    node_zero_grads, _ = scatter_all(node_packed)
    low, hidden_low, at_rows, partial, returned, edge_input_grad, edge_minor_zero, hidden_sum = (
        edge_backward(
            *edge_weights[0],
            pooled_grad,
            edge_grad,
            normed_zero,
            inverse_zero,
            pre_zero,
            at_receiver,
            at_both_t,
            small_params[0, 2:3],
            False,
            node_total,
        )
    )
    packed = edge_weight_grads(
        edge_in_own,
        table_zero,
        hidden_sum,
        at_rows,
        low,
        act_zero,
        node_total,
        nodes,
        hids,
        width,
        None,
    )
    masters = (edge_first, edge_second, node_first, node_second)
    weight_local = jnp.stack([jnp.sum(matrix * matrix, axis=(1, 2)) for matrix in masters], axis=1)
    minor_packed = jnp.concatenate(
        [edge_minor_zero, node_minor_zero, edge_minor_one, node_minor_one]
        + [jnp.pad(weight_local.reshape(1, -1), ((0, 0), (0, latent - weight_local.size)))],
        axis=0,
    )
    edge_zero_grads, minor_packed = scatter_all(packed, minor_packed)
    partial = from_edges(partial, returned)
    node_grad = node_grad + (partial + swap(partial.astype(BF16), "hid", 1).astype(F32))
    grad_node = to_own_rows(node_grad.astype(BF16))
    edge_input_grad = halve_sum(edge_input_grad.reshape(2, edge_part, latent), "hid", 1, 0)

    minor_total = minor_packed[: 8 * LAYERS].reshape(small_params.shape)
    weight_squares = minor_packed[8 * LAYERS, : weight_local.size].reshape(weight_local.shape)
    node_one_grads, edge_one_grads = layer_one_grads[:node_rows], layer_one_grads[node_rows:]
    node_first_rows = node_rows - second_rows
    grads = [
        jnp.stack([edge_zero_grads[:first_rows], edge_one_grads[:first_rows]]),
        jnp.stack([edge_zero_grads[first_rows:].T, edge_one_grads[first_rows:].T]),
        jnp.stack([node_zero_grads[:node_first_rows], node_one_grads[:node_first_rows]]),
        jnp.stack([node_zero_grads[node_first_rows:].T, node_one_grads[node_first_rows:].T]),
    ]
    firsts = (edge_first_m, edge_second_m, node_first_m, node_second_m)
    seconds = (edge_first_v, edge_second_v, node_first_v, node_second_v)
    moment_list = [
        adam_terms(masters[place], grads[place], firsts[place], seconds[place], WEIGHT_DECAY)
        for place in range(4)
    ]
    update_squares = sum_everywhere(
        jnp.stack([jnp.sum(entry[2] * entry[2], axis=(1, 2)) for entry in moment_list], axis=1)
    )
    weight_norm = jnp.sqrt(weight_squares)
    update_norm = jnp.sqrt(update_squares)
    new_weights = []
    for position in range(4):
        ratio = weight_norm[:, position] / update_norm[:, position]
        new_weights.append(
            masters[position] - learn_rate[0] * ratio[:, None, None] * moment_list[position][2]
        )
    small_first, small_second, small_update = adam_terms(
        small_params, minor_total, small_m, small_v, 0.0
    )
    small_wnorm = jnp.sqrt(jnp.sum(small_params * small_params, axis=2))
    small_unorm = jnp.sqrt(jnp.sum(small_update * small_update, axis=2))
    small_new = (
        small_params - learn_rate[0] * (small_wnorm / small_unorm)[:, :, None] * small_update
    )
    norms = jnp.stack(
        [
            jnp.concatenate([weight_norm, small_wnorm], axis=1),
            jnp.concatenate([update_norm, small_unorm], axis=1),
        ],
        axis=2,
    )
    return (
        node_out,
        grad_node,
        edge_input_grad.astype(BF16),
        *new_weights,
        *[entry[0] for entry in moment_list],
        *[entry[1] for entry in moment_list],
        *[weight.astype(BF16) for weight in new_weights],
        small_new,
        small_first,
        small_second,
        norms,
    )


def solution(mesh):
    whole = P()
    rows = P(None, "node", "hid")
    columns = P(None, "hid", "node")
    matrices = (rows, columns, rows, columns)
    in_specs = (
        P("node", None, None),
        P("node", None),
        P(("node", "hid"), None, None),
        P(("node", "hid")),
        P(("node", "hid"), None),
        P(),
        P("node"),
        P("node"),
        P("node", None),
        *matrices,
        *matrices,
        *matrices,
        whole,
        whole,
        whole,
        whole,
    )
    out_specs = (
        P(("node", "hid"), None, None),
        P(("node", "hid"), None, None),
        P(("node", "hid"), None),
        *matrices,
        *matrices,
        *matrices,
        *matrices,
        whole,
        whole,
        whole,
        whole,
    )
    return jax.shard_map(
        per_device, mesh=mesh, in_specs=in_specs, out_specs=out_specs, check_vma=False
    )
```

profile of v0, /device:TPU:0, one launch (start us, length us, event | category | flops | bytes accessed | tf_op | source)
XLA Modules:
  0.0 354.0 jit_solution(9578924139960651282)
XLA Ops:
  4.8 4.1 %collective-permute-start = (bf16[256,128]{1,0:T(8,128)(2,1)S(1)}, bf16[256,128]{1,0:T(8,128)(2,1)S(1)}, u32[]{:S(2)}, u32[]{:S(2)}) collective-permute-start(bf16[256,128]{1,0:T(8,128)(2,1)S(1)} %pad_maximum_fusion.25), channel_id=1, source_target_pairs={{0,16},{4,20},{8,24},{12,28},{16,0},{20,4},{24,8},{28,12},{1,17},{... | collective-permute-start | bytes 196616 | tf_op jit(solution)/shard_map/ppermute | solution.py:500
  22.4 3.1 collective-permute-done.1
  27.9 3.3 collective-permute-done.2
  53.8 6.1 %collective-permute-done.10 = bf16[2,2,2,192,128]{4,3,0,1,2:T(8,128)(2,1)S(1)} collective-permute-done((bf16[2,2,2,192,128]{4,3,0,1,2:T(8,128)(2,1)S(1)}, bf16[2,2,2,192,128]{4,3,0,1,2:T(8,128)(2,1)S(1)}, u32[]{:S(2)}, u32[]{:S(2)}) %collective-permute-start.10) | collective-permute-done | bytes 393248 | tf_op jit(solution)/shard_map/ppermute | solution.py:500
  75.0 10.3 %collective-permute-done.7 = bf16[2,2,2,448,128]{4,3,0,1,2:T(8,128)(2,1)} collective-permute-done((bf16[2,2,2,448,128]{4,3,0,1,2:T(8,128)(2,1)}, bf16[2,2,2,448,128]{4,3,0,1,2:T(8,128)(2,1)}, u32[]{:S(2)}, u32[]{:S(2)}) %collective-permute-start.7) | collective-permute-done | bytes 917536 | tf_op jit(solution)/shard_map/ppermute | solution.py:500
  89.9 11.7 %edge_forward.2 = (bf16[3,640,512]{2,1,0:T(8,128)(2,1)}, bf16[3,640,512]{2,1,0:T(8,128)(2,1)}, bf16[3,640,512]{2,1,0:T(8,128)(2,1)}, f32[3,640,1]{2,1,0:T(8,128)...) custom-call(bf16[8,4,256,128]{3,2,1,0:T(8,128)(2,1)} %bitcast.291, ...), custom_call_target="tpu_custom_call" | custom-call | flops 3806330880 | bytes 19926528 | tf_op jit(solution)/shard_map/edge_forward/pallas_call | solution.py:102
  108.4 6.4 %node_pass.2 = (bf16[3,160,512]{2,1,0:T(8,128)(2,1)}, bf16[3,160,512]{2,1,0:T(8,128)(2,1)}, bf16[3,160,512]{2,1,0:T(8,128)(2,1)}, bf16[3,160,512]{2,1,0:T(8,128)...) custom-call(bf16[8,4,192,128]{3,2,1,0:T(8,128)(2,1)} %bitcast.296, ...), custom_call_target="tpu_custom_call" | custom-call | flops 754974720 | bytes 8006528 | tf_op jit(solution)/shard_map/node_pass/pallas_call | solution.py:102
  117.8 2.8 collective-permute-start.19
  121.7 2.7 collective-permute-done.18
  130.6 10.9 %edge_forward.3 = (bf16[3,640,512]{2,1,0:T(8,128)(2,1)}, bf16[3,640,512]{2,1,0:T(8,128)(2,1)}, bf16[3,640,512]{2,1,0:T(8,128)(2,1)}, f32[3,640,1]{2,1,0:T(8,128)}, bf16[3,160,512]{2,1,0:T(8,128)(2,1)}) custom-call(bf16[8,4,448,128]{3,2,1,0:T(8,128)(2,1)} %bitcast.286, bf16[8,4,448,128]{3,2,1,0:T(8,128)(2,1)} %bitcast.287, bf16[3,240,512]{2,1,0:T(8,128)(2,1)} %copy-done.5, ...), custom_call_target="tpu_custom_call" | custom-call | flops 3806330880 | bytes 21106176 | tf_op jit(solution)/shard_map/edge_forward/pallas_call | solution.py:102
  144.4 10.0 %node_pass.3 = (bf16[3,160,512]{2,1,0:T(8,128)(2,1)}, bf16[3,160,512]{2,1,0:T(8,128)(2,1)}, f32[3,160,512]{2,1,0:T(8,128)}, bf16[8,4,192,128]{3,2,1,0:T(8,128)(2,1)}, f32[4,512]{1,0:T(4,128)}) custom-call(bf16[8,4,448,128]{3,2,1,0:T(8,128)(2,1)} %bitcast.288, bf16[3,240,512]{2,1,0:T(8,128)(2,1)} %copy-done.5, f32[3,160,512]{2,1,0:T(8,128)} %get-tuple-element.84.state, ...), custom_call_target="tpu_custom_call" | custom-call | flops 2264924160 | bytes 10429068 | tf_op jit(solution)/shard_map/node_pass/pallas_call | solution.py:102
  156.9 12.5 %edge_backward.2 = (bf16[3,640,512]{2,1,0:T(8,128)(2,1)}, bf16[3,640,512]{2,1,0:T(8,128)(2,1)}, bf16[3,400,512]{2,1,0:T(8,128)(2,1)}, f32[3,160,512]{2,1,0:T(8,1...) custom-call(bf16[8,4,448,128]{3,2,1,0:T(8,128)(2,1)} %bitcast.289, ...), custom_call_target="tpu_custom_call" | custom-call | flops 3586129920 | bytes 22820352 | tf_op jit(solution)/shard_map/edge_backward/pallas_call | solution.py:102
  170.4 2.7 collective-permute-start.25
  173.2 9.6 %edge_weight_grads.3 = bf16[8,4,448,128]{3,2,1,0:T(8,128)(2,1)} custom-call(bf16[3,640,512]{2,1,0:T(8,128)(2,1)} %get-tuple-element.85.low.edge_low, bf16[3,240,512]{2,1,0:T(8,128)(2,1)} %copy-done.5, bf16[3,640,512]{2,1,0:T(8,128)(2,1)} %get-tuple-element.129.hidden_low, bf16[3,400,512]{2,1,0:T(8,128)(2,1)} %get-tuple-element.130.at_rows, ...), custom_call_target="tpu_custom_call" | custom-call | flops 2013265920 | bytes 15073280 | tf_op jit(solution)/shard_map/edge_weight_grads/pallas_call | solution.py:102
  189.8 8.8 %node_backward.1 = (bf16[3,160,512]{2,1,0:T(8,128)(2,1)}, f32[3,160,512]{2,1,0:T(8,128)}, bf16[8,4,192,128]{3,2,1,0:T(8,128)(2,1)}, f32[4,512]{1,0:T(4,128)}) custom-call(bf16[8,4,192,128]{3,2,1,0:T(8,128)(2,1)} %bitcast.297, f32[3,160,512]{2,1,0:T(8,128)} %get-tuple-element.90.base, f32[3,160,512]{2,1,0:T(8,128)} %get-tuple-element.214.own, ...), custom_call_target="tpu_custom_call" | custom-call | flops 1509949440 | bytes 9808384 | tf_op jit(solution)/shard_map/node_backward/pallas_call | solution.py:102
  201.0 14.2 %edge_backward.3 = (bf16[3,640,512]{2,1,0:T(8,128)(2,1)}, bf16[3,640,512]{2,1,0:T(8,128)(2,1)}, bf16[3,400,512]{2,1,0:T(8,128)(2,1)}, f32[3,160,512]{2,1,0:T(8,1...) custom-call(bf16[8,4,256,128]{3,2,1,0:T(8,128)(2,1)} %bitcast.293, ...), custom_call_target="tpu_custom_call" | custom-call | flops 3586129920 | bytes 21640704 | tf_op jit(solution)/shard_map/edge_backward/pallas_call | solution.py:102
  216.9 4.7 %collective-permute-start.28 = (bf16[3,40,512]{2,1,0:T(8,128)(2,1)}, bf16[3,40,512]{2,1,0:T(8,128)(2,1)}, u32[]{:S(2)}, u32[]{:S(2)}) collective-permute-start(bf16[3,40,512]{2,1,0:T(8,128)(2,1)} %get-tuple-element.254), channel_id=1, source_target_pairs={{4,0},{8,4},{12,8},{16,12},{20,16},{24,20},{28,24},{0,28},{5,1},{9... | collective-permute-start | bytes 368648 | tf_op jit(solution)/shard_map/ppermute | solution.py:566
  229.4 13.3 %collective-permute-done.48 = bf16[2,2,2,192,128]{4,3,0,1,2:T(8,128)(2,1)S(1)} collective-permute-done((bf16[2,2,2,192,128]{4,3,0,1,2:T(8,128)(2,1)S(1)}, bf16[2,2,2,192,128]{4,3,0,1,2:T(8,128)(2,1)S(1)}, u32[]{:S(2)}, u32[]{:S(2)}) %collective-permute-start.48) | collective-permute-done | bytes 393248 | tf_op jit(solution)/shard_map/ppermute | solution.py:500
  242.9 7.5 %edge_weight_grads.2 = bf16[8,4,256,128]{3,2,1,0:T(8,128)(2,1)} custom-call(bf16[640,512]{1,0:T(8,128)(2,1)} %bitcast.301, bf16[3,240,512]{2,1,0:T(8,128)(2,1)} %pad_maximum_fusion.7.table, bf16[640,512]{1,0:T(8,128)(2,1)} %get-tuple-element.111.hidden_low, bf16[3,400,512]{2,1,0:T(8,128)(2,1)} %get-tuple-element.112.at_rows, ...), custom_call_target="tpu_custom_call" | custom-call | flops 2013265920 | bytes 9306112 | tf_op jit(solution)/shard_map/edge_weight_grads/pallas_call | solution.py:102
  252.3 9.3 %collective-permute-done.43 = bf16[2,2,2,448,128]{4,3,0,1,2:T(8,128)(2,1)S(1)} collective-permute-done((bf16[2,2,2,448,128]{4,3,0,1,2:T(8,128)(2,1)}, bf16[2,2,2,448,128]{4,3,0,1,2:T(8,128)(2,1)S(1)}, u32[]{:S(2)}, u32[]{:S(2)}) %collective-permute-start.43) | collective-permute-done | bytes 917536 | tf_op jit(solution)/shard_map/ppermute | solution.py:500
  263.5 2.8 collective-permute-done.50
  266.3 2.7 collective-permute-start.51
  269.0 4.7 %collective-permute-done.44 = bf16[2,2,448,128]{3,2,0,1:T(8,128)(2,1)S(1)} collective-permute-done((bf16[2,2,448,128]{3,2,0,1:T(8,128)(2,1)S(1)}, bf16[2,2,448,128]{3,2,0,1:T(8,128)(2,1)S(1)}, u32[]{:S(2)}, u32[]{:S(2)}) %collective-permute-start.44) | collective-permute-done | bytes 458784 | tf_op jit(solution)/shard_map/ppermute | solution.py:500
  275.8 4.2 %collective-permute-done.45 = bf16[2,448,128]{2,1,0:T(8,128)(2,1)S(1)} collective-permute-done((bf16[2,448,128]{2,1,0:T(8,128)(2,1)S(1)}, bf16[2,448,128]{2,1,0:T(8,128)(2,1)S(1)}, u32[]{:S(2)}, u32[]{:S(2)}) %collective-permute-start.45) | collective-permute-done | bytes 229408 | tf_op jit(solution)/shard_map/ppermute | solution.py:500
  280.1 4.1 %collective-permute-start.46 = (bf16[448,128]{1,0:T(8,128)(2,1)S(1)}, bf16[448,128]{1,0:T(8,128)(2,1)S(1)}, u32[]{:S(2)}, u32[]{:S(2)}) collective-permute-start(bf16[448,128]{1,0:T(8,128)(2,1)S(1)} %fusion.23), channel_id=1, source_target_pairs={{0,16},{4,20},{8,24},{12,28},{16,0},{20,4},{24,8},{28,12},{1,17},{... | collective-permute-start | bytes 344072 | tf_op jit(solution)/shard_map/ppermute | solution.py:500
  284.2 4.0 %collective-permute-done.46 = bf16[448,128]{1,0:T(8,128)(2,1)S(1)} collective-permute-done((bf16[448,128]{1,0:T(8,128)(2,1)S(1)}, bf16[448,128]{1,0:T(8,128)(2,1)S(1)}, u32[]{:S(2)}, u32[]{:S(2)}) %collective-permute-start.46) | collective-permute-done | bytes 114720 | tf_op jit(solution)/shard_map/ppermute | solution.py:500
  298.1 11.0 %collective-permute-done.35 = f32[17,512]{1,0:T(8,128)S(1)} collective-permute-done((f32[17,512]{1,0:T(8,128)S(1)}, f32[17,512]{1,0:T(8,128)S(1)}, u32[]{:S(2)}, u32[]{:S(2)}) %collective-permute-start.35) | collective-permute-done | bytes 34848 | tf_op jit(solution)/shard_map/ppermute | solution.py:500
  312.4 5.9 %collective-permute-done.37 = f32[17,512]{1,0:T(8,128)S(1)} collective-permute-done((f32[17,512]{1,0:T(8,128)S(1)}, f32[17,512]{1,0:T(8,128)S(1)}, u32[]{:S(2)}, u32[]{:S(2)}) %collective-permute-start.37) | collective-permute-done | bytes 34848 | tf_op jit(solution)/shard_map/ppermute | solution.py:500
  328.2 3.6 %collective-permute-done.41 = f32[17,512]{1,0:T(8,128)S(1)} collective-permute-done((f32[17,512]{1,0:T(8,128)S(1)}, f32[17,512]{1,0:T(8,128)S(1)}, u32[]{:S(2)}, u32[]{:S(2)}) %collective-permute-start.41) | collective-permute-done | bytes 34848 | tf_op jit(solution)/shard_map/ppermute | solution.py:500
  335.1 3.1 collective-permute-done.53
  342.1 3.3 collective-permute-done.55
  345.7 4.1 %collective-permute-done.56 = f32[2,4]{1,0:T(2,128)S(1)} collective-permute-done((f32[2,4]{1,0:T(2,128)S(1)}, f32[2,4]{1,0:T(2,128)S(1)}, u32[]{:S(2)}, u32[]{:S(2)}) %collective-permute-start.56) | collective-permute-done | bytes 64 | tf_op jit(solution)/shard_map/ppermute | solution.py:500
  (384 shorter events, 143.4 us)
Async XLA Ops:
  4.8 15.5 %collective-permute-start = (bf16[256,128]{1,0:T(8,128)(2,1)S(1)}, bf16[256,128]{1,0:T(8,128)(2,1)S(1)}, u32[]{:S(2)}, u32[]{:S(2)}) collective-permute-start(bf16[256,128]{1,0:T(8,128)(2,1)S(1)} %pad_maximum_fusion.25), channel_id=1, source_target_pairs={{0,16},{4,20},{8,24},{12,28},{16,0},{20,4},{24,8},{28,12},{1,17},{... | collective-permute-start | bytes 196616 | tf_op jit(solution)/shard_map/ppermute | solution.py:500
  12.9 57.9 %collective-permute-start.13 = (bf16[3,40,512]{2,1,0:T(8,128)(2,1)}, bf16[3,40,512]{2,1,0:T(8,128)(2,1)}, u32[]{:S(2)}, u32[]{:S(2)}) collective-permute-start(bf16[3,40,512]{2,1,0:T(8,128)(2,1)} %get-tuple-element.260), channel_id=1, source_target_pairs={{4,0},{8,4},{12,8},{16,12},{20,16},{24,20},{28,24},{0,28},{5,1},{9... | collective-permute-start | bytes 368648 | tf_op jit(solution)/shard_map/ppermute | solution.py:566
  15.1 55.7 %collective-permute-start.12 = (bf16[3,40,512]{2,1,0:T(8,128)(2,1)}, bf16[3,40,512]{2,1,0:T(8,128)(2,1)}, u32[]{:S(2)}, u32[]{:S(2)}) collective-permute-start(bf16[3,40,512]{2,1,0:T(8,128)(2,1)} %get-tuple-element.259), channel_id=1, source_target_pairs={{0,4},{4,8},{8,12},{12,16},{16,20},{20,24},{24,28},{28,0},{1,5},{5... | collective-permute-start | bytes 368648 | tf_op jit(solution)/shard_map/ppermute | solution.py:565
  48.3 11.6 %collective-permute-start.10 = (bf16[2,2,2,192,128]{4,3,0,1,2:T(8,128)(2,1)S(1)}, bf16[2,2,2,192,128]{4,3,0,1,2:T(8,128)(2,1)S(1)}, u32[]{:S(2)}, u32[]{:S(2)}) collective-permute-start(bf16[2,2,2,192,128]{4,3,0,1,2:T(8,128)(2,1)S(1)} %pad_maximum_fusion.13), channel_id=1, source_target_pairs={{0,2},{1,3},{2,0},{3,1},{4,6},{5,7},{6,4},{7,5},{8,10},{9,11},{10,... | collective-permute-start | bytes 1179656 | tf_op jit(solution)/shard_map/ppermute | solution.py:500
  50.6 10.5 %collective-permute-start.6 = (bf16[2,2,448,128]{3,2,0,1:T(8,128)(2,1)S(1)}, bf16[2,2,448,128]{3,2,0,1:T(8,128)(2,1)S(1)}, u32[]{:S(2)}, u32[]{:S(2)}) collective-permute-start(bf16[2,2,448,128]{3,2,0,1:T(8,128)(2,1)S(1)} %pad_maximum_fusion.12), channel_id=1, source_target_pairs={{0,4},{4,0},{8,12},{12,8},{16,20},{20,16},{24,28},{28,24},{1,5},{5... | collective-permute-start | bytes 1376264 | tf_op jit(solution)/shard_map/ppermute | solution.py:500
  52.2 13.3 %collective-permute-start.15 = (bf16[2,2,2,256,128]{4,3,0,1,2:T(8,128)(2,1)S(1)}, bf16[2,2,2,256,128]{4,3,0,1,2:T(8,128)(2,1)S(1)}, u32[]{:S(2)}, u32[]{:S(2)}) collective-permute-start(bf16[2,2,2,256,128]{4,3,0,1,2:T(8,128)(2,1)S(1)} %pad_maximum_fusion.9), channel_id=1, source_target_pairs={{0,2},{1,3},{2,0},{3,1},{4,6},{5,7},{6,4},{7,5},{8,10},{9,11},{10,... | collective-permute-start | bytes 1572872 | tf_op jit(solution)/shard_map/ppermute | solution.py:500
  61.0 11.7 %collective-permute-start.11 = (bf16[2,2,2,2,192,128]{5,4,0,1,2,3:T(8,128)(2,1)}, bf16[2,2,2,2,192,128]{5,4,0,1,2,3:T(8,128)(2,1)}, u32[]{:S(2)}, u32[]{:S(2)}) collective-permute-start(bf16[2,2,2,2,192,128]{5,4,0,1,2,3:T(8,128)(2,1)} %pad_maximum_fusion.6), channel_id=1, source_target_pairs={{0,1},{1,0},{2,3},{3,2},{4,5},{5,4},{6,7},{7,6},{8,9},{9,8},{10,11... | collective-permute-start | bytes 2359304 | tf_op jit(solution)/shard_map/ppermute | solution.py:500
  62.3 23.0 %collective-permute-start.7 = (bf16[2,2,2,448,128]{4,3,0,1,2:T(8,128)(2,1)}, bf16[2,2,2,448,128]{4,3,0,1,2:T(8,128)(2,1)}, u32[]{:S(2)}, u32[]{:S(2)}) collective-permute-start(bf16[2,2,2,448,128]{4,3,0,1,2:T(8,128)(2,1)} %pad_maximum_fusion.5), channel_id=1, source_target_pairs={{0,2},{1,3},{2,0},{3,1},{4,6},{5,7},{6,4},{7,5},{8,10},{9,11},{10,... | collective-permute-start | bytes 2752520 | tf_op jit(solution)/shard_map/ppermute | solution.py:500
  66.7 20.2 %collective-permute-start.16 = (bf16[2,2,2,2,256,128]{5,4,0,1,2,3:T(8,128)(2,1)}, bf16[2,2,2,2,256,128]{5,4,0,1,2,3:T(8,128)(2,1)}, u32[]{:S(2)}, u32[]{:S(2)}) collective-permute-start(bf16[2,2,2,2,256,128]{5,4,0,1,2,3:T(8,128)(2,1)} %pad_maximum_fusion.4), channel_id=1, source_target_pairs={{0,1},{1,0},{2,3},{3,2},{4,5},{5,4},{6,7},{7,6},{8,9},{9,8},{10,11... | collective-permute-start | bytes 3145736 | tf_op jit(solution)/shard_map/ppermute | solution.py:500
  86.8 39.3 %collective-permute-start.8 = (bf16[2,2,2,2,448,128]{5,4,0,1,2,3:T(8,128)(2,1)S(1)}, bf16[2,2,2,2,448,128]{5,4,0,1,2,3:T(8,128)(2,1)}, u32[]{:S(2)}, u32[]{:S(2)}) collective-permute-start(bf16[2,2,2,2,448,128]{5,4,0,1,2,3:T(8,128)(2,1)S(1)} %pad_maximum_fusion.2), channel_id=1, source_target_pairs={{0,1},{1,0},{2,3},{3,2},{4,5},{5,4},{6,7},{7,6},{8,9},{9,8},{10,11... | collective-permute-start | bytes 5505032 | tf_op jit(solution)/shard_map/ppermute | solution.py:500
  107.5 35.0 %collective-permute-start.22 = (bf16[2,40,3,512]{3,1,2,0:T(8,128)(2,1)S(1)}, bf16[2,40,3,512]{3,1,2,0:T(8,128)(2,1)S(1)}, u32[]{:S(2)}, u32[]{:S(2)}) collective-permute-start(bf16[2,40,3,512]{3,1,2,0:T(8,128)(2,1)S(1)} %pad_maximum_fusion.15), channel_id=1, source_target_pairs={{0,1},{1,0},{2,3},{3,2},{4,5},{5,4},{6,7},{7,6},{8,9},{9,8},{10,11... | collective-permute-start | bytes 737288 | tf_op jit(solution)/shard_map/ppermute | solution.py:500
  115.8 8.6 %collective-permute-start.18 = (bf16[3,40,512]{2,1,0:T(8,128)(2,1)S(1)}, bf16[3,40,512]{2,1,0:T(8,128)(2,1)S(1)}, u32[]{:S(2)}, u32[]{:S(2)}) collective-permute-start(bf16[3,40,512]{2,1,0:T(8,128)(2,1)S(1)} %get-tuple-element.258), channel_id=1, source_target_pairs={{0,4},{4,8},{8,12},{12,16},{16,20},{20,24},{24,28},{28,0},{1,5},{5... | collective-permute-start | bytes 368648 | tf_op jit(solution)/shard_map/ppermute | solution.py:565
  117.8 8.3 %collective-permute-start.19 = (bf16[3,40,512]{2,1,0:T(8,128)(2,1)S(1)}, bf16[3,40,512]{2,1,0:T(8,128)(2,1)S(1)}, u32[]{:S(2)}, u32[]{:S(2)}) collective-permute-start(bf16[3,40,512]{2,1,0:T(8,128)(2,1)S(1)} %get-tuple-element.257), channel_id=1, source_target_pairs={{4,0},{8,4},{12,8},{16,12},{20,16},{24,20},{28,24},{0,28},{5,1},{9... | collective-permute-start | bytes 368648 | tf_op jit(solution)/shard_map/ppermute | solution.py:566
  155.3 32.7 %collective-permute-start.23 = (bf16[40,3,512]{2,0,1:T(8,128)(2,1)S(1)}, bf16[40,3,512]{2,0,1:T(8,128)(2,1)S(1)}, u32[]{:S(2)}, u32[]{:S(2)}) collective-permute-start(bf16[40,3,512]{2,0,1:T(8,128)(2,1)S(1)} %dynamic-slice_bitcast_fusion.2), channel_id=1, source_target_pairs={{0,2},{1,3},{2,0},{3,1},{4,6},{5,7},{6,4},{7,5},{8,10},{9,11},{10,... | collective-permute-start | bytes 368648 | tf_op jit(solution)/shard_map/ppermute | solution.py:500
  170.4 12.4 %collective-permute-start.25 = (bf16[3,40,512]{2,1,0:T(8,128)(2,1)S(1)}, bf16[3,40,512]{2,1,0:T(8,128)(2,1)S(1)}, u32[]{:S(2)}, u32[]{:S(2)}) collective-permute-start(bf16[3,40,512]{2,1,0:T(8,128)(2,1)S(1)} %get-tuple-element.256), channel_id=1, source_target_pairs={{4,0},{8,4},{12,8},{16,12},{20,16},{24,20},{28,24},{0,28},{5,1},{9... | collective-permute-start | bytes 368648 | tf_op jit(solution)/shard_map/ppermute | solution.py:566
  173.2 9.7 %collective-permute-start.24 = (bf16[3,40,512]{2,1,0:T(8,128)(2,1)S(1)}, bf16[3,40,512]{2,1,0:T(8,128)(2,1)S(1)}, u32[]{:S(2)}, u32[]{:S(2)}) collective-permute-start(bf16[3,40,512]{2,1,0:T(8,128)(2,1)S(1)} %get-tuple-element.255), channel_id=1, source_target_pairs={{0,4},{4,8},{8,12},{12,16},{16,20},{20,24},{24,28},{28,0},{1,5},{5... | collective-permute-start | bytes 368648 | tf_op jit(solution)/shard_map/ppermute | solution.py:565
  186.9 39.0 %collective-permute-start.42 = (bf16[2,2,2,2,448,128]{5,4,0,1,2,3:T(8,128)(2,1)}, bf16[2,2,2,2,448,128]{5,4,0,1,2,3:T(8,128)(2,1)}, u32[]{:S(2)}, u32[]{:S(2)}) collective-permute-start(bf16[2,2,2,2,448,128]{5,4,0,1,2,3:T(8,128)(2,1)} %bitcast.280), channel_id=1, source_target_pairs={{0,1},{1,0},{2,3},{3,2},{4,5},{5,4},{6,7},{7,6},{8,9},{9,8},{10,11... | collective-permute-start | bytes 5505032 | tf_op jit(solution)/shard_map/ppermute | solution.py:500
  200.2 23.8 %collective-permute-start.47 = (bf16[2,2,2,2,192,128]{5,4,0,1,2,3:T(8,128)(2,1)S(1)}, bf16[2,2,2,2,192,128]{5,4,0,1,2,3:T(8,128)(2,1)S(1)}, u32[]{:S(2)}, u32[]{:S(2)}) collective-permute-start(bf16[2,2,2,2,192,128]{5,4,0,1,2,3:T(8,128)(2,1)S(1)} %bitcast.306), channel_id=1, source_target_pairs={{0,1},{1,0},{2,3},{3,2},{4,5},{5,4},{6,7},{7,6},{8,9},{9,8},{10,11... | collective-permute-start | bytes 2359304 | tf_op jit(solution)/shard_map/ppermute | solution.py:500
  216.9 45.0 %collective-permute-start.28 = (bf16[3,40,512]{2,1,0:T(8,128)(2,1)}, bf16[3,40,512]{2,1,0:T(8,128)(2,1)}, u32[]{:S(2)}, u32[]{:S(2)}) collective-permute-start(bf16[3,40,512]{2,1,0:T(8,128)(2,1)} %get-tuple-element.254), channel_id=1, source_target_pairs={{4,0},{8,4},{12,8},{16,12},{20,16},{24,20},{28,24},{0,28},{5,1},{9... | collective-permute-start | bytes 368648 | tf_op jit(solution)/shard_map/ppermute | solution.py:566
  221.6 40.5 %collective-permute-start.27 = (bf16[3,40,512]{2,1,0:T(8,128)(2,1)}, bf16[3,40,512]{2,1,0:T(8,128)(2,1)}, u32[]{:S(2)}, u32[]{:S(2)}) collective-permute-start(bf16[3,40,512]{2,1,0:T(8,128)(2,1)} %get-tuple-element.253), channel_id=1, source_target_pairs={{0,4},{4,8},{8,12},{12,16},{16,20},{20,24},{24,28},{28,0},{1,5},{5... | collective-permute-start | bytes 368648 | tf_op jit(solution)/shard_map/ppermute | solution.py:565
  223.5 72.8 %collective-permute-start.31 = (bf16[320,512]{1,0:T(8,128)(2,1)}, bf16[320,512]{1,0:T(8,128)(2,1)}, u32[]{:S(2)}, u32[]{:S(2)}) collective-permute-start(bf16[320,512]{1,0:T(8,128)(2,1)} %fusion.10), channel_id=1, source_target_pairs={{0,2},{1,3},{2,0},{3,1},{4,6},{5,7},{6,4},{7,5},{8,10},{9,11},{10,... | collective-permute-start | bytes 983048 | tf_op jit(solution)/shard_map/ppermute | solution.py:500
  224.2 18.5 %collective-permute-start.48 = (bf16[2,2,2,192,128]{4,3,0,1,2:T(8,128)(2,1)S(1)}, bf16[2,2,2,192,128]{4,3,0,1,2:T(8,128)(2,1)S(1)}, u32[]{:S(2)}, u32[]{:S(2)}) collective-permute-start(bf16[2,2,2,192,128]{4,3,0,1,2:T(8,128)(2,1)S(1)} %fusion.9), channel_id=1, source_target_pairs={{0,2},{1,3},{2,0},{3,1},{4,6},{5,7},{6,4},{7,5},{8,10},{9,11},{10,... | collective-permute-start | bytes 1179656 | tf_op jit(solution)/shard_map/ppermute | solution.py:500
  228.9 32.8 %collective-permute-start.43 = (bf16[2,2,2,448,128]{4,3,0,1,2:T(8,128)(2,1)}, bf16[2,2,2,448,128]{4,3,0,1,2:T(8,128)(2,1)S(1)}, u32[]{:S(2)}, u32[]{:S(2)}) collective-permute-start(bf16[2,2,2,448,128]{4,3,0,1,2:T(8,128)(2,1)} %fusion.1), channel_id=1, source_target_pairs={{0,2},{1,3},{2,0},{3,1},{4,6},{5,7},{6,4},{7,5},{8,10},{9,11},{10,... | collective-permute-start | bytes 2752520 | tf_op jit(solution)/shard_map/ppermute | solution.py:500
  242.8 9.3 %collective-permute-start.49 = (bf16[2,2,192,128]{3,2,0,1:T(8,128)(2,1)S(1)}, bf16[2,2,192,128]{3,2,0,1:T(8,128)(2,1)S(1)}, u32[]{:S(2)}, u32[]{:S(2)}) collective-permute-start(bf16[2,2,192,128]{3,2,0,1:T(8,128)(2,1)S(1)} %fusion.20), channel_id=1, source_target_pairs={{0,4},{4,0},{8,12},{12,8},{16,20},{20,16},{24,28},{28,24},{1,5},{5... | collective-permute-start | bytes 589832 | tf_op jit(solution)/shard_map/ppermute | solution.py:500
  252.2 39.9 %collective-permute-start.32 = (bf16[2,2,2,2,256,128]{5,4,0,1,2,3:T(8,128)(2,1)S(1)}, bf16[2,2,2,2,256,128]{5,4,0,1,2,3:T(8,128)(2,1)}, u32[]{:S(2)}, u32[]{:S(2)}) collective-permute-start(bf16[2,2,2,2,256,128]{5,4,0,1,2,3:T(8,128)(2,1)S(1)} %bitcast.305), channel_id=1, source_target_pairs={{0,1},{1,0},{2,3},{3,2},{4,5},{5,4},{6,7},{7,6},{8,9},{9,8},{10,11... | collective-permute-start | bytes 3145736 | tf_op jit(solution)/shard_map/ppermute | solution.py:500
  261.9 11.9 %collective-permute-start.44 = (bf16[2,2,448,128]{3,2,0,1:T(8,128)(2,1)S(1)}, bf16[2,2,448,128]{3,2,0,1:T(8,128)(2,1)S(1)}, u32[]{:S(2)}, u32[]{:S(2)}) collective-permute-start(bf16[2,2,448,128]{3,2,0,1:T(8,128)(2,1)S(1)} %fusion.7), channel_id=1, source_target_pairs={{0,4},{4,0},{8,12},{12,8},{16,20},{20,16},{24,28},{28,24},{1,5},{5... | collective-permute-start | bytes 1376264 | tf_op jit(solution)/shard_map/ppermute | solution.py:500
  266.3 9.5 %collective-permute-start.51 = (bf16[192,128]{1,0:T(8,128)(2,1)S(1)}, bf16[192,128]{1,0:T(8,128)(2,1)S(1)}, u32[]{:S(2)}, u32[]{:S(2)}) collective-permute-start(bf16[192,128]{1,0:T(8,128)(2,1)S(1)} %fusion.39), channel_id=1, source_target_pairs={{0,16},{4,20},{8,24},{12,28},{16,0},{20,4},{24,8},{28,12},{1,17},{... | collective-permute-start | bytes 147464 | tf_op jit(solution)/shard_map/ppermute | solution.py:500
  280.1 8.1 %collective-permute-start.46 = (bf16[448,128]{1,0:T(8,128)(2,1)S(1)}, bf16[448,128]{1,0:T(8,128)(2,1)S(1)}, u32[]{:S(2)}, u32[]{:S(2)}) collective-permute-start(bf16[448,128]{1,0:T(8,128)(2,1)S(1)} %fusion.23), channel_id=1, source_target_pairs={{0,16},{4,20},{8,24},{12,28},{16,0},{20,4},{24,8},{28,12},{1,17},{... | collective-permute-start | bytes 344072 | tf_op jit(solution)/shard_map/ppermute | solution.py:500
  293.7 15.4 %collective-permute-start.34 = (bf16[2,2,2,256,128]{4,3,0,1,2:T(8,128)(2,1)S(1)}, bf16[2,2,2,256,128]{4,3,0,1,2:T(8,128)(2,1)S(1)}, u32[]{:S(2)}, u32[]{:S(2)}) collective-permute-start(bf16[2,2,2,256,128]{4,3,0,1,2:T(8,128)(2,1)S(1)} %fusion.6), channel_id=1, source_target_pairs={{0,2},{1,3},{2,0},{3,1},{4,6},{5,7},{6,4},{7,5},{8,10},{9,11},{10,... | collective-permute-start | bytes 1572872 | tf_op jit(solution)/shard_map/ppermute | solution.py:500
  294.5 16.0 %collective-permute-start.29 = (bf16[3,160,512]{2,1,0:T(8,128)(2,1)S(1)}, bf16[3,160,512]{2,1,0:T(8,128)(2,1)S(1)}, u32[]{:S(2)}, u32[]{:S(2)}) collective-permute-start(bf16[3,160,512]{2,1,0:T(8,128)(2,1)S(1)} %get-tuple-element.211), channel_id=1, source_target_pairs={{0,1},{1,0},{2,3},{3,2},{4,5},{5,4},{6,7},{7,6},{8,9},{9,8},{10,11... | collective-permute-start | bytes 1474568 | tf_op jit(solution)/shard_map/ppermute | solution.py:500
  294.8 14.4 %collective-permute-start.35 = (f32[17,512]{1,0:T(8,128)S(1)}, f32[17,512]{1,0:T(8,128)S(1)}, u32[]{:S(2)}, u32[]{:S(2)}) collective-permute-start(f32[17,512]{1,0:T(8,128)S(1)} %add.319), channel_id=1, source_target_pairs={{0,2},{1,3},{2,0},{3,1},{4,6},{5,7},{6,4},{7,5},{8,10},{9,11},{10,... | collective-permute-start | bytes 104456 | tf_op jit(solution)/shard_map/ppermute | solution.py:500
  309.3 9.0 %collective-permute-start.36 = (bf16[2,2,256,128]{3,2,0,1:T(8,128)(2,1)S(1)}, bf16[2,2,256,128]{3,2,0,1:T(8,128)(2,1)S(1)}, u32[]{:S(2)}, u32[]{:S(2)}) collective-permute-start(bf16[2,2,256,128]{3,2,0,1:T(8,128)(2,1)S(1)} %fusion.11), channel_id=1, source_target_pairs={{0,4},{4,0},{8,12},{12,8},{16,20},{20,16},{24,28},{28,24},{1,5},{5... | collective-permute-start | bytes 786440 | tf_op jit(solution)/shard_map/ppermute | solution.py:500
  (85 other events, 939.0 us)
where the time goes:
time: 355 us; the launch traced here: 354 us
  waiting for transfers between devices  111 us (31%)
  Pallas kernels  91.7 us (26%)
  starting transfers between devices  65.2 us (18%)
  other arithmetic  50.2 us (14%)
  local copies, waits for them, and re-layouts  30.7 us (9%)
    ppermute x49, waiting for transfers between devices, swap(): lax.ppermute(values, axis, [(i, i ^ offset) for i in range(lax.axis_size(...  107 us
    pallas_call x9, Pallas kernels, run_kernel(): pl.pallas_call(kernel, name=name, grid=(samples,), in_specs=in_specs, out...  91.7 us
    ppermute x49, starting transfers between devices, swap(): lax.ppermute(values, axis, [(i, i ^ offset) for i in range(lax.axis_size(...  50.7 us
    another operation x32, other arithmetic, double_up(): return jnp.stack([low, high], axis=place)  14.1 us
    ppermute x4, starting transfers between devices, to_neighbours(): from_next = lax.ppermute(rows[:, :halo_width], 'node', back)  12.6 us
  transfers between devices with their start and end apart: 57, of which 27 were waited for; matrix products, arithmetic and copies ran while one was open for 20% of the time, Pallas kernels for 23%

commit v1 on v0

--- a/solution.py
+++ b/solution.py
@@ -59,20 +59,22 @@
     return jnp.sum(values, axis=0, keepdims=True)
 
 
-def assemble(source, rows, offset, target):
-    nodes, hids, _, width = source.shape
+def assemble(source, order, rows, offset, target):
+    width = source.shape[2]
+    nodes, hids = target.shape[0] // rows, target.shape[1] // width
     for i in range(nodes):
         for j in range(hids):
             target[i * rows : (i + 1) * rows, j * width : (j + 1) * width] = source[
-                i, j, offset : offset + rows, :
+                order[i * hids + j], offset : offset + rows, :
             ]
 
 
-def pack(values, rows, offset, target):
-    nodes, hids, _, width = target.shape
+def pack(values, order, rows, offset, target):
+    width = target.shape[2]
+    nodes, hids = values.shape[0] // rows, values.shape[1] // width
     for i in range(nodes):
         for j in range(hids):
-            target[i, j, offset : offset + rows, :] = values[
+            target[order[i * hids + j], offset : offset + rows, :] = values[
                 i * rows : (i + 1) * rows, j * width : (j + 1) * width
             ].astype(target.dtype)
 
@@ -87,8 +89,12 @@
 
 
 def weight_block(array, rows, place):
-    nodes, hids, _, width = array.shape
-    return pl.BlockSpec((nodes, hids, rows, width), lambda s: (0, 0, place, 0))
+    blocks, _, width = array.shape
+    return pl.BlockSpec((blocks, rows, width), lambda s: (0, place, 0))
+
+
+def in_scalars():
+    return pl.BlockSpec(memory_space=pltpu.SMEM)
 
 
 def shape_of(shape, dtype):
@@ -124,12 +130,12 @@
     return (result, constant(result))
 
 
-def edge_forward(first, second, table, edge_low, edge_state, at_both, at_nodes, params, node_total, last):
+def edge_forward(order, first, second, table, edge_low, edge_state, at_both, at_nodes, params, node_total, last):
     samples, table_total, latent = table.shape
     edges = edge_low.shape[1]
     alike = edge_low.shape[0] == 1
 
-    def kernel(w1, w2, table, low, state, both, nodes, params, pre, act, normed, inverse, *rest):
+    def kernel(order, w1, w2, table, low, state, both, nodes, params, pre, act, normed, inverse, *rest):
         if last:
             pooled, w1s, w2s, projected = rest
         else:
@@ -137,8 +143,8 @@
 
         @pl.when(pl.program_id(0) == 0)
         def _():
-            assemble(w1, w1.shape[2], 0, w1s)
-            assemble(w2, w2.shape[2], 0, w2s)
+            assemble(w1, order, w1.shape[1], 0, w1s)
+            assemble(w2, order, w2.shape[1], 0, w2s)
 
         rows = table[0]
         projected[:table_total] = matmul(rows, w1s[latent : 2 * latent]).astype(BF16)
@@ -151,7 +157,7 @@
         scaled, scale = norm_forward(output)
         normed[0] = scaled.astype(BF16)
         inverse[0] = scale
-        state_new = state[0] + scaled * params[2:3] + params[3:4]
+        state_new = state[0].astype(F32) + scaled * params[2:3] + params[3:4]
         low_new = state_new.astype(BF16)
         if not last:
             new_state[0] = state_new
@@ -168,8 +174,9 @@
         kernel,
         "edge_forward",
         samples,
-        [first[0], second[0], table, edge_low, edge_state, at_both, at_nodes, params],
+        [order, first[0], second[0], table, edge_low, edge_state, at_both, at_nodes, params],
         [
+            in_scalars(),
             weight_block(*first),
             weight_block(*second),
             per_sample(table),
@@ -189,12 +196,12 @@
     )
 
 
-def edge_backward(first, second, pooled_grad, edge_grad, normed, inverse, pre, at_receiver, at_both_t, gain, last, node_total):
+def edge_backward(order, first, second, pooled_grad, edge_grad, normed, inverse, pre, at_receiver, at_both_t, gain, last, node_total):
     samples, edges, latent = normed.shape
     at_total = at_both_t.shape[0]
     table_total = at_total - node_total
 
-    def kernel(w1, w2, upstream, *rest):
+    def kernel(order, w1, w2, upstream, *rest):
         if not last:
             later, rest = rest[0], rest[1:]
         normed, inverse, pre, receiver, both_t, gain, low, hidden_low, at_rows, partial, returned, grad_out, minor = rest[:13]
@@ -206,8 +213,8 @@
 
         @pl.when(step == 0)
         def _():
-            assemble(w1, w1.shape[2], 0, w1s)
-            assemble(w2, w2.shape[2], 0, w2s)
+            assemble(w1, order, w1.shape[1], 0, w1s)
+            assemble(w2, order, w2.shape[1], 0, w2s)
             minor[...] = jnp.zeros_like(minor)
 
         grad = matmul(receiver[...], upstream[0])
@@ -260,8 +267,8 @@
         shared((4, latent), F32),
     ]
     scratch = [pltpu.VMEM((3 * latent, latent), BF16), pltpu.VMEM((latent, latent), BF16)]
-    inputs = [first[0], second[0], pooled_grad]
-    specs = [weight_block(*first), weight_block(*second), per_sample(pooled_grad)]
+    inputs = [order, first[0], second[0], pooled_grad]
+    specs = [in_scalars(), weight_block(*first), weight_block(*second), per_sample(pooled_grad)]
     if not last:
         outputs.append(shared((edges, latent), BF16))
         scratch.append(pltpu.VMEM((edges, latent), F32))
@@ -288,13 +295,13 @@
     )
 
 
-def edge_weight_grads(edge_low, table, hidden_low, at_rows, low, act, node_total, nodes, hids, width, packed_before):
+def edge_weight_grads(order, edge_low, table, hidden_low, at_rows, low, act, node_total, nodes, width, packed_before):
     samples, table_total, latent = table.shape
     alike = edge_low.ndim == 2
     first_rows, second_rows = 3 * latent // nodes, latent // nodes
-    offset = 0 if packed_before is None else packed_before.shape[2]
-
-    def kernel(edge_low, table, hidden_low, at_rows, low, act, *rest):
+    offset = 0 if packed_before is None else packed_before.shape[1]
+
+    def kernel(order, edge_low, table, hidden_low, at_rows, low, act, *rest):
         if packed_before is not None:
             before, rest = rest[0], rest[1:]
         packed, first, second = rest
@@ -305,7 +312,7 @@
             first[...] = jnp.zeros_like(first)
             second[...] = jnp.zeros_like(second)
             if packed_before is not None:
-                packed[:, :, :offset, :] = before[...]
+                packed[:, :offset, :] = before[...]
             if alike:
                 first[:latent] = matmul_tn(edge_low[...], hidden_low[...])
 
@@ -317,12 +324,12 @@
 
         @pl.when(step == samples - 1)
         def _():
-            pack(first, first_rows, offset, packed)
-            pack(second, second_rows, offset + first_rows, packed)
+            pack(first, order, first_rows, offset, packed)
+            pack(second, order, second_rows, offset + first_rows, packed)
 
     of_edges = constant if alike else per_sample
-    inputs = [edge_low, table, hidden_low, at_rows, low, act]
-    specs = [of_edges(edge_low), per_sample(table), of_edges(hidden_low), per_sample(at_rows), per_sample(low), per_sample(act)]
+    inputs = [order, edge_low, table, hidden_low, at_rows, low, act]
+    specs = [in_scalars(), of_edges(edge_low), per_sample(table), of_edges(hidden_low), per_sample(at_rows), per_sample(low), per_sample(act)]
     if packed_before is not None:
         inputs.append(packed_before)
         specs.append(constant(packed_before))
@@ -332,163 +339,143 @@
         samples,
         inputs,
         specs,
-        [shared((nodes, hids, offset + first_rows + second_rows, width), BF16)],
+        [shared((order.shape[0], offset + first_rows + second_rows, width), BF16)],
         [pltpu.VMEM((3 * latent, latent), F32), pltpu.VMEM((latent, latent), F32)],
         4 * low.size * latent,
     )[0]
 
 
-def node_pass(weights, table, state, pooled_pair, params, at_halo, target, scaling, mask, node_total):
-    samples, _, latent = table.shape
+def node_pass(order, weights, nodes, node_low, state, pooled_pair, params, at_halo, target, scaling, mask):
+    samples, node_total, latent = node_low.shape
     array, rows, place = weights
-    nodes, hids, _, width = array.shape
     second_rows = latent // nodes
     first_rows = rows - second_rows
+    count = samples * node_total
     last = target is not None
 
-    def kernel(w, table, state, pooled_own, pooled_other, params, *rest):
+    def kernel(order, w, node_low, state, pooled_own, pooled_other, params, *rest):
         if last:
             target, scaling, mask, new_low, upstream, input_grad, packed, minor, w1s, w2s, first, second = rest
         else:
             at_halo, pooled_out, pre, act, normed, inverse, new_state, new_low, halo, w1s, w2s = rest
-        step = pl.program_id(0)
-
-        @pl.when(step == 0)
-        def _():
-            assemble(w, first_rows, 0, w1s)
-            assemble(w, second_rows, first_rows, w2s)
-
-        rows_low = table[0, :node_total]
-        pooled = (pooled_own[0].astype(F32) + pooled_other[0].astype(F32)).astype(BF16)
+        assemble(w, order, first_rows, 0, w1s)
+        assemble(w, order, second_rows, first_rows, w2s)
+        rows_low = node_low[...].reshape(count, latent)
+        pooled = (pooled_own[...].astype(F32) + pooled_other[...].astype(F32)).astype(BF16)
+        pooled = pooled.reshape(count, latent)
         hidden = matmul(rows_low, w1s[:latent]) + matmul(pooled, w1s[latent:]) + params[4:5]
         active = (hidden * sigmoid(hidden)).astype(BF16)
         output = matmul_nt(active, w2s[...]) + params[5:6]
         scaled, scale = norm_forward(output)
-        state_new = state[0] + scaled * params[6:7] + params[7:8]
-        low_new = state_new.astype(BF16)
-        new_low[0] = low_new
+        state_new = state[...].astype(F32).reshape(count, latent) + scaled * params[6:7] + params[7:8]
+        low_new = state_new.astype(BF16).reshape(new_low.shape)
+        new_low[...] = low_new
         if not last:
-            pooled_out[0] = pooled
-            pre[0] = hidden.astype(BF16)
-            act[0] = active
-            normed[0] = scaled.astype(BF16)
-            inverse[0] = scale
-            new_state[0] = state_new
-            halo[0] = matmul(at_halo[...], low_new).astype(BF16)
+            pooled_out[...] = pooled
+            pre[...] = hidden.astype(BF16)
+            act[...] = active
+            normed[...] = scaled.astype(BF16)
+            inverse[...] = scale
+            new_state[...] = state_new.reshape(new_state.shape)
+            for s in range(samples):
+                halo[s] = matmul(at_halo[...], new_low[s]).astype(BF16)
         else:
-            grad = target[0].astype(F32) * scaling[0]
+            grad = (target[...].astype(F32) * scaling[...]).reshape(count, latent)
             node_gradients(
-                step, samples, grad, scaled, scale, hidden, active, rows_low, pooled, params, mask,
-                w1s, w2s, first, second, upstream, input_grad, packed, minor, first_rows, second_rows,
+                grad, scaled, scale, hidden, active, rows_low, pooled, params, mask,
+                w1s, w2s, first, second, upstream, input_grad, packed, minor, order, first_rows, second_rows,
             )
 
-    rows_shape = (samples, node_total, latent)
-    inputs = [array, table, state, *pooled_pair, params]
-    specs = [weight_block(*weights), per_sample(table), per_sample(state), per_sample(pooled_pair[0]), per_sample(pooled_pair[1]), constant(params)]
+    shape = node_low.shape
+    inputs = [order, array, node_low, state, *pooled_pair, params]
     scratch = [pltpu.VMEM((2 * latent, latent), BF16), pltpu.VMEM((latent, latent), BF16)]
     if last:
         inputs += [target, scaling, mask]
-        specs += [per_sample(target), per_sample(scaling), constant(mask)]
-        outputs = [sampled(rows_shape, BF16), *gradient_outputs(samples, node_total, latent, nodes, hids, rows, width)]
+        outputs = [shared(shape, BF16), *gradient_outputs(shape, order.shape[0], rows, array.shape[2])]
         scratch += [pltpu.VMEM((2 * latent, latent), F32), pltpu.VMEM((latent, latent), F32)]
     else:
         inputs += [at_halo]
-        specs += [constant(at_halo)]
         outputs = [
-            sampled(rows_shape, BF16),
-            sampled(rows_shape, BF16),
-            sampled(rows_shape, BF16),
-            sampled(rows_shape, BF16),
-            sampled((samples, node_total, 1), F32),
-            sampled(rows_shape, F32),
-            sampled(rows_shape, BF16),
-            sampled((samples, at_halo.shape[0], latent), BF16),
+            shared((count, latent), BF16),
+            shared((count, latent), BF16),
+            shared((count, latent), BF16),
+            shared((count, latent), BF16),
+            shared((count, 1), F32),
+            shared(shape, F32),
+            shared(shape, BF16),
+            shared((samples, at_halo.shape[0], latent), BF16),
         ]
-    return run_kernel(kernel, "node_pass", samples, inputs, specs, outputs, scratch, 6 * samples * node_total * latent * latent * (3 if last else 1))
-
-
-def gradient_outputs(samples, node_total, latent, nodes, hids, rows, width):
+    specs = [in_scalars(), weight_block(*weights)] + [constant(a) for a in inputs[2:]]
+    return run_kernel(kernel, "node_pass", 1, inputs, specs, outputs, scratch, 6 * count * latent * latent * (3 if last else 1))
+
+
+def gradient_outputs(shape, blocks, rows, width):
     return [
-        sampled((samples, node_total, latent), BF16),
-        sampled((samples, node_total, latent), F32),
-        shared((nodes, hids, rows, width), BF16),
-        shared((4, latent), F32),
+        shared(shape, BF16),
+        shared(shape, F32),
+        shared((blocks, rows, width), BF16),
+        shared((4, shape[-1]), F32),
     ]
 
 
 def node_gradients(
-    step, samples, grad, scaled, scale, hidden, active, rows_low, pooled, params, mask,
-    w1s, w2s, first, second, upstream, input_grad, packed, minor, first_rows, second_rows,
+    grad, scaled, scale, hidden, active, rows_low, pooled, params, mask,
+    w1s, w2s, first, second, upstream, input_grad, packed, minor, order, first_rows, second_rows,
 ):
     latent = w2s.shape[0]
-
-    @pl.when(step == 0)
-    def _():
-        minor[...] = jnp.zeros_like(minor)
-        first[...] = jnp.zeros_like(first)
-        second[...] = jnp.zeros_like(second)
-
     output_grad = norm_backward(grad, scaled, scale, params[6:7]).astype(BF16)
     pre_grad = (matmul(output_grad, w2s[...]) * silu_slope(hidden)).astype(BF16)
-    upstream[0] = matmul_nt(pre_grad, w1s[latent:]).astype(BF16)
-    input_grad[0] = grad + matmul_nt(pre_grad, w1s[:latent])
+    upstream[...] = matmul_nt(pre_grad, w1s[latent:]).astype(BF16).reshape(upstream.shape)
+    input_grad[...] = (grad + matmul_nt(pre_grad, w1s[:latent])).reshape(input_grad.shape)
     chosen = mask[...] > 0.5
     output_mine = jnp.where(chosen, output_grad.astype(F32), 0.0)
     pre_mine = jnp.where(chosen, pre_grad.astype(F32), 0.0)
     grad_mine = jnp.where(chosen, grad, 0.0)
-    minor[0:1] += column_sum(pre_mine)
-    minor[1:2] += column_sum(output_mine)
-    minor[2:3] += column_sum(grad_mine * scaled)
-    minor[3:4] += column_sum(grad_mine)
+    minor[0:1] = column_sum(pre_mine)
+    minor[1:2] = column_sum(output_mine)
+    minor[2:3] = column_sum(grad_mine * scaled)
+    minor[3:4] = column_sum(grad_mine)
     pre_mine = pre_mine.astype(BF16)
-    first[:latent] += matmul_tn(rows_low, pre_mine)
-    first[latent:] += matmul_tn(pooled, pre_mine)
-    second[...] += matmul_tn(output_mine.astype(BF16), active)
-
-    @pl.when(step == samples - 1)
-    def _():
-        pack(first, first_rows, 0, packed)
-        pack(second, second_rows, first_rows, packed)
-
-
-def node_backward(weights, grads, table, pooled, pre, act, normed, inverse, params, mask, node_total):
-    samples, _, latent = table.shape
+    first[:latent] = matmul_tn(rows_low, pre_mine)
+    first[latent:] = matmul_tn(pooled, pre_mine)
+    second[...] = matmul_tn(output_mine.astype(BF16), active)
+    pack(first, order, first_rows, 0, packed)
+    pack(second, order, second_rows, first_rows, packed)
+
+
+def node_backward(order, weights, nodes, grads, node_low, pooled, pre, act, normed, inverse, params, mask):
+    samples, node_total, latent = node_low.shape
     array, rows, place = weights
-    nodes, hids, _, width = array.shape
     second_rows = latent // nodes
     first_rows = rows - second_rows
-
-    def kernel(w, base, own, other, table, pooled, pre, act, normed, inverse, params, mask, upstream, input_grad, packed, minor, w1s, w2s, first, second):
-        step = pl.program_id(0)
-
-        @pl.when(step == 0)
-        def _():
-            assemble(w, first_rows, 0, w1s)
-            assemble(w, second_rows, first_rows, w2s)
-
-        grad = base[0] + (own[0] + other[0].astype(F32))
+    count = samples * node_total
+
+    def kernel(order, w, base, own, other, node_low, pooled, pre, act, normed, inverse, params, mask, upstream, input_grad, packed, minor, w1s, w2s, first, second):
+        assemble(w, order, first_rows, 0, w1s)
+        assemble(w, order, second_rows, first_rows, w2s)
+        grad = (base[...] + (own[...] + other[...].astype(F32))).reshape(count, latent)
         node_gradients(
-            step, samples, grad, normed[0].astype(F32), inverse[0], pre[0].astype(F32), act[0],
-            table[0, :node_total], pooled[0], params, mask,
-            w1s, w2s, first, second, upstream, input_grad, packed, minor, first_rows, second_rows,
+            grad, normed[...].astype(F32), inverse[...], pre[...].astype(F32), act[...],
+            node_low[...].reshape(count, latent), pooled[...], params, mask,
+            w1s, w2s, first, second, upstream, input_grad, packed, minor, order, first_rows, second_rows,
         )
 
-    inputs = [array, *grads, table, pooled, pre, act, normed, inverse, params, mask]
-    specs = [weight_block(*weights)] + [per_sample(a) for a in inputs[1:10]] + [constant(params), constant(mask)]
+    inputs = [order, array, *grads, node_low, pooled, pre, act, normed, inverse, params, mask]
+    specs = [in_scalars(), weight_block(*weights)] + [constant(a) for a in inputs[2:]]
     return run_kernel(
         kernel,
         "node_backward",
-        samples,
+        1,
         inputs,
         specs,
-        gradient_outputs(samples, node_total, latent, nodes, hids, rows, width),
+        gradient_outputs(node_low.shape, order.shape[0], rows, array.shape[2]),
         [
             pltpu.VMEM((2 * latent, latent), BF16),
             pltpu.VMEM((latent, latent), BF16),
             pltpu.VMEM((2 * latent, latent), F32),
             pltpu.VMEM((latent, latent), F32),
         ],
-        12 * samples * node_total * latent * latent,
+        12 * count * latent * latent,
     )
 
 
@@ -530,26 +517,43 @@
     return kept.astype(F32) + swap(sent.astype(BF16), axis, 1 << bit).astype(F32)
 
 
-def gather_all(packed):
-    present, early = [], None
-    for key in all_bits():
-        present.append(key)
-        packed = double_up(packed, *key, len(present) - 1)
-        if len(present) == 2:
-            early = packed
-    return packed.reshape(lax.axis_size("node"), lax.axis_size("hid"), *packed.shape[-2:]), early
-
-
-def scatter_all(parts, values=None):
-    left = all_bits()
-    parts = parts.reshape((2,) * len(left) + parts.shape[2:])
-    while left:
-        axis, bit = left.pop()
-        parts = halve_sum(parts, axis, bit, len(left))
-        if values is not None:
-            values = values + swap(values, axis, 1 << bit)
-            parts, values = lax.optimization_barrier((parts, values))
-    return parts, values
+def places():
+    node_ids = jnp.arange(lax.axis_size("node"), dtype=jnp.int32) ^ lax.axis_index("node")
+    hid_ids = jnp.arange(lax.axis_size("hid"), dtype=jnp.int32) ^ lax.axis_index("hid")
+    place = 0
+    for step, (axis, bit) in enumerate(all_bits()):
+        ids = node_ids[:, None] if axis == "node" else hid_ids[None, :]
+        place = place + (((ids >> bit) & 1) << step)
+    return place.reshape(-1)
+
+
+def after(value, *earlier):
+    return lax.optimization_barrier((value, *earlier))[0]
+
+
+def gather_step(held, step):
+    axis, bit = all_bits()[step]
+    return jnp.concatenate([held, swap(held, axis, 1 << bit)], axis=0)
+
+
+def scatter_start(packed):
+    half = packed.shape[0] // 2
+    return packed[:half], packed[half:]
+
+
+def scatter_step(pair, step):
+    axis, bit = all_bits()[step]
+    kept, sent = pair
+    total = kept.astype(F32) + swap(sent, axis, 1 << bit).astype(F32)
+    if step == 0:
+        return total[0]
+    half = total.shape[0] // 2
+    return total[:half], total[half:].astype(BF16)
+
+
+def sum_step(values, step):
+    axis, bit = all_bits()[step]
+    return values + swap(values, axis, 1 << bit)
 
 
 def sum_everywhere(values):
@@ -627,19 +631,26 @@
     node_rows = node_first.shape[1] + second_rows
     width = edge_first.shape[2]
 
-    edge_zero, early = gather_all(pack_shards(edge_first[0], edge_second[0]))
-    piece, _ = lax.optimization_barrier((pack_shards(node_first[0], node_second[0]), early))
-    node_zero, early = gather_all(piece)
-    piece = jnp.concatenate(
+    order = places()
+    steps = len(all_bits())
+    edge_zero = pack_shards(edge_first[0], edge_second[0])[None]
+    for step in range(steps - 2):
+        edge_zero = gather_step(edge_zero, step)
+    setup = edge_zero
+    node_zero = after(pack_shards(node_first[0], node_second[0])[None], edge_zero)
+    layer_one = jnp.concatenate(
         [pack_shards(node_first[1], node_second[1]), pack_shards(edge_first[1], edge_second[1])], axis=0
-    )
-    piece, _ = lax.optimization_barrier((piece, early))
-    layer_one, _ = gather_all(piece)
-    edge_weights = [
-        ((edge_zero, first_rows, 0), (edge_zero, second_rows, first_rows // second_rows)),
-        ((layer_one, first_rows, 1), (layer_one, second_rows, 2 * first_rows // second_rows)),
-    ]
-    node_weights = [(node_zero, node_rows, 0), (layer_one, node_rows, 0)]
+    )[None]
+    for step in range(steps - 3):
+        node_zero = gather_step(node_zero, step)
+    layer_one = after(layer_one, node_zero)
+    layer_one = gather_step(layer_one, 0)
+    edge_zero = gather_step(edge_zero, steps - 2)
+    edge_zero = after(edge_zero, node_zero)
+    edge_zero = gather_step(edge_zero, steps - 1)
+    node_zero = gather_step(node_zero, steps - 3)
+    edge_zero = after(edge_zero, node_zero, layer_one)
+    edge_weights = [((edge_zero, first_rows, 0), (edge_zero, second_rows, first_rows // second_rows))]
 
     def own_edges(values):
         return lax.dynamic_index_in_dim(
@@ -661,6 +672,9 @@
         kept = lax.dynamic_index_in_dim(quarters, sample_half, 0, keepdims=False)
         return jnp.concatenate(ordered(sample_half, kept, swap(sent, "hid", 2)), axis=1)
 
+    send_slot, recv_local, halo_lists, node_in, edge_in = lax.optimization_barrier(
+        (send_slot, recv_local, halo_lists, node_in, edge_in, setup)
+    )[:5]
     sender = own_edges(send_slot)
     receiver = own_edges(recv_local)
     node_ids, table_ids = jnp.arange(node_total), jnp.arange(table_total)
@@ -673,34 +687,33 @@
         [(table_ids[:, None] == sender[None, :]).astype(BF16), at_nodes], axis=0
     )
     at_halo = (halo_lists.reshape(-1)[:, None] == node_ids[None, :]).astype(BF16)
-    mask = ((node_ids // node_part) % 2 == edge_half).astype(F32)[:, None]
-
-    valid_mask = (ocean_mask[:, None] * present_mask).astype(BF16)
-    masked = cotangent * valid_mask[:, :, None]
-    masked, _ = lax.optimization_barrier((masked, edge_zero))
-    sent = lax.dynamic_slice_in_dim(masked, (1 - sample_half) * samples, samples, 1)
-    masked = jnp.stack(ordered(sample_half, own_samples(masked), swap(sent, "hid", 2)), axis=0)
-    masked = double_up(masked, "hid", 0, 1).reshape(node_total, samples, latent)
-    scaling = node_total * lax.axis_size("node") / valid_counts.astype(F32)
-    scaling = lax.dynamic_slice_in_dim(scaling, sample_half * samples, samples, 0)
-    target = jnp.transpose(masked, (1, 0, 2))
-    scaling = scaling[:, None, None]
+    mask = ((node_ids // node_part) % 2 == edge_half).astype(F32)
+    mask = jnp.tile(mask, samples)[:, None]
 
     node_low = jnp.transpose(own_samples(node_in), (1, 0, 2))
     edge_in_own = own_edges(edge_in)
     halo_rows = dot("hn,snl->shl", at_halo, node_low).astype(BF16)
+    node_low_zero = node_low
     table_zero = jnp.concatenate([node_low, to_neighbours(halo_rows, halo_width)], axis=1)
     pre_zero, act_zero, normed_zero, inverse_zero, edge_state, edge_low, pooled = edge_forward(
+        order,
         *edge_weights[0],
         table_zero,
         edge_in_own[None],
-        edge_in_own.astype(F32)[None],
+        edge_in_own[None],
         at_both,
         at_nodes,
         small_params[0],
         node_total,
         False,
     )
+    for step in range(steps - 2, steps):
+        node_zero = gather_step(node_zero, step)
+    for step in range(1, steps - 2):
+        layer_one = gather_step(layer_one, step)
+    node_weights = [(node_zero, node_rows, 0)]
+    other = swap(pooled, "hid", 1)
+    pooled, other = lax.optimization_barrier((pooled, other, layer_one))[:2]
     (
         pooled_zero,
         node_pre,
@@ -711,19 +724,39 @@
         node_low,
         halo_rows,
     ) = node_pass(
+        order,
         node_weights[0],
-        table_zero,
-        node_low.astype(F32),
-        (pooled, swap(pooled, "hid", 1)),
+        nodes,
+        node_low_zero,
+        node_low_zero,
+        (pooled, other),
         small_params[0],
         at_halo,
         None,
         None,
         None,
-        node_total,
-    )
+    )
+    for step in range(steps - 2, steps):
+        layer_one = gather_step(layer_one, step)
+    edge_weights.append(
+        ((layer_one, first_rows, 1), (layer_one, second_rows, 2 * first_rows // second_rows))
+    )
+    node_weights.append((layer_one, node_rows, 0))
+
+    valid_mask = (ocean_mask[:, None] * present_mask).astype(BF16)
+    masked = after(cotangent, pooled) * valid_mask[:, :, None]
+    sent = lax.dynamic_slice_in_dim(masked, (1 - sample_half) * samples, samples, 1)
+    masked = jnp.stack(ordered(sample_half, own_samples(masked), swap(sent, "hid", 2)), axis=0)
+    masked = double_up(masked, "hid", 0, 1).reshape(node_total, samples, latent)
+    scaling = node_total * lax.axis_size("node") / valid_counts.astype(F32)
+    scaling = lax.dynamic_slice_in_dim(scaling, sample_half * samples, samples, 0)
+    target = jnp.transpose(masked, (1, 0, 2))
+    scaling = scaling[:, None, None]
+
+    node_low_one = node_low
     table_one = jnp.concatenate([node_low, to_neighbours(halo_rows, halo_width)], axis=1)
     pre_one, act_one, normed_one, inverse_one, pooled = edge_forward(
+        order,
         *edge_weights[1],
         table_one,
         edge_low,
@@ -735,8 +768,10 @@
         True,
     )
     node_low, pooled_grad, node_grad, node_packed, node_minor_one = node_pass(
+        order,
         node_weights[1],
-        table_one,
+        nodes,
+        node_low_one,
         node_state,
         (pooled, swap(pooled, "hid", 1)),
         small_params[1],
@@ -744,7 +779,10 @@
         target,
         scaling,
         mask,
-        node_total,
+    )
+    masters = (edge_first, edge_second, node_first, node_second)
+    weight_local = jnp.stack(
+        [jnp.sum(matrix * matrix, axis=(1, 2)) for matrix in after(masters, node_low)], axis=1
     )
     node_out = to_own_rows(node_low)
 
@@ -753,6 +791,7 @@
         return partial + dot("hn,shl->snl", at_halo, returned)
 
     low, hidden_low, at_rows, partial, returned, edge_grad, edge_minor_one = edge_backward(
+        order,
         *edge_weights[1],
         pooled_grad,
         None,
@@ -766,6 +805,7 @@
         node_total,
     )
     packed = edge_weight_grads(
+        order,
         edge_low,
         table_one,
         hidden_low,
@@ -774,16 +814,20 @@
         act_one,
         node_total,
         nodes,
-        hids,
         width,
         node_packed,
     )
-    layer_one_grads, _ = scatter_all(packed)
     partial = from_edges(partial, returned)
+    other = swap(partial.astype(BF16), "hid", 1)
+    chain_one = scatter_step(scatter_start(packed), steps - 1)
+    other, kept, sent = lax.optimization_barrier((other, *chain_one))
+    chain_one = (kept, sent)
     pooled_grad, node_grad, node_packed, node_minor_zero = node_backward(
+        order,
         node_weights[0],
-        (node_grad, partial, swap(partial.astype(BF16), "hid", 1)),
-        table_zero,
+        nodes,
+        (node_grad, partial, other),
+        node_low_zero,
         pooled_zero,
         node_pre,
         node_act,
@@ -791,11 +835,10 @@
         node_inverse,
         small_params[0],
         mask,
-        node_total,
-    )
-    node_zero_grads, _ = scatter_all(node_packed)
+    )
     low, hidden_low, at_rows, partial, returned, edge_input_grad, edge_minor_zero, hidden_sum = (
         edge_backward(
+            order,
             *edge_weights[0],
             pooled_grad,
             edge_grad,
@@ -809,7 +852,12 @@
             node_total,
         )
     )
+    chain_zero = scatter_step(scatter_start(node_packed), steps - 1)
+    chain_one = scatter_step(chain_one, steps - 2)
+    low, *held = lax.optimization_barrier((low, *chain_zero, *chain_one))
+    chain_zero, chain_one = held[:2], held[2:]
     packed = edge_weight_grads(
+        order,
         edge_in_own,
         table_zero,
         hidden_sum,
@@ -818,18 +866,30 @@
         act_zero,
         node_total,
         nodes,
-        hids,
         width,
         None,
     )
-    masters = (edge_first, edge_second, node_first, node_second)
-    weight_local = jnp.stack([jnp.sum(matrix * matrix, axis=(1, 2)) for matrix in masters], axis=1)
     minor_packed = jnp.concatenate(
         [edge_minor_zero, node_minor_zero, edge_minor_one, node_minor_one]
         + [jnp.pad(weight_local.reshape(1, -1), ((0, 0), (0, latent - weight_local.size)))],
         axis=0,
     )
-    edge_zero_grads, minor_packed = scatter_all(packed, minor_packed)
+    chain_zero = scatter_step(chain_zero, steps - 2)
+    chain_one = tuple(jnp.concatenate(pair, axis=1) for pair in zip(chain_one, chain_zero))
+    chain_edge = scatter_step(scatter_start(packed), steps - 1)
+    minor_packed = sum_step(minor_packed, steps - 1)
+    for step in reversed(range(steps - 1)):
+        minor_packed, *held = lax.optimization_barrier(
+            (minor_packed, *chain_edge, *chain_one)
+        )
+        chain_edge = held[:2]
+        if step > 0:
+            chain_one = scatter_step(held[2:], step - 1)
+        chain_edge = scatter_step(chain_edge, step)
+        minor_packed = sum_step(minor_packed, step)
+        if step == 1:
+            chain_one = (chain_one,)
+    edge_zero_grads, node_grads = chain_edge, chain_one[0]
     partial = from_edges(partial, returned)
     node_grad = node_grad + (partial + swap(partial.astype(BF16), "hid", 1).astype(F32))
     grad_node = to_own_rows(node_grad.astype(BF16))
@@ -837,7 +897,10 @@
 
     minor_total = minor_packed[: 8 * LAYERS].reshape(small_params.shape)
     weight_squares = minor_packed[8 * LAYERS, : weight_local.size].reshape(weight_local.shape)
-    node_one_grads, edge_one_grads = layer_one_grads[:node_rows], layer_one_grads[node_rows:]
+    edge_rows = first_rows + second_rows
+    node_one_grads = node_grads[:node_rows]
+    edge_one_grads = node_grads[node_rows : node_rows + edge_rows]
+    node_zero_grads = node_grads[node_rows + edge_rows :]
     node_first_rows = node_rows - second_rows
     grads = [
         jnp.stack([edge_zero_grads[:first_rows], edge_one_grads[:first_rows]]),

time: 355 us -> 307 us (0.86)
  waiting for transfers between devices: 111 us -> 86.8 us
  other arithmetic: 50.2 us -> 31.4 us
  local copies, waits for them, and re-layouts: 30.7 us -> 48.1 us
  starting transfers between devices: 65.2 us -> 49.1 us
  Pallas kernels: 91.7 us -> 86.4 us
    ppermute x49 -> x46, waiting for transfers between devices: 107 us -> 78.9 us  [swap(): lax.ppermute(values, axis, [(i, i ^ offset) for i in range(lax.axis_size(...]
    ppermute x49 -> x46, starting transfers between devices: 50.7 us -> 31.8 us  [swap(): lax.ppermute(values, axis, [(i, i ^ offset) for i in range(lax.axis_size(...]
    another operation x32 -> x2, other arithmetic: 14.1 us -> 0.09 us  [double_up(): return jnp.stack([low, high], axis=place)]
    unnamed x123 -> x136, local copies, waits for them, and re-layouts: 5.17 us -> 19 us
    slice x0 -> x34, local copies, waits for them, and re-layouts: none -> 8.82 us  [the longest x3 6.57 us: scatter_start(): return (packed[:half], packed[half:])]
    concatenate x0 -> x6, local copies, waits for them, and re-layouts: none -> 7.46 us  [the longest x5 7.45 us: gather_step(): return jnp.concatenate([held, swap(held, axis, 1 << bit)], axis=0)]
    pallas_call x9, Pallas kernels: 91.7 us -> 86.4 us  [run_kernel(): pl.pallas_call(kernel, name=name, grid=(samples,), in_specs=in_specs, out...]
    ppermute x4, waiting for transfers between devices: 2.73 us -> 7.83 us  [to_neighbours(): from_previous = lax.ppermute(rows[:, halo_width:], 'node', onward)]
  transfers between devices with their start and end apart: 57 -> 54, of which waited for: 27 -> 27; matrix products, arithmetic and copies ran while one was open for 20% -> 18% of each run, Pallas kernels for 23% -> 16%
where the time goes in v1:
time: 307 us; the launch traced here: 306 us
  waiting for transfers between devices  86.8 us (28%)
  Pallas kernels  86.4 us (28%)
  starting transfers between devices  49.1 us (16%)
  local copies, waits for them, and re-layouts  48.1 us (16%)
  other arithmetic  31.4 us (10%)
    pallas_call x9, Pallas kernels, run_kernel(): pl.pallas_call(kernel, name=name, grid=(samples,), in_specs=in_specs, out...  86.4 us
    ppermute x46, waiting for transfers between devices, swap(): lax.ppermute(values, axis, [(i, i ^ offset) for i in range(lax.axis_size(...  78.9 us
    ppermute x46, starting transfers between devices, swap(): lax.ppermute(values, axis, [(i, i ^ offset) for i in range(lax.axis_size(...  31.8 us
    unnamed x136, local copies, waits for them, and re-layouts  19 us
    ppermute x4, starting transfers between devices, to_neighbours(): from_next = lax.ppermute(rows[:, :halo_width], 'node', back)  15.4 us
    ppermute x4, waiting for transfers between devices, to_neighbours(): from_previous = lax.ppermute(rows[:, halo_width:], 'node', onward)  7.83 us
    concatenate x5, local copies, waits for them, and re-layouts, gather_step(): return jnp.concatenate([held, swap(held, axis, 1 << bit)], axis=0)  7.45 us
    slice x3, local copies, waits for them, and re-layouts, scatter_start(): return (packed[:half], packed[half:])  6.57 us
  transfers between devices with their start and end apart: 54, of which 27 were waited for; matrix products, arithmetic and copies ran while one was open for 18% of the time, Pallas kernels for 16%

profile of v1, /device:TPU:0, one launch (start us, length us, event | category | flops | bytes accessed | tf_op | source)
XLA Modules:
  0.0 305.7 jit_solution(2361684565199616139)
XLA Ops:
  4.1 4.1 %collective-permute-start = (bf16[1,256,128]{2,1,0:T(8,128)(2,1)S(1)}, bf16[1,256,128]{2,1,0:T(8,128)(2,1)S(1)}, u32[]{:S(2)}, u32[]{:S(2)}) collective-permute-start(bf16[1,256,128]{2,1,0:T(8,128)(2,1)S(1)} %get-tuple-element.320), channel_id=1, source_target_pairs={{0,16},{4,20},{8,24},{12,28},{16,0},{20,4},{24,8},{28,12},{1,17},{... | collective-permute-start | bytes 196616 | tf_op jit(solution)/shard_map/ppermute | solution.py:487
  14.9 3.4 %collective-permute-done.1 = bf16[2,256,128]{2,1,0:T(8,128)(2,1)S(1)} collective-permute-done((bf16[2,256,128]{2,1,0:T(8,128)(2,1)S(1)}, bf16[2,256,128]{2,1,0:T(8,128)(2,1)S(1)}, u32[]{:S(2)}, u32[]{:S(2)}) %collective-permute-start.1) | collective-permute-done | bytes 131104 | tf_op jit(solution)/shard_map/ppermute | solution.py:487
  32.6 3.2 %collective-permute-start.16 = (bf16[3,40,512]{2,1,0:T(8,128)(2,1)S(1)}, bf16[3,40,512]{2,1,0:T(8,128)(2,1)S(1)}, u32[]{:S(2)}, u32[]{:S(2)}) collective-permute-start(bf16[3,40,512]{2,1,0:T(8,128)(2,1)S(1)} %get-tuple-element.298), channel_id=1, source_target_pairs={{4,0},{8,4},{12,8},{16,12},{20,16},{24,20},{28,24},{0,28},{5,1},{9... | collective-permute-start | bytes 368648 | tf_op jit(solution)/shard_map/ppermute | solution.py:570
  38.0 4.0 %collective-permute-done.4 = bf16[2,192,128]{2,1,0:T(8,128)(2,1)S(1)} collective-permute-done((bf16[2,192,128]{2,1,0:T(8,128)(2,1)S(1)}, bf16[2,192,128]{2,1,0:T(8,128)(2,1)S(1)}, u32[]{:S(2)}, u32[]{:S(2)}) %collective-permute-start.4) | collective-permute-done | bytes 98336 | tf_op jit(solution)/shard_map/ppermute | solution.py:487
  43.3 5.8 %collective-permute-done.5 = bf16[1,448,128]{2,1,0:T(8,128)(2,1)S(1)} collective-permute-done((bf16[1,448,128]{2,1,0:T(8,128)(2,1)S(1)}, bf16[1,448,128]{2,1,0:T(8,128)(2,1)S(1)}, u32[]{:S(2)}, u32[]{:S(2)}) %collective-permute-start.5) | collective-permute-done | bytes 114720 | tf_op jit(solution)/shard_map/ppermute | solution.py:487
  51.1 4.8 %collective-permute-done.6 = bf16[2,448,128]{2,1,0:T(8,128)(2,1)S(1)} collective-permute-done((bf16[2,448,128]{2,1,0:T(8,128)(2,1)S(1)}, bf16[2,448,128]{2,1,0:T(8,128)(2,1)S(1)}, u32[]{:S(2)}, u32[]{:S(2)}) %collective-permute-start.6) | collective-permute-done | bytes 229408 | tf_op jit(solution)/shard_map/ppermute | solution.py:487
  60.7 4.8 %collective-permute-done.7 = bf16[4,448,128]{2,1,0:T(8,128)(2,1)S(1)} collective-permute-done((bf16[4,448,128]{2,1,0:T(8,128)(2,1)S(1)}, bf16[4,448,128]{2,1,0:T(8,128)(2,1)S(1)}, u32[]{:S(2)}, u32[]{:S(2)}) %collective-permute-start.7) | collective-permute-done | bytes 458784 | tf_op jit(solution)/shard_map/ppermute | solution.py:487
  75.0 11.6 %edge_forward.2 = (bf16[3,640,512]{2,1,0:T(8,128)(2,1)}, bf16[3,640,512]{2,1,0:T(8,128)(2,1)}, bf16[3,640,512]{2,1,0:T(8,128)(2,1)}, f32[3,640,1]{2,1,0:T(8,128)...) custom-call(s32[32]{0:T(128)} %add.273.order, ...), custom_call_target="tpu_custom_call" | custom-call | flops 3806330880 | bytes 19271296 | tf_op jit(solution)/shard_map/edge_forward/pallas_call | solution.py:108
  87.2 3.5 %collective-permute-done.8 = bf16[8,448,128]{2,1,0:T(8,128)(2,1)} collective-permute-done((bf16[8,448,128]{2,1,0:T(8,128)(2,1)}, bf16[8,448,128]{2,1,0:T(8,128)(2,1)}, u32[]{:S(2)}, u32[]{:S(2)}) %collective-permute-start.8) | collective-permute-done | bytes 917536 | tf_op jit(solution)/shard_map/ppermute | solution.py:487
  95.4 5.0 %node_pass.2 = (bf16[480,512]{1,0:T(8,128)(2,1)}, bf16[480,512]{1,0:T(8,128)(2,1)}, bf16[480,512]{1,0:T(8,128)(2,1)}, bf16[480,512]{1,0:T(8,128)(2,1)}, f32[480,...) custom-call(s32[32]{0:T(128)} %add.273.order, ...), custom_call_target="tpu_custom_call" | custom-call | flops 754974720 | bytes 7269376 | tf_op jit(solution)/shard_map/node_pass/pallas_call | solution.py:108
  101.4 3.0 collective-permute-start.19
  105.8 6.7 %collective-permute-done.18 = bf16[3,40,512]{2,1,0:T(8,128)(2,1)S(1)} collective-permute-done((bf16[3,40,512]{2,1,0:T(8,128)(2,1)S(1)}, bf16[3,40,512]{2,1,0:T(8,128)(2,1)S(1)}, u32[]{:S(2)}, u32[]{:S(2)}) %collective-permute-start.18) | collective-permute-done | bytes 122912 | tf_op jit(solution)/shard_map/ppermute | solution.py:569
  116.5 11.0 %edge_forward.3 = (bf16[3,640,512]{2,1,0:T(8,128)(2,1)}, bf16[3,640,512]{2,1,0:T(8,128)(2,1)}, bf16[3,640,512]{2,1,0:T(8,128)(2,1)}, f32[3,640,1]{2,1,0:T(8,128)}, bf16[3,160,512]{2,1,0:T(8,128)(2,1)}) custom-call(s32[32]{0:T(128)} %add.273.order, bf16[32,448,128]{2,1,0:T(8,128)(2,1)} %copy-done.2, bf16[32,448,128]{2,1,0:T(8,128)(2,1)} %copy-done.2, ...), custom_call_target="tpu_custom_call" | custom-call | flops 3806330880 | bytes 21106304 | tf_op jit(solution)/shard_map/edge_forward/pallas_call | solution.py:108
  130.4 7.5 %node_pass.3 = (bf16[3,160,512]{2,1,0:T(8,128)(2,1)}, bf16[3,160,512]{2,1,0:T(8,128)(2,1)}, f32[3,160,512]{2,1,0:T(8,128)}, bf16[32,192,128]{2,1,0:T(8,128)(2,1)}, f32[4,512]{1,0:T(4,128)}) custom-call(s32[32]{0:T(128)} %add.273.order, bf16[32,448,128]{2,1,0:T(8,128)(2,1)} %copy-done.2, bf16[3,160,512]{2,1,0:T(8,128)(2,1)} %get-tuple-element.120.node_low, ...), custom_call_target="tpu_custom_call" | custom-call | flops 2264924160 | bytes 10184716 | tf_op jit(solution)/shard_map/node_pass/pallas_call | solution.py:108
  137.9 12.6 %edge_backward.2 = (bf16[3,640,512]{2,1,0:T(8,128)(2,1)}, bf16[3,640,512]{2,1,0:T(8,128)(2,1)}, bf16[3,400,512]{2,1,0:T(8,128)(2,1)}, f32[3,160,512]{2,1,0:T(8,1...) custom-call(s32[32]{0:T(128)} %add.273.order, bf16[32,448,128]{2,1,0:T(8,128)(2,1)} %copy-done.2, ...), custom_call_target="tpu_custom_call" | custom-call | flops 3586129920 | bytes 22820480 | tf_op jit(solution)/shard_map/edge_backward/pallas_call | solution.py:108
  150.5 9.7 %edge_weight_grads.2 = bf16[32,448,128]{2,1,0:T(8,128)(2,1)} custom-call(s32[32]{0:T(128)} %add.273.order, bf16[3,640,512]{2,1,0:T(8,128)(2,1)} %get-tuple-element.123.low.edge_low, bf16[3,240,512]{2,1,0:T(8,128)(2,1)} %copy-done.11, bf16[3,640,512]{2,1,0:T(8,128)(2,1)} %get-tuple-element.135.hidden_low, bf16[3,400,512]{2,1,0:T(8,128)(2,1)} %get-tuple-element.136.at_rows, ...), custom_call_target="tpu_custom_call" | custom-call | flops 2013265920 | bytes 15073408 | tf_op jit(solution)/shard_map/edge_weight_grads/pallas_call | solution.py:108
  160.2 3.0 slice.320
  164.3 4.5 %collective-permute-start.25 = (bf16[3,40,512]{2,1,0:T(8,128)(2,1)S(1)}, bf16[3,40,512]{2,1,0:T(8,128)(2,1)S(1)}, u32[]{:S(2)}, u32[]{:S(2)}) collective-permute-start(bf16[3,40,512]{2,1,0:T(8,128)(2,1)S(1)} %get-tuple-element.294), channel_id=1, source_target_pairs={{4,0},{8,4},{12,8},{16,12},{20,16},{24,20},{28,24},{0,28},{5,1},{9... | collective-permute-start | bytes 368648 | tf_op jit(solution)/shard_map/ppermute | solution.py:570
  178.9 7.1 %node_backward.1 = (bf16[3,160,512]{2,1,0:T(8,128)(2,1)}, f32[3,160,512]{2,1,0:T(8,128)}, bf16[32,192,128]{2,1,0:T(8,128)(2,1)}, f32[4,512]{1,0:T(4,128)}) custom-call(s32[32]{0:T(128)} %add.273.order, bf16[32,192,128]{2,1,0:T(8,128)(2,1)} %copy-done.7, f32[3,160,512]{2,1,0:T(8,128)} %get-tuple-element.128.base, f32[3,160,512]{2,1,0:T(8,128)} %get-tuple-element.270.own, ...), custom_call_target="tpu_custom_call" | custom-call | flops 1509949440 | bytes 9564032 | tf_op jit(solution)/shard_map/node_backward/pallas_call | solution.py:108
  189.7 14.4 %edge_backward.3 = (bf16[3,640,512]{2,1,0:T(8,128)(2,1)}, bf16[3,640,512]{2,1,0:T(8,128)(2,1)}, bf16[3,400,512]{2,1,0:T(8,128)(2,1)}, f32[3,160,512]{2,1,0:T(8,1...) custom-call(s32[32]{0:T(128)} %add.273.order, ...), custom_call_target="tpu_custom_call" | custom-call | flops 3586129920 | bytes 21640832 | tf_op jit(solution)/shard_map/edge_backward/pallas_call | solution.py:108
  205.6 4.6 %collective-permute-done.35 = bf16[8,448,128]{2,1,0:T(8,128)(2,1)} collective-permute-done((bf16[8,448,128]{2,1,0:T(8,128)(2,1)S(1)}, bf16[8,448,128]{2,1,0:T(8,128)(2,1)}, u32[]{:S(2)}, u32[]{:S(2)}) %collective-permute-start.35) | collective-permute-done | bytes 917536 | tf_op jit(solution)/shard_map/ppermute | solution.py:487
  212.6 7.5 %edge_weight_grads.3 = bf16[32,256,128]{2,1,0:T(8,128)(2,1)} custom-call(s32[32]{0:T(128)} %add.273.order, bf16[640,512]{1,0:T(8,128)(2,1)} %bitcast.154, bf16[3,240,512]{2,1,0:T(8,128)(2,1)} %pad_maximum_fusion.2.table, bf16[640,512]{1,0:T(8,128)(2,1)} %get-tuple-element.163.hidden_low, bf16[3,400,512]{2,1,0:T(8,128)(2,1)} %get-tuple-element.164.at_rows, ...), custom_call_target="tpu_custom_call" | custom-call | flops 2013265920 | bytes 9306240 | tf_op jit(solution)/shard_map/edge_weight_grads/pallas_call | solution.py:108
  222.6 4.7 %collective-permute-start.29 = (bf16[3,40,512]{2,1,0:T(8,128)(2,1)S(1)}, bf16[3,40,512]{2,1,0:T(8,128)(2,1)S(1)}, u32[]{:S(2)}, u32[]{:S(2)}) collective-permute-start(bf16[3,40,512]{2,1,0:T(8,128)(2,1)S(1)} %get-tuple-element.292), channel_id=1, source_target_pairs={{4,0},{8,4},{12,8},{16,12},{20,16},{24,20},{28,24},{0,28},{5,1},{9... | collective-permute-start | bytes 368648 | tf_op jit(solution)/shard_map/ppermute | solution.py:570
  231.9 7.8 %collective-permute-done.37 = bf16[8,192,128]{2,1,0:T(8,128)(2,1)} collective-permute-done((bf16[8,192,128]{2,1,0:T(8,128)(2,1)}, bf16[8,192,128]{2,1,0:T(8,128)(2,1)}, u32[]{:S(2)}, u32[]{:S(2)}) %collective-permute-start.37) | collective-permute-done | bytes 393248 | tf_op jit(solution)/shard_map/ppermute | solution.py:487
  247.7 10.2 %collective-permute-done.38 = f32[17,512]{1,0:T(8,128)S(1)} collective-permute-done((f32[17,512]{1,0:T(8,128)S(1)}, f32[17,512]{1,0:T(8,128)S(1)}, u32[]{:S(2)}, u32[]{:S(2)}) %collective-permute-start.38) | collective-permute-done | bytes 34848 | tf_op jit(solution)/shard_map/ppermute | solution.py:487
  263.5 3.1 %collective-permute-done.41 = f32[17,512]{1,0:T(8,128)S(1)} collective-permute-done((f32[17,512]{1,0:T(8,128)S(1)}, f32[17,512]{1,0:T(8,128)S(1)}, u32[]{:S(2)}, u32[]{:S(2)}) %collective-permute-start.41) | collective-permute-done | bytes 34848 | tf_op jit(solution)/shard_map/ppermute | solution.py:487
  266.7 3.2 %collective-permute-done.43 = bf16[2,640,128]{2,1,0:T(8,128)(2,1)S(1)} collective-permute-done((bf16[2,640,128]{2,1,0:T(8,128)(2,1)S(1)}, bf16[2,640,128]{2,1,0:T(8,128)(2,1)S(1)}, u32[]{:S(2)}, u32[]{:S(2)}) %collective-permute-start.43) | collective-permute-done | bytes 327712 | tf_op jit(solution)/shard_map/ppermute | solution.py:487
  273.0 4.6 %collective-permute-done.44 = f32[17,512]{1,0:T(8,128)S(1)} collective-permute-done((f32[17,512]{1,0:T(8,128)S(1)}, f32[17,512]{1,0:T(8,128)S(1)}, u32[]{:S(2)}, u32[]{:S(2)}) %collective-permute-start.44) | collective-permute-done | bytes 34848 | tf_op jit(solution)/shard_map/ppermute | solution.py:487
  277.9 2.9 collective-permute-start.47
  289.9 3.6 %collective-permute-done.51 = f32[2,4]{1,0:T(2,128)S(1)} collective-permute-done((f32[2,4]{1,0:T(2,128)S(1)}, f32[2,4]{1,0:T(2,128)S(1)}, u32[]{:S(2)}, u32[]{:S(2)}) %collective-permute-start.51) | collective-permute-done | bytes 64 | tf_op jit(solution)/shard_map/ppermute | solution.py:487
  293.9 3.1 %collective-permute-done.52 = f32[2,4]{1,0:T(2,128)S(1)} collective-permute-done((f32[2,4]{1,0:T(2,128)S(1)}, f32[2,4]{1,0:T(2,128)S(1)}, u32[]{:S(2)}, u32[]{:S(2)}) %collective-permute-start.52) | collective-permute-done | bytes 64 | tf_op jit(solution)/shard_map/ppermute | solution.py:487
  298.7 2.8 collective-permute-done.53
  (387 shorter events, 115.2 us)
Async XLA Ops:
  4.1 9.1 %collective-permute-start = (bf16[1,256,128]{2,1,0:T(8,128)(2,1)S(1)}, bf16[1,256,128]{2,1,0:T(8,128)(2,1)S(1)}, u32[]{:S(2)}, u32[]{:S(2)}) collective-permute-start(bf16[1,256,128]{2,1,0:T(8,128)(2,1)S(1)} %get-tuple-element.320), channel_id=1, source_target_pairs={{0,16},{4,20},{8,24},{12,28},{16,0},{20,4},{24,8},{28,12},{1,17},{... | collective-permute-start | bytes 196616 | tf_op jit(solution)/shard_map/ppermute | solution.py:487
  25.8 30.1 %collective-permute-start.13 = (bf16[8,256,128]{2,1,0:T(8,128)(2,1)}, bf16[8,256,128]{2,1,0:T(8,128)(2,1)}, u32[]{:S(2)}, u32[]{:S(2)}) collective-permute-start(bf16[8,256,128]{2,1,0:T(8,128)(2,1)} %pad_maximum_fusion.5), channel_id=1, source_target_pairs={{0,2},{1,3},{2,0},{3,1},{4,6},{5,7},{6,4},{7,5},{8,10},{9,11},{10,... | collective-permute-start | bytes 1572872 | tf_op jit(solution)/shard_map/ppermute | solution.py:487
  27.8 9.4 %collective-permute-start.3 = (bf16[1,192,128]{2,1,0:T(8,128)(2,1)S(1)}, bf16[1,192,128]{2,1,0:T(8,128)(2,1)S(1)}, u32[]{:S(2)}, u32[]{:S(2)}) collective-permute-start(bf16[1,192,128]{2,1,0:T(8,128)(2,1)S(1)} %pad_maximum_fusion.20), channel_id=1, source_target_pairs={{0,16},{4,20},{8,24},{12,28},{16,0},{20,4},{24,8},{28,12},{1,17},{... | collective-permute-start | bytes 147464 | tf_op jit(solution)/shard_map/ppermute | solution.py:487
  31.1 38.0 %collective-permute-start.15 = (bf16[3,40,512]{2,1,0:T(8,128)(2,1)S(1)}, bf16[3,40,512]{2,1,0:T(8,128)(2,1)S(1)}, u32[]{:S(2)}, u32[]{:S(2)}) collective-permute-start(bf16[3,40,512]{2,1,0:T(8,128)(2,1)S(1)} %get-tuple-element.297), channel_id=1, source_target_pairs={{0,4},{4,8},{8,12},{12,16},{16,20},{20,24},{24,28},{28,0},{1,5},{5... | collective-permute-start | bytes 368648 | tf_op jit(solution)/shard_map/ppermute | solution.py:569
  32.6 36.5 %collective-permute-start.16 = (bf16[3,40,512]{2,1,0:T(8,128)(2,1)S(1)}, bf16[3,40,512]{2,1,0:T(8,128)(2,1)S(1)}, u32[]{:S(2)}, u32[]{:S(2)}) collective-permute-start(bf16[3,40,512]{2,1,0:T(8,128)(2,1)S(1)} %get-tuple-element.298), channel_id=1, source_target_pairs={{4,0},{8,4},{12,8},{16,12},{20,16},{24,20},{28,24},{0,28},{5,1},{9... | collective-permute-start | bytes 368648 | tf_op jit(solution)/shard_map/ppermute | solution.py:570
  50.0 8.7 %collective-permute-start.10 = (bf16[4,192,128]{2,1,0:T(8,128)(2,1)S(1)}, bf16[4,192,128]{2,1,0:T(8,128)(2,1)S(1)}, u32[]{:S(2)}, u32[]{:S(2)}) collective-permute-start(bf16[4,192,128]{2,1,0:T(8,128)(2,1)S(1)} %get-tuple-element.316), channel_id=1, source_target_pairs={{0,4},{4,0},{8,12},{12,8},{16,20},{20,16},{24,28},{28,24},{1,5},{5... | collective-permute-start | bytes 589832 | tf_op jit(solution)/shard_map/ppermute | solution.py:487
  55.9 9.7 %collective-permute-start.7 = (bf16[4,448,128]{2,1,0:T(8,128)(2,1)S(1)}, bf16[4,448,128]{2,1,0:T(8,128)(2,1)S(1)}, u32[]{:S(2)}, u32[]{:S(2)}) collective-permute-start(bf16[4,448,128]{2,1,0:T(8,128)(2,1)S(1)} %pad_maximum_fusion.8), channel_id=1, source_target_pairs={{0,4},{4,0},{8,12},{12,8},{16,20},{20,16},{24,28},{28,24},{1,5},{5... | collective-permute-start | bytes 1376264 | tf_op jit(solution)/shard_map/ppermute | solution.py:487
  57.9 14.4 %collective-permute-start.14 = (bf16[16,256,128]{2,1,0:T(8,128)(2,1)}, bf16[16,256,128]{2,1,0:T(8,128)(2,1)S(1)}, u32[]{:S(2)}, u32[]{:S(2)}) collective-permute-start(bf16[16,256,128]{2,1,0:T(8,128)(2,1)} %constant_dynamic-update-slice_fusion.35), channel_id=1, source_target_pairs={{0,1},{1,0},{2,3},{3,2},{4,5},{5,4},{6,7},{7,6},{8,9},{9,8},{10,11... | collective-permute-start | bytes 3145736 | tf_op jit(solution)/shard_map/ppermute | solution.py:487
  59.4 12.0 %collective-permute-start.11 = (bf16[8,192,128]{2,1,0:T(8,128)(2,1)S(1)}, bf16[8,192,128]{2,1,0:T(8,128)(2,1)S(1)}, u32[]{:S(2)}, u32[]{:S(2)}) collective-permute-start(bf16[8,192,128]{2,1,0:T(8,128)(2,1)S(1)} %get-tuple-element.304), channel_id=1, source_target_pairs={{0,2},{1,3},{2,0},{3,1},{4,6},{5,7},{6,4},{7,5},{8,10},{9,11},{10,... | collective-permute-start | bytes 1179656 | tf_op jit(solution)/shard_map/ppermute | solution.py:487
  66.6 24.2 %collective-permute-start.8 = (bf16[8,448,128]{2,1,0:T(8,128)(2,1)}, bf16[8,448,128]{2,1,0:T(8,128)(2,1)}, u32[]{:S(2)}, u32[]{:S(2)}) collective-permute-start(bf16[8,448,128]{2,1,0:T(8,128)(2,1)} %get-tuple-element.281), channel_id=1, source_target_pairs={{0,2},{1,3},{2,0},{3,1},{4,6},{5,7},{6,4},{7,5},{8,10},{9,11},{10,... | collective-permute-start | bytes 2752520 | tf_op jit(solution)/shard_map/ppermute | solution.py:487
  72.3 21.7 %collective-permute-start.12 = (bf16[16,192,128]{2,1,0:T(8,128)(2,1)}, bf16[16,192,128]{2,1,0:T(8,128)(2,1)S(1)}, u32[]{:S(2)}, u32[]{:S(2)}) collective-permute-start(bf16[16,192,128]{2,1,0:T(8,128)(2,1)} %get-tuple-element.282), channel_id=1, source_target_pairs={{0,1},{1,0},{2,3},{3,2},{4,5},{5,4},{6,7},{7,6},{8,9},{9,8},{10,11... | collective-permute-start | bytes 2359304 | tf_op jit(solution)/shard_map/ppermute | solution.py:487
  93.2 19.3 %collective-permute-start.9 = (bf16[16,448,128]{2,1,0:T(8,128)(2,1)}, bf16[16,448,128]{2,1,0:T(8,128)(2,1)}, u32[]{:S(2)}, u32[]{:S(2)}) collective-permute-start(bf16[16,448,128]{2,1,0:T(8,128)(2,1)} %get-tuple-element.271), channel_id=1, source_target_pairs={{0,1},{1,0},{2,3},{3,2},{4,5},{5,4},{6,7},{7,6},{8,9},{9,8},{10,11... | collective-permute-start | bytes 5505032 | tf_op jit(solution)/shard_map/ppermute | solution.py:487
  94.3 11.2 %collective-permute-start.21 = (bf16[40,3,512]{2,0,1:T(8,128)(2,1)S(1)}, bf16[40,3,512]{2,0,1:T(8,128)(2,1)S(1)}, u32[]{:S(2)}, u32[]{:S(2)}) collective-permute-start(bf16[40,3,512]{2,0,1:T(8,128)(2,1)S(1)} %constant_dynamic-slice_fusion), channel_id=1, source_target_pairs={{0,2},{1,3},{2,0},{3,1},{4,6},{5,7},{6,4},{7,5},{8,10},{9,11},{10,... | collective-permute-start | bytes 368648 | tf_op jit(solution)/shard_map/ppermute | solution.py:487
  101.4 11.1 %collective-permute-start.19 = (bf16[3,40,512]{2,1,0:T(8,128)(2,1)S(1)}, bf16[3,40,512]{2,1,0:T(8,128)(2,1)S(1)}, u32[]{:S(2)}, u32[]{:S(2)}) collective-permute-start(bf16[3,40,512]{2,1,0:T(8,128)(2,1)S(1)} %get-tuple-element.295), channel_id=1, source_target_pairs={{4,0},{8,4},{12,8},{16,12},{20,16},{24,20},{28,24},{0,28},{5,1},{9... | collective-permute-start | bytes 368648 | tf_op jit(solution)/shard_map/ppermute | solution.py:570
  104.4 8.1 %collective-permute-start.18 = (bf16[3,40,512]{2,1,0:T(8,128)(2,1)S(1)}, bf16[3,40,512]{2,1,0:T(8,128)(2,1)S(1)}, u32[]{:S(2)}, u32[]{:S(2)}) collective-permute-start(bf16[3,40,512]{2,1,0:T(8,128)(2,1)S(1)} %get-tuple-element.296), channel_id=1, source_target_pairs={{0,4},{4,8},{8,12},{12,16},{16,20},{20,24},{24,28},{28,0},{1,5},{5... | collective-permute-start | bytes 368648 | tf_op jit(solution)/shard_map/ppermute | solution.py:569
  105.5 22.9 %collective-permute-start.22 = (bf16[2,40,3,512]{3,1,2,0:T(8,128)(2,1)S(1)}, bf16[2,40,3,512]{3,1,2,0:T(8,128)(2,1)S(1)}, u32[]{:S(2)}, u32[]{:S(2)}) collective-permute-start(bf16[2,40,3,512]{3,1,2,0:T(8,128)(2,1)S(1)} %pad_maximum_fusion.10), channel_id=1, source_target_pairs={{0,1},{1,0},{2,3},{3,2},{4,5},{5,4},{6,7},{7,6},{8,9},{9,8},{10,11... | collective-permute-start | bytes 737288 | tf_op jit(solution)/shard_map/ppermute | solution.py:487
  163.2 12.6 %collective-permute-start.27 = (bf16[16,448,128]{2,1,0:T(8,128)(2,1)}, bf16[16,448,128]{2,1,0:T(8,128)(2,1)S(1)}, u32[]{:S(2)}, u32[]{:S(2)}) collective-permute-start(bf16[16,448,128]{2,1,0:T(8,128)(2,1)} %slice.320), channel_id=1, source_target_pairs={{0,1},{1,0},{2,3},{3,2},{4,5},{5,4},{6,7},{7,6},{8,9},{9,8},{10,11... | collective-permute-start | bytes 5505032 | tf_op jit(solution)/shard_map/ppermute | solution.py:487
  164.1 8.4 %collective-permute-start.24 = (bf16[3,40,512]{2,1,0:T(8,128)(2,1)S(1)}, bf16[3,40,512]{2,1,0:T(8,128)(2,1)S(1)}, u32[]{:S(2)}, u32[]{:S(2)}) collective-permute-start(bf16[3,40,512]{2,1,0:T(8,128)(2,1)S(1)} %get-tuple-element.293), channel_id=1, source_target_pairs={{0,4},{4,8},{8,12},{12,16},{16,20},{20,24},{24,28},{28,0},{1,5},{5... | collective-permute-start | bytes 368648 | tf_op jit(solution)/shard_map/ppermute | solution.py:569
  164.3 8.2 %collective-permute-start.25 = (bf16[3,40,512]{2,1,0:T(8,128)(2,1)S(1)}, bf16[3,40,512]{2,1,0:T(8,128)(2,1)S(1)}, u32[]{:S(2)}, u32[]{:S(2)}) collective-permute-start(bf16[3,40,512]{2,1,0:T(8,128)(2,1)S(1)} %get-tuple-element.294), channel_id=1, source_target_pairs={{4,0},{8,4},{12,8},{16,12},{20,16},{24,20},{28,24},{0,28},{5,1},{9... | collective-permute-start | bytes 368648 | tf_op jit(solution)/shard_map/ppermute | solution.py:570
  170.5 18.2 %collective-permute-start.23 = (bf16[40,3,512]{2,0,1:T(8,128)(2,1)}, bf16[40,3,512]{2,0,1:T(8,128)(2,1)S(1)}, u32[]{:S(2)}, u32[]{:S(2)}) collective-permute-start(bf16[40,3,512]{2,0,1:T(8,128)(2,1)} %dynamic-slice_bitcast_fusion.2), channel_id=1, source_target_pairs={{0,2},{1,3},{2,0},{3,1},{4,6},{5,7},{6,4},{7,5},{8,10},{9,11},{10,... | collective-permute-start | bytes 368648 | tf_op jit(solution)/shard_map/ppermute | solution.py:487
  187.2 16.9 %collective-permute-start.34 = (bf16[16,192,128]{2,1,0:T(8,128)(2,1)S(1)}, bf16[16,192,128]{2,1,0:T(8,128)(2,1)S(1)}, u32[]{:S(2)}, u32[]{:S(2)}) collective-permute-start(bf16[16,192,128]{2,1,0:T(8,128)(2,1)S(1)} %slice.266), channel_id=1, source_target_pairs={{0,1},{1,0},{2,3},{3,2},{4,5},{5,4},{6,7},{7,6},{8,9},{9,8},{10,11... | collective-permute-start | bytes 2359304 | tf_op jit(solution)/shard_map/ppermute | solution.py:487
  187.9 22.4 %collective-permute-start.35 = (bf16[8,448,128]{2,1,0:T(8,128)(2,1)S(1)}, bf16[8,448,128]{2,1,0:T(8,128)(2,1)}, u32[]{:S(2)}, u32[]{:S(2)}) collective-permute-start(bf16[8,448,128]{2,1,0:T(8,128)(2,1)S(1)} %slice.412), channel_id=1, source_target_pairs={{0,2},{1,3},{2,0},{3,1},{4,6},{5,7},{6,4},{7,5},{8,10},{9,11},{10,... | collective-permute-start | bytes 2752520 | tf_op jit(solution)/shard_map/ppermute | solution.py:487
  222.5 18.4 %collective-permute-start.36 = (bf16[16,256,128]{2,1,0:T(8,128)(2,1)}, bf16[16,256,128]{2,1,0:T(8,128)(2,1)}, u32[]{:S(2)}, u32[]{:S(2)}) collective-permute-start(bf16[16,256,128]{2,1,0:T(8,128)(2,1)} %slice.328), channel_id=1, source_target_pairs={{0,1},{1,0},{2,3},{3,2},{4,5},{5,4},{6,7},{7,6},{8,9},{9,8},{10,11... | collective-permute-start | bytes 3145736 | tf_op jit(solution)/shard_map/ppermute | solution.py:487
  222.6 8.9 %collective-permute-start.28 = (bf16[3,40,512]{2,1,0:T(8,128)(2,1)S(1)}, bf16[3,40,512]{2,1,0:T(8,128)(2,1)S(1)}, u32[]{:S(2)}, u32[]{:S(2)}) collective-permute-start(bf16[3,40,512]{2,1,0:T(8,128)(2,1)S(1)} %get-tuple-element.291), channel_id=1, source_target_pairs={{0,4},{4,8},{8,12},{12,16},{16,20},{20,24},{24,28},{28,0},{1,5},{5... | collective-permute-start | bytes 368648 | tf_op jit(solution)/shard_map/ppermute | solution.py:569
  222.6 8.8 %collective-permute-start.29 = (bf16[3,40,512]{2,1,0:T(8,128)(2,1)S(1)}, bf16[3,40,512]{2,1,0:T(8,128)(2,1)S(1)}, u32[]{:S(2)}, u32[]{:S(2)}) collective-permute-start(bf16[3,40,512]{2,1,0:T(8,128)(2,1)S(1)} %get-tuple-element.292), channel_id=1, source_target_pairs={{4,0},{8,4},{12,8},{16,12},{20,16},{24,20},{28,24},{0,28},{5,1},{9... | collective-permute-start | bytes 368648 | tf_op jit(solution)/shard_map/ppermute | solution.py:570
  227.3 12.3 %collective-permute-start.37 = (bf16[8,192,128]{2,1,0:T(8,128)(2,1)}, bf16[8,192,128]{2,1,0:T(8,128)(2,1)}, u32[]{:S(2)}, u32[]{:S(2)}) collective-permute-start(bf16[8,192,128]{2,1,0:T(8,128)(2,1)} %slice.415), channel_id=1, source_target_pairs={{0,2},{1,3},{2,0},{3,1},{4,6},{5,7},{6,4},{7,5},{8,10},{9,11},{10,... | collective-permute-start | bytes 1179656 | tf_op jit(solution)/shard_map/ppermute | solution.py:487
  230.1 16.8 %collective-permute-start.32 = (bf16[320,512]{1,0:T(8,128)(2,1)S(1)}, bf16[320,512]{1,0:T(8,128)(2,1)S(1)}, u32[]{:S(2)}, u32[]{:S(2)}) collective-permute-start(bf16[320,512]{1,0:T(8,128)(2,1)S(1)} %fusion.6), channel_id=1, source_target_pairs={{0,2},{1,3},{2,0},{3,1},{4,6},{5,7},{6,4},{7,5},{8,10},{9,11},{10,... | collective-permute-start | bytes 983048 | tf_op jit(solution)/shard_map/ppermute | solution.py:487
  244.0 13.9 %collective-permute-start.39 = (bf16[8,256,128]{2,1,0:T(8,128)(2,1)S(1)}, bf16[8,256,128]{2,1,0:T(8,128)(2,1)S(1)}, u32[]{:S(2)}, u32[]{:S(2)}) collective-permute-start(bf16[8,256,128]{2,1,0:T(8,128)(2,1)S(1)} %slice.413), channel_id=1, source_target_pairs={{0,2},{1,3},{2,0},{3,1},{4,6},{5,7},{6,4},{7,5},{8,10},{9,11},{10,... | collective-permute-start | bytes 1572872 | tf_op jit(solution)/shard_map/ppermute | solution.py:487
  244.7 14.6 %collective-permute-start.40 = (bf16[4,640,128]{2,1,0:T(8,128)(2,1)S(1)}, bf16[4,640,128]{2,1,0:T(8,128)(2,1)S(1)}, u32[]{:S(2)}, u32[]{:S(2)}) collective-permute-start(bf16[4,640,128]{2,1,0:T(8,128)(2,1)S(1)} %pad_maximum_fusion.4), channel_id=1, source_target_pairs={{0,4},{4,0},{8,12},{12,8},{16,20},{20,16},{24,28},{28,24},{1,5},{5... | collective-permute-start | bytes 1966088 | tf_op jit(solution)/shard_map/ppermute | solution.py:487
  246.1 13.8 %collective-permute-start.30 = (bf16[3,160,512]{2,1,0:T(8,128)(2,1)S(1)}, bf16[3,160,512]{2,1,0:T(8,128)(2,1)S(1)}, u32[]{:S(2)}, u32[]{:S(2)}) collective-permute-start(bf16[3,160,512]{2,1,0:T(8,128)(2,1)S(1)} %get-tuple-element.267), channel_id=1, source_target_pairs={{0,1},{1,0},{2,3},{3,2},{4,5},{5,4},{6,7},{7,6},{8,9},{9,8},{10,11... | collective-permute-start | bytes 1474568 | tf_op jit(solution)/shard_map/ppermute | solution.py:487
  246.1 11.8 %collective-permute-start.38 = (f32[17,512]{1,0:T(8,128)S(1)}, f32[17,512]{1,0:T(8,128)S(1)}, u32[]{:S(2)}, u32[]{:S(2)}) collective-permute-start(f32[17,512]{1,0:T(8,128)S(1)} %add.288), channel_id=1, source_target_pairs={{0,2},{1,3},{2,0},{3,1},{4,6},{5,7},{6,4},{7,5},{8,10},{9,11},{10,... | collective-permute-start | bytes 104456 | tf_op jit(solution)/shard_map/ppermute | solution.py:487
  262.0 8.2 %collective-permute-start.31 = (bf16[40,3,512]{2,0,1:T(8,128)(2,1)S(1)}, bf16[40,3,512]{2,0,1:T(8,128)(2,1)S(1)}, u32[]{:S(2)}, u32[]{:S(2)}) collective-permute-start(bf16[40,3,512]{2,0,1:T(8,128)(2,1)S(1)} %dynamic-slice_bitcast_fusion.1), channel_id=1, source_target_pairs={{0,2},{1,3},{2,0},{3,1},{4,6},{5,7},{6,4},{7,5},{8,10},{9,11},{10,... | collective-permute-start | bytes 368648 | tf_op jit(solution)/shard_map/ppermute | solution.py:487
  (89 other events, 860.3 us)

commit v2 on v1

--- a/solution.py
+++ b/solution.py
@@ -69,14 +69,26 @@
             ]
 
 
-def pack(values, order, rows, offset, target):
-    width = target.shape[2]
-    nodes, hids = values.shape[0] // rows, values.shape[1] // width
-    for i in range(nodes):
-        for j in range(hids):
-            target[order[i * hids + j], offset : offset + rows, :] = values[
-                i * rows : (i + 1) * rows, j * width : (j + 1) * width
-            ].astype(target.dtype)
+def store(target, begin, values):
+    rows, width = values.shape[0], target.shape[2]
+    for j in range(target.shape[0]):
+        target[j, begin : begin + rows] = values[:, j * width : (j + 1) * width]
+
+
+def add(target, begin, values):
+    rows, width = values.shape[0], target.shape[2]
+    for j in range(target.shape[0]):
+        target[j, begin : begin + rows] += values[:, j * width : (j + 1) * width]
+
+
+def pack(values, owners, rows, offset, kept, sent):
+    half = kept.shape[0]
+    for place in range(2 * half):
+        target = kept if place < half else sent
+        begin = pl.multiple_of(owners[2 * place] * rows, rows)
+        target[place % half, offset : offset + rows, :] = values[
+            owners[2 * place + 1], pl.ds(begin, rows), :
+        ].astype(BF16)
 
 
 def per_sample(array):
@@ -116,7 +128,7 @@
         compiler_params=pltpu.CompilerParams(
             dimension_semantics=("arbitrary",), vmem_limit_bytes=VMEM_BYTES
         ),
-        cost_estimate=pl.CostEstimate(flops=flops, bytes_accessed=moved, transcendentals=0),
+        cost_estimate=pl.CostEstimate(flops=4 * flops, bytes_accessed=moved, transcendentals=0),
     )(*inputs)
 
 
@@ -295,67 +307,70 @@
     )
 
 
-def edge_weight_grads(order, edge_low, table, hidden_low, at_rows, low, act, node_total, nodes, width, packed_before):
+def edge_weight_grads(owners, edge_low, table, hidden_low, at_rows, low, act, node_total, nodes, width, packed_before):
     samples, table_total, latent = table.shape
     alike = edge_low.ndim == 2
     first_rows, second_rows = 3 * latent // nodes, latent // nodes
-    offset = 0 if packed_before is None else packed_before.shape[1]
-
-    def kernel(order, edge_low, table, hidden_low, at_rows, low, act, *rest):
-        if packed_before is not None:
-            before, rest = rest[0], rest[1:]
-        packed, first, second = rest
+    offset = 0 if packed_before is None else packed_before[0].shape[1]
+    blocks, hids = owners.shape[0] // 2, latent // width
+
+    def kernel(owners, edge_low, table, hidden_low, at_rows, low, act, *rest):
+        before, rest = rest[:-4], rest[-4:]
+        kept, sent, first, second = rest
         step = pl.program_id(0)
 
         @pl.when(step == 0)
         def _():
             first[...] = jnp.zeros_like(first)
             second[...] = jnp.zeros_like(second)
-            if packed_before is not None:
-                packed[:, :offset, :] = before[...]
+            for source, target in zip(before, (kept, sent)):
+                target[:, :offset, :] = source[...]
             if alike:
-                first[:latent] = matmul_tn(edge_low[...], hidden_low[...])
+                add(first, 0, matmul_tn(edge_low[...], hidden_low[...]))
 
         if not alike:
-            first[:latent] += matmul_tn(edge_low[0], hidden_low[0])
-        first[latent : 2 * latent] += matmul_tn(table[0], at_rows[0, :table_total])
-        first[2 * latent :] += matmul_tn(table[0, :node_total], at_rows[0, table_total:])
-        second[...] += matmul_tn(low[0], act[0])
+            add(first, 0, matmul_tn(edge_low[0], hidden_low[0]))
+        add(first, latent, matmul_tn(table[0], at_rows[0, :table_total]))
+        add(first, 2 * latent, matmul_tn(table[0, :node_total], at_rows[0, table_total:]))
+        add(second, 0, matmul_tn(low[0], act[0]))
 
         @pl.when(step == samples - 1)
         def _():
-            pack(first, order, first_rows, offset, packed)
-            pack(second, order, second_rows, offset + first_rows, packed)
+            pack(first, owners, first_rows, offset, kept, sent)
+            pack(second, owners, second_rows, offset + first_rows, kept, sent)
 
     of_edges = constant if alike else per_sample
-    inputs = [order, edge_low, table, hidden_low, at_rows, low, act]
+    inputs = [owners, edge_low, table, hidden_low, at_rows, low, act]
     specs = [in_scalars(), of_edges(edge_low), per_sample(table), of_edges(hidden_low), per_sample(at_rows), per_sample(low), per_sample(act)]
     if packed_before is not None:
-        inputs.append(packed_before)
-        specs.append(constant(packed_before))
+        inputs += packed_before
+        specs += [constant(a) for a in packed_before]
     return run_kernel(
         kernel,
         "edge_weight_grads",
         samples,
         inputs,
         specs,
-        [shared((order.shape[0], offset + first_rows + second_rows, width), BF16)],
-        [pltpu.VMEM((3 * latent, latent), F32), pltpu.VMEM((latent, latent), F32)],
+        [shared((blocks // 2, offset + first_rows + second_rows, width), BF16)] * 2,
+        [pltpu.VMEM((hids, 3 * latent, width), F32), pltpu.VMEM((hids, latent, width), F32)],
         4 * low.size * latent,
-    )[0]
-
-
-def node_pass(order, weights, nodes, node_low, state, pooled_pair, params, at_halo, target, scaling, mask):
+    )
+
+
+def node_pass(order, owners, weights, nodes, node_low, state, pooled_pair, params, at_halo, target, scaling, mask):
     samples, node_total, latent = node_low.shape
     array, rows, place = weights
-    second_rows = latent // nodes
+    second_rows, hids = latent // nodes, latent // array.shape[2]
     first_rows = rows - second_rows
     count = samples * node_total
     last = target is not None
 
-    def kernel(order, w, node_low, state, pooled_own, pooled_other, params, *rest):
+    def kernel(order, *rest):
         if last:
-            target, scaling, mask, new_low, upstream, input_grad, packed, minor, w1s, w2s, first, second = rest
+            owners, rest = rest[0], rest[1:]
+        w, node_low, state, pooled_own, pooled_other, params, *rest = rest
+        if last:
+            target, scaling, mask, new_low, upstream, input_grad, kept, sent, minor, w1s, w2s, first, second = rest
         else:
             at_halo, pooled_out, pre, act, normed, inverse, new_state, new_low, halo, w1s, w2s = rest
         assemble(w, order, first_rows, 0, w1s)
@@ -383,16 +398,16 @@
             grad = (target[...].astype(F32) * scaling[...]).reshape(count, latent)
             node_gradients(
                 grad, scaled, scale, hidden, active, rows_low, pooled, params, mask,
-                w1s, w2s, first, second, upstream, input_grad, packed, minor, order, first_rows, second_rows,
+                w1s, w2s, first, second, upstream, input_grad, kept, sent, minor, owners, first_rows, second_rows,
             )
 
     shape = node_low.shape
-    inputs = [order, array, node_low, state, *pooled_pair, params]
+    inputs = [array, node_low, state, *pooled_pair, params]
     scratch = [pltpu.VMEM((2 * latent, latent), BF16), pltpu.VMEM((latent, latent), BF16)]
     if last:
         inputs += [target, scaling, mask]
         outputs = [shared(shape, BF16), *gradient_outputs(shape, order.shape[0], rows, array.shape[2])]
-        scratch += [pltpu.VMEM((2 * latent, latent), F32), pltpu.VMEM((latent, latent), F32)]
+        scratch += [pltpu.VMEM((hids, 2 * latent, latent // hids), F32), pltpu.VMEM((hids, latent, latent // hids), F32)]
     else:
         inputs += [at_halo]
         outputs = [
@@ -405,7 +420,9 @@
             shared(shape, BF16),
             shared((samples, at_halo.shape[0], latent), BF16),
         ]
-    specs = [in_scalars(), weight_block(*weights)] + [constant(a) for a in inputs[2:]]
+    tables = [order, owners] if last else [order]
+    specs = [in_scalars() for _ in tables] + [weight_block(*weights)] + [constant(a) for a in inputs[1:]]
+    inputs = tables + inputs
     return run_kernel(kernel, "node_pass", 1, inputs, specs, outputs, scratch, 6 * count * latent * latent * (3 if last else 1))
 
 
@@ -413,14 +430,15 @@
     return [
         shared(shape, BF16),
         shared(shape, F32),
-        shared((blocks, rows, width), BF16),
+        shared((blocks // 2, rows, width), BF16),
+        shared((blocks // 2, rows, width), BF16),
         shared((4, shape[-1]), F32),
     ]
 
 
 def node_gradients(
     grad, scaled, scale, hidden, active, rows_low, pooled, params, mask,
-    w1s, w2s, first, second, upstream, input_grad, packed, minor, order, first_rows, second_rows,
+    w1s, w2s, first, second, upstream, input_grad, kept, sent, minor, owners, first_rows, second_rows,
 ):
     latent = w2s.shape[0]
     output_grad = norm_backward(grad, scaled, scale, params[6:7]).astype(BF16)
@@ -436,32 +454,32 @@
     minor[2:3] = column_sum(grad_mine * scaled)
     minor[3:4] = column_sum(grad_mine)
     pre_mine = pre_mine.astype(BF16)
-    first[:latent] = matmul_tn(rows_low, pre_mine)
-    first[latent:] = matmul_tn(pooled, pre_mine)
-    second[...] = matmul_tn(output_mine.astype(BF16), active)
-    pack(first, order, first_rows, 0, packed)
-    pack(second, order, second_rows, first_rows, packed)
-
-
-def node_backward(order, weights, nodes, grads, node_low, pooled, pre, act, normed, inverse, params, mask):
+    store(first, 0, matmul_tn(rows_low, pre_mine))
+    store(first, latent, matmul_tn(pooled, pre_mine))
+    store(second, 0, matmul_tn(output_mine.astype(BF16), active))
+    pack(first, owners, first_rows, 0, kept, sent)
+    pack(second, owners, second_rows, first_rows, kept, sent)
+
+
+def node_backward(order, owners, weights, nodes, grads, node_low, pooled, pre, act, normed, inverse, params, mask):
     samples, node_total, latent = node_low.shape
     array, rows, place = weights
-    second_rows = latent // nodes
+    second_rows, hids = latent // nodes, latent // array.shape[2]
     first_rows = rows - second_rows
     count = samples * node_total
 
-    def kernel(order, w, base, own, other, node_low, pooled, pre, act, normed, inverse, params, mask, upstream, input_grad, packed, minor, w1s, w2s, first, second):
+    def kernel(order, owners, w, base, own, other, node_low, pooled, pre, act, normed, inverse, params, mask, upstream, input_grad, kept, sent, minor, w1s, w2s, first, second):
         assemble(w, order, first_rows, 0, w1s)
         assemble(w, order, second_rows, first_rows, w2s)
         grad = (base[...] + (own[...] + other[...].astype(F32))).reshape(count, latent)
         node_gradients(
             grad, normed[...].astype(F32), inverse[...], pre[...].astype(F32), act[...],
             node_low[...].reshape(count, latent), pooled[...], params, mask,
-            w1s, w2s, first, second, upstream, input_grad, packed, minor, order, first_rows, second_rows,
+            w1s, w2s, first, second, upstream, input_grad, kept, sent, minor, owners, first_rows, second_rows,
         )
 
-    inputs = [order, array, *grads, node_low, pooled, pre, act, normed, inverse, params, mask]
-    specs = [in_scalars(), weight_block(*weights)] + [constant(a) for a in inputs[2:]]
+    inputs = [order, owners, array, *grads, node_low, pooled, pre, act, normed, inverse, params, mask]
+    specs = [in_scalars(), in_scalars(), weight_block(*weights)] + [constant(a) for a in inputs[3:]]
     return run_kernel(
         kernel,
         "node_backward",
@@ -472,8 +490,8 @@
         [
             pltpu.VMEM((2 * latent, latent), BF16),
             pltpu.VMEM((latent, latent), BF16),
-            pltpu.VMEM((2 * latent, latent), F32),
-            pltpu.VMEM((latent, latent), F32),
+            pltpu.VMEM((hids, 2 * latent, latent // hids), F32),
+            pltpu.VMEM((hids, latent, latent // hids), F32),
         ],
         12 * count * latent * latent,
     )
@@ -527,24 +545,29 @@
     return place.reshape(-1)
 
 
+def owners_of_places():
+    place = jnp.arange(1 << len(all_bits()), dtype=jnp.int32)
+    owner = {"node": lax.axis_index("node"), "hid": lax.axis_index("hid")}
+    for step, (axis, bit) in enumerate(all_bits()):
+        owner[axis] = owner[axis] ^ (((place >> step) & 1) << bit)
+    return jnp.stack([owner["node"], owner["hid"]], axis=1).reshape(-1)
+
+
 def after(value, *earlier):
     return lax.optimization_barrier((value, *earlier))[0]
 
 
-def gather_step(held, step):
-    axis, bit = all_bits()[step]
-    return jnp.concatenate([held, swap(held, axis, 1 << bit)], axis=0)
-
-
-def scatter_start(packed):
-    half = packed.shape[0] // 2
-    return packed[:half], packed[half:]
-
-
-def scatter_step(pair, step):
+def gather_steps(held, begin, end, *under):
+    for axis, bit in all_bits()[begin:end]:
+        arrived = after(swap(held, axis, 1 << bit), *under)
+        held = jnp.concatenate([held, arrived], axis=0)
+    return held
+
+
+def scatter_step(pair, step, *under):
     axis, bit = all_bits()[step]
     kept, sent = pair
-    total = kept.astype(F32) + swap(sent, axis, 1 << bit).astype(F32)
+    total = kept.astype(F32) + after(swap(sent, axis, 1 << bit), *under).astype(F32)
     if step == 0:
         return total[0]
     half = total.shape[0] // 2
@@ -557,8 +580,19 @@
 
 
 def sum_everywhere(values):
-    for axis, bit in reversed(all_bits()):
-        values = values + swap(values, axis, 1 << bit)
+    axes = ("node", "hid")
+    bits = sum(bits_of(axis) for axis in axes)
+    total = 1 << bits
+    done = 0
+    while done < bits:
+        step = 1 if (bits - done) % 2 else 2
+        terms = [values]
+        for i in range(1, 1 << step):
+            pairs = [(k, k ^ (i << done)) for k in range(total)]
+            terms.append(lax.ppermute(values, axes, pairs))
+        while len(terms) > 1:
+            terms = [terms[i] + terms[i + 1] for i in range(0, len(terms), 2)]
+        values, done = terms[0], done + step
     return values
 
 
@@ -631,26 +665,25 @@
     node_rows = node_first.shape[1] + second_rows
     width = edge_first.shape[2]
 
-    order = places()
+    order, owners = places(), owners_of_places()
     steps = len(all_bits())
-    edge_zero = pack_shards(edge_first[0], edge_second[0])[None]
-    for step in range(steps - 2):
-        edge_zero = gather_step(edge_zero, step)
+    edge_zero = gather_steps(pack_shards(edge_first[0], edge_second[0])[None], 0, steps - 2)
     setup = edge_zero
-    node_zero = after(pack_shards(node_first[0], node_second[0])[None], edge_zero)
-    layer_one = jnp.concatenate(
-        [pack_shards(node_first[1], node_second[1]), pack_shards(edge_first[1], edge_second[1])], axis=0
-    )[None]
-    for step in range(steps - 3):
-        node_zero = gather_step(node_zero, step)
-    layer_one = after(layer_one, node_zero)
-    layer_one = gather_step(layer_one, 0)
-    edge_zero = gather_step(edge_zero, steps - 2)
-    edge_zero = after(edge_zero, node_zero)
-    edge_zero = gather_step(edge_zero, steps - 1)
-    node_zero = gather_step(node_zero, steps - 3)
-    edge_zero = after(edge_zero, node_zero, layer_one)
-    edge_weights = [((edge_zero, first_rows, 0), (edge_zero, second_rows, first_rows // second_rows))]
+    first, second = after((node_first[0], node_second[0]), edge_zero)
+    node_zero = gather_steps(pack_shards(first, second)[None], 0, steps - 3)
+    edge_zero = gather_steps(edge_zero, steps - 2, steps - 1)
+    first, second = after((edge_first[1], edge_second[1]), edge_zero)
+    edge_zero = gather_steps(after(edge_zero, node_zero), steps - 1, steps)
+    node_zero = gather_steps(node_zero, steps - 3, steps - 2)
+    edge_one = gather_steps(pack_shards(first, second)[None], 0, 1)
+    masters = (edge_first, edge_second, node_first, node_second)
+    weight_local = jnp.stack(
+        [jnp.sum(matrix * matrix, axis=(1, 2)) for matrix in after(masters, setup)], axis=1
+    )
+    edge_zero = after(edge_zero, node_zero, edge_one, weight_local)
+
+    def edge_blocks(whole):
+        return ((whole, first_rows, 0), (whole, second_rows, first_rows // second_rows))
 
     def own_edges(values):
         return lax.dynamic_index_in_dim(
@@ -697,7 +730,7 @@
     table_zero = jnp.concatenate([node_low, to_neighbours(halo_rows, halo_width)], axis=1)
     pre_zero, act_zero, normed_zero, inverse_zero, edge_state, edge_low, pooled = edge_forward(
         order,
-        *edge_weights[0],
+        *edge_blocks(edge_zero),
         table_zero,
         edge_in_own[None],
         edge_in_own[None],
@@ -707,13 +740,13 @@
         node_total,
         False,
     )
-    for step in range(steps - 2, steps):
-        node_zero = gather_step(node_zero, step)
-    for step in range(1, steps - 2):
-        layer_one = gather_step(layer_one, step)
-    node_weights = [(node_zero, node_rows, 0)]
-    other = swap(pooled, "hid", 1)
-    pooled, other = lax.optimization_barrier((pooled, other, layer_one))[:2]
+    node_zero = gather_steps(node_zero, steps - 2, steps - 1, pooled)
+    node_zero = gather_steps(node_zero, steps - 1, steps)
+    edge_one = gather_steps(edge_one, 1, steps - 3, pooled)
+    edge_one = gather_steps(edge_one, steps - 3, steps - 2)
+    other = after(swap(pooled, "hid", 1), edge_one)
+    first, second = after((node_first[1], node_second[1]), edge_one)
+    node_one = gather_steps(pack_shards(first, second)[None], 0, steps - 3)
     (
         pooled_zero,
         node_pre,
@@ -725,7 +758,8 @@
         halo_rows,
     ) = node_pass(
         order,
-        node_weights[0],
+        None,
+        (node_zero, node_rows, 0),
         nodes,
         node_low_zero,
         node_low_zero,
@@ -736,12 +770,10 @@
         None,
         None,
     )
-    for step in range(steps - 2, steps):
-        layer_one = gather_step(layer_one, step)
-    edge_weights.append(
-        ((layer_one, first_rows, 1), (layer_one, second_rows, 2 * first_rows // second_rows))
-    )
-    node_weights.append((layer_one, node_rows, 0))
+    edge_one = gather_steps(edge_one, steps - 2, steps - 1, halo_rows)
+    edge_one = gather_steps(after(edge_one, node_one), steps - 1, steps)
+    node_one = gather_steps(node_one, steps - 3, steps - 2)
+    edge_one = after(edge_one, node_one)
 
     valid_mask = (ocean_mask[:, None] * present_mask).astype(BF16)
     masked = after(cotangent, pooled) * valid_mask[:, :, None]
@@ -757,7 +789,7 @@
     table_one = jnp.concatenate([node_low, to_neighbours(halo_rows, halo_width)], axis=1)
     pre_one, act_one, normed_one, inverse_one, pooled = edge_forward(
         order,
-        *edge_weights[1],
+        *edge_blocks(edge_one),
         table_one,
         edge_low,
         edge_state,
@@ -767,9 +799,12 @@
         node_total,
         True,
     )
-    node_low, pooled_grad, node_grad, node_packed, node_minor_one = node_pass(
+    node_one = gather_steps(node_one, steps - 2, steps - 1, pooled)
+    node_one = gather_steps(node_one, steps - 1, steps)
+    node_low, pooled_grad, node_grad, kept, sent, node_minor_one = node_pass(
         order,
-        node_weights[1],
+        owners,
+        (node_one, node_rows, 0),
         nodes,
         node_low_one,
         node_state,
@@ -780,19 +815,13 @@
         scaling,
         mask,
     )
-    masters = (edge_first, edge_second, node_first, node_second)
-    weight_local = jnp.stack(
-        [jnp.sum(matrix * matrix, axis=(1, 2)) for matrix in after(masters, node_low)], axis=1
-    )
-    node_out = to_own_rows(node_low)
 
     def from_edges(partial, returned):
-        returned = to_neighbours(returned, halo_width)
         return partial + dot("hn,shl->snl", at_halo, returned)
 
     low, hidden_low, at_rows, partial, returned, edge_grad, edge_minor_one = edge_backward(
         order,
-        *edge_weights[1],
+        *edge_blocks(edge_one),
         pooled_grad,
         None,
         normed_one,
@@ -804,8 +833,8 @@
         True,
         node_total,
     )
-    packed = edge_weight_grads(
-        order,
+    chain_one = edge_weight_grads(
+        owners,
         edge_low,
         table_one,
         hidden_low,
@@ -815,16 +844,18 @@
         node_total,
         nodes,
         width,
-        node_packed,
+        [kept, sent],
+    )
+    returned, *chain_one = lax.optimization_barrier(
+        (to_neighbours(returned, halo_width), *chain_one)
     )
     partial = from_edges(partial, returned)
-    other = swap(partial.astype(BF16), "hid", 1)
-    chain_one = scatter_step(scatter_start(packed), steps - 1)
-    other, kept, sent = lax.optimization_barrier((other, *chain_one))
-    chain_one = (kept, sent)
-    pooled_grad, node_grad, node_packed, node_minor_zero = node_backward(
+    chain_one = scatter_step(chain_one, steps - 1)
+    other, *chain_one = lax.optimization_barrier((swap(partial.astype(BF16), "hid", 1), *chain_one))
+    pooled_grad, node_grad, kept, sent, node_minor_zero = node_backward(
         order,
-        node_weights[0],
+        owners,
+        (node_zero, node_rows, 0),
         nodes,
         (node_grad, partial, other),
         node_low_zero,
@@ -839,7 +870,7 @@
     low, hidden_low, at_rows, partial, returned, edge_input_grad, edge_minor_zero, hidden_sum = (
         edge_backward(
             order,
-            *edge_weights[0],
+            *edge_blocks(edge_zero),
             pooled_grad,
             edge_grad,
             normed_zero,
@@ -852,12 +883,12 @@
             node_total,
         )
     )
-    chain_zero = scatter_step(scatter_start(node_packed), steps - 1)
-    chain_one = scatter_step(chain_one, steps - 2)
-    low, *held = lax.optimization_barrier((low, *chain_zero, *chain_one))
-    chain_zero, chain_one = held[:2], held[2:]
-    packed = edge_weight_grads(
-        order,
+    chain_one = scatter_step(chain_one, steps - 2, low)
+    chain_zero = scatter_step((kept, sent), steps - 1, low)
+    low = after(low, *chain_one, *chain_zero)
+    node_out = to_own_rows(after(node_low, low))
+    chain_edge = edge_weight_grads(
+        owners,
         edge_in_own,
         table_zero,
         hidden_sum,
@@ -874,9 +905,10 @@
         + [jnp.pad(weight_local.reshape(1, -1), ((0, 0), (0, latent - weight_local.size)))],
         axis=0,
     )
-    chain_zero = scatter_step(chain_zero, steps - 2)
+    chain_zero = scatter_step(chain_zero, steps - 2, chain_edge[1])
     chain_one = tuple(jnp.concatenate(pair, axis=1) for pair in zip(chain_one, chain_zero))
-    chain_edge = scatter_step(scatter_start(packed), steps - 1)
+    chain_edge = [chain_edge[0], after(chain_edge[1], *chain_one)]
+    chain_edge = scatter_step(chain_edge, steps - 1)
     minor_packed = sum_step(minor_packed, steps - 1)
     for step in reversed(range(steps - 1)):
         minor_packed, *held = lax.optimization_barrier(
@@ -890,7 +922,7 @@
         if step == 1:
             chain_one = (chain_one,)
     edge_zero_grads, node_grads = chain_edge, chain_one[0]
-    partial = from_edges(partial, returned)
+    partial = from_edges(partial, to_neighbours(returned, halo_width))
     node_grad = node_grad + (partial + swap(partial.astype(BF16), "hid", 1).astype(F32))
     grad_node = to_own_rows(node_grad.astype(BF16))
     edge_input_grad = halve_sum(edge_input_grad.reshape(2, edge_part, latent), "hid", 1, 0)

time: 307 us -> 300 us (0.977)
  starting transfers between devices: 49.1 us -> 62.2 us
  local copies, waits for them, and re-layouts: 48.1 us -> 35.2 us
  waiting for transfers between devices: 86.8 us -> 81 us
    ppermute x46, waiting for transfers between devices: 78.9 us -> 70.3 us  [swap(): lax.ppermute(values, axis, [(i, i ^ offset) for i in range(lax.axis_size(...]
    ppermute x0 -> x7, starting transfers between devices: none -> 7.88 us  [sum_everywhere(): terms.append(lax.ppermute(values, axes, pairs))]
    unnamed x136 -> x169, local copies, waits for them, and re-layouts: 19 us -> 12.5 us
    ppermute x0 -> x7, waiting for transfers between devices: none -> 6.09 us  [sum_everywhere(): terms.append(lax.ppermute(values, axes, pairs))]
    slice x5 -> x1, local copies, waits for them, and re-layouts: 6.59 us -> 1.06 us  [per_device(): edge_first[0]]
    ppermute x4, waiting for transfers between devices: 7.83 us -> 3.48 us  [to_neighbours(): from_previous = lax.ppermute(rows[:, halo_width:], 'node', onward)]
    another operation x4 -> x1, other arithmetic: 3.65 us -> 0.01 us  [owners_of_places(): return jnp.stack([owner['node'], owner['hid']], axis=1).reshape(-1)]
    ppermute x46, starting transfers between devices: 31.8 us -> 35.2 us  [swap(): lax.ppermute(values, axis, [(i, i ^ offset) for i in range(lax.axis_size(...]
  transfers between devices with their start and end apart: 54 -> 61, of which waited for: 27 -> 26; matrix products, arithmetic and copies ran while one was open for 18% -> 16% of each run, Pallas kernels for 16% -> 20%
where the time goes in v2:
time: 300 us; the launch traced here: 299 us
  Pallas kernels  86.8 us (29%)
  waiting for transfers between devices  81 us (27%)
  starting transfers between devices  62.2 us (21%)
  local copies, waits for them, and re-layouts  35.2 us (12%)
  other arithmetic  29 us (10%)
    pallas_call x9, Pallas kernels, run_kernel(): pl.pallas_call(kernel, name=name, grid=(samples,), in_specs=in_specs, out...  86.8 us
    ppermute x46, waiting for transfers between devices, swap(): lax.ppermute(values, axis, [(i, i ^ offset) for i in range(lax.axis_size(...  70.3 us
    ppermute x46, starting transfers between devices, swap(): lax.ppermute(values, axis, [(i, i ^ offset) for i in range(lax.axis_size(...  35.2 us
    ppermute x4, starting transfers between devices, to_neighbours(): from_next = lax.ppermute(rows[:, :halo_width], 'node', back)  15.5 us
    unnamed x169, local copies, waits for them, and re-layouts  12.5 us
    ppermute x7, starting transfers between devices, sum_everywhere(): terms.append(lax.ppermute(values, axes, pairs))  7.88 us
    concatenate x14, other arithmetic, gather_steps(): held = jnp.concatenate([held, arrived], axis=0)  6.51 us
    ppermute x7, waiting for transfers between devices, sum_everywhere(): terms.append(lax.ppermute(values, axes, pairs))  6.09 us
  transfers between devices with their start and end apart: 61, of which 26 were waited for; matrix products, arithmetic and copies ran while one was open for 16% of the time, Pallas kernels for 20%

profile of v2, /device:TPU:0, one launch (start us, length us, event | category | flops | bytes accessed | tf_op | source)
XLA Modules:
  0.0 299.3 jit_solution(11064124552087165867)
XLA Ops:
  3.2 4.1 %collective-permute-start = (bf16[1,256,128]{2,1,0:T(8,128)(2,1)S(1)}, bf16[1,256,128]{2,1,0:T(8,128)(2,1)S(1)}, u32[]{:S(2)}, u32[]{:S(2)}) collective-permute-start(bf16[1,256,128]{2,1,0:T(8,128)(2,1)S(1)} %get-tuple-element.371), channel_id=1, source_target_pairs={{0,16},{4,20},{8,24},{12,28},{16,0},{20,4},{24,8},{28,12},{1,17},{... | collective-permute-start | bytes 196616 | tf_op jit(solution)/shard_map/ppermute | solution.py:505
  16.6 3.4 %collective-permute-done.1 = bf16[2,256,128]{2,1,0:T(8,128)(2,1)S(1)} collective-permute-done((bf16[2,256,128]{2,1,0:T(8,128)(2,1)S(1)}, bf16[2,256,128]{2,1,0:T(8,128)(2,1)S(1)}, u32[]{:S(2)}, u32[]{:S(2)}) %collective-permute-start.1) | collective-permute-done | bytes 131104 | tf_op jit(solution)/shard_map/ppermute | solution.py:505
  24.5 2.1 collective-permute-done.2
  34.6 3.2 %collective-permute-start.11 = (bf16[3,40,512]{2,1,0:T(8,128)(2,1)}, bf16[3,40,512]{2,1,0:T(8,128)(2,1)}, u32[]{:S(2)}, u32[]{:S(2)}) collective-permute-start(bf16[3,40,512]{2,1,0:T(8,128)(2,1)} %get-tuple-element.354), channel_id=1, source_target_pairs={{4,0},{8,4},{12,8},{16,12},{20,16},{24,20},{28,24},{0,28},{5,1},{9... | collective-permute-start | bytes 368648 | tf_op jit(solution)/shard_map/ppermute | solution.py:604
  42.6 4.5 %collective-permute-done.7 = bf16[2,192,128]{2,1,0:T(8,128)(2,1)S(1)} collective-permute-done((bf16[2,192,128]{2,1,0:T(8,128)(2,1)S(1)}, bf16[2,192,128]{2,1,0:T(8,128)(2,1)S(1)}, u32[]{:S(2)}, u32[]{:S(2)}) %collective-permute-start.7) | collective-permute-done | bytes 98336 | tf_op jit(solution)/shard_map/ppermute | solution.py:505
  53.7 4.7 %collective-permute-done.9 = bf16[4,192,128]{2,1,0:T(8,128)(2,1)S(1)} collective-permute-done((bf16[4,192,128]{2,1,0:T(8,128)(2,1)S(1)}, bf16[4,192,128]{2,1,0:T(8,128)(2,1)S(1)}, u32[]{:S(2)}, u32[]{:S(2)}) %collective-permute-start.9) | collective-permute-done | bytes 196640 | tf_op jit(solution)/shard_map/ppermute | solution.py:505
  61.4 4.3 %collective-permute-done.4 = bf16[1,256,128]{2,1,0:T(8,128)(2,1)S(1)} collective-permute-done((bf16[1,256,128]{2,1,0:T(8,128)(2,1)S(1)}, bf16[1,256,128]{2,1,0:T(8,128)(2,1)S(1)}, u32[]{:S(2)}, u32[]{:S(2)}) %collective-permute-start.4) | collective-permute-done | bytes 65568 | tf_op jit(solution)/shard_map/ppermute | solution.py:505
  67.5 11.7 %edge_forward.2 = (bf16[3,640,512]{2,1,0:T(8,128)(2,1)}, bf16[3,640,512]{2,1,0:T(8,128)(2,1)}, bf16[3,640,512]{2,1,0:T(8,128)(2,1)}, f32[3,640,1]{2,1,0:T(8,128)...) custom-call(s32[32]{0:T(128)} %add.279.order, ...), custom_call_target="tpu_custom_call" | custom-call | flops 15225323520 | bytes 19271296 | tf_op jit(solution)/shard_map/edge_forward/pallas_call | solution.py:120
  81.8 6.2 %collective-permute-done.12 = bf16[4,256,128]{2,1,0:T(8,128)(2,1)S(1)} collective-permute-done((bf16[4,256,128]{2,1,0:T(8,128)(2,1)S(1)}, bf16[4,256,128]{2,1,0:T(8,128)(2,1)S(1)}, u32[]{:S(2)}, u32[]{:S(2)}) %collective-permute-start.12) | collective-permute-done | bytes 262176 | tf_op jit(solution)/shard_map/ppermute | solution.py:505
  88.7 2.3 collective-permute-start.13
  95.8 3.1 %collective-permute-done.14 = bf16[2,192,128]{2,1,0:T(8,128)(2,1)S(1)} collective-permute-done((bf16[2,192,128]{2,1,0:T(8,128)(2,1)S(1)}, bf16[2,192,128]{2,1,0:T(8,128)(2,1)S(1)}, u32[]{:S(2)}, u32[]{:S(2)}) %collective-permute-start.14) | collective-permute-done | bytes 98336 | tf_op jit(solution)/shard_map/ppermute | solution.py:505
  100.4 5.0 %node_pass.2 = (bf16[480,512]{1,0:T(8,128)(2,1)}, bf16[480,512]{1,0:T(8,128)(2,1)}, bf16[480,512]{1,0:T(8,128)(2,1)}, bf16[480,512]{1,0:T(8,128)(2,1)}, f32[480,...) custom-call(s32[32]{0:T(128)} %add.279.order, ...), custom_call_target="tpu_custom_call" | custom-call | flops 3019898880 | bytes 7269376 | tf_op jit(solution)/shard_map/node_pass/pallas_call | solution.py:120
  110.4 3.2 %collective-permute-start.23 = (bf16[3,40,512]{2,1,0:T(8,128)(2,1)S(1)}, bf16[3,40,512]{2,1,0:T(8,128)(2,1)S(1)}, u32[]{:S(2)}, u32[]{:S(2)}) collective-permute-start(bf16[3,40,512]{2,1,0:T(8,128)(2,1)S(1)} %get-tuple-element.351), channel_id=1, source_target_pairs={{4,0},{8,4},{12,8},{16,12},{20,16},{24,20},{28,24},{0,28},{5,1},{9... | collective-permute-start | bytes 368648 | tf_op jit(solution)/shard_map/ppermute | solution.py:604
  113.6 3.5 %collective-permute-done.22 = bf16[3,40,512]{2,1,0:T(8,128)(2,1)S(1)} collective-permute-done((bf16[3,40,512]{2,1,0:T(8,128)(2,1)S(1)}, bf16[3,40,512]{2,1,0:T(8,128)(2,1)S(1)}, u32[]{:S(2)}, u32[]{:S(2)}) %collective-permute-start.22) | collective-permute-done | bytes 122912 | tf_op jit(solution)/shard_map/ppermute | solution.py:603
  119.8 11.0 %edge_forward.3 = (bf16[3,640,512]{2,1,0:T(8,128)(2,1)}, bf16[3,640,512]{2,1,0:T(8,128)(2,1)}, bf16[3,640,512]{2,1,0:T(8,128)(2,1)}, f32[3,640,1]{2,1,0:T(8,128)}, bf16[3,160,512]{2,1,0:T(8,128)(2,1)}) custom-call(s32[32]{0:T(128)} %add.279.order, bf16[32,256,128]{2,1,0:T(8,128)(2,1)} %pad_maximum_fusion.1.w1.w2, ...), custom_call_target="tpu_custom_call" | custom-call | flops 15225323520 | bytes 17960576 | tf_op jit(solution)/shard_map/edge_forward/pallas_call | solution.py:120
  136.7 7.6 %node_pass.3 = (bf16[3,160,512]{2,1,0:T(8,128)(2,1)}, bf16[3,160,512]{2,1,0:T(8,128)(2,1)}, f32[3,160,512]{2,1,0:T(8,128)}, bf16[16,192,128]{2,1,0:T(8,128)(2,1)...) custom-call(s32[32]{0:T(128)} %add.279.order, s32[64]{0:T(128)} %reshape.456.rest_0_.owners, ...), custom_call_target="tpu_custom_call" | custom-call | flops 9059696640 | bytes 8087820 | tf_op jit(solution)/shard_map/node_pass/pallas_call | solution.py:120
  144.3 12.6 %edge_backward.2 = (bf16[3,640,512]{2,1,0:T(8,128)(2,1)}, bf16[3,640,512]{2,1,0:T(8,128)(2,1)}, bf16[3,400,512]{2,1,0:T(8,128)(2,1)}, f32[3,160,512]{2,1,0:T(8,1...) custom-call(s32[32]{0:T(128)} %add.279.order, ...), custom_call_target="tpu_custom_call" | custom-call | flops 14344519680 | bytes 19674752 | tf_op jit(solution)/shard_map/edge_backward/pallas_call | solution.py:120
  158.3 4.4 %collective-permute-start.29 = (bf16[3,40,512]{2,1,0:T(8,128)(2,1)S(1)}, bf16[3,40,512]{2,1,0:T(8,128)(2,1)S(1)}, u32[]{:S(2)}, u32[]{:S(2)}) collective-permute-start(bf16[3,40,512]{2,1,0:T(8,128)(2,1)S(1)} %get-tuple-element.350), channel_id=1, source_target_pairs={{4,0},{8,4},{12,8},{16,12},{20,16},{24,20},{28,24},{0,28},{5,1},{9... | collective-permute-start | bytes 368648 | tf_op jit(solution)/shard_map/ppermute | solution.py:604
  162.7 9.5 %edge_weight_grads.2 = (bf16[16,448,128]{2,1,0:T(8,128)(2,1)}, bf16[16,448,128]{2,1,0:T(8,128)(2,1)}) custom-call(s32[64]{0:T(128)} %reshape.456.rest_0_.owners, bf16[3,640,512]{2,1,0:T(8,128)(2,1)} %get-tuple-element.153.low.edge_low, bf16[3,240,512]{2,1,0:T(8,128)(2,1)} %copy-done.35, bf16[3,640,512]{2,1,0:T(8,128)(2,1)} %get-tuple-element.167.hidden_low, ...), custom_call_target="tpu_custom_call" | custom-call | flops 8053063680 | bytes 15073536 | tf_op jit(solution)/shard_map/edge_weight_grads/pallas_call | solution.py:120
  179.7 7.1 %node_backward.1 = (bf16[3,160,512]{2,1,0:T(8,128)(2,1)}, f32[3,160,512]{2,1,0:T(8,128)}, bf16[16,192,128]{2,1,0:T(8,128)(2,1)}, bf16[16,192,128]{2,1,0:T(8,128)(2,1)}, f32[4,512]{1,0:T(4,128)}) custom-call(s32[32]{0:T(128)} %add.279.order, s32[64]{0:T(128)} %reshape.456.rest_0_.owners, bf16[32,192,128]{2,1,0:T(8,128)(2,1)} %constant_dynamic-update-slice_fusion.10.rest_0_.w, ...), custom_call_target="tpu_custom_call" | custom-call | flops 6039797760 | bytes 9564288 | tf_op jit(solution)/shard_map/node_backward/pallas_call | solution.py:120
  187.9 14.3 %edge_backward.3 = (bf16[3,640,512]{2,1,0:T(8,128)(2,1)}, bf16[3,640,512]{2,1,0:T(8,128)(2,1)}, bf16[3,400,512]{2,1,0:T(8,128)(2,1)}, f32[3,160,512]{2,1,0:T(8,1...) custom-call(s32[32]{0:T(128)} %add.279.order, ...), custom_call_target="tpu_custom_call" | custom-call | flops 14344519680 | bytes 21640832 | tf_op jit(solution)/shard_map/edge_backward/pallas_call | solution.py:120
  203.6 6.5 %collective-permute-done.32 = bf16[8,448,128]{2,1,0:T(8,128)(2,1)S(1)} collective-permute-done((bf16[8,448,128]{2,1,0:T(8,128)(2,1)S(1)}, bf16[8,448,128]{2,1,0:T(8,128)(2,1)S(1)}, u32[]{:S(2)}, u32[]{:S(2)}) %collective-permute-start.32) | collective-permute-done | bytes 917536 | tf_op jit(solution)/shard_map/ppermute | solution.py:505
  210.4 8.1 %edge_weight_grads.3 = (bf16[16,256,128]{2,1,0:T(8,128)(2,1)}, bf16[16,256,128]{2,1,0:T(8,128)(2,1)}) custom-call(s32[64]{0:T(128)} %reshape.456.rest_0_.owners, bf16[640,512]{1,0:T(8,128)(2,1)} %bitcast.191, bf16[3,240,512]{2,1,0:T(8,128)(2,1)} %pad_maximum_fusion.3.table, bf16[640,512]{1,0:T(8,128)(2,1)} %get-tuple-element.206.hidden_low, ...), custom_call_target="tpu_custom_call" | custom-call | flops 8053063680 | bytes 9306368 | tf_op jit(solution)/shard_map/edge_weight_grads/pallas_call | solution.py:120
  221.0 4.7 %collective-permute-start.36 = (bf16[3,40,512]{2,1,0:T(8,128)(2,1)S(1)}, bf16[3,40,512]{2,1,0:T(8,128)(2,1)S(1)}, u32[]{:S(2)}, u32[]{:S(2)}) collective-permute-start(bf16[3,40,512]{2,1,0:T(8,128)(2,1)S(1)} %get-tuple-element.348), channel_id=1, source_target_pairs={{4,0},{8,4},{12,8},{16,12},{20,16},{24,20},{28,24},{0,28},{5,1},{9... | collective-permute-start | bytes 368648 | tf_op jit(solution)/shard_map/ppermute | solution.py:604
  233.5 5.0 %collective-permute-done.39 = bf16[320,512]{1,0:T(8,128)(2,1)S(1)} collective-permute-done((bf16[320,512]{1,0:T(8,128)(2,1)S(1)}, bf16[320,512]{1,0:T(8,128)(2,1)S(1)}, u32[]{:S(2)}, u32[]{:S(2)}) %collective-permute-start.39) | collective-permute-done | bytes 327712 | tf_op jit(solution)/shard_map/ppermute | solution.py:505
  241.8 9.0 %collective-permute-done.43 = f32[17,512]{1,0:T(8,128)S(1)} collective-permute-done((f32[17,512]{1,0:T(8,128)S(1)}, f32[17,512]{1,0:T(8,128)S(1)}, u32[]{:S(2)}, u32[]{:S(2)}) %collective-permute-start.43) | collective-permute-done | bytes 34848 | tf_op jit(solution)/shard_map/ppermute | solution.py:505
  251.0 4.2 %collective-permute-done.45 = bf16[4,640,128]{2,1,0:T(8,128)(2,1)S(1)} collective-permute-done((bf16[4,640,128]{2,1,0:T(8,128)(2,1)S(1)}, bf16[4,640,128]{2,1,0:T(8,128)(2,1)S(1)}, u32[]{:S(2)}, u32[]{:S(2)}) %collective-permute-start.45) | collective-permute-done | bytes 655392 | tf_op jit(solution)/shard_map/ppermute | solution.py:505
  259.3 3.7 %collective-permute-done.46 = f32[17,512]{1,0:T(8,128)S(1)} collective-permute-done((f32[17,512]{1,0:T(8,128)S(1)}, f32[17,512]{1,0:T(8,128)S(1)}, u32[]{:S(2)}, u32[]{:S(2)}) %collective-permute-start.46) | collective-permute-done | bytes 34848 | tf_op jit(solution)/shard_map/ppermute | solution.py:505
  267.4 3.8 %collective-permute-done.49 = f32[17,512]{1,0:T(8,128)S(1)} collective-permute-done((f32[17,512]{1,0:T(8,128)S(1)}, f32[17,512]{1,0:T(8,128)S(1)}, u32[]{:S(2)}, u32[]{:S(2)}) %collective-permute-start.49) | collective-permute-done | bytes 34848 | tf_op jit(solution)/shard_map/ppermute | solution.py:505
  271.5 2.9 collective-permute-start.52
  274.4 4.1 %collective-permute-done.53 = bf16[1,640,128]{2,1,0:T(8,128)(2,1)S(1)} collective-permute-done((bf16[1,640,128]{2,1,0:T(8,128)(2,1)S(1)}, bf16[1,640,128]{2,1,0:T(8,128)(2,1)S(1)}, u32[]{:S(2)}, u32[]{:S(2)}) %collective-permute-start.53) | collective-permute-done | bytes 163872 | tf_op jit(solution)/shard_map/ppermute | solution.py:505
  289.7 3.6 %collective-permute-start.60 = (f32[2,4]{1,0:T(2,128)S(1)}, f32[2,4]{1,0:T(2,128)S(1)}, u32[]{:S(2)}, u32[]{:S(2)}) collective-permute-start(f32[2,4]{1,0:T(2,128)S(1)} %add_add_fusion.1), channel_id=1, source_target_pairs={{0,24},{1,25},{2,26},{3,27},{4,28},{5,29},{6,30},{7,31},{8,16},{9,... | collective-permute-start | bytes 104 | tf_op jit(solution)/shard_map/ppermute | solution.py:592
  (436 shorter events, 113.0 us)
Async XLA Ops:
  3.2 11.7 %collective-permute-start = (bf16[1,256,128]{2,1,0:T(8,128)(2,1)S(1)}, bf16[1,256,128]{2,1,0:T(8,128)(2,1)S(1)}, u32[]{:S(2)}, u32[]{:S(2)}) collective-permute-start(bf16[1,256,128]{2,1,0:T(8,128)(2,1)S(1)} %get-tuple-element.371), channel_id=1, source_target_pairs={{0,16},{4,20},{8,24},{12,28},{16,0},{20,4},{24,8},{28,12},{1,17},{... | collective-permute-start | bytes 196616 | tf_op jit(solution)/shard_map/ppermute | solution.py:505
  27.5 20.4 %collective-permute-start.3 = (bf16[8,256,128]{2,1,0:T(8,128)(2,1)}, bf16[8,256,128]{2,1,0:T(8,128)(2,1)}, u32[]{:S(2)}, u32[]{:S(2)}) collective-permute-start(bf16[8,256,128]{2,1,0:T(8,128)(2,1)} %pad_maximum_fusion.6), channel_id=1, source_target_pairs={{0,2},{1,3},{2,0},{3,1},{4,6},{5,7},{6,4},{7,5},{8,10},{9,11},{10,... | collective-permute-start | bytes 1572872 | tf_op jit(solution)/shard_map/ppermute | solution.py:505
  30.9 10.8 %collective-permute-start.6 = (bf16[1,192,128]{2,1,0:T(8,128)(2,1)}, bf16[1,192,128]{2,1,0:T(8,128)(2,1)}, u32[]{:S(2)}, u32[]{:S(2)}) collective-permute-start(bf16[1,192,128]{2,1,0:T(8,128)(2,1)} %get-tuple-element.384), channel_id=1, source_target_pairs={{0,16},{4,20},{8,24},{12,28},{16,0},{20,4},{24,8},{28,12},{1,17},{... | collective-permute-start | bytes 147464 | tf_op jit(solution)/shard_map/ppermute | solution.py:505
  33.1 18.0 %collective-permute-start.10 = (bf16[3,40,512]{2,1,0:T(8,128)(2,1)}, bf16[3,40,512]{2,1,0:T(8,128)(2,1)}, u32[]{:S(2)}, u32[]{:S(2)}) collective-permute-start(bf16[3,40,512]{2,1,0:T(8,128)(2,1)} %get-tuple-element.353), channel_id=1, source_target_pairs={{0,4},{4,8},{8,12},{12,16},{16,20},{20,24},{24,28},{28,0},{1,5},{5... | collective-permute-start | bytes 368648 | tf_op jit(solution)/shard_map/ppermute | solution.py:603
  34.6 16.6 %collective-permute-start.11 = (bf16[3,40,512]{2,1,0:T(8,128)(2,1)}, bf16[3,40,512]{2,1,0:T(8,128)(2,1)}, u32[]{:S(2)}, u32[]{:S(2)}) collective-permute-start(bf16[3,40,512]{2,1,0:T(8,128)(2,1)} %get-tuple-element.354), channel_id=1, source_target_pairs={{4,0},{8,4},{12,8},{16,12},{20,16},{24,20},{28,24},{0,28},{5,1},{9... | collective-permute-start | bytes 368648 | tf_op jit(solution)/shard_map/ppermute | solution.py:604
  49.0 16.8 %collective-permute-start.8 = (bf16[16,256,128]{2,1,0:T(8,128)(2,1)S(1)}, bf16[16,256,128]{2,1,0:T(8,128)(2,1)S(1)}, u32[]{:S(2)}, u32[]{:S(2)}) collective-permute-start(bf16[16,256,128]{2,1,0:T(8,128)(2,1)S(1)} %constant_dynamic-update-slice_fusion), channel_id=1, source_target_pairs={{0,1},{1,0},{2,3},{3,2},{4,5},{5,4},{6,7},{7,6},{8,9},{9,8},{10,11... | collective-permute-start | bytes 3145736 | tf_op jit(solution)/shard_map/ppermute | solution.py:505
  59.3 21.6 %collective-permute-start.18 = (bf16[8,192,128]{2,1,0:T(8,128)(2,1)S(1)}, bf16[8,192,128]{2,1,0:T(8,128)(2,1)S(1)}, u32[]{:S(2)}, u32[]{:S(2)}) collective-permute-start(bf16[8,192,128]{2,1,0:T(8,128)(2,1)S(1)} %pad_maximum_fusion.10), channel_id=1, source_target_pairs={{0,2},{1,3},{2,0},{3,1},{4,6},{5,7},{6,4},{7,5},{8,10},{9,11},{10,... | collective-permute-start | bytes 1179656 | tf_op jit(solution)/shard_map/ppermute | solution.py:505
  65.8 13.4 %collective-permute-start.5 = (bf16[2,256,128]{2,1,0:T(8,128)(2,1)S(1)}, bf16[2,256,128]{2,1,0:T(8,128)(2,1)S(1)}, u32[]{:S(2)}, u32[]{:S(2)}) collective-permute-start(bf16[2,256,128]{2,1,0:T(8,128)(2,1)S(1)} %pad_maximum_fusion.22), channel_id=1, source_target_pairs={{0,8},{4,12},{8,0},{12,4},{16,24},{20,28},{24,16},{28,20},{1,9},{5... | collective-permute-start | bytes 393224 | tf_op jit(solution)/shard_map/ppermute | solution.py:505
  79.1 20.2 %collective-permute-start.20 = (bf16[3,160,512]{2,1,0:T(8,128)(2,1)}, bf16[3,160,512]{2,1,0:T(8,128)(2,1)S(1)}, u32[]{:S(2)}, u32[]{:S(2)}) collective-permute-start(bf16[3,160,512]{2,1,0:T(8,128)(2,1)} %get-tuple-element.142.rest_3_), channel_id=1, source_target_pairs={{0,1},{1,0},{2,3},{3,2},{4,5},{5,4},{6,7},{7,6},{8,9},{9,8},{10,11... | collective-permute-start | bytes 1474568 | tf_op jit(solution)/shard_map/ppermute | solution.py:505
  79.2 8.8 %collective-permute-start.12 = (bf16[4,256,128]{2,1,0:T(8,128)(2,1)S(1)}, bf16[4,256,128]{2,1,0:T(8,128)(2,1)S(1)}, u32[]{:S(2)}, u32[]{:S(2)}) collective-permute-start(bf16[4,256,128]{2,1,0:T(8,128)(2,1)S(1)} %pad_maximum_fusion.13), channel_id=1, source_target_pairs={{0,4},{4,0},{8,12},{12,8},{16,20},{20,16},{24,28},{28,24},{1,5},{5... | collective-permute-start | bytes 786440 | tf_op jit(solution)/shard_map/ppermute | solution.py:505
  79.8 11.2 %collective-permute-start.26 = (bf16[40,3,512]{2,0,1:T(8,128)(2,1)S(1)}, bf16[40,3,512]{2,0,1:T(8,128)(2,1)S(1)}, u32[]{:S(2)}, u32[]{:S(2)}) collective-permute-start(bf16[40,3,512]{2,0,1:T(8,128)(2,1)S(1)} %constant_dynamic-slice_fusion), channel_id=1, source_target_pairs={{0,2},{1,3},{2,0},{3,1},{4,6},{5,7},{6,4},{7,5},{8,10},{9,11},{10,... | collective-permute-start | bytes 368648 | tf_op jit(solution)/shard_map/ppermute | solution.py:505
  81.8 17.6 %collective-permute-start.19 = (bf16[16,192,128]{2,1,0:T(8,128)(2,1)S(1)}, bf16[16,192,128]{2,1,0:T(8,128)(2,1)S(1)}, u32[]{:S(2)}, u32[]{:S(2)}) collective-permute-start(bf16[16,192,128]{2,1,0:T(8,128)(2,1)S(1)} %get-tuple-element.338), channel_id=1, source_target_pairs={{0,1},{1,0},{2,3},{3,2},{4,5},{5,4},{6,7},{7,6},{8,9},{9,8},{10,11... | collective-permute-start | bytes 2359304 | tf_op jit(solution)/shard_map/ppermute | solution.py:505
  91.0 14.4 %collective-permute-start.17 = (bf16[8,256,128]{2,1,0:T(8,128)(2,1)S(1)}, bf16[8,256,128]{2,1,0:T(8,128)(2,1)S(1)}, u32[]{:S(2)}, u32[]{:S(2)}) collective-permute-start(bf16[8,256,128]{2,1,0:T(8,128)(2,1)S(1)} %pad_maximum_fusion.7), channel_id=1, source_target_pairs={{0,2},{1,3},{2,0},{3,1},{4,6},{5,7},{6,4},{7,5},{8,10},{9,11},{10,... | collective-permute-start | bytes 1572872 | tf_op jit(solution)/shard_map/ppermute | solution.py:505
  105.5 12.8 %collective-permute-start.21 = (bf16[16,256,128]{2,1,0:T(8,128)(2,1)S(1)}, bf16[16,256,128]{2,1,0:T(8,128)(2,1)S(1)}, u32[]{:S(2)}, u32[]{:S(2)}) collective-permute-start(bf16[16,256,128]{2,1,0:T(8,128)(2,1)S(1)} %constant_dynamic-update-slice_fusion.16), channel_id=1, source_target_pairs={{0,1},{1,0},{2,3},{3,2},{4,5},{5,4},{6,7},{7,6},{8,9},{9,8},{10,11... | collective-permute-start | bytes 3145736 | tf_op jit(solution)/shard_map/ppermute | solution.py:505
  106.9 23.9 %collective-permute-start.16 = (bf16[8,192,128]{2,1,0:T(8,128)(2,1)S(1)}, bf16[8,192,128]{2,1,0:T(8,128)(2,1)S(1)}, u32[]{:S(2)}, u32[]{:S(2)}) collective-permute-start(bf16[8,192,128]{2,1,0:T(8,128)(2,1)S(1)} %pad_maximum_fusion.11), channel_id=1, source_target_pairs={{0,2},{1,3},{2,0},{3,1},{4,6},{5,7},{6,4},{7,5},{8,10},{9,11},{10,... | collective-permute-start | bytes 1179656 | tf_op jit(solution)/shard_map/ppermute | solution.py:505
  108.8 8.3 %collective-permute-start.22 = (bf16[3,40,512]{2,1,0:T(8,128)(2,1)S(1)}, bf16[3,40,512]{2,1,0:T(8,128)(2,1)S(1)}, u32[]{:S(2)}, u32[]{:S(2)}) collective-permute-start(bf16[3,40,512]{2,1,0:T(8,128)(2,1)S(1)} %get-tuple-element.352), channel_id=1, source_target_pairs={{0,4},{4,8},{8,12},{12,16},{16,20},{20,24},{24,28},{28,0},{1,5},{5... | collective-permute-start | bytes 368648 | tf_op jit(solution)/shard_map/ppermute | solution.py:603
  157.9 14.3 %collective-permute-start.28 = (bf16[3,40,512]{2,1,0:T(8,128)(2,1)S(1)}, bf16[3,40,512]{2,1,0:T(8,128)(2,1)S(1)}, u32[]{:S(2)}, u32[]{:S(2)}) collective-permute-start(bf16[3,40,512]{2,1,0:T(8,128)(2,1)S(1)} %get-tuple-element.349), channel_id=1, source_target_pairs={{0,4},{4,8},{8,12},{12,16},{16,20},{20,24},{24,28},{28,0},{1,5},{5... | collective-permute-start | bytes 368648 | tf_op jit(solution)/shard_map/ppermute | solution.py:603
  158.3 14.0 %collective-permute-start.29 = (bf16[3,40,512]{2,1,0:T(8,128)(2,1)S(1)}, bf16[3,40,512]{2,1,0:T(8,128)(2,1)S(1)}, u32[]{:S(2)}, u32[]{:S(2)}) collective-permute-start(bf16[3,40,512]{2,1,0:T(8,128)(2,1)S(1)} %get-tuple-element.350), channel_id=1, source_target_pairs={{4,0},{8,4},{12,8},{16,12},{20,16},{24,20},{28,24},{0,28},{5,1},{9... | collective-permute-start | bytes 368648 | tf_op jit(solution)/shard_map/ppermute | solution.py:604
  186.7 15.5 %collective-permute-start.33 = (bf16[16,192,128]{2,1,0:T(8,128)(2,1)}, bf16[16,192,128]{2,1,0:T(8,128)(2,1)S(1)}, u32[]{:S(2)}, u32[]{:S(2)}) collective-permute-start(bf16[16,192,128]{2,1,0:T(8,128)(2,1)} %get-tuple-element.194), channel_id=1, source_target_pairs={{0,1},{1,0},{2,3},{3,2},{4,5},{5,4},{6,7},{7,6},{8,9},{9,8},{10,11... | collective-permute-start | bytes 2359304 | tf_op jit(solution)/shard_map/ppermute | solution.py:505
  186.9 23.2 %collective-permute-start.32 = (bf16[8,448,128]{2,1,0:T(8,128)(2,1)S(1)}, bf16[8,448,128]{2,1,0:T(8,128)(2,1)S(1)}, u32[]{:S(2)}, u32[]{:S(2)}) collective-permute-start(bf16[8,448,128]{2,1,0:T(8,128)(2,1)S(1)} %slice.374), channel_id=1, source_target_pairs={{0,2},{1,3},{2,0},{3,1},{4,6},{5,7},{6,4},{7,5},{8,10},{9,11},{10,... | collective-permute-start | bytes 2752520 | tf_op jit(solution)/shard_map/ppermute | solution.py:505
  202.5 15.9 %collective-permute-start.41 = (bf16[8,192,128]{2,1,0:T(8,128)(2,1)S(1)}, bf16[8,192,128]{2,1,0:T(8,128)(2,1)S(1)}, u32[]{:S(2)}, u32[]{:S(2)}) collective-permute-start(bf16[8,192,128]{2,1,0:T(8,128)(2,1)S(1)} %slice.377), channel_id=1, source_target_pairs={{0,2},{1,3},{2,0},{3,1},{4,6},{5,7},{6,4},{7,5},{8,10},{9,11},{10,... | collective-permute-start | bytes 1179656 | tf_op jit(solution)/shard_map/ppermute | solution.py:505
  220.1 10.8 %collective-permute-start.42 = (bf16[16,256,128]{2,1,0:T(8,128)(2,1)}, bf16[16,256,128]{2,1,0:T(8,128)(2,1)S(1)}, u32[]{:S(2)}, u32[]{:S(2)}) collective-permute-start(bf16[16,256,128]{2,1,0:T(8,128)(2,1)} %get-tuple-element.212), channel_id=1, source_target_pairs={{0,1},{1,0},{2,3},{3,2},{4,5},{5,4},{6,7},{7,6},{8,9},{9,8},{10,11... | collective-permute-start | bytes 3145736 | tf_op jit(solution)/shard_map/ppermute | solution.py:505
  220.9 8.1 %collective-permute-start.35 = (bf16[3,40,512]{2,1,0:T(8,128)(2,1)S(1)}, bf16[3,40,512]{2,1,0:T(8,128)(2,1)S(1)}, u32[]{:S(2)}, u32[]{:S(2)}) collective-permute-start(bf16[3,40,512]{2,1,0:T(8,128)(2,1)S(1)} %get-tuple-element.347), channel_id=1, source_target_pairs={{0,4},{4,8},{8,12},{12,16},{16,20},{20,24},{24,28},{28,0},{1,5},{5... | collective-permute-start | bytes 368648 | tf_op jit(solution)/shard_map/ppermute | solution.py:603
  221.0 8.0 %collective-permute-start.36 = (bf16[3,40,512]{2,1,0:T(8,128)(2,1)S(1)}, bf16[3,40,512]{2,1,0:T(8,128)(2,1)S(1)}, u32[]{:S(2)}, u32[]{:S(2)}) collective-permute-start(bf16[3,40,512]{2,1,0:T(8,128)(2,1)S(1)} %get-tuple-element.348), channel_id=1, source_target_pairs={{4,0},{8,4},{12,8},{16,12},{20,16},{24,20},{28,24},{0,28},{5,1},{9... | collective-permute-start | bytes 368648 | tf_op jit(solution)/shard_map/ppermute | solution.py:604
  227.9 10.6 %collective-permute-start.39 = (bf16[320,512]{1,0:T(8,128)(2,1)S(1)}, bf16[320,512]{1,0:T(8,128)(2,1)S(1)}, u32[]{:S(2)}, u32[]{:S(2)}) collective-permute-start(bf16[320,512]{1,0:T(8,128)(2,1)S(1)} %fusion.7), channel_id=1, source_target_pairs={{0,2},{1,3},{2,0},{3,1},{4,6},{5,7},{6,4},{7,5},{8,10},{9,11},{10,... | collective-permute-start | bytes 983048 | tf_op jit(solution)/shard_map/ppermute | solution.py:505
  230.6 8.7 %collective-permute-start.37 = (bf16[3,160,512]{2,1,0:T(8,128)(2,1)S(1)}, bf16[3,160,512]{2,1,0:T(8,128)(2,1)S(1)}, u32[]{:S(2)}, u32[]{:S(2)}) collective-permute-start(bf16[3,160,512]{2,1,0:T(8,128)(2,1)S(1)} %get-tuple-element.392), channel_id=1, source_target_pairs={{0,1},{1,0},{2,3},{3,2},{4,5},{5,4},{6,7},{7,6},{8,9},{9,8},{10,11... | collective-permute-start | bytes 1474568 | tf_op jit(solution)/shard_map/ppermute | solution.py:505
  232.5 18.3 %collective-permute-start.44 = (bf16[8,256,128]{2,1,0:T(8,128)(2,1)S(1)}, bf16[8,256,128]{2,1,0:T(8,128)(2,1)S(1)}, u32[]{:S(2)}, u32[]{:S(2)}) collective-permute-start(bf16[8,256,128]{2,1,0:T(8,128)(2,1)S(1)} %slice.375), channel_id=1, source_target_pairs={{0,2},{1,3},{2,0},{3,1},{4,6},{5,7},{6,4},{7,5},{8,10},{9,11},{10,... | collective-permute-start | bytes 1572872 | tf_op jit(solution)/shard_map/ppermute | solution.py:505
  239.3 15.8 %collective-permute-start.45 = (bf16[4,640,128]{2,1,0:T(8,128)(2,1)S(1)}, bf16[4,640,128]{2,1,0:T(8,128)(2,1)S(1)}, u32[]{:S(2)}, u32[]{:S(2)}) collective-permute-start(bf16[4,640,128]{2,1,0:T(8,128)(2,1)S(1)} %copy-done.27), channel_id=1, source_target_pairs={{0,4},{4,0},{8,12},{12,8},{16,20},{20,16},{24,28},{28,24},{1,5},{5... | collective-permute-start | bytes 1966088 | tf_op jit(solution)/shard_map/ppermute | solution.py:505
  239.6 11.1 %collective-permute-start.43 = (f32[17,512]{1,0:T(8,128)S(1)}, f32[17,512]{1,0:T(8,128)S(1)}, u32[]{:S(2)}, u32[]{:S(2)}) collective-permute-start(f32[17,512]{1,0:T(8,128)S(1)} %add.296), channel_id=1, source_target_pairs={{0,2},{1,3},{2,0},{3,1},{4,6},{5,7},{6,4},{7,5},{8,10},{9,11},{10,... | collective-permute-start | bytes 104456 | tf_op jit(solution)/shard_map/ppermute | solution.py:505
  240.8 15.0 %collective-permute-start.38 = (bf16[40,3,512]{2,0,1:T(8,128)(2,1)S(1)}, bf16[40,3,512]{2,0,1:T(8,128)(2,1)S(1)}, u32[]{:S(2)}, u32[]{:S(2)}) collective-permute-start(bf16[40,3,512]{2,0,1:T(8,128)(2,1)S(1)} %dynamic-slice_bitcast_fusion.1), channel_id=1, source_target_pairs={{0,2},{1,3},{2,0},{3,1},{4,6},{5,7},{6,4},{7,5},{8,10},{9,11},{10,... | collective-permute-start | bytes 368648 | tf_op jit(solution)/shard_map/ppermute | solution.py:505
  267.4 11.1 %collective-permute-start.53 = (bf16[1,640,128]{2,1,0:T(8,128)(2,1)S(1)}, bf16[1,640,128]{2,1,0:T(8,128)(2,1)S(1)}, u32[]{:S(2)}, u32[]{:S(2)}) collective-permute-start(bf16[1,640,128]{2,1,0:T(8,128)(2,1)S(1)} %slice.381), channel_id=1, source_target_pairs={{0,16},{4,20},{8,24},{12,28},{16,0},{20,4},{24,8},{28,12},{1,17},{... | collective-permute-start | bytes 491528 | tf_op jit(solution)/shard_map/ppermute | solution.py:505
  271.5 8.8 %collective-permute-start.52 = (bf16[1,256,128]{2,1,0:T(8,128)(2,1)S(1)}, bf16[1,256,128]{2,1,0:T(8,128)(2,1)S(1)}, u32[]{:S(2)}, u32[]{:S(2)}) collective-permute-start(bf16[1,256,128]{2,1,0:T(8,128)(2,1)S(1)} %slice.383), channel_id=1, source_target_pairs={{0,16},{4,20},{8,24},{12,28},{16,0},{20,4},{24,8},{28,12},{1,17},{... | collective-permute-start | bytes 196616 | tf_op jit(solution)/shard_map/ppermute | solution.py:505
  (111 other events, 862.2 us)

commit v3 on v2

--- a/solution.py
+++ b/solution.py
@@ -83,12 +83,16 @@
 
 def pack(values, owners, rows, offset, kept, sent):
     half = kept.shape[0]
-    for place in range(2 * half):
-        target = kept if place < half else sent
-        begin = pl.multiple_of(owners[2 * place] * rows, rows)
-        target[place % half, offset : offset + rows, :] = values[
-            owners[2 * place + 1], pl.ds(begin, rows), :
-        ].astype(BF16)
+
+    def one(index, carry):
+        for target, place in ((kept, index), (sent, index + half)):
+            begin = pl.multiple_of(owners[2 * place] * rows, rows)
+            target[index, offset : offset + rows, :] = values[
+                owners[2 * place + 1], pl.ds(begin, rows), :
+            ].astype(BF16)
+        return carry
+
+    lax.fori_loop(0, half, one, 0)
 
 
 def per_sample(array):
@@ -557,42 +561,62 @@
     return lax.optimization_barrier((value, *earlier))[0]
 
 
-def gather_steps(held, begin, end, *under):
-    for axis, bit in all_bits()[begin:end]:
-        arrived = after(swap(held, axis, 1 << bit), *under)
-        held = jnp.concatenate([held, arrived], axis=0)
-    return held
-
-
-def scatter_step(pair, step, *under):
-    axis, bit = all_bits()[step]
-    kept, sent = pair
-    total = kept.astype(F32) + after(swap(sent, axis, 1 << bit), *under).astype(F32)
-    if step == 0:
-        return total[0]
-    half = total.shape[0] // 2
-    return total[:half], total[half:].astype(BF16)
-
-
-def sum_step(values, step):
-    axis, bit = all_bits()[step]
-    return values + swap(values, axis, 1 << bit)
+def exchange(values, first_step, flips):
+    hid_bits = bits_of("hid")
+    mask = 0
+    for k in range(flips.bit_length()):
+        if (flips >> k) & 1:
+            axis, bit = all_bits()[first_step + k]
+            mask |= 1 << (bit if axis == "hid" else bit + hid_bits)
+    total = 1 << len(all_bits())
+    return lax.ppermute(values, ("node", "hid"), [(i, i ^ mask) for i in range(total)])
+
+
+def rounds(begin, end):
+    return [(step, min(step + 2, end)) for step in range(begin, end, 2)]
+
+
+def gather_round(held, begin, end, *under):
+    arrived = [exchange(held, begin, flips) for flips in range(1, 1 << (end - begin))]
+    if under:
+        arrived = lax.optimization_barrier((*arrived, *under))[: len(arrived)]
+    return jnp.concatenate([held, *arrived], axis=0)
+
+
+def split(total, count):
+    size = total.shape[0] // count
+    pieces = [total[i * size : (i + 1) * size] for i in range(count)]
+    return [pieces[0]] + [piece.astype(BF16) for piece in pieces[1:]]
+
+
+def scatter_round(pieces, begin, *under):
+    arrived = [exchange(pieces[flips], begin, flips) for flips in range(1, len(pieces))]
+    if under:
+        arrived = lax.optimization_barrier((*arrived, *under))[: len(arrived)]
+    total = pieces[0].astype(F32)
+    for piece in arrived:
+        total = total + piece.astype(F32)
+    return total
+
+
+def scatter_rest(total, end, *under):
+    for begin, stop in reversed(rounds(0, end)):
+        total = scatter_round(split(total, 1 << (stop - begin)), begin, *under)
+    return total[0]
+
+
+def sum_round(values, begin, end):
+    terms = [values] + [exchange(values, begin, flips) for flips in range(1, 1 << (end - begin))]
+    while len(terms) > 1:
+        terms = [terms[i] + terms[i + 1] for i in range(0, len(terms), 2)]
+    return terms[0]
 
 
 def sum_everywhere(values):
-    axes = ("node", "hid")
-    bits = sum(bits_of(axis) for axis in axes)
-    total = 1 << bits
-    done = 0
-    while done < bits:
-        step = 1 if (bits - done) % 2 else 2
-        terms = [values]
-        for i in range(1, 1 << step):
-            pairs = [(k, k ^ (i << done)) for k in range(total)]
-            terms.append(lax.ppermute(values, axes, pairs))
-        while len(terms) > 1:
-            terms = [terms[i] + terms[i + 1] for i in range(0, len(terms), 2)]
-        values, done = terms[0], done + step
+    steps = len(all_bits())
+    values = sum_round(values, steps - 1, steps)
+    for begin, end in reversed(rounds(0, steps - 1)):
+        values = sum_round(values, begin, end)
     return values
 
 
@@ -667,20 +691,33 @@
 
     order, owners = places(), owners_of_places()
     steps = len(all_bits())
-    edge_zero = gather_steps(pack_shards(edge_first[0], edge_second[0])[None], 0, steps - 2)
-    setup = edge_zero
-    first, second = after((node_first[0], node_second[0]), edge_zero)
-    node_zero = gather_steps(pack_shards(first, second)[None], 0, steps - 3)
-    edge_zero = gather_steps(edge_zero, steps - 2, steps - 1)
-    first, second = after((edge_first[1], edge_second[1]), edge_zero)
-    edge_zero = gather_steps(after(edge_zero, node_zero), steps - 1, steps)
-    node_zero = gather_steps(node_zero, steps - 3, steps - 2)
-    edge_one = gather_steps(pack_shards(first, second)[None], 0, 1)
+
+    def layer_shards(depth, *earlier):
+        shards = (node_first[depth], node_second[depth], edge_first[depth], edge_second[depth])
+        if earlier:
+            shards = after(shards, *earlier)
+        return jnp.concatenate([pack_shards(*shards[:2]), pack_shards(*shards[2:])], axis=0)[None]
+
+    def parted(held):
+        return held[:, :node_rows], held[:, node_rows:]
+
+    layer_zero = layer_shards(0)
+    for begin, end in rounds(0, steps - 3):
+        layer_zero = gather_round(layer_zero, begin, end)
+    setup = layer_zero
+    layer_zero = gather_round(layer_zero, steps - 3, steps - 2)
+    node_zero, edge_zero = parted(layer_zero)
+    layer_one = layer_shards(1, setup)
+    for begin, end in rounds(0, steps - 3):
+        layer_one = gather_round(after(layer_one, edge_zero), begin, end)
+    edge_zero = gather_round(edge_zero, steps - 2, steps - 1)
     masters = (edge_first, edge_second, node_first, node_second)
     weight_local = jnp.stack(
         [jnp.sum(matrix * matrix, axis=(1, 2)) for matrix in after(masters, setup)], axis=1
     )
-    edge_zero = after(edge_zero, node_zero, edge_one, weight_local)
+    node_zero = after(node_zero, edge_zero)
+    edge_zero = gather_round(after(edge_zero, layer_one), steps - 1, steps)
+    edge_zero = after(edge_zero, weight_local)
 
     def edge_blocks(whole):
         return ((whole, first_rows, 0), (whole, second_rows, first_rows // second_rows))
@@ -740,13 +777,14 @@
         node_total,
         False,
     )
-    node_zero = gather_steps(node_zero, steps - 2, steps - 1, pooled)
-    node_zero = gather_steps(node_zero, steps - 1, steps)
-    edge_one = gather_steps(edge_one, 1, steps - 3, pooled)
-    edge_one = gather_steps(edge_one, steps - 3, steps - 2)
+    pooled, *arrived = lax.optimization_barrier(
+        (pooled, exchange(node_zero, steps - 2, 1), exchange(layer_one, steps - 3, 1))
+    )
+    node_zero = jnp.concatenate([node_zero, arrived[0]], axis=0)
+    node_zero = gather_round(node_zero, steps - 1, steps)
+    layer_one = jnp.concatenate([layer_one, arrived[1]], axis=0)
+    node_one, edge_one = parted(layer_one)
     other = after(swap(pooled, "hid", 1), edge_one)
-    first, second = after((node_first[1], node_second[1]), edge_one)
-    node_one = gather_steps(pack_shards(first, second)[None], 0, steps - 3)
     (
         pooled_zero,
         node_pre,
@@ -770,10 +808,13 @@
         None,
         None,
     )
-    edge_one = gather_steps(edge_one, steps - 2, steps - 1, halo_rows)
-    edge_one = gather_steps(after(edge_one, node_one), steps - 1, steps)
-    node_one = gather_steps(node_one, steps - 3, steps - 2)
-    edge_one = after(edge_one, node_one)
+    halo_rows = to_neighbours(halo_rows, halo_width)
+    arrived, halo_rows = lax.optimization_barrier(
+        (exchange(edge_one, steps - 2, 1), halo_rows)
+    )
+    edge_one = jnp.concatenate([edge_one, arrived], axis=0)
+    node_one = after(node_one, edge_one)
+    edge_one = gather_round(edge_one, steps - 1, steps)
 
     valid_mask = (ocean_mask[:, None] * present_mask).astype(BF16)
     masked = after(cotangent, pooled) * valid_mask[:, :, None]
@@ -786,7 +827,7 @@
     scaling = scaling[:, None, None]
 
     node_low_one = node_low
-    table_one = jnp.concatenate([node_low, to_neighbours(halo_rows, halo_width)], axis=1)
+    table_one = jnp.concatenate([node_low, halo_rows], axis=1)
     pre_one, act_one, normed_one, inverse_one, pooled = edge_forward(
         order,
         *edge_blocks(edge_one),
@@ -799,8 +840,8 @@
         node_total,
         True,
     )
-    node_one = gather_steps(node_one, steps - 2, steps - 1, pooled)
-    node_one = gather_steps(node_one, steps - 1, steps)
+    node_one = gather_round(node_one, steps - 2, steps - 1, pooled)
+    node_one = gather_round(node_one, steps - 1, steps)
     node_low, pooled_grad, node_grad, kept, sent, node_minor_one = node_pass(
         order,
         owners,
@@ -850,7 +891,7 @@
         (to_neighbours(returned, halo_width), *chain_one)
     )
     partial = from_edges(partial, returned)
-    chain_one = scatter_step(chain_one, steps - 1)
+    chain_one = split(scatter_round(chain_one, steps - 1), 2)
     other, *chain_one = lax.optimization_barrier((swap(partial.astype(BF16), "hid", 1), *chain_one))
     pooled_grad, node_grad, kept, sent, node_minor_zero = node_backward(
         order,
@@ -883,10 +924,9 @@
             node_total,
         )
     )
-    chain_one = scatter_step(chain_one, steps - 2, low)
-    chain_zero = scatter_step((kept, sent), steps - 1, low)
+    chain_one = split(scatter_round(chain_one, steps - 2, low), 2)
+    chain_zero = split(scatter_round((kept, sent), steps - 1, low), 2)
     low = after(low, *chain_one, *chain_zero)
-    node_out = to_own_rows(after(node_low, low))
     chain_edge = edge_weight_grads(
         owners,
         edge_in_own,
@@ -905,34 +945,42 @@
         + [jnp.pad(weight_local.reshape(1, -1), ((0, 0), (0, latent - weight_local.size)))],
         axis=0,
     )
-    chain_zero = scatter_step(chain_zero, steps - 2, chain_edge[1])
-    chain_one = tuple(jnp.concatenate(pair, axis=1) for pair in zip(chain_one, chain_zero))
-    chain_edge = [chain_edge[0], after(chain_edge[1], *chain_one)]
-    chain_edge = scatter_step(chain_edge, steps - 1)
-    minor_packed = sum_step(minor_packed, steps - 1)
-    for step in reversed(range(steps - 1)):
-        minor_packed, *held = lax.optimization_barrier(
-            (minor_packed, *chain_edge, *chain_one)
-        )
-        chain_edge = held[:2]
-        if step > 0:
-            chain_one = scatter_step(held[2:], step - 1)
-        chain_edge = scatter_step(chain_edge, step)
-        minor_packed = sum_step(minor_packed, step)
-        if step == 1:
-            chain_one = (chain_one,)
-    edge_zero_grads, node_grads = chain_edge, chain_one[0]
-    partial = from_edges(partial, to_neighbours(returned, halo_width))
-    node_grad = node_grad + (partial + swap(partial.astype(BF16), "hid", 1).astype(F32))
+    chain_zero = split(scatter_round(chain_zero, steps - 2, chain_edge[1]), 2)
+    chain_one = scatter_round(chain_one, steps - 3, chain_edge[1])
+    kept, sent, chain_one, *chain_zero = lax.optimization_barrier(
+        (*chain_edge, chain_one, *chain_zero)
+    )
+    chain_edge = split(scatter_round((kept, sent), steps - 1), 2)
+    minor_packed = sum_round(minor_packed, steps - 1, steps)
+    returned, minor_packed, *held = lax.optimization_barrier(
+        (returned, minor_packed, *chain_zero, *chain_edge)
+    )
+    chain_zero, chain_edge = held[:2], held[2:]
+    chain_edge = split(scatter_round(chain_edge, steps - 2), 2)
+    minor_packed = sum_round(minor_packed, steps - 2, steps - 1)
+    layer_one_grads = scatter_rest(chain_one, steps - 3, chain_edge[1])
+    chain_zero = scatter_round(chain_zero, steps - 3, chain_edge[1])
+    returned = after(to_neighbours(returned, halo_width), chain_edge[1])
+    node_low, edge_input_grad, minor_packed, *chain_edge = lax.optimization_barrier(
+        (node_low, edge_input_grad, minor_packed, *chain_edge)
+    )
+    chain_edge = scatter_round(chain_edge, steps - 3)
+    minor_packed = sum_round(minor_packed, steps - 3, steps - 2)
+    node_zero_grads = scatter_rest(chain_zero, steps - 3, chain_edge)
+    partial = from_edges(partial, returned)
+    other = swap(partial.astype(BF16), "hid", 1)
+    chain_edge, minor_packed, other = lax.optimization_barrier((chain_edge, minor_packed, other))
+    edge_zero_grads = scatter_rest(chain_edge, steps - 3)
+    for begin, end in reversed(rounds(0, steps - 3)):
+        minor_packed = sum_round(minor_packed, begin, end)
+    node_out = to_own_rows(node_low)
+    edge_input_grad = halve_sum(edge_input_grad.reshape(2, edge_part, latent), "hid", 1, 0)
+    node_grad = node_grad + (partial + other.astype(F32))
     grad_node = to_own_rows(node_grad.astype(BF16))
-    edge_input_grad = halve_sum(edge_input_grad.reshape(2, edge_part, latent), "hid", 1, 0)
 
     minor_total = minor_packed[: 8 * LAYERS].reshape(small_params.shape)
     weight_squares = minor_packed[8 * LAYERS, : weight_local.size].reshape(weight_local.shape)
-    edge_rows = first_rows + second_rows
-    node_one_grads = node_grads[:node_rows]
-    edge_one_grads = node_grads[node_rows : node_rows + edge_rows]
-    node_zero_grads = node_grads[node_rows + edge_rows :]
+    node_one_grads, edge_one_grads = layer_one_grads[:node_rows], layer_one_grads[node_rows:]
     node_first_rows = node_rows - second_rows
     grads = [
         jnp.stack([edge_zero_grads[:first_rows], edge_one_grads[:first_rows]]),
@@ -946,9 +994,13 @@
         adam_terms(masters[place], grads[place], firsts[place], seconds[place], WEIGHT_DECAY)
         for place in range(4)
     ]
-    update_squares = sum_everywhere(
-        jnp.stack([jnp.sum(entry[2] * entry[2], axis=(1, 2)) for entry in moment_list], axis=1)
-    )
+    update_local = jnp.stack(
+        [jnp.sum(entry[2] * entry[2], axis=(1, 2)) for entry in moment_list], axis=1
+    )
+    update_local, grad_node, edge_input_grad = lax.optimization_barrier(
+        (update_local, grad_node, edge_input_grad)
+    )
+    update_squares = sum_everywhere(update_local)
     weight_norm = jnp.sqrt(weight_squares)
     update_norm = jnp.sqrt(update_squares)
     new_weights = []

time: 300 us -> 303 us (1.010)
  starting transfers between devices: 62.2 us -> 70.3 us
  local copies, waits for them, and re-layouts: 35.2 us -> 30 us
  waiting for transfers between devices: 81 us -> 77.4 us
    ppermute x46 -> x9, waiting for transfers between devices: 70.3 us -> 13.7 us  [swap(): lax.ppermute(values, axis, [(i, i ^ offset) for i in range(lax.axis_size(...]
    ppermute x7 -> x47, waiting for transfers between devices: 6.09 us -> 60.4 us  [exchange(): lax.ppermute(values, ('node', 'hid'), [(i, i ^ mask) for i in range(total)])]
    ppermute x7 -> x47, starting transfers between devices: 7.88 us -> 48.1 us  [exchange(): lax.ppermute(values, ('node', 'hid'), [(i, i ^ mask) for i in range(total)])]
    ppermute x46 -> x9, starting transfers between devices: 35.2 us -> 5.38 us  [swap(): lax.ppermute(values, axis, [(i, i ^ offset) for i in range(lax.axis_size(...]
    concatenate x8 -> x5, local copies, waits for them, and re-layouts: 5.56 us -> 2.31 us  [the longest x3 1.22 us: gather_round(): return jnp.concatenate([held, *arrived], axis=0)]
    unnamed x169 -> x144, local copies, waits for them, and re-layouts: 12.5 us -> 9.67 us
    concatenate x17 -> x8, other arithmetic: 7.51 us -> 6.39 us  [the longest x6 5.35 us: gather_round(): return jnp.concatenate([held, *arrived], axis=0)]
  transfers between devices with their start and end apart: 61 -> 64, of which waited for: 26 -> 26; matrix products, arithmetic and copies ran while one was open for 16% -> 13% of each run, Pallas kernels for 20% -> 20%
where the time goes in v3:
time: 303 us; the launch traced here: 302 us
  Pallas kernels  88.3 us (29%)
  waiting for transfers between devices  77.4 us (26%)
  starting transfers between devices  70.3 us (23%)
  other arithmetic  31.9 us (11%)
  local copies, waits for them, and re-layouts  30 us (10%)
    pallas_call x9, Pallas kernels, run_kernel(): pl.pallas_call(kernel, name=name, grid=(samples,), in_specs=in_specs, out...  88.3 us
    ppermute x47, waiting for transfers between devices, exchange(): lax.ppermute(values, ('node', 'hid'), [(i, i ^ mask) for i in range(total)])  60.4 us
    ppermute x47, starting transfers between devices, exchange(): lax.ppermute(values, ('node', 'hid'), [(i, i ^ mask) for i in range(total)])  48.1 us
    ppermute x4, starting transfers between devices, to_neighbours(): from_next = lax.ppermute(rows[:, :halo_width], 'node', back)  15.7 us
    ppermute x9, waiting for transfers between devices, swap(): lax.ppermute(values, axis, [(i, i ^ offset) for i in range(lax.axis_size(...  13.7 us
    unnamed x144, local copies, waits for them, and re-layouts  9.67 us
  transfers between devices with their start and end apart: 64, of which 26 were waited for; matrix products, arithmetic and copies ran while one was open for 13% of the time, Pallas kernels for 20%

profile of v3, /device:TPU:0, one launch (start us, length us, event | category | flops | bytes accessed | tf_op | source)
XLA Modules:
  0.0 301.8 jit_solution(745909918539584933)
XLA Ops:
  5.3 4.1 %collective-permute-start = (bf16[1,448,128]{2,1,0:T(8,128)(2,1)S(1)}, bf16[1,448,128]{2,1,0:T(8,128)(2,1)S(1)}, u32[]{:S(2)}, u32[]{:S(2)}) collective-permute-start(bf16[1,448,128]{2,1,0:T(8,128)(2,1)S(1)} %maximum_bitcast_fusion), channel_id=1, source_target_pairs={{0,16},{1,17},{2,18},{3,19},{4,20},{5,21},{6,22},{7,23},{8,24},{9,... | collective-permute-start | bytes 344072 | tf_op jit(solution)/shard_map/ppermute | solution.py:572
  23.1 2.4 collective-permute-start.10
  28.4 6.7 %collective-permute-done.3 = bf16[4,448,128]{2,1,0:T(8,128)(2,1)} collective-permute-done((bf16[4,448,128]{2,1,0:T(8,128)(2,1)}, bf16[4,448,128]{2,1,0:T(8,128)(2,1)}, u32[]{:S(2)}, u32[]{:S(2)}) %collective-permute-start.3) | collective-permute-done | bytes 458784 | tf_op jit(solution)/shard_map/ppermute | solution.py:572
  38.3 4.6 %collective-permute-start.4 = (bf16[1,448,128]{2,1,0:T(8,128)(2,1)S(1)}, bf16[1,448,128]{2,1,0:T(8,128)(2,1)S(1)}, u32[]{:S(2)}, u32[]{:S(2)}) collective-permute-start(bf16[1,448,128]{2,1,0:T(8,128)(2,1)S(1)} %copy-done.28), channel_id=1, source_target_pairs={{0,16},{1,17},{2,18},{3,19},{4,20},{5,21},{6,22},{7,23},{8,24},{9,... | collective-permute-start | bytes 344072 | tf_op jit(solution)/shard_map/ppermute | solution.py:572
  43.0 4.5 %collective-permute-done.4 = bf16[1,448,128]{2,1,0:T(8,128)(2,1)S(1)} collective-permute-done((bf16[1,448,128]{2,1,0:T(8,128)(2,1)S(1)}, bf16[1,448,128]{2,1,0:T(8,128)(2,1)S(1)}, u32[]{:S(2)}, u32[]{:S(2)}) %collective-permute-start.4) | collective-permute-done | bytes 114720 | tf_op jit(solution)/shard_map/ppermute | solution.py:572
  48.3 5.8 %collective-permute-done.6 = bf16[1,448,128]{2,1,0:T(8,128)(2,1)S(1)} collective-permute-done((bf16[1,448,128]{2,1,0:T(8,128)(2,1)S(1)}, bf16[1,448,128]{2,1,0:T(8,128)(2,1)S(1)}, u32[]{:S(2)}, u32[]{:S(2)}) %collective-permute-start.6) | collective-permute-done | bytes 114720 | tf_op jit(solution)/shard_map/ppermute | solution.py:572
  57.4 1.9 pad_maximum_fusion.7.table
  63.0 11.5 %edge_forward.2 = (bf16[3,640,512]{2,1,0:T(8,128)(2,1)}, bf16[3,640,512]{2,1,0:T(8,128)(2,1)}, bf16[3,640,512]{2,1,0:T(8,128)(2,1)}, f32[3,640,1]{2,1,0:T(8,128)...) custom-call(s32[32]{0:T(128)} %add.300.order, ...), custom_call_target="tpu_custom_call" | custom-call | flops 15225323520 | bytes 19271296 | tf_op jit(solution)/shard_map/edge_forward/pallas_call | solution.py:124
  83.9 5.0 %node_pass.2 = (bf16[480,512]{1,0:T(8,128)(2,1)}, bf16[480,512]{1,0:T(8,128)(2,1)}, bf16[480,512]{1,0:T(8,128)(2,1)}, bf16[480,512]{1,0:T(8,128)(2,1)}, f32[480,...) custom-call(s32[32]{0:T(128)} %add.300.order, ...), custom_call_target="tpu_custom_call" | custom-call | flops 3019898880 | bytes 7269376 | tf_op jit(solution)/shard_map/node_pass/pallas_call | solution.py:124
  90.5 4.2 %collective-permute-start.17 = (bf16[3,40,512]{2,1,0:T(8,128)(2,1)S(1)}, bf16[3,40,512]{2,1,0:T(8,128)(2,1)S(1)}, u32[]{:S(2)}, u32[]{:S(2)}) collective-permute-start(bf16[3,40,512]{2,1,0:T(8,128)(2,1)S(1)} %get-tuple-element.373), channel_id=1, source_target_pairs={{4,0},{8,4},{12,8},{16,12},{20,16},{24,20},{28,24},{0,28},{5,1},{9... | collective-permute-start | bytes 368648 | tf_op jit(solution)/shard_map/ppermute | solution.py:628
  94.7 3.0 %collective-permute-done.16 = bf16[3,40,512]{2,1,0:T(8,128)(2,1)S(1)} collective-permute-done((bf16[3,40,512]{2,1,0:T(8,128)(2,1)S(1)}, bf16[3,40,512]{2,1,0:T(8,128)(2,1)S(1)}, u32[]{:S(2)}, u32[]{:S(2)}) %collective-permute-start.16) | collective-permute-done | bytes 122912 | tf_op jit(solution)/shard_map/ppermute | solution.py:627
  99.6 4.6 %collective-permute-done.22 = bf16[40,3,512]{2,0,1:T(8,128)(2,1)S(1)} collective-permute-done((bf16[40,3,512]{2,0,1:T(8,128)(2,1)S(1)}, bf16[40,3,512]{2,0,1:T(8,128)(2,1)S(1)}, u32[]{:S(2)}, u32[]{:S(2)}) %collective-permute-start.22) | collective-permute-done | bytes 122912 | tf_op jit(solution)/shard_map/ppermute | solution.py:509
  106.4 10.9 %edge_forward.3 = (bf16[3,640,512]{2,1,0:T(8,128)(2,1)}, bf16[3,640,512]{2,1,0:T(8,128)(2,1)}, bf16[3,640,512]{2,1,0:T(8,128)(2,1)}, f32[3,640,1]{2,1,0:T(8,128)}, bf16[3,160,512]{2,1,0:T(8,128)(2,1)}) custom-call(s32[32]{0:T(128)} %add.300.order, bf16[32,256,128]{2,1,0:T(8,128)(2,1)} %pad_maximum_fusion.1.w1.w2, ...), custom_call_target="tpu_custom_call" | custom-call | flops 15225323520 | bytes 17960576 | tf_op jit(solution)/shard_map/edge_forward/pallas_call | solution.py:124
  123.2 8.2 %node_pass.3 = (bf16[3,160,512]{2,1,0:T(8,128)(2,1)}, bf16[3,160,512]{2,1,0:T(8,128)(2,1)}, f32[3,160,512]{2,1,0:T(8,128)}, bf16[16,192,128]{2,1,0:T(8,128)(2,1)...) custom-call(s32[32]{0:T(128)} %add.300.order, s32[64]{0:T(128)} %reshape.334.rest_0_.owners, ...), custom_call_target="tpu_custom_call" | custom-call | flops 9059696640 | bytes 8087820 | tf_op jit(solution)/shard_map/node_pass/pallas_call | solution.py:124
  131.4 12.6 %edge_backward.2 = (bf16[3,640,512]{2,1,0:T(8,128)(2,1)}, bf16[3,640,512]{2,1,0:T(8,128)(2,1)}, bf16[3,400,512]{2,1,0:T(8,128)(2,1)}, f32[3,160,512]{2,1,0:T(8,1...) custom-call(s32[32]{0:T(128)} %add.300.order, ...), custom_call_target="tpu_custom_call" | custom-call | flops 14344519680 | bytes 19674752 | tf_op jit(solution)/shard_map/edge_backward/pallas_call | solution.py:124
  145.2 4.6 %collective-permute-start.25 = (bf16[3,40,512]{2,1,0:T(8,128)(2,1)S(1)}, bf16[3,40,512]{2,1,0:T(8,128)(2,1)S(1)}, u32[]{:S(2)}, u32[]{:S(2)}) collective-permute-start(bf16[3,40,512]{2,1,0:T(8,128)(2,1)S(1)} %get-tuple-element.371), channel_id=1, source_target_pairs={{4,0},{8,4},{12,8},{16,12},{20,16},{24,20},{28,24},{0,28},{5,1},{9... | collective-permute-start | bytes 368648 | tf_op jit(solution)/shard_map/ppermute | solution.py:628
  149.8 9.9 %edge_weight_grads.2 = (bf16[16,448,128]{2,1,0:T(8,128)(2,1)}, bf16[16,448,128]{2,1,0:T(8,128)(2,1)}) custom-call(s32[64]{0:T(128)} %reshape.334.rest_0_.owners, bf16[3,640,512]{2,1,0:T(8,128)(2,1)} %get-tuple-element.166.low.edge_low, bf16[3,240,512]{2,1,0:T(8,128)(2,1)} %copy-done.29, bf16[3,640,512]{2,1,0:T(8,128)(2,1)} %get-tuple-element.180.hidden_low, ...), custom_call_target="tpu_custom_call" | custom-call | flops 8053063680 | bytes 15073536 | tf_op jit(solution)/shard_map/edge_weight_grads/pallas_call | solution.py:124
  167.1 8.0 %node_backward.1 = (bf16[3,160,512]{2,1,0:T(8,128)(2,1)}, f32[3,160,512]{2,1,0:T(8,128)}, bf16[16,192,128]{2,1,0:T(8,128)(2,1)}, bf16[16,192,128]{2,1,0:T(8,128)(2,1)}, f32[4,512]{1,0:T(4,128)}) custom-call(s32[32]{0:T(128)} %add.300.order, s32[64]{0:T(128)} %reshape.334.rest_0_.owners, bf16[32,192,128]{2,1,0:T(8,128)(2,1)} %copy-done.43, ...), custom_call_target="tpu_custom_call" | custom-call | flops 6039797760 | bytes 9564288 | tf_op jit(solution)/shard_map/node_backward/pallas_call | solution.py:124
  176.8 14.3 %edge_backward.3 = (bf16[3,640,512]{2,1,0:T(8,128)(2,1)}, bf16[3,640,512]{2,1,0:T(8,128)(2,1)}, bf16[3,400,512]{2,1,0:T(8,128)(2,1)}, f32[3,160,512]{2,1,0:T(8,1...) custom-call(s32[32]{0:T(128)} %add.300.order, ...), custom_call_target="tpu_custom_call" | custom-call | flops 14344519680 | bytes 21640832 | tf_op jit(solution)/shard_map/edge_backward/pallas_call | solution.py:124
  192.0 6.5 %collective-permute-done.29 = bf16[8,448,128]{2,1,0:T(8,128)(2,1)S(1)} collective-permute-done((bf16[8,448,128]{2,1,0:T(8,128)(2,1)S(1)}, bf16[8,448,128]{2,1,0:T(8,128)(2,1)S(1)}, u32[]{:S(2)}, u32[]{:S(2)}) %collective-permute-start.29) | collective-permute-done | bytes 917536 | tf_op jit(solution)/shard_map/ppermute | solution.py:572
  198.8 7.8 %edge_weight_grads.3 = (bf16[16,256,128]{2,1,0:T(8,128)(2,1)}, bf16[16,256,128]{2,1,0:T(8,128)(2,1)}) custom-call(s32[64]{0:T(128)} %reshape.334.rest_0_.owners, bf16[640,512]{1,0:T(8,128)(2,1)} %bitcast.172, bf16[3,240,512]{2,1,0:T(8,128)(2,1)} %pad_maximum_fusion.7.table, bf16[640,512]{1,0:T(8,128)(2,1)} %get-tuple-element.208.hidden_low, ...), custom_call_target="tpu_custom_call" | custom-call | flops 8053063680 | bytes 9306368 | tf_op jit(solution)/shard_map/edge_weight_grads/pallas_call | solution.py:124
  206.8 3.3 %collective-permute-done.31 = bf16[4,448,128]{2,1,0:T(8,128)(2,1)S(1)} collective-permute-done((bf16[4,448,128]{2,1,0:T(8,128)(2,1)S(1)}, bf16[4,448,128]{2,1,0:T(8,128)(2,1)S(1)}, u32[]{:S(2)}, u32[]{:S(2)}) %collective-permute-start.31) | collective-permute-done | bytes 458784 | tf_op jit(solution)/shard_map/ppermute | solution.py:572
  217.9 4.4 %collective-permute-start.40 = (bf16[3,40,512]{2,1,0:T(8,128)(2,1)S(1)}, bf16[3,40,512]{2,1,0:T(8,128)(2,1)S(1)}, u32[]{:S(2)}, u32[]{:S(2)}) collective-permute-start(bf16[3,40,512]{2,1,0:T(8,128)(2,1)S(1)} %get-tuple-element.369), channel_id=1, source_target_pairs={{4,0},{8,4},{12,8},{16,12},{20,16},{24,20},{28,24},{0,28},{5,1},{9... | collective-permute-start | bytes 368648 | tf_op jit(solution)/shard_map/ppermute | solution.py:628
  223.1 7.9 %collective-permute-done.34 = f32[17,512]{1,0:T(8,128)S(1)} collective-permute-done((f32[17,512]{1,0:T(8,128)S(1)}, f32[17,512]{1,0:T(8,128)S(1)}, u32[]{:S(2)}, u32[]{:S(2)}) %collective-permute-start.34) | collective-permute-done | bytes 34848 | tf_op jit(solution)/shard_map/ppermute | solution.py:572
  233.4 4.8 %collective-permute-done.46 = bf16[1,448,128]{2,1,0:T(8,128)(2,1)S(1)} collective-permute-done((bf16[1,448,128]{2,1,0:T(8,128)(2,1)S(1)}, bf16[1,448,128]{2,1,0:T(8,128)(2,1)S(1)}, u32[]{:S(2)}, u32[]{:S(2)}) %collective-permute-start.46) | collective-permute-done | bytes 114720 | tf_op jit(solution)/shard_map/ppermute | solution.py:572
  245.4 8.1 %collective-permute-done.36 = bf16[40,3,512]{2,0,1:T(8,128)(2,1)S(1)} collective-permute-done((bf16[40,3,512]{2,0,1:T(8,128)(2,1)S(1)}, bf16[40,3,512]{2,0,1:T(8,128)(2,1)S(1)}, u32[]{:S(2)}, u32[]{:S(2)}) %collective-permute-start.36) | collective-permute-done | bytes 122912 | tf_op jit(solution)/shard_map/ppermute | solution.py:509
  257.6 3.9 %collective-permute-done.51 = bf16[1,192,128]{2,1,0:T(8,128)(2,1)S(1)} collective-permute-done((bf16[1,192,128]{2,1,0:T(8,128)(2,1)S(1)}, bf16[1,192,128]{2,1,0:T(8,128)(2,1)S(1)}, u32[]{:S(2)}, u32[]{:S(2)}) %collective-permute-start.51) | collective-permute-done | bytes 49184 | tf_op jit(solution)/shard_map/ppermute | solution.py:572
  264.6 2.6 collective-permute-start.56
  271.6 2.6 collective-permute-start.44
  284.7 2.0 collective-permute-start.60
  289.2 2.6 collective-permute-start.62
  293.6 3.5 %collective-permute-done.63 = f32[2,4]{0,1:T(4,128)S(1)} collective-permute-done((f32[2,4]{0,1:T(4,128)S(1)}, f32[2,4]{0,1:T(4,128)S(1)}, u32[]{:S(2)}, u32[]{:S(2)}) %collective-permute-start.63) | collective-permute-done | bytes 64 | tf_op jit(solution)/shard_map/ppermute | solution.py:572
  (409 shorter events, 111.7 us)
Async XLA Ops:
  5.3 11.4 %collective-permute-start = (bf16[1,448,128]{2,1,0:T(8,128)(2,1)S(1)}, bf16[1,448,128]{2,1,0:T(8,128)(2,1)S(1)}, u32[]{:S(2)}, u32[]{:S(2)}) collective-permute-start(bf16[1,448,128]{2,1,0:T(8,128)(2,1)S(1)} %maximum_bitcast_fusion), channel_id=1, source_target_pairs={{0,16},{1,17},{2,18},{3,19},{4,20},{5,21},{6,22},{7,23},{8,24},{9,... | collective-permute-start | bytes 344072 | tf_op jit(solution)/shard_map/ppermute | solution.py:572
  11.0 7.6 %collective-permute-start.2 = (bf16[1,448,128]{2,1,0:T(8,128)(2,1)S(1)}, bf16[1,448,128]{2,1,0:T(8,128)(2,1)S(1)}, u32[]{:S(2)}, u32[]{:S(2)}) collective-permute-start(bf16[1,448,128]{2,1,0:T(8,128)(2,1)S(1)} %maximum_bitcast_fusion), channel_id=1, source_target_pairs={{0,24},{1,25},{2,26},{3,27},{4,28},{5,29},{6,30},{7,31},{8,16},{9,... | collective-permute-start | bytes 344072 | tf_op jit(solution)/shard_map/ppermute | solution.py:572
  19.4 15.7 %collective-permute-start.3 = (bf16[4,448,128]{2,1,0:T(8,128)(2,1)}, bf16[4,448,128]{2,1,0:T(8,128)(2,1)}, u32[]{:S(2)}, u32[]{:S(2)}) collective-permute-start(bf16[4,448,128]{2,1,0:T(8,128)(2,1)} %pad_maximum_fusion.11), channel_id=1, source_target_pairs={{0,4},{1,5},{2,6},{3,7},{4,0},{5,1},{6,2},{7,3},{8,12},{9,13},{10,... | collective-permute-start | bytes 1376264 | tf_op jit(solution)/shard_map/ppermute | solution.py:572
  23.1 34.3 %collective-permute-start.10 = (bf16[3,40,512]{2,1,0:T(8,128)(2,1)}, bf16[3,40,512]{2,1,0:T(8,128)(2,1)}, u32[]{:S(2)}, u32[]{:S(2)}) collective-permute-start(bf16[3,40,512]{2,1,0:T(8,128)(2,1)} %get-tuple-element.375), channel_id=1, source_target_pairs={{4,0},{8,4},{12,8},{16,12},{20,16},{24,20},{28,24},{0,28},{5,1},{9... | collective-permute-start | bytes 368648 | tf_op jit(solution)/shard_map/ppermute | solution.py:628
  25.6 31.9 %collective-permute-start.9 = (bf16[3,40,512]{2,1,0:T(8,128)(2,1)}, bf16[3,40,512]{2,1,0:T(8,128)(2,1)}, u32[]{:S(2)}, u32[]{:S(2)}) collective-permute-start(bf16[3,40,512]{2,1,0:T(8,128)(2,1)} %get-tuple-element.374), channel_id=1, source_target_pairs={{0,4},{4,8},{8,12},{12,16},{16,20},{20,24},{24,28},{28,0},{1,5},{5... | collective-permute-start | bytes 368648 | tf_op jit(solution)/shard_map/ppermute | solution.py:627
  36.2 18.8 %collective-permute-start.7 = (bf16[8,256,128]{2,1,0:T(8,128)(2,1)S(1)}, bf16[8,256,128]{2,1,0:T(8,128)(2,1)S(1)}, u32[]{:S(2)}, u32[]{:S(2)}) collective-permute-start(bf16[8,256,128]{2,1,0:T(8,128)(2,1)S(1)} %slice.318), channel_id=1, source_target_pairs={{0,2},{1,3},{2,0},{3,1},{4,6},{5,7},{6,4},{7,5},{8,10},{9,11},{10,... | collective-permute-start | bytes 1572872 | tf_op jit(solution)/shard_map/ppermute | solution.py:572
  38.3 9.2 %collective-permute-start.4 = (bf16[1,448,128]{2,1,0:T(8,128)(2,1)S(1)}, bf16[1,448,128]{2,1,0:T(8,128)(2,1)S(1)}, u32[]{:S(2)}, u32[]{:S(2)}) collective-permute-start(bf16[1,448,128]{2,1,0:T(8,128)(2,1)S(1)} %copy-done.28), channel_id=1, source_target_pairs={{0,16},{1,17},{2,18},{3,19},{4,20},{5,21},{6,22},{7,23},{8,24},{9,... | collective-permute-start | bytes 344072 | tf_op jit(solution)/shard_map/ppermute | solution.py:572
  59.4 15.1 %collective-permute-start.12 = (bf16[4,448,128]{2,1,0:T(8,128)(2,1)S(1)}, bf16[4,448,128]{2,1,0:T(8,128)(2,1)S(1)}, u32[]{:S(2)}, u32[]{:S(2)}) collective-permute-start(bf16[4,448,128]{2,1,0:T(8,128)(2,1)S(1)} %get-tuple-element.385), channel_id=1, source_target_pairs={{0,4},{1,5},{2,6},{3,7},{4,0},{5,1},{6,2},{7,3},{8,12},{9,13},{10,... | collective-permute-start | bytes 1376264 | tf_op jit(solution)/shard_map/ppermute | solution.py:572
  60.9 13.6 %collective-permute-start.11 = (bf16[8,192,128]{2,1,0:T(8,128)(2,1)S(1)}, bf16[8,192,128]{2,1,0:T(8,128)(2,1)S(1)}, u32[]{:S(2)}, u32[]{:S(2)}) collective-permute-start(bf16[8,192,128]{2,1,0:T(8,128)(2,1)S(1)} %slice.321), channel_id=1, source_target_pairs={{0,2},{1,3},{2,0},{3,1},{4,6},{5,7},{6,4},{7,5},{8,10},{9,11},{10,... | collective-permute-start | bytes 1179656 | tf_op jit(solution)/shard_map/ppermute | solution.py:572
  80.3 17.8 %collective-permute-start.13 = (bf16[8,256,128]{2,1,0:T(8,128)(2,1)S(1)}, bf16[8,256,128]{2,1,0:T(8,128)(2,1)S(1)}, u32[]{:S(2)}, u32[]{:S(2)}) collective-permute-start(bf16[8,256,128]{2,1,0:T(8,128)(2,1)S(1)} %slice.323), channel_id=1, source_target_pairs={{0,2},{1,3},{2,0},{3,1},{4,6},{5,7},{6,4},{7,5},{8,10},{9,11},{10,... | collective-permute-start | bytes 1572872 | tf_op jit(solution)/shard_map/ppermute | solution.py:572
  89.9 7.8 %collective-permute-start.16 = (bf16[3,40,512]{2,1,0:T(8,128)(2,1)S(1)}, bf16[3,40,512]{2,1,0:T(8,128)(2,1)S(1)}, u32[]{:S(2)}, u32[]{:S(2)}) collective-permute-start(bf16[3,40,512]{2,1,0:T(8,128)(2,1)S(1)} %get-tuple-element.372), channel_id=1, source_target_pairs={{0,4},{4,8},{8,12},{12,16},{16,20},{20,24},{24,28},{28,0},{1,5},{5... | collective-permute-start | bytes 368648 | tf_op jit(solution)/shard_map/ppermute | solution.py:627
  104.2 13.1 %collective-permute-start.18 = (bf16[8,192,128]{2,1,0:T(8,128)(2,1)S(1)}, bf16[8,192,128]{2,1,0:T(8,128)(2,1)S(1)}, u32[]{:S(2)}, u32[]{:S(2)}) collective-permute-start(bf16[8,192,128]{2,1,0:T(8,128)(2,1)S(1)} %slice.322), channel_id=1, source_target_pairs={{0,2},{1,3},{2,0},{3,1},{4,6},{5,7},{6,4},{7,5},{8,10},{9,11},{10,... | collective-permute-start | bytes 1179656 | tf_op jit(solution)/shard_map/ppermute | solution.py:572
  145.0 14.7 %collective-permute-start.24 = (bf16[3,40,512]{2,1,0:T(8,128)(2,1)S(1)}, bf16[3,40,512]{2,1,0:T(8,128)(2,1)S(1)}, u32[]{:S(2)}, u32[]{:S(2)}) collective-permute-start(bf16[3,40,512]{2,1,0:T(8,128)(2,1)S(1)} %get-tuple-element.370), channel_id=1, source_target_pairs={{0,4},{4,8},{8,12},{12,16},{16,20},{20,24},{24,28},{28,0},{1,5},{5... | collective-permute-start | bytes 368648 | tf_op jit(solution)/shard_map/ppermute | solution.py:627
  145.2 14.6 %collective-permute-start.25 = (bf16[3,40,512]{2,1,0:T(8,128)(2,1)S(1)}, bf16[3,40,512]{2,1,0:T(8,128)(2,1)S(1)}, u32[]{:S(2)}, u32[]{:S(2)}) collective-permute-start(bf16[3,40,512]{2,1,0:T(8,128)(2,1)S(1)} %get-tuple-element.371), channel_id=1, source_target_pairs={{4,0},{8,4},{12,8},{16,12},{20,16},{24,20},{28,24},{0,28},{5,1},{9... | collective-permute-start | bytes 368648 | tf_op jit(solution)/shard_map/ppermute | solution.py:628
  175.1 16.0 %collective-permute-start.30 = (bf16[16,192,128]{2,1,0:T(8,128)(2,1)}, bf16[16,192,128]{2,1,0:T(8,128)(2,1)S(1)}, u32[]{:S(2)}, u32[]{:S(2)}) collective-permute-start(bf16[16,192,128]{2,1,0:T(8,128)(2,1)} %get-tuple-element.215), channel_id=1, source_target_pairs={{0,1},{1,0},{2,3},{3,2},{4,5},{5,4},{6,7},{7,6},{8,9},{9,8},{10,11... | collective-permute-start | bytes 2359304 | tf_op jit(solution)/shard_map/ppermute | solution.py:572
  175.2 23.2 %collective-permute-start.29 = (bf16[8,448,128]{2,1,0:T(8,128)(2,1)S(1)}, bf16[8,448,128]{2,1,0:T(8,128)(2,1)S(1)}, u32[]{:S(2)}, u32[]{:S(2)}) collective-permute-start(bf16[8,448,128]{2,1,0:T(8,128)(2,1)S(1)} %slice.415), channel_id=1, source_target_pairs={{0,2},{1,3},{2,0},{3,1},{4,6},{5,7},{6,4},{7,5},{8,10},{9,11},{10,... | collective-permute-start | bytes 2752520 | tf_op jit(solution)/shard_map/ppermute | solution.py:572
  191.4 15.3 %collective-permute-start.32 = (bf16[8,192,128]{2,1,0:T(8,128)(2,1)S(1)}, bf16[8,192,128]{2,1,0:T(8,128)(2,1)S(1)}, u32[]{:S(2)}, u32[]{:S(2)}) collective-permute-start(bf16[8,192,128]{2,1,0:T(8,128)(2,1)S(1)} %slice.418), channel_id=1, source_target_pairs={{0,2},{1,3},{2,0},{3,1},{4,6},{5,7},{6,4},{7,5},{8,10},{9,11},{10,... | collective-permute-start | bytes 1179656 | tf_op jit(solution)/shard_map/ppermute | solution.py:572
  198.7 11.4 %collective-permute-start.31 = (bf16[4,448,128]{2,1,0:T(8,128)(2,1)S(1)}, bf16[4,448,128]{2,1,0:T(8,128)(2,1)S(1)}, u32[]{:S(2)}, u32[]{:S(2)}) collective-permute-start(bf16[4,448,128]{2,1,0:T(8,128)(2,1)S(1)} %slice.417), channel_id=1, source_target_pairs={{0,4},{1,5},{2,6},{3,7},{4,0},{5,1},{6,2},{7,3},{8,12},{9,13},{10,... | collective-permute-start | bytes 1376264 | tf_op jit(solution)/shard_map/ppermute | solution.py:572
  215.9 17.3 %collective-permute-start.35 = (bf16[8,256,128]{2,1,0:T(8,128)(2,1)S(1)}, bf16[8,256,128]{2,1,0:T(8,128)(2,1)S(1)}, u32[]{:S(2)}, u32[]{:S(2)}) collective-permute-start(bf16[8,256,128]{2,1,0:T(8,128)(2,1)S(1)} %slice.416), channel_id=1, source_target_pairs={{0,2},{1,3},{2,0},{3,1},{4,6},{5,7},{6,4},{7,5},{8,10},{9,11},{10,... | collective-permute-start | bytes 1572872 | tf_op jit(solution)/shard_map/ppermute | solution.py:572
  217.6 13.5 %collective-permute-start.39 = (bf16[3,40,512]{2,1,0:T(8,128)(2,1)S(1)}, bf16[3,40,512]{2,1,0:T(8,128)(2,1)S(1)}, u32[]{:S(2)}, u32[]{:S(2)}) collective-permute-start(bf16[3,40,512]{2,1,0:T(8,128)(2,1)S(1)} %get-tuple-element.368), channel_id=1, source_target_pairs={{0,4},{4,8},{8,12},{12,16},{16,20},{20,24},{24,28},{28,0},{1,5},{5... | collective-permute-start | bytes 368648 | tf_op jit(solution)/shard_map/ppermute | solution.py:627
  217.9 13.6 %collective-permute-start.40 = (bf16[3,40,512]{2,1,0:T(8,128)(2,1)S(1)}, bf16[3,40,512]{2,1,0:T(8,128)(2,1)S(1)}, u32[]{:S(2)}, u32[]{:S(2)}) collective-permute-start(bf16[3,40,512]{2,1,0:T(8,128)(2,1)S(1)} %get-tuple-element.369), channel_id=1, source_target_pairs={{4,0},{8,4},{12,8},{16,12},{20,16},{24,20},{28,24},{0,28},{5,1},{9... | collective-permute-start | bytes 368648 | tf_op jit(solution)/shard_map/ppermute | solution.py:628
  222.3 8.7 %collective-permute-start.34 = (f32[17,512]{1,0:T(8,128)S(1)}, f32[17,512]{1,0:T(8,128)S(1)}, u32[]{:S(2)}, u32[]{:S(2)}) collective-permute-start(f32[17,512]{1,0:T(8,128)S(1)} %add.307), channel_id=1, source_target_pairs={{0,2},{1,3},{2,0},{3,1},{4,6},{5,7},{6,4},{7,5},{8,10},{9,11},{10,... | collective-permute-start | bytes 104456 | tf_op jit(solution)/shard_map/ppermute | solution.py:572
  223.1 10.4 %collective-permute-start.45 = (bf16[1,448,128]{2,1,0:T(8,128)(2,1)S(1)}, bf16[1,448,128]{2,1,0:T(8,128)(2,1)S(1)}, u32[]{:S(2)}, u32[]{:S(2)}) collective-permute-start(bf16[1,448,128]{2,1,0:T(8,128)(2,1)S(1)} %get-tuple-element.362), channel_id=1, source_target_pairs={{0,16},{1,17},{2,18},{3,19},{4,20},{5,21},{6,22},{7,23},{8,24},{9,... | collective-permute-start | bytes 344072 | tf_op jit(solution)/shard_map/ppermute | solution.py:572
  231.5 12.0 %collective-permute-start.48 = (bf16[4,192,128]{2,1,0:T(8,128)(2,1)S(1)}, bf16[4,192,128]{2,1,0:T(8,128)(2,1)S(1)}, u32[]{:S(2)}, u32[]{:S(2)}) collective-permute-start(bf16[4,192,128]{2,1,0:T(8,128)(2,1)S(1)} %slice.420), channel_id=1, source_target_pairs={{0,4},{1,5},{2,6},{3,7},{4,0},{5,1},{6,2},{7,3},{8,12},{9,13},{10,... | collective-permute-start | bytes 589832 | tf_op jit(solution)/shard_map/ppermute | solution.py:572
  239.1 23.7 %collective-permute-start.41 = (bf16[3,160,512]{2,1,0:T(8,128)(2,1)S(1)}, bf16[3,160,512]{2,1,0:T(8,128)(2,1)S(1)}, u32[]{:S(2)}, u32[]{:S(2)}) collective-permute-start(bf16[3,160,512]{2,1,0:T(8,128)(2,1)S(1)} %get-tuple-element.342), channel_id=1, source_target_pairs={{0,1},{1,0},{2,3},{3,2},{4,5},{5,4},{6,7},{7,6},{8,9},{9,8},{10,11... | collective-permute-start | bytes 1474568 | tf_op jit(solution)/shard_map/ppermute | solution.py:509
  239.5 16.1 %collective-permute-start.37 = (bf16[4,256,128]{2,1,0:T(8,128)(2,1)S(1)}, bf16[4,256,128]{2,1,0:T(8,128)(2,1)S(1)}, u32[]{:S(2)}, u32[]{:S(2)}) collective-permute-start(bf16[4,256,128]{2,1,0:T(8,128)(2,1)S(1)} %slice.419), channel_id=1, source_target_pairs={{0,4},{1,5},{2,6},{3,7},{4,0},{5,1},{6,2},{7,3},{8,12},{9,13},{10,... | collective-permute-start | bytes 786440 | tf_op jit(solution)/shard_map/ppermute | solution.py:572
  241.3 20.7 %collective-permute-start.53 = (bf16[320,512]{1,0:T(8,128)(2,1)S(1)}, bf16[320,512]{1,0:T(8,128)(2,1)S(1)}, u32[]{:S(2)}, u32[]{:S(2)}) collective-permute-start(bf16[320,512]{1,0:T(8,128)(2,1)S(1)} %fusion.5), channel_id=1, source_target_pairs={{0,2},{1,3},{2,0},{3,1},{4,6},{5,7},{6,4},{7,5},{8,10},{9,11},{10,... | collective-permute-start | bytes 983048 | tf_op jit(solution)/shard_map/ppermute | solution.py:509
  243.5 10.0 %collective-permute-start.36 = (bf16[40,3,512]{2,0,1:T(8,128)(2,1)S(1)}, bf16[40,3,512]{2,0,1:T(8,128)(2,1)S(1)}, u32[]{:S(2)}, u32[]{:S(2)}) collective-permute-start(bf16[40,3,512]{2,0,1:T(8,128)(2,1)S(1)} %dynamic-slice_bitcast_fusion.2), channel_id=1, source_target_pairs={{0,2},{1,3},{2,0},{3,1},{4,6},{5,7},{6,4},{7,5},{8,10},{9,11},{10,... | collective-permute-start | bytes 368648 | tf_op jit(solution)/shard_map/ppermute | solution.py:509
  244.2 12.6 %collective-permute-start.49 = (bf16[1,192,128]{2,1,0:T(8,128)(2,1)S(1)}, bf16[1,192,128]{2,1,0:T(8,128)(2,1)S(1)}, u32[]{:S(2)}, u32[]{:S(2)}) collective-permute-start(bf16[1,192,128]{2,1,0:T(8,128)(2,1)S(1)} %get-tuple-element.380), channel_id=1, source_target_pairs={{0,16},{1,17},{2,18},{3,19},{4,20},{5,21},{6,22},{7,23},{8,24},{9,... | collective-permute-start | bytes 147464 | tf_op jit(solution)/shard_map/ppermute | solution.py:572
  262.8 8.8 %collective-permute-start.55 = (f32[17,512]{1,0:T(8,128)S(1)}, f32[17,512]{1,0:T(8,128)S(1)}, u32[]{:S(2)}, u32[]{:S(2)}) collective-permute-start(f32[17,512]{1,0:T(8,128)S(1)} %add.318), channel_id=1, source_target_pairs={{0,8},{1,9},{2,10},{3,11},{4,12},{5,13},{6,14},{7,15},{8,0},{9,1},... | collective-permute-start | bytes 104456 | tf_op jit(solution)/shard_map/ppermute | solution.py:572
  264.6 9.7 %collective-permute-start.56 = (f32[17,512]{1,0:T(8,128)S(1)}, f32[17,512]{1,0:T(8,128)S(1)}, u32[]{:S(2)}, u32[]{:S(2)}) collective-permute-start(f32[17,512]{1,0:T(8,128)S(1)} %add.318), channel_id=1, source_target_pairs={{0,24},{1,25},{2,26},{3,27},{4,28},{5,29},{6,30},{7,31},{8,16},{9,... | collective-permute-start | bytes 104456 | tf_op jit(solution)/shard_map/ppermute | solution.py:572
  268.2 12.1 %collective-permute-start.52 = (bf16[40,3,512]{2,0,1:T(8,128)(2,1)}, bf16[40,3,512]{2,0,1:T(8,128)(2,1)}, u32[]{:S(2)}, u32[]{:S(2)}) collective-permute-start(bf16[40,3,512]{2,0,1:T(8,128)(2,1)} %dynamic-slice_bitcast_fusion.1), channel_id=1, source_target_pairs={{0,2},{1,3},{2,0},{3,1},{4,6},{5,7},{6,4},{7,5},{8,10},{9,11},{10,... | collective-permute-start | bytes 368648 | tf_op jit(solution)/shard_map/ppermute | solution.py:509
  (102 other events, 909.5 us)

commit v4 on v3

--- a/solution.py
+++ b/solution.py
@@ -708,17 +708,15 @@
     layer_zero = gather_round(layer_zero, steps - 3, steps - 2)
     node_zero, edge_zero = parted(layer_zero)
     layer_one = layer_shards(1, setup)
-    for begin, end in rounds(0, steps - 3):
-        layer_one = gather_round(after(layer_one, edge_zero), begin, end)
-    edge_zero = gather_round(edge_zero, steps - 2, steps - 1)
+    layer_one = after(layer_one, edge_zero)
+    z_rounds = rounds(0, steps - 3)
+    for begin, end in z_rounds[:-1]:
+        layer_one = gather_round(layer_one, begin, end)
+    halo_gate = edge_zero
     masters = (edge_first, edge_second, node_first, node_second)
     weight_local = jnp.stack(
         [jnp.sum(matrix * matrix, axis=(1, 2)) for matrix in after(masters, setup)], axis=1
     )
-    node_zero = after(node_zero, edge_zero)
-    edge_zero = gather_round(after(edge_zero, layer_one), steps - 1, steps)
-    edge_zero = after(edge_zero, weight_local)
-
     def edge_blocks(whole):
         return ((whole, first_rows, 0), (whole, second_rows, first_rows // second_rows))
 
@@ -735,12 +733,15 @@
     def own_samples(values):
         return lax.dynamic_slice_in_dim(values, sample_half * samples, samples, 1)
 
-    def to_own_rows(values):
+    def own_rows_exchanged(values):
         quarters = jnp.moveaxis(values.reshape(samples, 2, 2, node_part, latent), 0, 3)
         quarters = lax.dynamic_index_in_dim(quarters, edge_half, 1, keepdims=False)
         sent = lax.dynamic_index_in_dim(quarters, 1 - sample_half, 0, keepdims=False)
         kept = lax.dynamic_index_in_dim(quarters, sample_half, 0, keepdims=False)
-        return jnp.concatenate(ordered(sample_half, kept, swap(sent, "hid", 2)), axis=1)
+        return kept, swap(sent, "hid", 2)
+
+    def all_samples(kept, arrived):
+        return jnp.concatenate(ordered(sample_half, kept, arrived), axis=1)
 
     send_slot, recv_local, halo_lists, node_in, edge_in = lax.optimization_barrier(
         (send_slot, recv_local, halo_lists, node_in, edge_in, setup)
@@ -764,7 +765,17 @@
     edge_in_own = own_edges(edge_in)
     halo_rows = dot("hn,snl->shl", at_halo, node_low).astype(BF16)
     node_low_zero = node_low
-    table_zero = jnp.concatenate([node_low, to_neighbours(halo_rows, halo_width)], axis=1)
+    halo_rows = to_neighbours(after(halo_rows, halo_gate), halo_width)
+    begin, end = z_rounds[-1]
+    arrived = [exchange(layer_one, begin, flips) for flips in range(1, 1 << (end - begin))]
+    edge_arrived, halo_rows, weight_local, *arrived = lax.optimization_barrier(
+        (exchange(edge_zero, steps - 2, 1), halo_rows, weight_local, *arrived)
+    )
+    edge_zero = jnp.concatenate([edge_zero, edge_arrived], axis=0)
+    layer_one = jnp.concatenate([layer_one, *arrived], axis=0)
+    node_zero = after(node_zero, edge_zero)
+    edge_zero = gather_round(edge_zero, steps - 1, steps)
+    table_zero = jnp.concatenate([node_low, halo_rows], axis=1)
     pre_zero, act_zero, normed_zero, inverse_zero, edge_state, edge_low, pooled = edge_forward(
         order,
         *edge_blocks(edge_zero),
@@ -874,6 +885,8 @@
         True,
         node_total,
     )
+    low, *node_out = lax.optimization_barrier((low, *own_rows_exchanged(node_low)))
+    node_out = all_samples(*node_out)
     chain_one = edge_weight_grads(
         owners,
         edge_low,
@@ -940,46 +953,49 @@
         width,
         None,
     )
-    minor_packed = jnp.concatenate(
-        [edge_minor_zero, node_minor_zero, edge_minor_one, node_minor_one]
-        + [jnp.pad(weight_local.reshape(1, -1), ((0, 0), (0, latent - weight_local.size)))],
-        axis=0,
-    )
     chain_zero = split(scatter_round(chain_zero, steps - 2, chain_edge[1]), 2)
-    chain_one = scatter_round(chain_one, steps - 3, chain_edge[1])
-    kept, sent, chain_one, *chain_zero = lax.optimization_barrier(
-        (*chain_edge, chain_one, *chain_zero)
-    )
+    chain_one = [jnp.concatenate(pair, axis=1) for pair in zip(chain_one, chain_zero)]
+    kept, sent, *chain_one = lax.optimization_barrier((*chain_edge, *chain_one))
     chain_edge = split(scatter_round((kept, sent), steps - 1), 2)
-    minor_packed = sum_round(minor_packed, steps - 1, steps)
-    returned, minor_packed, *held = lax.optimization_barrier(
-        (returned, minor_packed, *chain_zero, *chain_edge)
-    )
-    chain_zero, chain_edge = held[:2], held[2:]
-    chain_edge = split(scatter_round(chain_edge, steps - 2), 2)
-    minor_packed = sum_round(minor_packed, steps - 2, steps - 1)
-    layer_one_grads = scatter_rest(chain_one, steps - 3, chain_edge[1])
-    chain_zero = scatter_round(chain_zero, steps - 3, chain_edge[1])
-    returned = after(to_neighbours(returned, halo_width), chain_edge[1])
-    node_low, edge_input_grad, minor_packed, *chain_edge = lax.optimization_barrier(
-        (node_low, edge_input_grad, minor_packed, *chain_edge)
-    )
-    chain_edge = scatter_round(chain_edge, steps - 3)
-    minor_packed = sum_round(minor_packed, steps - 3, steps - 2)
-    node_zero_grads = scatter_rest(chain_zero, steps - 3, chain_edge)
+    returned = to_neighbours(after(returned, chain_edge[1]), halo_width)
+    arrived, returned = lax.optimization_barrier((exchange(chain_one[1], steps - 3, 1), returned))
+    chain_one = chain_one[0].astype(F32) + arrived.astype(F32)
+    for begin, end in reversed(z_rounds[1:]):
+        chain_one = scatter_round(split(chain_one, 1 << (end - begin)), begin)
+    begin, end = z_rounds[0]
+    chain_one = split(chain_one, 1 << (end - begin))
     partial = from_edges(partial, returned)
     other = swap(partial.astype(BF16), "hid", 1)
-    chain_edge, minor_packed, other = lax.optimization_barrier((chain_edge, minor_packed, other))
+    arrived, edge_input_grad, other, *chain_one = lax.optimization_barrier(
+        (exchange(chain_edge[1], steps - 2, 1), edge_input_grad, other, *chain_one)
+    )
+    chain_edge = split(chain_edge[0] + arrived.astype(F32), 2)
+    arrived, *others = lax.optimization_barrier(
+        (
+            exchange(chain_edge[1], steps - 3, 1),
+            *[exchange(chain_one[flips], begin, flips) for flips in range(1, len(chain_one))],
+        )
+    )
+    chain_edge = chain_edge[0] + arrived.astype(F32)
+    joined_grads = chain_one[0]
+    for piece in others:
+        joined_grads = joined_grads + piece.astype(F32)
+    joined_grads = joined_grads[0]
+    node_grad = node_grad + (partial + other.astype(F32))
+    grad_node = own_rows_exchanged(node_grad.astype(BF16))
+    halves = edge_input_grad.reshape(2, edge_part, latent)
+    sent = lax.dynamic_index_in_dim(halves, 1 - sample_half, 0, keepdims=False).astype(BF16)
+    kept = lax.dynamic_index_in_dim(halves, sample_half, 0, keepdims=False)
     edge_zero_grads = scatter_rest(chain_edge, steps - 3)
-    for begin, end in reversed(rounds(0, steps - 3)):
-        minor_packed = sum_round(minor_packed, begin, end)
-    node_out = to_own_rows(node_low)
-    edge_input_grad = halve_sum(edge_input_grad.reshape(2, edge_part, latent), "hid", 1, 0)
-    node_grad = node_grad + (partial + other.astype(F32))
-    grad_node = to_own_rows(node_grad.astype(BF16))
-
-    minor_total = minor_packed[: 8 * LAYERS].reshape(small_params.shape)
-    weight_squares = minor_packed[8 * LAYERS, : weight_local.size].reshape(weight_local.shape)
+    edge_zero_grads, joined_grads, arrived, *grad_node = lax.optimization_barrier(
+        (edge_zero_grads, joined_grads, swap(sent, "hid", 2), *grad_node)
+    )
+    edge_input_grad = kept + arrived.astype(F32)
+    grad_node = all_samples(*grad_node)
+
+    edge_rows = first_rows + second_rows
+    layer_one_grads = joined_grads[: node_rows + edge_rows]
+    node_zero_grads = joined_grads[node_rows + edge_rows :]
     node_one_grads, edge_one_grads = layer_one_grads[:node_rows], layer_one_grads[node_rows:]
     node_first_rows = node_rows - second_rows
     grads = [
@@ -997,10 +1013,17 @@
     update_local = jnp.stack(
         [jnp.sum(entry[2] * entry[2], axis=(1, 2)) for entry in moment_list], axis=1
     )
-    update_local, grad_node, edge_input_grad = lax.optimization_barrier(
-        (update_local, grad_node, edge_input_grad)
-    )
-    update_squares = sum_everywhere(update_local)
+    squares = jnp.concatenate([weight_local.reshape(1, -1), update_local.reshape(1, -1)], axis=1)
+    minor_packed = sum_everywhere(
+        jnp.concatenate(
+            [edge_minor_zero, node_minor_zero, edge_minor_one, node_minor_one]
+            + [jnp.pad(squares, ((0, 0), (0, latent - squares.size)))],
+            axis=0,
+        )
+    )
+    minor_total = minor_packed[: 8 * LAYERS].reshape(small_params.shape)
+    squares = minor_packed[8 * LAYERS, : squares.size].reshape(2, *weight_local.shape)
+    weight_squares, update_squares = squares[0], squares[1]
     weight_norm = jnp.sqrt(weight_squares)
     update_norm = jnp.sqrt(update_squares)
     new_weights = []

time: 303 us -> 278 us (0.917)
  waiting for transfers between devices: 77.4 us -> 61 us
  starting transfers between devices: 70.3 us -> 64.6 us
  other arithmetic: 31.9 us -> 28.3 us
    ppermute x47 -> x37, waiting for transfers between devices: 60.4 us -> 37.4 us  [exchange(): lax.ppermute(values, ('node', 'hid'), [(i, i ^ mask) for i in range(total)])]
    ppermute x4, waiting for transfers between devices: 3.03 us -> 14.8 us  [to_neighbours(): from_previous = lax.ppermute(rows[:, halo_width:], 'node', onward)]
    ppermute x47 -> x37, starting transfers between devices: 48.1 us -> 39.6 us  [exchange(): lax.ppermute(values, ('node', 'hid'), [(i, i ^ mask) for i in range(total)])]
    ppermute x9, waiting for transfers between devices: 13.7 us -> 6.46 us  [swap(): lax.ppermute(values, axis, [(i, i ^ offset) for i in range(lax.axis_size(...]
    unnamed x144 -> x129, local copies, waits for them, and re-layouts: 9.67 us -> 9.73 us
  transfers between devices with their start and end apart: 64 -> 54, of which waited for: 26 -> 29; matrix products, arithmetic and copies ran while one was open for 13% -> 13% of each run, Pallas kernels for 20% -> 26%
where the time goes in v4:
time: 278 us; the launch traced here: 277 us
  Pallas kernels  88.8 us (32%)
  starting transfers between devices  64.6 us (23%)
  waiting for transfers between devices  61 us (22%)
  local copies, waits for them, and re-layouts  30.1 us (11%)
  other arithmetic  28.3 us (10%)
    pallas_call x9, Pallas kernels, run_kernel(): pl.pallas_call(kernel, name=name, grid=(samples,), in_specs=in_specs, out...  88.8 us
    ppermute x37, starting transfers between devices, exchange(): lax.ppermute(values, ('node', 'hid'), [(i, i ^ mask) for i in range(total)])  39.6 us
    ppermute x37, waiting for transfers between devices, exchange(): lax.ppermute(values, ('node', 'hid'), [(i, i ^ mask) for i in range(total)])  37.4 us
    ppermute x4, starting transfers between devices, to_neighbours(): from_next = lax.ppermute(rows[:, :halo_width], 'node', back)  16.6 us
    ppermute x4, waiting for transfers between devices, to_neighbours(): from_previous = lax.ppermute(rows[:, halo_width:], 'node', onward)  14.8 us
    unnamed x129, local copies, waits for them, and re-layouts  9.73 us
    ppermute x9, waiting for transfers between devices, swap(): lax.ppermute(values, axis, [(i, i ^ offset) for i in range(lax.axis_size(...  6.46 us
    ppermute x9, starting transfers between devices, swap(): lax.ppermute(values, axis, [(i, i ^ offset) for i in range(lax.axis_size(...  5.88 us
  transfers between devices with their start and end apart: 54, of which 29 were waited for; matrix products, arithmetic and copies ran while one was open for 13% of the time, Pallas kernels for 26%

profile of v4, /device:TPU:0, one launch (start us, length us, event | category | flops | bytes accessed | tf_op | source)
XLA Modules:
  0.0 277.2 jit_solution(14907769251792911802)
XLA Ops:
  3.5 5.1 %collective-permute-start.2 = (bf16[1,448,128]{2,1,0:T(8,128)(2,1)S(1)}, bf16[1,448,128]{2,1,0:T(8,128)(2,1)S(1)}, u32[]{:S(2)}, u32[]{:S(2)}) collective-permute-start(bf16[1,448,128]{2,1,0:T(8,128)(2,1)S(1)} %maximum_bitcast_fusion), channel_id=1, source_target_pairs={{0,24},{1,25},{2,26},{3,27},{4,28},{5,29},{6,30},{7,31},{8,16},{9,... | collective-permute-start | bytes 344072 | tf_op jit(solution)/shard_map/ppermute | solution.py:572
  15.4 3.0 %collective-permute-done = bf16[1,448,128]{2,1,0:T(8,128)(2,1)S(1)} collective-permute-done((bf16[1,448,128]{2,1,0:T(8,128)(2,1)S(1)}, bf16[1,448,128]{2,1,0:T(8,128)(2,1)S(1)}, u32[]{:S(2)}, u32[]{:S(2)}) %collective-permute-start) | collective-permute-done | bytes 114720 | tf_op jit(solution)/shard_map/ppermute | solution.py:572
  26.3 4.7 %collective-permute-done.3 = bf16[4,448,128]{2,1,0:T(8,128)(2,1)S(1)} collective-permute-done((bf16[4,448,128]{2,1,0:T(8,128)(2,1)}, bf16[4,448,128]{2,1,0:T(8,128)(2,1)S(1)}, u32[]{:S(2)}, u32[]{:S(2)}) %collective-permute-start.3) | collective-permute-done | bytes 458784 | tf_op jit(solution)/shard_map/ppermute | solution.py:572
  37.2 3.2 %collective-permute-start.6 = (bf16[3,40,512]{2,1,0:T(8,128)(2,1)S(1)}, bf16[3,40,512]{2,1,0:T(8,128)(2,1)S(1)}, u32[]{:S(2)}, u32[]{:S(2)}) collective-permute-start(bf16[3,40,512]{2,1,0:T(8,128)(2,1)S(1)} %get-tuple-element.392), channel_id=1, source_target_pairs={{4,0},{8,4},{12,8},{16,12},{20,16},{24,20},{28,24},{0,28},{5,1},{9... | collective-permute-start | bytes 368648 | tf_op jit(solution)/shard_map/ppermute | solution.py:628
  42.5 2.1 collective-permute-done.5
  45.8 3.6 %collective-permute-done.9 = bf16[1,448,128]{2,1,0:T(8,128)(2,1)S(1)} collective-permute-done((bf16[1,448,128]{2,1,0:T(8,128)(2,1)}, bf16[1,448,128]{2,1,0:T(8,128)(2,1)S(1)}, u32[]{:S(2)}, u32[]{:S(2)}) %collective-permute-start.9) | collective-permute-done | bytes 114720 | tf_op jit(solution)/shard_map/ppermute | solution.py:572
  59.2 11.6 %edge_forward.2 = (bf16[3,640,512]{2,1,0:T(8,128)(2,1)}, bf16[3,640,512]{2,1,0:T(8,128)(2,1)}, bf16[3,640,512]{2,1,0:T(8,128)(2,1)}, f32[3,640,1]{2,1,0:T(8,128)...) custom-call(s32[32]{0:T(128)} %add.265.order, ...), custom_call_target="tpu_custom_call" | custom-call | flops 15225323520 | bytes 19271296 | tf_op jit(solution)/shard_map/edge_forward/pallas_call | solution.py:124
  75.9 5.0 %node_pass.2 = (bf16[480,512]{1,0:T(8,128)(2,1)}, bf16[480,512]{1,0:T(8,128)(2,1)}, bf16[480,512]{1,0:T(8,128)(2,1)}, bf16[480,512]{1,0:T(8,128)(2,1)}, f32[480,...) custom-call(s32[32]{0:T(128)} %add.265.order, ...), custom_call_target="tpu_custom_call" | custom-call | flops 3019898880 | bytes 7269376 | tf_op jit(solution)/shard_map/node_pass/pallas_call | solution.py:124
  82.5 4.2 %collective-permute-start.17 = (bf16[3,40,512]{2,1,0:T(8,128)(2,1)S(1)}, bf16[3,40,512]{2,1,0:T(8,128)(2,1)S(1)}, u32[]{:S(2)}, u32[]{:S(2)}) collective-permute-start(bf16[3,40,512]{2,1,0:T(8,128)(2,1)S(1)} %get-tuple-element.390), channel_id=1, source_target_pairs={{4,0},{8,4},{12,8},{16,12},{20,16},{24,20},{28,24},{0,28},{5,1},{9... | collective-permute-start | bytes 368648 | tf_op jit(solution)/shard_map/ppermute | solution.py:628
  86.8 3.4 %collective-permute-done.16 = bf16[3,40,512]{2,1,0:T(8,128)(2,1)S(1)} collective-permute-done((bf16[3,40,512]{2,1,0:T(8,128)(2,1)S(1)}, bf16[3,40,512]{2,1,0:T(8,128)(2,1)S(1)}, u32[]{:S(2)}, u32[]{:S(2)}) %collective-permute-start.16) | collective-permute-done | bytes 122912 | tf_op jit(solution)/shard_map/ppermute | solution.py:627
  92.8 3.6 %collective-permute-done.22 = bf16[40,3,512]{2,0,1:T(8,128)(2,1)S(1)} collective-permute-done((bf16[40,3,512]{2,0,1:T(8,128)(2,1)S(1)}, bf16[40,3,512]{2,0,1:T(8,128)(2,1)S(1)}, u32[]{:S(2)}, u32[]{:S(2)}) %collective-permute-start.22) | collective-permute-done | bytes 122912 | tf_op jit(solution)/shard_map/ppermute | solution.py:509
  99.7 10.9 %edge_forward.3 = (bf16[3,640,512]{2,1,0:T(8,128)(2,1)}, bf16[3,640,512]{2,1,0:T(8,128)(2,1)}, bf16[3,640,512]{2,1,0:T(8,128)(2,1)}, f32[3,640,1]{2,1,0:T(8,128)}, bf16[3,160,512]{2,1,0:T(8,128)(2,1)}) custom-call(s32[32]{0:T(128)} %add.265.order, bf16[32,256,128]{2,1,0:T(8,128)(2,1)} %pad_maximum_fusion.1.w1.w2, ...), custom_call_target="tpu_custom_call" | custom-call | flops 15225323520 | bytes 17960576 | tf_op jit(solution)/shard_map/edge_forward/pallas_call | solution.py:124
  116.4 8.2 %node_pass.3 = (bf16[3,160,512]{2,1,0:T(8,128)(2,1)}, bf16[3,160,512]{2,1,0:T(8,128)(2,1)}, f32[3,160,512]{2,1,0:T(8,128)}, bf16[16,192,128]{2,1,0:T(8,128)(2,1)...) custom-call(s32[32]{0:T(128)} %add.265.order, s32[64]{0:T(128)} %reshape.331.rest_0_.owners, ...), custom_call_target="tpu_custom_call" | custom-call | flops 9059696640 | bytes 8087820 | tf_op jit(solution)/shard_map/node_pass/pallas_call | solution.py:124
  126.2 12.7 %edge_backward.2 = (bf16[3,640,512]{2,1,0:T(8,128)(2,1)}, bf16[3,640,512]{2,1,0:T(8,128)(2,1)}, bf16[3,400,512]{2,1,0:T(8,128)(2,1)}, f32[3,160,512]{2,1,0:T(8,1...) custom-call(s32[32]{0:T(128)} %add.265.order, ...), custom_call_target="tpu_custom_call" | custom-call | flops 14344519680 | bytes 19674752 | tf_op jit(solution)/shard_map/edge_backward/pallas_call | solution.py:124
  140.2 4.5 %collective-permute-start.26 = (bf16[3,40,512]{2,1,0:T(8,128)(2,1)S(1)}, bf16[3,40,512]{2,1,0:T(8,128)(2,1)S(1)}, u32[]{:S(2)}, u32[]{:S(2)}) collective-permute-start(bf16[3,40,512]{2,1,0:T(8,128)(2,1)S(1)} %get-tuple-element.386), channel_id=1, source_target_pairs={{4,0},{8,4},{12,8},{16,12},{20,16},{24,20},{28,24},{0,28},{5,1},{9... | collective-permute-start | bytes 368648 | tf_op jit(solution)/shard_map/ppermute | solution.py:628
  144.6 9.9 %edge_weight_grads.2 = (bf16[16,448,128]{2,1,0:T(8,128)(2,1)}, bf16[16,448,128]{2,1,0:T(8,128)(2,1)}) custom-call(s32[64]{0:T(128)} %reshape.331.rest_0_.owners, bf16[3,640,512]{2,1,0:T(8,128)(2,1)} %get-tuple-element.170.low.edge_low, bf16[3,240,512]{2,1,0:T(8,128)(2,1)} %copy-done.25, bf16[3,640,512]{2,1,0:T(8,128)(2,1)} %get-tuple-element.187.hidden_low, ...), custom_call_target="tpu_custom_call" | custom-call | flops 8053063680 | bytes 15073536 | tf_op jit(solution)/shard_map/edge_weight_grads/pallas_call | solution.py:124
  161.8 7.8 %node_backward.1 = (bf16[3,160,512]{2,1,0:T(8,128)(2,1)}, f32[3,160,512]{2,1,0:T(8,128)}, bf16[16,192,128]{2,1,0:T(8,128)(2,1)}, bf16[16,192,128]{2,1,0:T(8,128)(2,1)}, f32[4,512]{1,0:T(4,128)}) custom-call(s32[32]{0:T(128)} %add.265.order, s32[64]{0:T(128)} %reshape.331.rest_0_.owners, bf16[32,192,128]{2,1,0:T(8,128)(2,1)} %copy-done.40, ...), custom_call_target="tpu_custom_call" | custom-call | flops 6039797760 | bytes 9564288 | tf_op jit(solution)/shard_map/node_backward/pallas_call | solution.py:124
  171.3 14.3 %edge_backward.3 = (bf16[3,640,512]{2,1,0:T(8,128)(2,1)}, bf16[3,640,512]{2,1,0:T(8,128)(2,1)}, bf16[3,400,512]{2,1,0:T(8,128)(2,1)}, f32[3,160,512]{2,1,0:T(8,1...) custom-call(s32[32]{0:T(128)} %add.265.order, ...), custom_call_target="tpu_custom_call" | custom-call | flops 14344519680 | bytes 21640832 | tf_op jit(solution)/shard_map/edge_backward/pallas_call | solution.py:124
  186.5 6.5 %collective-permute-done.29 = bf16[8,448,128]{2,1,0:T(8,128)(2,1)S(1)} collective-permute-done((bf16[8,448,128]{2,1,0:T(8,128)(2,1)S(1)}, bf16[8,448,128]{2,1,0:T(8,128)(2,1)S(1)}, u32[]{:S(2)}, u32[]{:S(2)}) %collective-permute-start.29) | collective-permute-done | bytes 917536 | tf_op jit(solution)/shard_map/ppermute | solution.py:572
  193.3 8.3 %edge_weight_grads.3 = (bf16[16,256,128]{2,1,0:T(8,128)(2,1)}, bf16[16,256,128]{2,1,0:T(8,128)(2,1)}) custom-call(s32[64]{0:T(128)} %reshape.331.rest_0_.owners, bf16[640,512]{1,0:T(8,128)(2,1)} %bitcast.167, bf16[3,240,512]{2,1,0:T(8,128)(2,1)} %pad_maximum_fusion.8.table, bf16[640,512]{1,0:T(8,128)(2,1)} %get-tuple-element.209.hidden_low, ...), custom_call_target="tpu_custom_call" | custom-call | flops 8053063680 | bytes 9306368 | tf_op jit(solution)/shard_map/edge_weight_grads/pallas_call | solution.py:124
  204.6 2.2 collective-permute-done.32
  208.7 4.7 %collective-permute-start.36 = (bf16[3,40,512]{2,1,0:T(8,128)(2,1)S(1)}, bf16[3,40,512]{2,1,0:T(8,128)(2,1)S(1)}, u32[]{:S(2)}, u32[]{:S(2)}) collective-permute-start(bf16[3,40,512]{2,1,0:T(8,128)(2,1)S(1)} %get-tuple-element.384), channel_id=1, source_target_pairs={{4,0},{8,4},{12,8},{16,12},{20,16},{24,20},{28,24},{0,28},{5,1},{9... | collective-permute-start | bytes 368648 | tf_op jit(solution)/shard_map/ppermute | solution.py:628
  215.7 9.3 %collective-permute-done.35 = bf16[3,40,512]{2,1,0:T(8,128)(2,1)S(1)} collective-permute-done((bf16[3,40,512]{2,1,0:T(8,128)(2,1)S(1)}, bf16[3,40,512]{2,1,0:T(8,128)(2,1)S(1)}, u32[]{:S(2)}, u32[]{:S(2)}) %collective-permute-start.35) | collective-permute-done | bytes 122912 | tf_op jit(solution)/shard_map/ppermute | solution.py:627
  225.0 2.2 collective-permute-done.36
  230.0 2.4 collective-permute-start.40
  232.4 1.9 collective-permute-start.41
  236.7 3.8 %collective-permute-done.39 = bf16[1,640,128]{2,1,0:T(8,128)(2,1)S(1)} collective-permute-done((bf16[1,640,128]{2,1,0:T(8,128)(2,1)S(1)}, bf16[1,640,128]{2,1,0:T(8,128)(2,1)S(1)}, u32[]{:S(2)}, u32[]{:S(2)}) %collective-permute-start.39) | collective-permute-done | bytes 163872 | tf_op jit(solution)/shard_map/ppermute | solution.py:572
  243.9 4.4 %collective-permute-start.42 = (bf16[1,256,128]{2,1,0:T(8,128)(2,1)S(1)}, bf16[1,256,128]{2,1,0:T(8,128)(2,1)S(1)}, u32[]{:S(2)}, u32[]{:S(2)}) collective-permute-start(bf16[1,256,128]{2,1,0:T(8,128)(2,1)S(1)} %get-tuple-element.378), channel_id=1, source_target_pairs={{0,16},{1,17},{2,18},{3,19},{4,20},{5,21},{6,22},{7,23},{8,24},{9,... | collective-permute-start | bytes 196616 | tf_op jit(solution)/shard_map/ppermute | solution.py:572
  248.2 1.9 collective-permute-start.44
  250.2 3.0 %collective-permute-done.42 = bf16[1,256,128]{2,1,0:T(8,128)(2,1)S(1)} collective-permute-done((bf16[1,256,128]{2,1,0:T(8,128)(2,1)S(1)}, bf16[1,256,128]{2,1,0:T(8,128)(2,1)S(1)}, u32[]{:S(2)}, u32[]{:S(2)}) %collective-permute-start.42) | collective-permute-done | bytes 65568 | tf_op jit(solution)/shard_map/ppermute | solution.py:572
  264.0 2.0 collective-permute-start.53
  266.0 2.5 collective-permute-start.51
  (364 shorter events, 101.5 us)
Async XLA Ops:
  3.5 11.6 %collective-permute-start.2 = (bf16[1,448,128]{2,1,0:T(8,128)(2,1)S(1)}, bf16[1,448,128]{2,1,0:T(8,128)(2,1)S(1)}, u32[]{:S(2)}, u32[]{:S(2)}) collective-permute-start(bf16[1,448,128]{2,1,0:T(8,128)(2,1)S(1)} %maximum_bitcast_fusion), channel_id=1, source_target_pairs={{0,24},{1,25},{2,26},{3,27},{4,28},{5,29},{6,30},{7,31},{8,16},{9,... | collective-permute-start | bytes 344072 | tf_op jit(solution)/shard_map/ppermute | solution.py:572
  8.7 9.7 %collective-permute-start = (bf16[1,448,128]{2,1,0:T(8,128)(2,1)S(1)}, bf16[1,448,128]{2,1,0:T(8,128)(2,1)S(1)}, u32[]{:S(2)}, u32[]{:S(2)}) collective-permute-start(bf16[1,448,128]{2,1,0:T(8,128)(2,1)S(1)} %maximum_bitcast_fusion), channel_id=1, source_target_pairs={{0,16},{1,17},{2,18},{3,19},{4,20},{5,21},{6,22},{7,23},{8,24},{9,... | collective-permute-start | bytes 344072 | tf_op jit(solution)/shard_map/ppermute | solution.py:572
  19.2 11.8 %collective-permute-start.3 = (bf16[4,448,128]{2,1,0:T(8,128)(2,1)}, bf16[4,448,128]{2,1,0:T(8,128)(2,1)S(1)}, u32[]{:S(2)}, u32[]{:S(2)}) collective-permute-start(bf16[4,448,128]{2,1,0:T(8,128)(2,1)} %pad_maximum_fusion.13), channel_id=1, source_target_pairs={{0,4},{1,5},{2,6},{3,7},{4,0},{5,1},{6,2},{7,3},{8,12},{9,13},{10,... | collective-permute-start | bytes 1376264 | tf_op jit(solution)/shard_map/ppermute | solution.py:572
  32.9 17.7 %collective-permute-start.4 = (bf16[8,256,128]{2,1,0:T(8,128)(2,1)S(1)}, bf16[8,256,128]{2,1,0:T(8,128)(2,1)S(1)}, u32[]{:S(2)}, u32[]{:S(2)}) collective-permute-start(bf16[8,256,128]{2,1,0:T(8,128)(2,1)S(1)} %slice.292), channel_id=1, source_target_pairs={{0,2},{1,3},{2,0},{3,1},{4,6},{5,7},{6,4},{7,5},{8,10},{9,11},{10,... | collective-permute-start | bytes 1572872 | tf_op jit(solution)/shard_map/ppermute | solution.py:572
  35.7 8.9 %collective-permute-start.5 = (bf16[3,40,512]{2,1,0:T(8,128)(2,1)S(1)}, bf16[3,40,512]{2,1,0:T(8,128)(2,1)S(1)}, u32[]{:S(2)}, u32[]{:S(2)}) collective-permute-start(bf16[3,40,512]{2,1,0:T(8,128)(2,1)S(1)} %get-tuple-element.391), channel_id=1, source_target_pairs={{0,4},{4,8},{8,12},{12,16},{16,20},{20,24},{24,28},{28,0},{1,5},{5... | collective-permute-start | bytes 368648 | tf_op jit(solution)/shard_map/ppermute | solution.py:627
  37.2 8.5 %collective-permute-start.6 = (bf16[3,40,512]{2,1,0:T(8,128)(2,1)S(1)}, bf16[3,40,512]{2,1,0:T(8,128)(2,1)S(1)}, u32[]{:S(2)}, u32[]{:S(2)}) collective-permute-start(bf16[3,40,512]{2,1,0:T(8,128)(2,1)S(1)} %get-tuple-element.392), channel_id=1, source_target_pairs={{4,0},{8,4},{12,8},{16,12},{20,16},{24,20},{28,24},{0,28},{5,1},{9... | collective-permute-start | bytes 368648 | tf_op jit(solution)/shard_map/ppermute | solution.py:628
  41.3 8.0 %collective-permute-start.9 = (bf16[1,448,128]{2,1,0:T(8,128)(2,1)}, bf16[1,448,128]{2,1,0:T(8,128)(2,1)S(1)}, u32[]{:S(2)}, u32[]{:S(2)}) collective-permute-start(bf16[1,448,128]{2,1,0:T(8,128)(2,1)} %maximum_bitcast_fusion.1), channel_id=1, source_target_pairs={{0,24},{1,25},{2,26},{3,27},{4,28},{5,29},{6,30},{7,31},{8,16},{9,... | collective-permute-start | bytes 344072 | tf_op jit(solution)/shard_map/ppermute | solution.py:572
  50.7 6.9 %collective-permute-start.10 = (bf16[16,256,128]{2,1,0:T(8,128)(2,1)S(1)}, bf16[16,256,128]{2,1,0:T(8,128)(2,1)S(1)}, u32[]{:S(2)}, u32[]{:S(2)}) collective-permute-start(bf16[16,256,128]{2,1,0:T(8,128)(2,1)S(1)} %pad_maximum_fusion.4), channel_id=1, source_target_pairs={{0,1},{1,0},{2,3},{3,2},{4,5},{5,4},{6,7},{7,6},{8,9},{9,8},{10,11... | collective-permute-start | bytes 3145736 | tf_op jit(solution)/shard_map/ppermute | solution.py:572
  54.6 16.2 %collective-permute-start.12 = (bf16[4,448,128]{2,1,0:T(8,128)(2,1)S(1)}, bf16[4,448,128]{2,1,0:T(8,128)(2,1)S(1)}, u32[]{:S(2)}, u32[]{:S(2)}) collective-permute-start(bf16[4,448,128]{2,1,0:T(8,128)(2,1)S(1)} %pad_maximum_fusion.14), channel_id=1, source_target_pairs={{0,4},{1,5},{2,6},{3,7},{4,0},{5,1},{6,2},{7,3},{8,12},{9,13},{10,... | collective-permute-start | bytes 1376264 | tf_op jit(solution)/shard_map/ppermute | solution.py:572
  56.2 14.6 %collective-permute-start.11 = (bf16[8,192,128]{2,1,0:T(8,128)(2,1)S(1)}, bf16[8,192,128]{2,1,0:T(8,128)(2,1)S(1)}, u32[]{:S(2)}, u32[]{:S(2)}) collective-permute-start(bf16[8,192,128]{2,1,0:T(8,128)(2,1)S(1)} %slice.293), channel_id=1, source_target_pairs={{0,2},{1,3},{2,0},{3,1},{4,6},{5,7},{6,4},{7,5},{8,10},{9,11},{10,... | collective-permute-start | bytes 1179656 | tf_op jit(solution)/shard_map/ppermute | solution.py:572
  72.0 18.3 %collective-permute-start.13 = (bf16[8,256,128]{2,1,0:T(8,128)(2,1)S(1)}, bf16[8,256,128]{2,1,0:T(8,128)(2,1)S(1)}, u32[]{:S(2)}, u32[]{:S(2)}) collective-permute-start(bf16[8,256,128]{2,1,0:T(8,128)(2,1)S(1)} %slice.294), channel_id=1, source_target_pairs={{0,2},{1,3},{2,0},{3,1},{4,6},{5,7},{6,4},{7,5},{8,10},{9,11},{10,... | collective-permute-start | bytes 1572872 | tf_op jit(solution)/shard_map/ppermute | solution.py:572
  82.0 8.2 %collective-permute-start.16 = (bf16[3,40,512]{2,1,0:T(8,128)(2,1)S(1)}, bf16[3,40,512]{2,1,0:T(8,128)(2,1)S(1)}, u32[]{:S(2)}, u32[]{:S(2)}) collective-permute-start(bf16[3,40,512]{2,1,0:T(8,128)(2,1)S(1)} %get-tuple-element.389), channel_id=1, source_target_pairs={{0,4},{4,8},{8,12},{12,16},{16,20},{20,24},{24,28},{28,0},{1,5},{5... | collective-permute-start | bytes 368648 | tf_op jit(solution)/shard_map/ppermute | solution.py:627
  82.5 7.7 %collective-permute-start.17 = (bf16[3,40,512]{2,1,0:T(8,128)(2,1)S(1)}, bf16[3,40,512]{2,1,0:T(8,128)(2,1)S(1)}, u32[]{:S(2)}, u32[]{:S(2)}) collective-permute-start(bf16[3,40,512]{2,1,0:T(8,128)(2,1)S(1)} %get-tuple-element.390), channel_id=1, source_target_pairs={{4,0},{8,4},{12,8},{16,12},{20,16},{24,20},{28,24},{0,28},{5,1},{9... | collective-permute-start | bytes 368648 | tf_op jit(solution)/shard_map/ppermute | solution.py:628
  90.4 7.7 %collective-permute-start.18 = (bf16[16,256,128]{2,1,0:T(8,128)(2,1)S(1)}, bf16[16,256,128]{2,1,0:T(8,128)(2,1)S(1)}, u32[]{:S(2)}, u32[]{:S(2)}) collective-permute-start(bf16[16,256,128]{2,1,0:T(8,128)(2,1)S(1)} %pad_maximum_fusion.5), channel_id=1, source_target_pairs={{0,1},{1,0},{2,3},{3,2},{4,5},{5,4},{6,7},{7,6},{8,9},{9,8},{10,11... | collective-permute-start | bytes 3145736 | tf_op jit(solution)/shard_map/ppermute | solution.py:572
  96.5 14.1 %collective-permute-start.19 = (bf16[8,192,128]{2,1,0:T(8,128)(2,1)S(1)}, bf16[8,192,128]{2,1,0:T(8,128)(2,1)S(1)}, u32[]{:S(2)}, u32[]{:S(2)}) collective-permute-start(bf16[8,192,128]{2,1,0:T(8,128)(2,1)S(1)} %slice.295), channel_id=1, source_target_pairs={{0,2},{1,3},{2,0},{3,1},{4,6},{5,7},{6,4},{7,5},{8,10},{9,11},{10,... | collective-permute-start | bytes 1179656 | tf_op jit(solution)/shard_map/ppermute | solution.py:572
  125.6 19.0 %collective-permute-start.24 = (bf16[40,3,512]{2,0,1:T(8,128)(2,1)S(1)}, bf16[40,3,512]{2,0,1:T(8,128)(2,1)S(1)}, u32[]{:S(2)}, u32[]{:S(2)}) collective-permute-start(bf16[40,3,512]{2,0,1:T(8,128)(2,1)S(1)} %get-tuple-element.367), channel_id=1, source_target_pairs={{0,2},{1,3},{2,0},{3,1},{4,6},{5,7},{6,4},{7,5},{8,10},{9,11},{10,... | collective-permute-start | bytes 368648 | tf_op jit(solution)/shard_map/ppermute | solution.py:509
  139.9 14.7 %collective-permute-start.25 = (bf16[3,40,512]{2,1,0:T(8,128)(2,1)S(1)}, bf16[3,40,512]{2,1,0:T(8,128)(2,1)S(1)}, u32[]{:S(2)}, u32[]{:S(2)}) collective-permute-start(bf16[3,40,512]{2,1,0:T(8,128)(2,1)S(1)} %get-tuple-element.385), channel_id=1, source_target_pairs={{0,4},{4,8},{8,12},{12,16},{16,20},{20,24},{24,28},{28,0},{1,5},{5... | collective-permute-start | bytes 368648 | tf_op jit(solution)/shard_map/ppermute | solution.py:627
  140.2 14.4 %collective-permute-start.26 = (bf16[3,40,512]{2,1,0:T(8,128)(2,1)S(1)}, bf16[3,40,512]{2,1,0:T(8,128)(2,1)S(1)}, u32[]{:S(2)}, u32[]{:S(2)}) collective-permute-start(bf16[3,40,512]{2,1,0:T(8,128)(2,1)S(1)} %get-tuple-element.386), channel_id=1, source_target_pairs={{4,0},{8,4},{12,8},{16,12},{20,16},{24,20},{28,24},{0,28},{5,1},{9... | collective-permute-start | bytes 368648 | tf_op jit(solution)/shard_map/ppermute | solution.py:628
  169.6 16.0 %collective-permute-start.30 = (bf16[16,192,128]{2,1,0:T(8,128)(2,1)}, bf16[16,192,128]{2,1,0:T(8,128)(2,1)S(1)}, u32[]{:S(2)}, u32[]{:S(2)}) collective-permute-start(bf16[16,192,128]{2,1,0:T(8,128)(2,1)} %get-tuple-element.216), channel_id=1, source_target_pairs={{0,1},{1,0},{2,3},{3,2},{4,5},{5,4},{6,7},{7,6},{8,9},{9,8},{10,11... | collective-permute-start | bytes 2359304 | tf_op jit(solution)/shard_map/ppermute | solution.py:572
  169.8 23.2 %collective-permute-start.29 = (bf16[8,448,128]{2,1,0:T(8,128)(2,1)S(1)}, bf16[8,448,128]{2,1,0:T(8,128)(2,1)S(1)}, u32[]{:S(2)}, u32[]{:S(2)}) collective-permute-start(bf16[8,448,128]{2,1,0:T(8,128)(2,1)S(1)} %slice.398), channel_id=1, source_target_pairs={{0,2},{1,3},{2,0},{3,1},{4,6},{5,7},{6,4},{7,5},{8,10},{9,11},{10,... | collective-permute-start | bytes 2752520 | tf_op jit(solution)/shard_map/ppermute | solution.py:572
  185.9 15.7 %collective-permute-start.31 = (bf16[8,192,128]{2,1,0:T(8,128)(2,1)S(1)}, bf16[8,192,128]{2,1,0:T(8,128)(2,1)S(1)}, u32[]{:S(2)}, u32[]{:S(2)}) collective-permute-start(bf16[8,192,128]{2,1,0:T(8,128)(2,1)S(1)} %slice.401), channel_id=1, source_target_pairs={{0,2},{1,3},{2,0},{3,1},{4,6},{5,7},{6,4},{7,5},{8,10},{9,11},{10,... | collective-permute-start | bytes 1179656 | tf_op jit(solution)/shard_map/ppermute | solution.py:572
  204.6 22.6 %collective-permute-start.34 = (bf16[4,640,128]{2,1,0:T(8,128)(2,1)}, bf16[4,640,128]{2,1,0:T(8,128)(2,1)S(1)}, u32[]{:S(2)}, u32[]{:S(2)}) collective-permute-start(bf16[4,640,128]{2,1,0:T(8,128)(2,1)} %pad_maximum_fusion.10), channel_id=1, source_target_pairs={{0,4},{1,5},{2,6},{3,7},{4,0},{5,1},{6,2},{7,3},{8,12},{9,13},{10,... | collective-permute-start | bytes 1966088 | tf_op jit(solution)/shard_map/ppermute | solution.py:572
  208.7 16.3 %collective-permute-start.35 = (bf16[3,40,512]{2,1,0:T(8,128)(2,1)S(1)}, bf16[3,40,512]{2,1,0:T(8,128)(2,1)S(1)}, u32[]{:S(2)}, u32[]{:S(2)}) collective-permute-start(bf16[3,40,512]{2,1,0:T(8,128)(2,1)S(1)} %get-tuple-element.383), channel_id=1, source_target_pairs={{0,4},{4,8},{8,12},{12,16},{16,20},{20,24},{24,28},{28,0},{1,5},{5... | collective-permute-start | bytes 368648 | tf_op jit(solution)/shard_map/ppermute | solution.py:627
  208.7 18.4 %collective-permute-start.36 = (bf16[3,40,512]{2,1,0:T(8,128)(2,1)S(1)}, bf16[3,40,512]{2,1,0:T(8,128)(2,1)S(1)}, u32[]{:S(2)}, u32[]{:S(2)}) collective-permute-start(bf16[3,40,512]{2,1,0:T(8,128)(2,1)S(1)} %get-tuple-element.384), channel_id=1, source_target_pairs={{4,0},{8,4},{12,8},{16,12},{20,16},{24,20},{28,24},{0,28},{5,1},{9... | collective-permute-start | bytes 368648 | tf_op jit(solution)/shard_map/ppermute | solution.py:628
  214.2 14.1 %collective-permute-start.33 = (bf16[8,256,128]{2,1,0:T(8,128)(2,1)S(1)}, bf16[8,256,128]{2,1,0:T(8,128)(2,1)S(1)}, u32[]{:S(2)}, u32[]{:S(2)}) collective-permute-start(bf16[8,256,128]{2,1,0:T(8,128)(2,1)S(1)} %slice.399), channel_id=1, source_target_pairs={{0,2},{1,3},{2,0},{3,1},{4,6},{5,7},{6,4},{7,5},{8,10},{9,11},{10,... | collective-permute-start | bytes 1572872 | tf_op jit(solution)/shard_map/ppermute | solution.py:572
  229.9 10.7 %collective-permute-start.39 = (bf16[1,640,128]{2,1,0:T(8,128)(2,1)S(1)}, bf16[1,640,128]{2,1,0:T(8,128)(2,1)S(1)}, u32[]{:S(2)}, u32[]{:S(2)}) collective-permute-start(bf16[1,640,128]{2,1,0:T(8,128)(2,1)S(1)} %get-tuple-element.234), channel_id=1, source_target_pairs={{0,16},{1,17},{2,18},{3,19},{4,20},{5,21},{6,22},{7,23},{8,24},{9,... | collective-permute-start | bytes 491528 | tf_op jit(solution)/shard_map/ppermute | solution.py:572
  230.0 13.7 %collective-permute-start.40 = (bf16[1,640,128]{2,1,0:T(8,128)(2,1)S(1)}, bf16[1,640,128]{2,1,0:T(8,128)(2,1)S(1)}, u32[]{:S(2)}, u32[]{:S(2)}) collective-permute-start(bf16[1,640,128]{2,1,0:T(8,128)(2,1)S(1)} %get-tuple-element.235), channel_id=1, source_target_pairs={{0,8},{1,9},{2,10},{3,11},{4,12},{5,13},{6,14},{7,15},{8,0},{9,1},... | collective-permute-start | bytes 491528 | tf_op jit(solution)/shard_map/ppermute | solution.py:572
  232.4 11.2 %collective-permute-start.41 = (bf16[1,640,128]{2,1,0:T(8,128)(2,1)S(1)}, bf16[1,640,128]{2,1,0:T(8,128)(2,1)S(1)}, u32[]{:S(2)}, u32[]{:S(2)}) collective-permute-start(bf16[1,640,128]{2,1,0:T(8,128)(2,1)S(1)} %get-tuple-element.236), channel_id=1, source_target_pairs={{0,24},{1,25},{2,26},{3,27},{4,28},{5,29},{6,30},{7,31},{8,16},{9,... | collective-permute-start | bytes 491528 | tf_op jit(solution)/shard_map/ppermute | solution.py:572
  234.4 9.3 %collective-permute-start.38 = (bf16[4,256,128]{2,1,0:T(8,128)(2,1)S(1)}, bf16[4,256,128]{2,1,0:T(8,128)(2,1)S(1)}, u32[]{:S(2)}, u32[]{:S(2)}) collective-permute-start(bf16[4,256,128]{2,1,0:T(8,128)(2,1)S(1)} %slice.402), channel_id=1, source_target_pairs={{0,4},{1,5},{2,6},{3,7},{4,0},{5,1},{6,2},{7,3},{8,12},{9,13},{10,... | collective-permute-start | bytes 786440 | tf_op jit(solution)/shard_map/ppermute | solution.py:572
  235.1 20.1 %collective-permute-start.46 = (bf16[40,3,512]{2,0,1:T(8,128)(2,1)S(1)}, bf16[40,3,512]{2,0,1:T(8,128)(2,1)S(1)}, u32[]{:S(2)}, u32[]{:S(2)}) collective-permute-start(bf16[40,3,512]{2,0,1:T(8,128)(2,1)S(1)} %get-tuple-element.365), channel_id=1, source_target_pairs={{0,2},{1,3},{2,0},{3,1},{4,6},{5,7},{6,4},{7,5},{8,10},{9,11},{10,... | collective-permute-start | bytes 368648 | tf_op jit(solution)/shard_map/ppermute | solution.py:509
  240.6 14.6 %collective-permute-start.45 = (bf16[320,512]{1,0:T(8,128)(2,1)S(1)}, bf16[320,512]{1,0:T(8,128)(2,1)S(1)}, u32[]{:S(2)}, u32[]{:S(2)}) collective-permute-start(bf16[320,512]{1,0:T(8,128)(2,1)S(1)} %fusion.6), channel_id=1, source_target_pairs={{0,2},{1,3},{2,0},{3,1},{4,6},{5,7},{6,4},{7,5},{8,10},{9,11},{10,... | collective-permute-start | bytes 983048 | tf_op jit(solution)/shard_map/ppermute | solution.py:509
  243.9 9.4 %collective-permute-start.42 = (bf16[1,256,128]{2,1,0:T(8,128)(2,1)S(1)}, bf16[1,256,128]{2,1,0:T(8,128)(2,1)S(1)}, u32[]{:S(2)}, u32[]{:S(2)}) collective-permute-start(bf16[1,256,128]{2,1,0:T(8,128)(2,1)S(1)} %get-tuple-element.378), channel_id=1, source_target_pairs={{0,16},{1,17},{2,18},{3,19},{4,20},{5,21},{6,22},{7,23},{8,24},{9,... | collective-permute-start | bytes 196616 | tf_op jit(solution)/shard_map/ppermute | solution.py:572
  (83 other events, 748.8 us)

commit v5 on v4

--- a/solution.py
+++ b/solution.py
@@ -31,7 +31,7 @@
 
 
 def sigmoid(values):
-    return 1.0 / (1.0 + jnp.exp(-values))
+    return 0.5 + 0.5 * jnp.tanh(0.5 * values)
 
 
 def silu_slope(values):
@@ -620,13 +620,22 @@
     return values
 
 
-def to_neighbours(rows, halo_width):
+def neighbour_swaps(rows, halo_width):
     count = lax.axis_size("node")
-    onward = [(i, (i + 1) % count) for i in range(count)]
-    back = [(target, source) for source, target in onward]
-    from_previous = lax.ppermute(rows[:, halo_width:], "node", onward)
-    from_next = lax.ppermute(rows[:, :halo_width], "node", back)
-    return jnp.concatenate([from_previous, from_next], axis=1)
+    even = lax.axis_index("node") % 2 == 0
+    to_previous, to_next = rows[:, :halo_width], rows[:, halo_width:]
+    one = [(i, i ^ 1) for i in range(count)]
+    two = [(i, (((i + 1) ^ 1) - 1) % count) for i in range(count)]
+    first = lax.ppermute(jnp.where(even, to_next, to_previous), "node", one)
+    second = lax.ppermute(jnp.where(even, to_previous, to_next), "node", two)
+    return first, second
+
+
+def from_neighbours(first, second):
+    even = lax.axis_index("node") % 2 == 0
+    return jnp.concatenate(
+        [jnp.where(even, second, first), jnp.where(even, first, second)], axis=1
+    )
 
 
 def adam_terms(weight, grad, first, second, decay):
@@ -765,12 +774,13 @@
     edge_in_own = own_edges(edge_in)
     halo_rows = dot("hn,snl->shl", at_halo, node_low).astype(BF16)
     node_low_zero = node_low
-    halo_rows = to_neighbours(after(halo_rows, halo_gate), halo_width)
+    halo_rows = neighbour_swaps(after(halo_rows, halo_gate), halo_width)
     begin, end = z_rounds[-1]
     arrived = [exchange(layer_one, begin, flips) for flips in range(1, 1 << (end - begin))]
-    edge_arrived, halo_rows, weight_local, *arrived = lax.optimization_barrier(
-        (exchange(edge_zero, steps - 2, 1), halo_rows, weight_local, *arrived)
-    )
+    edge_arrived, first, second, weight_local, *arrived = lax.optimization_barrier(
+        (exchange(edge_zero, steps - 2, 1), *halo_rows, weight_local, *arrived)
+    )
+    halo_rows = from_neighbours(first, second)
     edge_zero = jnp.concatenate([edge_zero, edge_arrived], axis=0)
     layer_one = jnp.concatenate([layer_one, *arrived], axis=0)
     node_zero = after(node_zero, edge_zero)
@@ -788,9 +798,21 @@
         node_total,
         False,
     )
-    pooled, *arrived = lax.optimization_barrier(
-        (pooled, exchange(node_zero, steps - 2, 1), exchange(layer_one, steps - 3, 1))
-    )
+    valid_mask = (ocean_mask[:, None] * present_mask).astype(BF16)
+    masked = after(cotangent, halo_gate) * valid_mask[:, :, None]
+    sent = lax.dynamic_slice_in_dim(masked, (1 - sample_half) * samples, samples, 1)
+    scaling = node_total * lax.axis_size("node") / valid_counts.astype(F32)
+    scaling = lax.dynamic_slice_in_dim(scaling, sample_half * samples, samples, 0)
+    scaling = scaling[:, None, None]
+    pooled, cotangent_other, *arrived = lax.optimization_barrier(
+        (
+            pooled,
+            swap(sent, "hid", 2),
+            exchange(node_zero, steps - 2, 1),
+            exchange(layer_one, steps - 3, 1),
+        )
+    )
+    masked = jnp.stack(ordered(sample_half, own_samples(masked), cotangent_other), axis=0)
     node_zero = jnp.concatenate([node_zero, arrived[0]], axis=0)
     node_zero = gather_round(node_zero, steps - 1, steps)
     layer_one = jnp.concatenate([layer_one, arrived[1]], axis=0)
@@ -819,23 +841,19 @@
         None,
         None,
     )
-    halo_rows = to_neighbours(halo_rows, halo_width)
-    arrived, halo_rows = lax.optimization_barrier(
-        (exchange(edge_one, steps - 2, 1), halo_rows)
-    )
+    arrived, cotangent_other, *halo_rows = lax.optimization_barrier(
+        (
+            exchange(edge_one, steps - 2, 1),
+            swap(masked, "hid", 1),
+            *neighbour_swaps(halo_rows, halo_width),
+        )
+    )
+    halo_rows = from_neighbours(*halo_rows)
+    masked = jnp.stack(ordered(edge_half, masked, cotangent_other), axis=1)
+    target = jnp.transpose(masked.reshape(node_total, samples, latent), (1, 0, 2))
     edge_one = jnp.concatenate([edge_one, arrived], axis=0)
     node_one = after(node_one, edge_one)
     edge_one = gather_round(edge_one, steps - 1, steps)
-
-    valid_mask = (ocean_mask[:, None] * present_mask).astype(BF16)
-    masked = after(cotangent, pooled) * valid_mask[:, :, None]
-    sent = lax.dynamic_slice_in_dim(masked, (1 - sample_half) * samples, samples, 1)
-    masked = jnp.stack(ordered(sample_half, own_samples(masked), swap(sent, "hid", 2)), axis=0)
-    masked = double_up(masked, "hid", 0, 1).reshape(node_total, samples, latent)
-    scaling = node_total * lax.axis_size("node") / valid_counts.astype(F32)
-    scaling = lax.dynamic_slice_in_dim(scaling, sample_half * samples, samples, 0)
-    target = jnp.transpose(masked, (1, 0, 2))
-    scaling = scaling[:, None, None]
 
     node_low_one = node_low
     table_one = jnp.concatenate([node_low, halo_rows], axis=1)
@@ -900,9 +918,10 @@
         width,
         [kept, sent],
     )
-    returned, *chain_one = lax.optimization_barrier(
-        (to_neighbours(returned, halo_width), *chain_one)
-    )
+    *returned, kept, sent = lax.optimization_barrier(
+        (*neighbour_swaps(returned, halo_width), *chain_one)
+    )
+    returned, chain_one = from_neighbours(*returned), (kept, sent)
     partial = from_edges(partial, returned)
     chain_one = split(scatter_round(chain_one, steps - 1), 2)
     other, *chain_one = lax.optimization_barrier((swap(partial.astype(BF16), "hid", 1), *chain_one))
@@ -953,45 +972,50 @@
         width,
         None,
     )
-    chain_zero = split(scatter_round(chain_zero, steps - 2, chain_edge[1]), 2)
-    chain_one = [jnp.concatenate(pair, axis=1) for pair in zip(chain_one, chain_zero)]
-    kept, sent, *chain_one = lax.optimization_barrier((*chain_edge, *chain_one))
-    chain_edge = split(scatter_round((kept, sent), steps - 1), 2)
-    returned = to_neighbours(after(returned, chain_edge[1]), halo_width)
-    arrived, returned = lax.optimization_barrier((exchange(chain_one[1], steps - 3, 1), returned))
-    chain_one = chain_one[0].astype(F32) + arrived.astype(F32)
+    kept, sent, one_arrived, zero_arrived = lax.optimization_barrier(
+        (
+            *chain_edge,
+            exchange(chain_one[1], steps - 3, 1),
+            exchange(chain_zero[1], steps - 2, 1),
+        )
+    )
+    chain_one = chain_one[0].astype(F32) + one_arrived.astype(F32)
+    chain_zero = split(chain_zero[0].astype(F32) + zero_arrived.astype(F32), 2)
+    edge_arrived, zero_arrived = lax.optimization_barrier(
+        (exchange(sent, steps - 1, 1), exchange(chain_zero[1], steps - 3, 1))
+    )
+    chain_edge = split(kept.astype(F32) + edge_arrived.astype(F32), 2)
+    chain_one = jnp.concatenate(
+        [chain_one, chain_zero[0].astype(F32) + zero_arrived.astype(F32)], axis=1
+    )
     for begin, end in reversed(z_rounds[1:]):
         chain_one = scatter_round(split(chain_one, 1 << (end - begin)), begin)
     begin, end = z_rounds[0]
     chain_one = split(chain_one, 1 << (end - begin))
-    partial = from_edges(partial, returned)
-    other = swap(partial.astype(BF16), "hid", 1)
-    arrived, edge_input_grad, other, *chain_one = lax.optimization_barrier(
-        (exchange(chain_edge[1], steps - 2, 1), edge_input_grad, other, *chain_one)
-    )
-    chain_edge = split(chain_edge[0] + arrived.astype(F32), 2)
-    arrived, *others = lax.optimization_barrier(
+    arrived, edge_input_grad, *others = lax.optimization_barrier(
         (
-            exchange(chain_edge[1], steps - 3, 1),
+            exchange(chain_edge[1], steps - 2, 1),
+            edge_input_grad,
             *[exchange(chain_one[flips], begin, flips) for flips in range(1, len(chain_one))],
         )
     )
-    chain_edge = chain_edge[0] + arrived.astype(F32)
     joined_grads = chain_one[0]
     for piece in others:
         joined_grads = joined_grads + piece.astype(F32)
     joined_grads = joined_grads[0]
-    node_grad = node_grad + (partial + other.astype(F32))
-    grad_node = own_rows_exchanged(node_grad.astype(BF16))
+    chain_edge = split(chain_edge[0] + arrived.astype(F32), 2)
+    arrived, returned = lax.optimization_barrier((exchange(chain_edge[1], steps - 3, 1), returned))
+    chain_edge = chain_edge[0] + arrived.astype(F32)
     halves = edge_input_grad.reshape(2, edge_part, latent)
     sent = lax.dynamic_index_in_dim(halves, 1 - sample_half, 0, keepdims=False).astype(BF16)
     kept = lax.dynamic_index_in_dim(halves, sample_half, 0, keepdims=False)
+    returned = neighbour_swaps(returned, halo_width)
     edge_zero_grads = scatter_rest(chain_edge, steps - 3)
-    edge_zero_grads, joined_grads, arrived, *grad_node = lax.optimization_barrier(
-        (edge_zero_grads, joined_grads, swap(sent, "hid", 2), *grad_node)
+    edge_zero_grads, arrived, *returned = lax.optimization_barrier(
+        (edge_zero_grads, swap(sent, "hid", 2), *returned)
     )
     edge_input_grad = kept + arrived.astype(F32)
-    grad_node = all_samples(*grad_node)
+    partial = from_edges(partial, from_neighbours(*returned))
 
     edge_rows = first_rows + second_rows
     layer_one_grads = joined_grads[: node_rows + edge_rows]
@@ -1014,13 +1038,23 @@
         [jnp.sum(entry[2] * entry[2], axis=(1, 2)) for entry in moment_list], axis=1
     )
     squares = jnp.concatenate([weight_local.reshape(1, -1), update_local.reshape(1, -1)], axis=1)
-    minor_packed = sum_everywhere(
-        jnp.concatenate(
-            [edge_minor_zero, node_minor_zero, edge_minor_one, node_minor_one]
-            + [jnp.pad(squares, ((0, 0), (0, latent - squares.size)))],
-            axis=0,
-        )
-    )
+    minor_packed = jnp.concatenate(
+        [edge_minor_zero, node_minor_zero, edge_minor_one, node_minor_one]
+        + [jnp.pad(squares, ((0, 0), (0, latent - squares.size)))],
+        axis=0,
+    )
+    minor_packed = sum_round(minor_packed, steps - 1, steps)
+    minor_packed, other = lax.optimization_barrier(
+        (minor_packed, swap(partial.astype(BF16), "hid", 1))
+    )
+    node_grad = node_grad + (partial + other.astype(F32))
+    grad_node = own_rows_exchanged(node_grad.astype(BF16))
+    last_rounds = list(reversed(rounds(0, steps - 1)))
+    for begin, end in last_rounds[:-1]:
+        minor_packed = sum_round(minor_packed, begin, end)
+    minor_packed, *grad_node = lax.optimization_barrier((minor_packed, *grad_node))
+    grad_node = all_samples(*grad_node)
+    minor_packed = sum_round(minor_packed, *last_rounds[-1])
     minor_total = minor_packed[: 8 * LAYERS].reshape(small_params.shape)
     squares = minor_packed[8 * LAYERS, : squares.size].reshape(2, *weight_local.shape)
     weight_squares, update_squares = squares[0], squares[1]

time: 278 us -> 287 us (1.032)
  other arithmetic: 28.3 us -> 41.3 us
  starting transfers between devices: 64.6 us -> 61.5 us
    ppermute x37 -> x38, waiting for transfers between devices: 37.4 us -> 47.7 us  [exchange(): lax.ppermute(values, ('node', 'hid'), [(i, i ^ mask) for i in range(total)])]
    ppermute x8, waiting for transfers between devices: 17.1 us -> 11.6 us  [the longest x4 7.25 us: neighbour_swaps(): second = lax.ppermute(jnp.where(even, to_previous, to_next), 'node', two)]
    ppermute x8, starting transfers between devices: 19.1 us -> 14.6 us  [the longest x4 11.8 us: neighbour_swaps(): second = lax.ppermute(jnp.where(even, to_previous, to_next), 'node', two)]
    ppermute x37 -> x38, starting transfers between devices: 39.6 us -> 43.6 us  [exchange(): lax.ppermute(values, ('node', 'hid'), [(i, i ^ mask) for i in range(total)])]
    ppermute x9, waiting for transfers between devices: 6.46 us -> 2.97 us  [swap(): lax.ppermute(values, axis, [(i, i ^ offset) for i in range(lax.axis_size(...]
    select_n x0 -> x8, other arithmetic: none -> 3.02 us  [the longest x4 2.02 us: neighbour_swaps(): second = lax.ppermute(jnp.where(even, to_previous, to_next), 'node', two)]
    slice x4 -> x3, local copies, waits for them, and re-layouts: 3.01 us -> 0.02 us  [the longest x1 0.01 us: per_device(): node_zero_grads[:node_first_rows]]
    unnamed x129 -> x144, local copies, waits for them, and re-layouts: 9.73 us -> 8.55 us
  transfers between devices with their start and end apart: 54 -> 55, of which waited for: 29 -> 27; matrix products, arithmetic and copies ran while one was open for 13% -> 16% of each run, Pallas kernels for 26% -> 25%
where the time goes in v5:
time: 287 us; the launch traced here: 286 us
  Pallas kernels  88.1 us (31%)
  waiting for transfers between devices  62.2 us (22%)
  starting transfers between devices  61.5 us (21%)
  other arithmetic  41.3 us (14%)
  local copies, waits for them, and re-layouts  28.7 us (10%)
    pallas_call x9, Pallas kernels, run_kernel(): pl.pallas_call(kernel, name=name, grid=(samples,), in_specs=in_specs, out...  88.1 us
    ppermute x38, waiting for transfers between devices, exchange(): lax.ppermute(values, ('node', 'hid'), [(i, i ^ mask) for i in range(total)])  47.7 us
    ppermute x38, starting transfers between devices, exchange(): lax.ppermute(values, ('node', 'hid'), [(i, i ^ mask) for i in range(total)])  43.6 us
    ppermute x4, starting transfers between devices, neighbour_swaps(): second = lax.ppermute(jnp.where(even, to_previous, to_next), 'node', two)  11.8 us
    unnamed x144, local copies, waits for them, and re-layouts  8.55 us
    concatenate x5, other arithmetic, gather_round(): return jnp.concatenate([held, *arrived], axis=0)  7.67 us
    ppermute x4, waiting for transfers between devices, neighbour_swaps(): second = lax.ppermute(jnp.where(even, to_previous, to_next), 'node', two)  7.25 us
  transfers between devices with their start and end apart: 55, of which 27 were waited for; matrix products, arithmetic and copies ran while one was open for 16% of the time, Pallas kernels for 25%

profile of v5, /device:TPU:0, one launch (start us, length us, event | category | flops | bytes accessed | tf_op | source)
XLA Modules:
  0.0 285.5 jit_solution(13848130627700300140)
XLA Ops:
  4.1 5.1 %collective-permute-start.2 = (bf16[1,448,128]{2,1,0:T(8,128)(2,1)S(1)}, bf16[1,448,128]{2,1,0:T(8,128)(2,1)S(1)}, u32[]{:S(2)}, u32[]{:S(2)}) collective-permute-start(bf16[1,448,128]{2,1,0:T(8,128)(2,1)S(1)} %maximum_bitcast_fusion), channel_id=1, source_target_pairs={{0,24},{1,25},{2,26},{3,27},{4,28},{5,29},{6,30},{7,31},{8,16},{9,... | collective-permute-start | bytes 344072 | tf_op jit(solution)/shard_map/ppermute | solution.py:572
  13.3 2.7 collective-permute-done.1
  15.9 3.0 %collective-permute-done = bf16[1,448,128]{2,1,0:T(8,128)(2,1)S(1)} collective-permute-done((bf16[1,448,128]{2,1,0:T(8,128)(2,1)S(1)}, bf16[1,448,128]{2,1,0:T(8,128)(2,1)S(1)}, u32[]{:S(2)}, u32[]{:S(2)}) %collective-permute-start) | collective-permute-done | bytes 114720 | tf_op jit(solution)/shard_map/ppermute | solution.py:572
  28.7 4.1 %collective-permute-done.3 = bf16[4,448,128]{2,1,0:T(8,128)(2,1)} collective-permute-done((bf16[4,448,128]{2,1,0:T(8,128)(2,1)}, bf16[4,448,128]{2,1,0:T(8,128)(2,1)}, u32[]{:S(2)}, u32[]{:S(2)}) %collective-permute-start.3) | collective-permute-done | bytes 458784 | tf_op jit(solution)/shard_map/ppermute | solution.py:572
  35.7 3.0 %collective-permute-start.9 = (bf16[1,448,128]{2,1,0:T(8,128)(2,1)S(1)}, bf16[1,448,128]{2,1,0:T(8,128)(2,1)S(1)}, u32[]{:S(2)}, u32[]{:S(2)}) collective-permute-start(bf16[1,448,128]{2,1,0:T(8,128)(2,1)S(1)} %maximum_bitcast_fusion.1), channel_id=1, source_target_pairs={{0,24},{1,25},{2,26},{3,27},{4,28},{5,29},{6,30},{7,31},{8,16},{9,... | collective-permute-start | bytes 344072 | tf_op jit(solution)/shard_map/ppermute | solution.py:572
  40.1 4.0 %collective-permute-start.6 = (bf16[3,40,512]{2,1,0:T(8,128)(2,1)S(1)}, bf16[3,40,512]{2,1,0:T(8,128)(2,1)S(1)}, u32[]{:S(2)}, u32[]{:S(2)}) collective-permute-start(bf16[3,40,512]{2,1,0:T(8,128)(2,1)S(1)} %get-tuple-element.403), channel_id=1, source_target_pairs={{0,28},{4,8},{8,4},{12,16},{16,12},{20,24},{24,20},{28,0},{1,29},{... | collective-permute-start | bytes 368648 | tf_op jit(solution)/shard_map/ppermute | solution.py:630
  47.0 2.7 collective-permute-done.6
  56.1 11.5 %edge_forward.2 = (bf16[3,640,512]{2,1,0:T(8,128)(2,1)}, bf16[3,640,512]{2,1,0:T(8,128)(2,1)}, bf16[3,640,512]{2,1,0:T(8,128)(2,1)}, f32[3,640,1]{2,1,0:T(8,128)...) custom-call(s32[32]{0:T(128)} %add.279.order, ...), custom_call_target="tpu_custom_call" | custom-call | flops 15225323520 | bytes 19271296 | tf_op jit(solution)/shard_map/edge_forward/pallas_call | solution.py:124
  71.9 4.9 %node_pass.2 = (bf16[480,512]{1,0:T(8,128)(2,1)}, bf16[480,512]{1,0:T(8,128)(2,1)}, bf16[480,512]{1,0:T(8,128)(2,1)}, bf16[480,512]{1,0:T(8,128)(2,1)}, f32[480,...) custom-call(s32[32]{0:T(128)} %add.279.order, ...), custom_call_target="tpu_custom_call" | custom-call | flops 3019898880 | bytes 7269376 | tf_op jit(solution)/shard_map/node_pass/pallas_call | solution.py:124
  77.8 3.4 %collective-permute-start.19 = (bf16[3,40,512]{2,1,0:T(8,128)(2,1)S(1)}, bf16[3,40,512]{2,1,0:T(8,128)(2,1)S(1)}, u32[]{:S(2)}, u32[]{:S(2)}) collective-permute-start(bf16[3,40,512]{2,1,0:T(8,128)(2,1)S(1)} %get-tuple-element.399), channel_id=1, source_target_pairs={{0,28},{4,8},{8,4},{12,16},{16,12},{20,24},{24,20},{28,0},{1,29},{... | collective-permute-start | bytes 368648 | tf_op jit(solution)/shard_map/ppermute | solution.py:630
  81.2 2.6 collective-permute-done.14
  86.1 2.5 collective-permute-done.18
  97.0 2.8 pad_maximum_fusion.1.w1.w2
  99.8 10.6 %edge_forward.3 = (bf16[3,640,512]{2,1,0:T(8,128)(2,1)}, bf16[3,640,512]{2,1,0:T(8,128)(2,1)}, bf16[3,640,512]{2,1,0:T(8,128)(2,1)}, f32[3,640,1]{2,1,0:T(8,128)}, bf16[3,160,512]{2,1,0:T(8,128)(2,1)}) custom-call(s32[32]{0:T(128)} %add.279.order, bf16[32,256,128]{2,1,0:T(8,128)(2,1)} %pad_maximum_fusion.1.w1.w2, ...), custom_call_target="tpu_custom_call" | custom-call | flops 15225323520 | bytes 17960576 | tf_op jit(solution)/shard_map/edge_forward/pallas_call | solution.py:124
  113.9 2.4 pad_maximum_fusion.3.rest_1_
  117.1 8.2 %node_pass.3 = (bf16[3,160,512]{2,1,0:T(8,128)(2,1)}, bf16[3,160,512]{2,1,0:T(8,128)(2,1)}, f32[3,160,512]{2,1,0:T(8,128)}, bf16[16,192,128]{2,1,0:T(8,128)(2,1)...) custom-call(s32[32]{0:T(128)} %add.279.order, s32[64]{0:T(128)} %reshape.344.rest_0_.owners, ...), custom_call_target="tpu_custom_call" | custom-call | flops 9059696640 | bytes 8087820 | tf_op jit(solution)/shard_map/node_pass/pallas_call | solution.py:124
  127.5 13.0 %edge_backward.2 = (bf16[3,640,512]{2,1,0:T(8,128)(2,1)}, bf16[3,640,512]{2,1,0:T(8,128)(2,1)}, bf16[3,400,512]{2,1,0:T(8,128)(2,1)}, f32[3,160,512]{2,1,0:T(8,1...) custom-call(s32[32]{0:T(128)} %add.279.order, ...), custom_call_target="tpu_custom_call" | custom-call | flops 14344519680 | bytes 19674752 | tf_op jit(solution)/shard_map/edge_backward/pallas_call | solution.py:124
  143.2 9.8 %edge_weight_grads.2 = (bf16[16,448,128]{2,1,0:T(8,128)(2,1)}, bf16[16,448,128]{2,1,0:T(8,128)(2,1)}) custom-call(s32[64]{0:T(128)} %reshape.344.rest_0_.owners, bf16[3,640,512]{2,1,0:T(8,128)(2,1)} %get-tuple-element.177.low.edge_low, bf16[3,240,512]{2,1,0:T(8,128)(2,1)} %pad_maximum_fusion.9.table, bf16[3,640,512]{2,1,0:T(8,128)(2,1)} %get-tuple-element.194.hidden_low, ...), custom_call_target="tpu_custom_call" | custom-call | flops 8053063680 | bytes 15073536 | tf_op jit(solution)/shard_map/edge_weight_grads/pallas_call | solution.py:124
  160.3 7.9 %node_backward.1 = (bf16[3,160,512]{2,1,0:T(8,128)(2,1)}, f32[3,160,512]{2,1,0:T(8,128)}, bf16[16,192,128]{2,1,0:T(8,128)(2,1)}, bf16[16,192,128]{2,1,0:T(8,128)(2,1)}, f32[4,512]{1,0:T(4,128)}) custom-call(s32[32]{0:T(128)} %add.279.order, s32[64]{0:T(128)} %reshape.344.rest_0_.owners, bf16[32,192,128]{2,1,0:T(8,128)(2,1)} %constant_dynamic-update-slice_fusion.10.rest_0_.w, ...), custom_call_target="tpu_custom_call" | custom-call | flops 6039797760 | bytes 9564288 | tf_op jit(solution)/shard_map/node_backward/pallas_call | solution.py:124
  169.9 14.4 %edge_backward.3 = (bf16[3,640,512]{2,1,0:T(8,128)(2,1)}, bf16[3,640,512]{2,1,0:T(8,128)(2,1)}, bf16[3,400,512]{2,1,0:T(8,128)(2,1)}, f32[3,160,512]{2,1,0:T(8,1...) custom-call(s32[32]{0:T(128)} %add.279.order, ...), custom_call_target="tpu_custom_call" | custom-call | flops 14344519680 | bytes 21640832 | tf_op jit(solution)/shard_map/edge_backward/pallas_call | solution.py:124
  185.1 6.5 %collective-permute-done.29 = bf16[8,448,128]{2,1,0:T(8,128)(2,1)S(1)} collective-permute-done((bf16[8,448,128]{2,1,0:T(8,128)(2,1)S(1)}, bf16[8,448,128]{2,1,0:T(8,128)(2,1)S(1)}, u32[]{:S(2)}, u32[]{:S(2)}) %collective-permute-start.29) | collective-permute-done | bytes 917536 | tf_op jit(solution)/shard_map/ppermute | solution.py:572
  193.9 7.8 %edge_weight_grads.3 = (bf16[16,256,128]{2,1,0:T(8,128)(2,1)}, bf16[16,256,128]{2,1,0:T(8,128)(2,1)}) custom-call(s32[64]{0:T(128)} %reshape.344.rest_0_.owners, bf16[640,512]{1,0:T(8,128)(2,1)} %bitcast.163, bf16[3,240,512]{2,1,0:T(8,128)(2,1)} %pad_maximum_fusion.8.table, bf16[640,512]{1,0:T(8,128)(2,1)} %get-tuple-element.222.hidden_low, ...), custom_call_target="tpu_custom_call" | custom-call | flops 8053063680 | bytes 9306368 | tf_op jit(solution)/shard_map/edge_weight_grads/pallas_call | solution.py:124
  208.7 5.5 %collective-permute-done.34 = bf16[4,192,128]{2,1,0:T(8,128)(2,1)S(1)} collective-permute-done((bf16[4,192,128]{2,1,0:T(8,128)(2,1)S(1)}, bf16[4,192,128]{2,1,0:T(8,128)(2,1)S(1)}, u32[]{:S(2)}, u32[]{:S(2)}) %collective-permute-start.34) | collective-permute-done | bytes 196640 | tf_op jit(solution)/shard_map/ppermute | solution.py:572
  217.6 3.3 %collective-permute-start.38 = (bf16[1,640,128]{2,1,0:T(8,128)(2,1)S(1)}, bf16[1,640,128]{2,1,0:T(8,128)(2,1)S(1)}, u32[]{:S(2)}, u32[]{:S(2)}) collective-permute-start(bf16[1,640,128]{2,1,0:T(8,128)(2,1)S(1)} %get-tuple-element.366), channel_id=1, source_target_pairs={{0,24},{1,25},{2,26},{3,27},{4,28},{5,29},{6,30},{7,31},{8,16},{9,... | collective-permute-start | bytes 491528 | tf_op jit(solution)/shard_map/ppermute | solution.py:572
  222.8 3.7 %collective-permute-done.38 = bf16[1,640,128]{2,1,0:T(8,128)(2,1)S(1)} collective-permute-done((bf16[1,640,128]{2,1,0:T(8,128)(2,1)S(1)}, bf16[1,640,128]{2,1,0:T(8,128)(2,1)S(1)}, u32[]{:S(2)}, u32[]{:S(2)}) %collective-permute-start.38) | collective-permute-done | bytes 163872 | tf_op jit(solution)/shard_map/ppermute | solution.py:572
  226.5 4.3 %collective-permute-done.37 = bf16[1,640,128]{2,1,0:T(8,128)(2,1)S(1)} collective-permute-done((bf16[1,640,128]{2,1,0:T(8,128)(2,1)S(1)}, bf16[1,640,128]{2,1,0:T(8,128)(2,1)S(1)}, u32[]{:S(2)}, u32[]{:S(2)}) %collective-permute-start.37) | collective-permute-done | bytes 163872 | tf_op jit(solution)/shard_map/ppermute | solution.py:572
  230.8 2.5 collective-permute-done.36
  237.9 2.9 %collective-permute-done.39 = bf16[4,256,128]{2,1,0:T(8,128)(2,1)S(1)} collective-permute-done((bf16[4,256,128]{2,1,0:T(8,128)(2,1)S(1)}, bf16[4,256,128]{2,1,0:T(8,128)(2,1)S(1)}, u32[]{:S(2)}, u32[]{:S(2)}) %collective-permute-start.39) | collective-permute-done | bytes 262176 | tf_op jit(solution)/shard_map/ppermute | solution.py:572
  241.7 2.6 collective-permute-start.42
  244.8 2.7 collective-permute-start.45
  268.3 2.9 %collective-permute-done.51 = bf16[40,3,512]{2,0,1:T(8,128)(2,1)S(1)} collective-permute-done((bf16[40,3,512]{2,0,1:T(8,128)(2,1)S(1)}, bf16[40,3,512]{2,0,1:T(8,128)(2,1)S(1)}, u32[]{:S(2)}, u32[]{:S(2)}) %collective-permute-start.51) | collective-permute-done | bytes 122912 | tf_op jit(solution)/shard_map/ppermute | solution.py:509
  271.2 2.5 collective-permute-start.54
  (378 shorter events, 117.2 us)
Async XLA Ops:
  4.1 9.2 %collective-permute-start.2 = (bf16[1,448,128]{2,1,0:T(8,128)(2,1)S(1)}, bf16[1,448,128]{2,1,0:T(8,128)(2,1)S(1)}, u32[]{:S(2)}, u32[]{:S(2)}) collective-permute-start(bf16[1,448,128]{2,1,0:T(8,128)(2,1)S(1)} %maximum_bitcast_fusion), channel_id=1, source_target_pairs={{0,24},{1,25},{2,26},{3,27},{4,28},{5,29},{6,30},{7,31},{8,16},{9,... | collective-permute-start | bytes 344072 | tf_op jit(solution)/shard_map/ppermute | solution.py:572
  9.3 9.7 %collective-permute-start = (bf16[1,448,128]{2,1,0:T(8,128)(2,1)S(1)}, bf16[1,448,128]{2,1,0:T(8,128)(2,1)S(1)}, u32[]{:S(2)}, u32[]{:S(2)}) collective-permute-start(bf16[1,448,128]{2,1,0:T(8,128)(2,1)S(1)} %maximum_bitcast_fusion), channel_id=1, source_target_pairs={{0,16},{1,17},{2,18},{3,19},{4,20},{5,21},{6,22},{7,23},{8,24},{9,... | collective-permute-start | bytes 344072 | tf_op jit(solution)/shard_map/ppermute | solution.py:572
  20.9 12.0 %collective-permute-start.3 = (bf16[4,448,128]{2,1,0:T(8,128)(2,1)}, bf16[4,448,128]{2,1,0:T(8,128)(2,1)}, u32[]{:S(2)}, u32[]{:S(2)}) collective-permute-start(bf16[4,448,128]{2,1,0:T(8,128)(2,1)} %pad_maximum_fusion.13), channel_id=1, source_target_pairs={{0,4},{1,5},{2,6},{3,7},{4,0},{5,1},{6,2},{7,3},{8,12},{9,13},{10,... | collective-permute-start | bytes 1376264 | tf_op jit(solution)/shard_map/ppermute | solution.py:572
  34.0 16.3 %collective-permute-start.4 = (bf16[8,256,128]{2,1,0:T(8,128)(2,1)S(1)}, bf16[8,256,128]{2,1,0:T(8,128)(2,1)S(1)}, u32[]{:S(2)}, u32[]{:S(2)}) collective-permute-start(bf16[8,256,128]{2,1,0:T(8,128)(2,1)S(1)} %slice.311), channel_id=1, source_target_pairs={{0,2},{1,3},{2,0},{3,1},{4,6},{5,7},{6,4},{7,5},{8,10},{9,11},{10,... | collective-permute-start | bytes 1572872 | tf_op jit(solution)/shard_map/ppermute | solution.py:572
  35.7 8.4 %collective-permute-start.9 = (bf16[1,448,128]{2,1,0:T(8,128)(2,1)S(1)}, bf16[1,448,128]{2,1,0:T(8,128)(2,1)S(1)}, u32[]{:S(2)}, u32[]{:S(2)}) collective-permute-start(bf16[1,448,128]{2,1,0:T(8,128)(2,1)S(1)} %maximum_bitcast_fusion.1), channel_id=1, source_target_pairs={{0,24},{1,25},{2,26},{3,27},{4,28},{5,29},{6,30},{7,31},{8,16},{9,... | collective-permute-start | bytes 344072 | tf_op jit(solution)/shard_map/ppermute | solution.py:572
  38.6 8.3 %collective-permute-start.8 = (bf16[1,448,128]{2,1,0:T(8,128)(2,1)S(1)}, bf16[1,448,128]{2,1,0:T(8,128)(2,1)S(1)}, u32[]{:S(2)}, u32[]{:S(2)}) collective-permute-start(bf16[1,448,128]{2,1,0:T(8,128)(2,1)S(1)} %maximum_bitcast_fusion.1), channel_id=1, source_target_pairs={{0,8},{1,9},{2,10},{3,11},{4,12},{5,13},{6,14},{7,15},{8,0},{9,1},... | collective-permute-start | bytes 344072 | tf_op jit(solution)/shard_map/ppermute | solution.py:572
  38.6 8.3 %collective-permute-start.7 = (bf16[1,448,128]{2,1,0:T(8,128)(2,1)S(1)}, bf16[1,448,128]{2,1,0:T(8,128)(2,1)S(1)}, u32[]{:S(2)}, u32[]{:S(2)}) collective-permute-start(bf16[1,448,128]{2,1,0:T(8,128)(2,1)S(1)} %maximum_bitcast_fusion.1), channel_id=1, source_target_pairs={{0,16},{1,17},{2,18},{3,19},{4,20},{5,21},{6,22},{7,23},{8,24},{9,... | collective-permute-start | bytes 344072 | tf_op jit(solution)/shard_map/ppermute | solution.py:572
  40.1 9.6 %collective-permute-start.6 = (bf16[3,40,512]{2,1,0:T(8,128)(2,1)S(1)}, bf16[3,40,512]{2,1,0:T(8,128)(2,1)S(1)}, u32[]{:S(2)}, u32[]{:S(2)}) collective-permute-start(bf16[3,40,512]{2,1,0:T(8,128)(2,1)S(1)} %get-tuple-element.403), channel_id=1, source_target_pairs={{0,28},{4,8},{8,4},{12,16},{16,12},{20,24},{24,20},{28,0},{1,29},{... | collective-permute-start | bytes 368648 | tf_op jit(solution)/shard_map/ppermute | solution.py:630
  50.7 17.0 %collective-permute-start.11 = (bf16[40,3,512]{2,0,1:T(8,128)(2,1)S(1)}, bf16[40,3,512]{2,0,1:T(8,128)(2,1)S(1)}, u32[]{:S(2)}, u32[]{:S(2)}) collective-permute-start(bf16[40,3,512]{2,0,1:T(8,128)(2,1)S(1)} %constant_dynamic-slice_fusion), channel_id=1, source_target_pairs={{0,2},{1,3},{2,0},{3,1},{4,6},{5,7},{6,4},{7,5},{8,10},{9,11},{10,... | collective-permute-start | bytes 368648 | tf_op jit(solution)/shard_map/ppermute | solution.py:509
  51.3 16.3 %collective-permute-start.13 = (bf16[4,448,128]{2,1,0:T(8,128)(2,1)S(1)}, bf16[4,448,128]{2,1,0:T(8,128)(2,1)S(1)}, u32[]{:S(2)}, u32[]{:S(2)}) collective-permute-start(bf16[4,448,128]{2,1,0:T(8,128)(2,1)S(1)} %pad_maximum_fusion.14), channel_id=1, source_target_pairs={{0,4},{1,5},{2,6},{3,7},{4,0},{5,1},{6,2},{7,3},{8,12},{9,13},{10,... | collective-permute-start | bytes 1376264 | tf_op jit(solution)/shard_map/ppermute | solution.py:572
  52.0 15.6 %collective-permute-start.12 = (bf16[8,192,128]{2,1,0:T(8,128)(2,1)S(1)}, bf16[8,192,128]{2,1,0:T(8,128)(2,1)S(1)}, u32[]{:S(2)}, u32[]{:S(2)}) collective-permute-start(bf16[8,192,128]{2,1,0:T(8,128)(2,1)S(1)} %slice.312), channel_id=1, source_target_pairs={{0,2},{1,3},{2,0},{3,1},{4,6},{5,7},{6,4},{7,5},{8,10},{9,11},{10,... | collective-permute-start | bytes 1179656 | tf_op jit(solution)/shard_map/ppermute | solution.py:572
  69.2 12.0 %collective-permute-start.15 = (bf16[2,40,3,512]{3,1,2,0:T(8,128)(2,1)S(1)}, bf16[2,40,3,512]{3,1,2,0:T(8,128)(2,1)S(1)}, u32[]{:S(2)}, u32[]{:S(2)}) collective-permute-start(bf16[2,40,3,512]{3,1,2,0:T(8,128)(2,1)S(1)} %pad_maximum_fusion.15), channel_id=1, source_target_pairs={{0,1},{1,0},{2,3},{3,2},{4,5},{5,4},{6,7},{7,6},{8,9},{9,8},{10,11... | collective-permute-start | bytes 737288 | tf_op jit(solution)/shard_map/ppermute | solution.py:509
  69.4 14.4 %collective-permute-start.14 = (bf16[8,256,128]{2,1,0:T(8,128)(2,1)S(1)}, bf16[8,256,128]{2,1,0:T(8,128)(2,1)S(1)}, u32[]{:S(2)}, u32[]{:S(2)}) collective-permute-start(bf16[8,256,128]{2,1,0:T(8,128)(2,1)S(1)} %slice.313), channel_id=1, source_target_pairs={{0,2},{1,3},{2,0},{3,1},{4,6},{5,7},{6,4},{7,5},{8,10},{9,11},{10,... | collective-permute-start | bytes 1572872 | tf_op jit(solution)/shard_map/ppermute | solution.py:572
  77.8 8.3 %collective-permute-start.19 = (bf16[3,40,512]{2,1,0:T(8,128)(2,1)S(1)}, bf16[3,40,512]{2,1,0:T(8,128)(2,1)S(1)}, u32[]{:S(2)}, u32[]{:S(2)}) collective-permute-start(bf16[3,40,512]{2,1,0:T(8,128)(2,1)S(1)} %get-tuple-element.399), channel_id=1, source_target_pairs={{0,28},{4,8},{8,4},{12,16},{16,12},{20,24},{24,20},{28,0},{1,29},{... | collective-permute-start | bytes 368648 | tf_op jit(solution)/shard_map/ppermute | solution.py:630
  81.2 7.5 %collective-permute-start.18 = (bf16[3,40,512]{2,1,0:T(8,128)(2,1)S(1)}, bf16[3,40,512]{2,1,0:T(8,128)(2,1)S(1)}, u32[]{:S(2)}, u32[]{:S(2)}) collective-permute-start(bf16[3,40,512]{2,1,0:T(8,128)(2,1)S(1)} %get-tuple-element.400), channel_id=1, source_target_pairs={{0,4},{4,0},{8,12},{12,8},{16,20},{20,16},{24,28},{28,24},{1,5},{5... | collective-permute-start | bytes 368648 | tf_op jit(solution)/shard_map/ppermute | solution.py:629
  92.6 17.8 %collective-permute-start.21 = (bf16[8,192,128]{2,1,0:T(8,128)(2,1)S(1)}, bf16[8,192,128]{2,1,0:T(8,128)(2,1)S(1)}, u32[]{:S(2)}, u32[]{:S(2)}) collective-permute-start(bf16[8,192,128]{2,1,0:T(8,128)(2,1)S(1)} %slice.314), channel_id=1, source_target_pairs={{0,2},{1,3},{2,0},{3,1},{4,6},{5,7},{6,4},{7,5},{8,10},{9,11},{10,... | collective-permute-start | bytes 1179656 | tf_op jit(solution)/shard_map/ppermute | solution.py:572
  126.9 16.3 %collective-permute-start.24 = (bf16[40,3,512]{2,0,1:T(8,128)(2,1)S(1)}, bf16[40,3,512]{2,0,1:T(8,128)(2,1)S(1)}, u32[]{:S(2)}, u32[]{:S(2)}) collective-permute-start(bf16[40,3,512]{2,0,1:T(8,128)(2,1)S(1)} %get-tuple-element.371), channel_id=1, source_target_pairs={{0,2},{1,3},{2,0},{3,1},{4,6},{5,7},{6,4},{7,5},{8,10},{9,11},{10,... | collective-permute-start | bytes 368648 | tf_op jit(solution)/shard_map/ppermute | solution.py:509
  141.5 11.6 %collective-permute-start.26 = (bf16[3,40,512]{2,1,0:T(8,128)(2,1)S(1)}, bf16[3,40,512]{2,1,0:T(8,128)(2,1)S(1)}, u32[]{:S(2)}, u32[]{:S(2)}) collective-permute-start(bf16[3,40,512]{2,1,0:T(8,128)(2,1)S(1)} %get-tuple-element.393), channel_id=1, source_target_pairs={{0,28},{4,8},{8,4},{12,16},{16,12},{20,24},{24,20},{28,0},{1,29},{... | collective-permute-start | bytes 368648 | tf_op jit(solution)/shard_map/ppermute | solution.py:630
  143.2 9.9 %collective-permute-start.25 = (bf16[3,40,512]{2,1,0:T(8,128)(2,1)S(1)}, bf16[3,40,512]{2,1,0:T(8,128)(2,1)S(1)}, u32[]{:S(2)}, u32[]{:S(2)}) collective-permute-start(bf16[3,40,512]{2,1,0:T(8,128)(2,1)S(1)} %get-tuple-element.394), channel_id=1, source_target_pairs={{0,4},{4,0},{8,12},{12,8},{16,20},{20,16},{24,28},{28,24},{1,5},{5... | collective-permute-start | bytes 368648 | tf_op jit(solution)/shard_map/ppermute | solution.py:629
  168.2 16.0 %collective-permute-start.30 = (bf16[16,192,128]{2,1,0:T(8,128)(2,1)}, bf16[16,192,128]{2,1,0:T(8,128)(2,1)S(1)}, u32[]{:S(2)}, u32[]{:S(2)}) collective-permute-start(bf16[16,192,128]{2,1,0:T(8,128)(2,1)} %get-tuple-element.229), channel_id=1, source_target_pairs={{0,1},{1,0},{2,3},{3,2},{4,5},{5,4},{6,7},{7,6},{8,9},{9,8},{10,11... | collective-permute-start | bytes 2359304 | tf_op jit(solution)/shard_map/ppermute | solution.py:572
  168.3 23.2 %collective-permute-start.29 = (bf16[8,448,128]{2,1,0:T(8,128)(2,1)S(1)}, bf16[8,448,128]{2,1,0:T(8,128)(2,1)S(1)}, u32[]{:S(2)}, u32[]{:S(2)}) collective-permute-start(bf16[8,448,128]{2,1,0:T(8,128)(2,1)S(1)} %slice.451), channel_id=1, source_target_pairs={{0,2},{1,3},{2,0},{3,1},{4,6},{5,7},{6,4},{7,5},{8,10},{9,11},{10,... | collective-permute-start | bytes 2752520 | tf_op jit(solution)/shard_map/ppermute | solution.py:572
  184.5 17.2 %collective-permute-start.32 = (bf16[8,192,128]{2,1,0:T(8,128)(2,1)S(1)}, bf16[8,192,128]{2,1,0:T(8,128)(2,1)S(1)}, u32[]{:S(2)}, u32[]{:S(2)}) collective-permute-start(bf16[8,192,128]{2,1,0:T(8,128)(2,1)S(1)} %slice.454), channel_id=1, source_target_pairs={{0,2},{1,3},{2,0},{3,1},{4,6},{5,7},{6,4},{7,5},{8,10},{9,11},{10,... | collective-permute-start | bytes 1179656 | tf_op jit(solution)/shard_map/ppermute | solution.py:572
  191.9 11.7 %collective-permute-start.31 = (bf16[4,448,128]{2,1,0:T(8,128)(2,1)S(1)}, bf16[4,448,128]{2,1,0:T(8,128)(2,1)S(1)}, u32[]{:S(2)}, u32[]{:S(2)}) collective-permute-start(bf16[4,448,128]{2,1,0:T(8,128)(2,1)S(1)} %slice.453), channel_id=1, source_target_pairs={{0,4},{1,5},{2,6},{3,7},{4,0},{5,1},{6,2},{7,3},{8,12},{9,13},{10,... | collective-permute-start | bytes 1376264 | tf_op jit(solution)/shard_map/ppermute | solution.py:572
  204.3 9.9 %collective-permute-start.33 = (bf16[16,256,128]{2,1,0:T(8,128)(2,1)}, bf16[16,256,128]{2,1,0:T(8,128)(2,1)}, u32[]{:S(2)}, u32[]{:S(2)}) collective-permute-start(bf16[16,256,128]{2,1,0:T(8,128)(2,1)} %get-tuple-element.236), channel_id=1, source_target_pairs={{0,1},{1,0},{2,3},{3,2},{4,5},{5,4},{6,7},{7,6},{8,9},{9,8},{10,11... | collective-permute-start | bytes 3145736 | tf_op jit(solution)/shard_map/ppermute | solution.py:572
  206.9 7.4 %collective-permute-start.34 = (bf16[4,192,128]{2,1,0:T(8,128)(2,1)S(1)}, bf16[4,192,128]{2,1,0:T(8,128)(2,1)S(1)}, u32[]{:S(2)}, u32[]{:S(2)}) collective-permute-start(bf16[4,192,128]{2,1,0:T(8,128)(2,1)S(1)} %slice.456), channel_id=1, source_target_pairs={{0,4},{1,5},{2,6},{3,7},{4,0},{5,1},{6,2},{7,3},{8,12},{9,13},{10,... | collective-permute-start | bytes 589832 | tf_op jit(solution)/shard_map/ppermute | solution.py:572
  215.9 17.4 %collective-permute-start.35 = (bf16[8,256,128]{2,1,0:T(8,128)(2,1)S(1)}, bf16[8,256,128]{2,1,0:T(8,128)(2,1)S(1)}, u32[]{:S(2)}, u32[]{:S(2)}) collective-permute-start(bf16[8,256,128]{2,1,0:T(8,128)(2,1)S(1)} %slice.452), channel_id=1, source_target_pairs={{0,2},{1,3},{2,0},{3,1},{4,6},{5,7},{6,4},{7,5},{8,10},{9,11},{10,... | collective-permute-start | bytes 1572872 | tf_op jit(solution)/shard_map/ppermute | solution.py:572
  217.6 8.9 %collective-permute-start.38 = (bf16[1,640,128]{2,1,0:T(8,128)(2,1)S(1)}, bf16[1,640,128]{2,1,0:T(8,128)(2,1)S(1)}, u32[]{:S(2)}, u32[]{:S(2)}) collective-permute-start(bf16[1,640,128]{2,1,0:T(8,128)(2,1)S(1)} %get-tuple-element.366), channel_id=1, source_target_pairs={{0,24},{1,25},{2,26},{3,27},{4,28},{5,29},{6,30},{7,31},{8,16},{9,... | collective-permute-start | bytes 491528 | tf_op jit(solution)/shard_map/ppermute | solution.py:572
  220.9 9.9 %collective-permute-start.37 = (bf16[1,640,128]{2,1,0:T(8,128)(2,1)S(1)}, bf16[1,640,128]{2,1,0:T(8,128)(2,1)S(1)}, u32[]{:S(2)}, u32[]{:S(2)}) collective-permute-start(bf16[1,640,128]{2,1,0:T(8,128)(2,1)S(1)} %get-tuple-element.367), channel_id=1, source_target_pairs={{0,8},{1,9},{2,10},{3,11},{4,12},{5,13},{6,14},{7,15},{8,0},{9,1},... | collective-permute-start | bytes 491528 | tf_op jit(solution)/shard_map/ppermute | solution.py:572
  220.9 12.4 %collective-permute-start.36 = (bf16[1,640,128]{2,1,0:T(8,128)(2,1)S(1)}, bf16[1,640,128]{2,1,0:T(8,128)(2,1)S(1)}, u32[]{:S(2)}, u32[]{:S(2)}) collective-permute-start(bf16[1,640,128]{2,1,0:T(8,128)(2,1)S(1)} %get-tuple-element.368), channel_id=1, source_target_pairs={{0,16},{1,17},{2,18},{3,19},{4,20},{5,21},{6,22},{7,23},{8,24},{9,... | collective-permute-start | bytes 491528 | tf_op jit(solution)/shard_map/ppermute | solution.py:572
  236.5 13.8 %collective-permute-start.43 = (bf16[320,512]{1,0:T(8,128)(2,1)S(1)}, bf16[320,512]{1,0:T(8,128)(2,1)S(1)}, u32[]{:S(2)}, u32[]{:S(2)}) collective-permute-start(bf16[320,512]{1,0:T(8,128)(2,1)S(1)} %fusion.7), channel_id=1, source_target_pairs={{0,2},{1,3},{2,0},{3,1},{4,6},{5,7},{6,4},{7,5},{8,10},{9,11},{10,... | collective-permute-start | bytes 983048 | tf_op jit(solution)/shard_map/ppermute | solution.py:509
  241.7 8.6 %collective-permute-start.42 = (bf16[1,256,128]{2,1,0:T(8,128)(2,1)S(1)}, bf16[1,256,128]{2,1,0:T(8,128)(2,1)S(1)}, u32[]{:S(2)}, u32[]{:S(2)}) collective-permute-start(bf16[1,256,128]{2,1,0:T(8,128)(2,1)S(1)} %get-tuple-element.383), channel_id=1, source_target_pairs={{0,24},{1,25},{2,26},{3,27},{4,28},{5,29},{6,30},{7,31},{8,16},{9,... | collective-permute-start | bytes 196616 | tf_op jit(solution)/shard_map/ppermute | solution.py:572
  244.8 7.7 %collective-permute-start.45 = (bf16[3,40,512]{2,1,0:T(8,128)(2,1)S(1)}, bf16[3,40,512]{2,1,0:T(8,128)(2,1)S(1)}, u32[]{:S(2)}, u32[]{:S(2)}) collective-permute-start(bf16[3,40,512]{2,1,0:T(8,128)(2,1)S(1)} %get-tuple-element.389), channel_id=1, source_target_pairs={{0,28},{4,8},{8,4},{12,16},{16,12},{20,24},{24,20},{28,0},{1,29},{... | collective-permute-start | bytes 368648 | tf_op jit(solution)/shard_map/ppermute | solution.py:630
  (92 other events, 796.3 us)

commit v6 on v5

--- a/solution.py
+++ b/solution.py
@@ -618,6 +618,15 @@
     for begin, end in reversed(rounds(0, steps - 1)):
         values = sum_round(values, begin, end)
     return values
+
+
+def to_neighbours(rows, halo_width):
+    count = lax.axis_size("node")
+    onward = [(i, (i + 1) % count) for i in range(count)]
+    back = [(target, source) for source, target in onward]
+    from_previous = lax.ppermute(rows[:, halo_width:], "node", onward)
+    from_next = lax.ppermute(rows[:, :halo_width], "node", back)
+    return jnp.concatenate([from_previous, from_next], axis=1)
 
 
 def neighbour_swaps(rows, halo_width):
@@ -798,21 +807,9 @@
         node_total,
         False,
     )
-    valid_mask = (ocean_mask[:, None] * present_mask).astype(BF16)
-    masked = after(cotangent, halo_gate) * valid_mask[:, :, None]
-    sent = lax.dynamic_slice_in_dim(masked, (1 - sample_half) * samples, samples, 1)
-    scaling = node_total * lax.axis_size("node") / valid_counts.astype(F32)
-    scaling = lax.dynamic_slice_in_dim(scaling, sample_half * samples, samples, 0)
-    scaling = scaling[:, None, None]
-    pooled, cotangent_other, *arrived = lax.optimization_barrier(
-        (
-            pooled,
-            swap(sent, "hid", 2),
-            exchange(node_zero, steps - 2, 1),
-            exchange(layer_one, steps - 3, 1),
-        )
-    )
-    masked = jnp.stack(ordered(sample_half, own_samples(masked), cotangent_other), axis=0)
+    pooled, *arrived = lax.optimization_barrier(
+        (pooled, exchange(node_zero, steps - 2, 1), exchange(layer_one, steps - 3, 1))
+    )
     node_zero = jnp.concatenate([node_zero, arrived[0]], axis=0)
     node_zero = gather_round(node_zero, steps - 1, steps)
     layer_one = jnp.concatenate([layer_one, arrived[1]], axis=0)
@@ -841,19 +838,18 @@
         None,
         None,
     )
-    arrived, cotangent_other, *halo_rows = lax.optimization_barrier(
-        (
-            exchange(edge_one, steps - 2, 1),
-            swap(masked, "hid", 1),
-            *neighbour_swaps(halo_rows, halo_width),
-        )
-    )
-    halo_rows = from_neighbours(*halo_rows)
-    masked = jnp.stack(ordered(edge_half, masked, cotangent_other), axis=1)
-    target = jnp.transpose(masked.reshape(node_total, samples, latent), (1, 0, 2))
+    halo_rows = to_neighbours(halo_rows, halo_width)
+    arrived, halo_rows = lax.optimization_barrier((exchange(edge_one, steps - 2, 1), halo_rows))
     edge_one = jnp.concatenate([edge_one, arrived], axis=0)
     node_one = after(node_one, edge_one)
     edge_one = gather_round(edge_one, steps - 1, steps)
+
+    valid_mask = (ocean_mask[:, None] * present_mask).astype(BF16)
+    masked = after(cotangent, pooled) * valid_mask[:, :, None]
+    sent = lax.dynamic_slice_in_dim(masked, (1 - sample_half) * samples, samples, 1)
+    scaling = node_total * lax.axis_size("node") / valid_counts.astype(F32)
+    scaling = lax.dynamic_slice_in_dim(scaling, sample_half * samples, samples, 0)
+    scaling = scaling[:, None, None]
 
     node_low_one = node_low
     table_one = jnp.concatenate([node_low, halo_rows], axis=1)
@@ -869,7 +865,13 @@
         node_total,
         True,
     )
-    node_one = gather_round(node_one, steps - 2, steps - 1, pooled)
+    pooled, arrived, cotangent_other = lax.optimization_barrier(
+        (pooled, exchange(node_one, steps - 2, 1), swap(sent, "hid", 2))
+    )
+    node_one = jnp.concatenate([node_one, arrived], axis=0)
+    masked = jnp.stack(ordered(sample_half, own_samples(masked), cotangent_other), axis=0)
+    masked = double_up(masked, "hid", 0, 1).reshape(node_total, samples, latent)
+    target = jnp.transpose(masked, (1, 0, 2))
     node_one = gather_round(node_one, steps - 1, steps)
     node_low, pooled_grad, node_grad, kept, sent, node_minor_one = node_pass(
         order,
@@ -972,19 +974,20 @@
         width,
         None,
     )
-    kept, sent, one_arrived, zero_arrived = lax.optimization_barrier(
+    kept, sent, one_arrived, zero_arrived, *returned = lax.optimization_barrier(
         (
             *chain_edge,
             exchange(chain_one[1], steps - 3, 1),
             exchange(chain_zero[1], steps - 2, 1),
+            *neighbour_swaps(returned, halo_width),
         )
     )
     chain_one = chain_one[0].astype(F32) + one_arrived.astype(F32)
     chain_zero = split(chain_zero[0].astype(F32) + zero_arrived.astype(F32), 2)
-    edge_arrived, zero_arrived = lax.optimization_barrier(
-        (exchange(sent, steps - 1, 1), exchange(chain_zero[1], steps - 3, 1))
-    )
-    chain_edge = split(kept.astype(F32) + edge_arrived.astype(F32), 2)
+    edge_arrived = exchange(sent, steps - 1, 1)
+    kept, sent = split(kept.astype(F32) + edge_arrived.astype(F32), 2)
+    zero_arrived = after(exchange(chain_zero[1], steps - 3, 1), sent)
+    returned = after(returned, sent)
     chain_one = jnp.concatenate(
         [chain_one, chain_zero[0].astype(F32) + zero_arrived.astype(F32)], axis=1
     )
@@ -992,10 +995,12 @@
         chain_one = scatter_round(split(chain_one, 1 << (end - begin)), begin)
     begin, end = z_rounds[0]
     chain_one = split(chain_one, 1 << (end - begin))
-    arrived, edge_input_grad, *others = lax.optimization_barrier(
+    partial = from_edges(partial, from_neighbours(*returned))
+    arrived, edge_input_grad, other, *others = lax.optimization_barrier(
         (
-            exchange(chain_edge[1], steps - 2, 1),
+            exchange(sent, steps - 2, 1),
             edge_input_grad,
+            swap(partial.astype(BF16), "hid", 1),
             *[exchange(chain_one[flips], begin, flips) for flips in range(1, len(chain_one))],
         )
     )
@@ -1003,19 +1008,19 @@
     for piece in others:
         joined_grads = joined_grads + piece.astype(F32)
     joined_grads = joined_grads[0]
-    chain_edge = split(chain_edge[0] + arrived.astype(F32), 2)
-    arrived, returned = lax.optimization_barrier((exchange(chain_edge[1], steps - 3, 1), returned))
-    chain_edge = chain_edge[0] + arrived.astype(F32)
+    chain_edge = split(kept + arrived.astype(F32), 2)
+    chain_edge = scatter_round(chain_edge, steps - 3)
     halves = edge_input_grad.reshape(2, edge_part, latent)
     sent = lax.dynamic_index_in_dim(halves, 1 - sample_half, 0, keepdims=False).astype(BF16)
     kept = lax.dynamic_index_in_dim(halves, sample_half, 0, keepdims=False)
-    returned = neighbour_swaps(returned, halo_width)
+    node_grad = node_grad + (partial + other.astype(F32))
+    grad_node = own_rows_exchanged(node_grad.astype(BF16))
     edge_zero_grads = scatter_rest(chain_edge, steps - 3)
-    edge_zero_grads, arrived, *returned = lax.optimization_barrier(
-        (edge_zero_grads, swap(sent, "hid", 2), *returned)
+    edge_zero_grads, arrived, *grad_node = lax.optimization_barrier(
+        (edge_zero_grads, swap(sent, "hid", 2), *grad_node)
     )
     edge_input_grad = kept + arrived.astype(F32)
-    partial = from_edges(partial, from_neighbours(*returned))
+    grad_node = all_samples(*grad_node)
 
     edge_rows = first_rows + second_rows
     layer_one_grads = joined_grads[: node_rows + edge_rows]
@@ -1043,18 +1048,7 @@
         + [jnp.pad(squares, ((0, 0), (0, latent - squares.size)))],
         axis=0,
     )
-    minor_packed = sum_round(minor_packed, steps - 1, steps)
-    minor_packed, other = lax.optimization_barrier(
-        (minor_packed, swap(partial.astype(BF16), "hid", 1))
-    )
-    node_grad = node_grad + (partial + other.astype(F32))
-    grad_node = own_rows_exchanged(node_grad.astype(BF16))
-    last_rounds = list(reversed(rounds(0, steps - 1)))
-    for begin, end in last_rounds[:-1]:
-        minor_packed = sum_round(minor_packed, begin, end)
-    minor_packed, *grad_node = lax.optimization_barrier((minor_packed, *grad_node))
-    grad_node = all_samples(*grad_node)
-    minor_packed = sum_round(minor_packed, *last_rounds[-1])
+    minor_packed = sum_everywhere(minor_packed)
     minor_total = minor_packed[: 8 * LAYERS].reshape(small_params.shape)
     squares = minor_packed[8 * LAYERS, : squares.size].reshape(2, *weight_local.shape)
     weight_squares, update_squares = squares[0], squares[1]

time: 287 us -> 273 us (0.951)
  other arithmetic: 41.3 us -> 32.4 us
    ppermute x0 -> x2, starting transfers between devices: none -> 4.78 us  [the longest x1 3.34 us: to_neighbours(): from_next = lax.ppermute(rows[:, :halo_width], 'node', back)]
    ppermute x4 -> x3, waiting for transfers between devices: 7.25 us -> 2.75 us  [neighbour_swaps(): second = lax.ppermute(jnp.where(even, to_previous, to_next), 'node', two)]
    ppermute x0 -> x2, waiting for transfers between devices: none -> 4.45 us  [the longest x1 3.5 us: to_neighbours(): from_previous = lax.ppermute(rows[:, halo_width:], 'node', onward)]
    ppermute x4 -> x3, waiting for transfers between devices: 4.37 us -> 0.59 us  [neighbour_swaps(): first = lax.ppermute(jnp.where(even, to_next, to_previous), 'node', one)]
    ppermute x4 -> x3, starting transfers between devices: 11.8 us -> 8.77 us  [neighbour_swaps(): second = lax.ppermute(jnp.where(even, to_previous, to_next), 'node', two)]
    unnamed x144 -> x155, local copies, waits for them, and re-layouts: 8.55 us -> 10.2 us
    concatenate x5 -> x4, other arithmetic: 7.67 us -> 6.71 us  [gather_round(): return jnp.concatenate([held, *arrived], axis=0)]
  transfers between devices with their start and end apart: 55 -> 55, of which waited for: 27 -> 26; matrix products, arithmetic and copies ran while one was open for 16% -> 15% of each run, Pallas kernels for 25% -> 26%
where the time goes in v6:
time: 273 us; the launch traced here: 272 us
  Pallas kernels  87.2 us (32%)
  waiting for transfers between devices  59.6 us (22%)
  starting transfers between devices  59.4 us (22%)
  other arithmetic  32.4 us (12%)
  local copies, waits for them, and re-layouts  29.2 us (11%)
  between operations  2.82 us (1%)
    pallas_call x9, Pallas kernels, run_kernel(): pl.pallas_call(kernel, name=name, grid=(samples,), in_specs=in_specs, out...  87.2 us
    ppermute x38, waiting for transfers between devices, exchange(): lax.ppermute(values, ('node', 'hid'), [(i, i ^ mask) for i in range(total)])  49.4 us
    ppermute x38, starting transfers between devices, exchange(): lax.ppermute(values, ('node', 'hid'), [(i, i ^ mask) for i in range(total)])  41.8 us
    unnamed x155, local copies, waits for them, and re-layouts  10.2 us
    ppermute x3, starting transfers between devices, neighbour_swaps(): second = lax.ppermute(jnp.where(even, to_previous, to_next), 'node', two)  8.77 us
    concatenate x4, other arithmetic, gather_round(): return jnp.concatenate([held, *arrived], axis=0)  6.71 us
  transfers between devices with their start and end apart: 55, of which 26 were waited for; matrix products, arithmetic and copies ran while one was open for 15% of the time, Pallas kernels for 26%

profile of v6, /device:TPU:0, one launch (start us, length us, event | category | flops | bytes accessed | tf_op | source)
XLA Modules:
  0.0 271.7 jit_solution(13373080047511770596)
XLA Ops:
  3.5 5.1 %collective-permute-start.2 = (bf16[1,448,128]{2,1,0:T(8,128)(2,1)S(1)}, bf16[1,448,128]{2,1,0:T(8,128)(2,1)S(1)}, u32[]{:S(2)}, u32[]{:S(2)}) collective-permute-start(bf16[1,448,128]{2,1,0:T(8,128)(2,1)S(1)} %maximum_bitcast_fusion), channel_id=1, source_target_pairs={{0,24},{1,25},{2,26},{3,27},{4,28},{5,29},{6,30},{7,31},{8,16},{9,... | collective-permute-start | bytes 344072 | tf_op jit(solution)/shard_map/ppermute | solution.py:572
  12.7 2.7 collective-permute-done.1
  15.4 3.0 %collective-permute-done = bf16[1,448,128]{2,1,0:T(8,128)(2,1)S(1)} collective-permute-done((bf16[1,448,128]{2,1,0:T(8,128)(2,1)S(1)}, bf16[1,448,128]{2,1,0:T(8,128)(2,1)S(1)}, u32[]{:S(2)}, u32[]{:S(2)}) %collective-permute-start) | collective-permute-done | bytes 114720 | tf_op jit(solution)/shard_map/ppermute | solution.py:572
  23.5 7.6 %collective-permute-done.3 = bf16[4,448,128]{2,1,0:T(8,128)(2,1)} collective-permute-done((bf16[4,448,128]{2,1,0:T(8,128)(2,1)}, bf16[4,448,128]{2,1,0:T(8,128)(2,1)}, u32[]{:S(2)}, u32[]{:S(2)}) %collective-permute-start.3) | collective-permute-done | bytes 458784 | tf_op jit(solution)/shard_map/ppermute | solution.py:572
  33.9 3.0 %collective-permute-start.9 = (bf16[1,448,128]{2,1,0:T(8,128)(2,1)S(1)}, bf16[1,448,128]{2,1,0:T(8,128)(2,1)S(1)}, u32[]{:S(2)}, u32[]{:S(2)}) collective-permute-start(bf16[1,448,128]{2,1,0:T(8,128)(2,1)S(1)} %maximum_bitcast_fusion.1), channel_id=1, source_target_pairs={{0,24},{1,25},{2,26},{3,27},{4,28},{5,29},{6,30},{7,31},{8,16},{9,... | collective-permute-start | bytes 344072 | tf_op jit(solution)/shard_map/ppermute | solution.py:572
  38.3 4.0 %collective-permute-start.6 = (bf16[3,40,512]{2,1,0:T(8,128)(2,1)S(1)}, bf16[3,40,512]{2,1,0:T(8,128)(2,1)S(1)}, u32[]{:S(2)}, u32[]{:S(2)}) collective-permute-start(bf16[3,40,512]{2,1,0:T(8,128)(2,1)S(1)} %get-tuple-element.393), channel_id=1, source_target_pairs={{0,28},{4,8},{8,4},{12,16},{16,12},{20,24},{24,20},{28,0},{1,29},{... | collective-permute-start | bytes 368648 | tf_op jit(solution)/shard_map/ppermute | solution.py:639
  43.0 2.2 collective-permute-done.8
  45.2 2.7 %collective-permute-done.6 = bf16[3,40,512]{2,1,0:T(8,128)(2,1)S(1)} collective-permute-done((bf16[3,40,512]{2,1,0:T(8,128)(2,1)S(1)}, bf16[3,40,512]{2,1,0:T(8,128)(2,1)S(1)}, u32[]{:S(2)}, u32[]{:S(2)}) %collective-permute-start.6) | collective-permute-done | bytes 122912 | tf_op jit(solution)/shard_map/ppermute | solution.py:639
  55.0 11.3 %edge_forward.2 = (bf16[3,640,512]{2,1,0:T(8,128)(2,1)}, bf16[3,640,512]{2,1,0:T(8,128)(2,1)}, bf16[3,640,512]{2,1,0:T(8,128)(2,1)}, f32[3,640,1]{2,1,0:T(8,128)...) custom-call(s32[32]{0:T(128)} %add.277.order, ...), custom_call_target="tpu_custom_call" | custom-call | flops 15225323520 | bytes 19271296 | tf_op jit(solution)/shard_map/edge_forward/pallas_call | solution.py:124
  71.7 4.9 %node_pass.2 = (bf16[480,512]{1,0:T(8,128)(2,1)}, bf16[480,512]{1,0:T(8,128)(2,1)}, bf16[480,512]{1,0:T(8,128)(2,1)}, bf16[480,512]{1,0:T(8,128)(2,1)}, f32[480,...) custom-call(s32[32]{0:T(128)} %add.277.order, ...), custom_call_target="tpu_custom_call" | custom-call | flops 3019898880 | bytes 7269376 | tf_op jit(solution)/shard_map/node_pass/pallas_call | solution.py:124
  79.1 3.3 %collective-permute-start.17 = (bf16[3,40,512]{2,1,0:T(8,128)(2,1)S(1)}, bf16[3,40,512]{2,1,0:T(8,128)(2,1)S(1)}, u32[]{:S(2)}, u32[]{:S(2)}) collective-permute-start(bf16[3,40,512]{2,1,0:T(8,128)(2,1)S(1)} %get-tuple-element.390), channel_id=1, source_target_pairs={{4,0},{8,4},{12,8},{16,12},{20,16},{24,20},{28,24},{0,28},{5,1},{9... | collective-permute-start | bytes 368648 | tf_op jit(solution)/shard_map/ppermute | solution.py:628
  82.5 3.5 %collective-permute-done.16 = bf16[3,40,512]{2,1,0:T(8,128)(2,1)S(1)} collective-permute-done((bf16[3,40,512]{2,1,0:T(8,128)(2,1)S(1)}, bf16[3,40,512]{2,1,0:T(8,128)(2,1)S(1)}, u32[]{:S(2)}, u32[]{:S(2)}) %collective-permute-start.16) | collective-permute-done | bytes 122912 | tf_op jit(solution)/shard_map/ppermute | solution.py:627
  95.0 3.0 %pad_maximum_fusion.1.w1.w2 = bf16[32,256,128]{2,1,0:T(8,128)(2,1)} fusion(bf16[16,256,128]{2,1,0:T(8,128)(2,1)} %collective-permute-done.18, bf16[8,256,128]{2,1,0:T(8,128)(2,1)S(1)} %collective-permute-done.13, bf16[8,256,128]{2,1,0:T(8,128)(2,1)S(1)} %slice.313), kind=kLoop, calls=%fused_computation.2 | loop fusion | flops 2097152 | bytes 4194304 | tf_op jit(solution)/shard_map/concatenate | solution.py:583
  98.0 10.6 %edge_forward.3 = (bf16[3,640,512]{2,1,0:T(8,128)(2,1)}, bf16[3,640,512]{2,1,0:T(8,128)(2,1)}, bf16[3,640,512]{2,1,0:T(8,128)(2,1)}, f32[3,640,1]{2,1,0:T(8,128)}, bf16[3,160,512]{2,1,0:T(8,128)(2,1)}) custom-call(s32[32]{0:T(128)} %add.277.order, bf16[32,256,128]{2,1,0:T(8,128)(2,1)} %pad_maximum_fusion.1.w1.w2, ...), custom_call_target="tpu_custom_call" | custom-call | flops 15225323520 | bytes 17960576 | tf_op jit(solution)/shard_map/edge_forward/pallas_call | solution.py:124
  114.4 8.1 %node_pass.3 = (bf16[3,160,512]{2,1,0:T(8,128)(2,1)}, bf16[3,160,512]{2,1,0:T(8,128)(2,1)}, f32[3,160,512]{2,1,0:T(8,128)}, bf16[16,192,128]{2,1,0:T(8,128)(2,1)...) custom-call(s32[32]{0:T(128)} %add.277.order, s32[64]{0:T(128)} %reshape.344.rest_0_.owners, ...), custom_call_target="tpu_custom_call" | custom-call | flops 9059696640 | bytes 8087820 | tf_op jit(solution)/shard_map/node_pass/pallas_call | solution.py:124
  124.7 12.7 %edge_backward.2 = (bf16[3,640,512]{2,1,0:T(8,128)(2,1)}, bf16[3,640,512]{2,1,0:T(8,128)(2,1)}, bf16[3,400,512]{2,1,0:T(8,128)(2,1)}, f32[3,160,512]{2,1,0:T(8,1...) custom-call(s32[32]{0:T(128)} %add.277.order, ...), custom_call_target="tpu_custom_call" | custom-call | flops 14344519680 | bytes 19674752 | tf_op jit(solution)/shard_map/edge_backward/pallas_call | solution.py:124
  138.4 3.4 %collective-permute-start.26 = (bf16[3,40,512]{2,1,0:T(8,128)(2,1)S(1)}, bf16[3,40,512]{2,1,0:T(8,128)(2,1)S(1)}, u32[]{:S(2)}, u32[]{:S(2)}) collective-permute-start(bf16[3,40,512]{2,1,0:T(8,128)(2,1)S(1)} %get-tuple-element.385), channel_id=1, source_target_pairs={{0,28},{4,8},{8,4},{12,16},{16,12},{20,24},{24,20},{28,0},{1,29},{... | collective-permute-start | bytes 368648 | tf_op jit(solution)/shard_map/ppermute | solution.py:639
  141.9 9.8 %edge_weight_grads.2 = (bf16[16,448,128]{2,1,0:T(8,128)(2,1)}, bf16[16,448,128]{2,1,0:T(8,128)(2,1)}) custom-call(s32[64]{0:T(128)} %reshape.344.rest_0_.owners, bf16[3,640,512]{2,1,0:T(8,128)(2,1)} %get-tuple-element.170.low.edge_low, bf16[3,240,512]{2,1,0:T(8,128)(2,1)} %copy-done.30, bf16[3,640,512]{2,1,0:T(8,128)(2,1)} %get-tuple-element.189.hidden_low, ...), custom_call_target="tpu_custom_call" | custom-call | flops 8053063680 | bytes 15073536 | tf_op jit(solution)/shard_map/edge_weight_grads/pallas_call | solution.py:124
  159.0 7.9 %node_backward.1 = (bf16[3,160,512]{2,1,0:T(8,128)(2,1)}, f32[3,160,512]{2,1,0:T(8,128)}, bf16[16,192,128]{2,1,0:T(8,128)(2,1)}, bf16[16,192,128]{2,1,0:T(8,128)(2,1)}, f32[4,512]{1,0:T(4,128)}) custom-call(s32[32]{0:T(128)} %add.277.order, s32[64]{0:T(128)} %reshape.344.rest_0_.owners, bf16[32,192,128]{2,1,0:T(8,128)(2,1)} %constant_dynamic-update-slice_fusion.10.rest_0_.w, ...), custom_call_target="tpu_custom_call" | custom-call | flops 6039797760 | bytes 9564288 | tf_op jit(solution)/shard_map/node_backward/pallas_call | solution.py:124
  168.5 14.1 %edge_backward.3 = (bf16[3,640,512]{2,1,0:T(8,128)(2,1)}, bf16[3,640,512]{2,1,0:T(8,128)(2,1)}, bf16[3,400,512]{2,1,0:T(8,128)(2,1)}, f32[3,160,512]{2,1,0:T(8,1...) custom-call(s32[32]{0:T(128)} %add.277.order, ...), custom_call_target="tpu_custom_call" | custom-call | flops 14344519680 | bytes 21640832 | tf_op jit(solution)/shard_map/edge_backward/pallas_call | solution.py:124
  186.6 3.6 %collective-permute-done.29 = bf16[8,448,128]{2,1,0:T(8,128)(2,1)S(1)} collective-permute-done((bf16[8,448,128]{2,1,0:T(8,128)(2,1)S(1)}, bf16[8,448,128]{2,1,0:T(8,128)(2,1)S(1)}, u32[]{:S(2)}, u32[]{:S(2)}) %collective-permute-start.29) | collective-permute-done | bytes 917536 | tf_op jit(solution)/shard_map/ppermute | solution.py:572
  190.5 2.1 collective-permute-start.31
  192.6 7.8 %edge_weight_grads.3 = (bf16[16,256,128]{2,1,0:T(8,128)(2,1)}, bf16[16,256,128]{2,1,0:T(8,128)(2,1)}) custom-call(s32[64]{0:T(128)} %reshape.344.rest_0_.owners, bf16[640,512]{1,0:T(8,128)(2,1)} %bitcast.163, bf16[3,240,512]{2,1,0:T(8,128)(2,1)} %pad_maximum_fusion.8.table, bf16[640,512]{1,0:T(8,128)(2,1)} %get-tuple-element.212.hidden_low, ...), custom_call_target="tpu_custom_call" | custom-call | flops 8053063680 | bytes 9306368 | tf_op jit(solution)/shard_map/edge_weight_grads/pallas_call | solution.py:124
  200.4 2.1 collective-permute-done.31
  210.6 2.6 collective-permute-done.38
  216.1 2.6 collective-permute-start.39
  219.4 3.8 %collective-permute-done.41 = bf16[1,640,128]{2,1,0:T(8,128)(2,1)S(1)} collective-permute-done((bf16[1,640,128]{2,1,0:T(8,128)(2,1)S(1)}, bf16[1,640,128]{2,1,0:T(8,128)(2,1)S(1)}, u32[]{:S(2)}, u32[]{:S(2)}) %collective-permute-start.41) | collective-permute-done | bytes 163872 | tf_op jit(solution)/shard_map/ppermute | solution.py:572
  223.2 4.5 %collective-permute-done.40 = bf16[1,640,128]{2,1,0:T(8,128)(2,1)S(1)} collective-permute-done((bf16[1,640,128]{2,1,0:T(8,128)(2,1)S(1)}, bf16[1,640,128]{2,1,0:T(8,128)(2,1)S(1)}, u32[]{:S(2)}, u32[]{:S(2)}) %collective-permute-start.40) | collective-permute-done | bytes 163872 | tf_op jit(solution)/shard_map/ppermute | solution.py:572
  227.7 3.8 %collective-permute-done.39 = bf16[1,640,128]{2,1,0:T(8,128)(2,1)S(1)} collective-permute-done((bf16[1,640,128]{2,1,0:T(8,128)(2,1)S(1)}, bf16[1,640,128]{2,1,0:T(8,128)(2,1)S(1)}, u32[]{:S(2)}, u32[]{:S(2)}) %collective-permute-start.39) | collective-permute-done | bytes 163872 | tf_op jit(solution)/shard_map/ppermute | solution.py:572
  235.6 4.2 %collective-permute-done.42 = bf16[4,256,128]{2,1,0:T(8,128)(2,1)S(1)} collective-permute-done((bf16[4,256,128]{2,1,0:T(8,128)(2,1)S(1)}, bf16[4,256,128]{2,1,0:T(8,128)(2,1)S(1)}, u32[]{:S(2)}, u32[]{:S(2)}) %collective-permute-start.42) | collective-permute-done | bytes 262176 | tf_op jit(solution)/shard_map/ppermute | solution.py:572
  244.0 2.4 collective-permute-done.43
  261.3 2.3 collective-permute-start.52
  (389 shorter events, 104.0 us)
Async XLA Ops:
  3.5 9.2 %collective-permute-start.2 = (bf16[1,448,128]{2,1,0:T(8,128)(2,1)S(1)}, bf16[1,448,128]{2,1,0:T(8,128)(2,1)S(1)}, u32[]{:S(2)}, u32[]{:S(2)}) collective-permute-start(bf16[1,448,128]{2,1,0:T(8,128)(2,1)S(1)} %maximum_bitcast_fusion), channel_id=1, source_target_pairs={{0,24},{1,25},{2,26},{3,27},{4,28},{5,29},{6,30},{7,31},{8,16},{9,... | collective-permute-start | bytes 344072 | tf_op jit(solution)/shard_map/ppermute | solution.py:572
  8.7 9.7 %collective-permute-start = (bf16[1,448,128]{2,1,0:T(8,128)(2,1)S(1)}, bf16[1,448,128]{2,1,0:T(8,128)(2,1)S(1)}, u32[]{:S(2)}, u32[]{:S(2)}) collective-permute-start(bf16[1,448,128]{2,1,0:T(8,128)(2,1)S(1)} %maximum_bitcast_fusion), channel_id=1, source_target_pairs={{0,16},{1,17},{2,18},{3,19},{4,20},{5,21},{6,22},{7,23},{8,24},{9,... | collective-permute-start | bytes 344072 | tf_op jit(solution)/shard_map/ppermute | solution.py:572
  19.2 11.9 %collective-permute-start.3 = (bf16[4,448,128]{2,1,0:T(8,128)(2,1)}, bf16[4,448,128]{2,1,0:T(8,128)(2,1)}, u32[]{:S(2)}, u32[]{:S(2)}) collective-permute-start(bf16[4,448,128]{2,1,0:T(8,128)(2,1)} %pad_maximum_fusion.12), channel_id=1, source_target_pairs={{0,4},{1,5},{2,6},{3,7},{4,0},{5,1},{6,2},{7,3},{8,12},{9,13},{10,... | collective-permute-start | bytes 1376264 | tf_op jit(solution)/shard_map/ppermute | solution.py:572
  32.2 16.3 %collective-permute-start.4 = (bf16[8,256,128]{2,1,0:T(8,128)(2,1)S(1)}, bf16[8,256,128]{2,1,0:T(8,128)(2,1)S(1)}, u32[]{:S(2)}, u32[]{:S(2)}) collective-permute-start(bf16[8,256,128]{2,1,0:T(8,128)(2,1)S(1)} %slice.311), channel_id=1, source_target_pairs={{0,2},{1,3},{2,0},{3,1},{4,6},{5,7},{6,4},{7,5},{8,10},{9,11},{10,... | collective-permute-start | bytes 1572872 | tf_op jit(solution)/shard_map/ppermute | solution.py:572
  33.9 8.4 %collective-permute-start.9 = (bf16[1,448,128]{2,1,0:T(8,128)(2,1)S(1)}, bf16[1,448,128]{2,1,0:T(8,128)(2,1)S(1)}, u32[]{:S(2)}, u32[]{:S(2)}) collective-permute-start(bf16[1,448,128]{2,1,0:T(8,128)(2,1)S(1)} %maximum_bitcast_fusion.1), channel_id=1, source_target_pairs={{0,24},{1,25},{2,26},{3,27},{4,28},{5,29},{6,30},{7,31},{8,16},{9,... | collective-permute-start | bytes 344072 | tf_op jit(solution)/shard_map/ppermute | solution.py:572
  36.9 8.3 %collective-permute-start.8 = (bf16[1,448,128]{2,1,0:T(8,128)(2,1)S(1)}, bf16[1,448,128]{2,1,0:T(8,128)(2,1)S(1)}, u32[]{:S(2)}, u32[]{:S(2)}) collective-permute-start(bf16[1,448,128]{2,1,0:T(8,128)(2,1)S(1)} %maximum_bitcast_fusion.1), channel_id=1, source_target_pairs={{0,8},{1,9},{2,10},{3,11},{4,12},{5,13},{6,14},{7,15},{8,0},{9,1},... | collective-permute-start | bytes 344072 | tf_op jit(solution)/shard_map/ppermute | solution.py:572
  36.9 8.3 %collective-permute-start.7 = (bf16[1,448,128]{2,1,0:T(8,128)(2,1)S(1)}, bf16[1,448,128]{2,1,0:T(8,128)(2,1)S(1)}, u32[]{:S(2)}, u32[]{:S(2)}) collective-permute-start(bf16[1,448,128]{2,1,0:T(8,128)(2,1)S(1)} %maximum_bitcast_fusion.1), channel_id=1, source_target_pairs={{0,16},{1,17},{2,18},{3,19},{4,20},{5,21},{6,22},{7,23},{8,24},{9,... | collective-permute-start | bytes 344072 | tf_op jit(solution)/shard_map/ppermute | solution.py:572
  38.3 9.6 %collective-permute-start.6 = (bf16[3,40,512]{2,1,0:T(8,128)(2,1)S(1)}, bf16[3,40,512]{2,1,0:T(8,128)(2,1)S(1)}, u32[]{:S(2)}, u32[]{:S(2)}) collective-permute-start(bf16[3,40,512]{2,1,0:T(8,128)(2,1)S(1)} %get-tuple-element.393), channel_id=1, source_target_pairs={{0,28},{4,8},{8,4},{12,16},{16,12},{20,24},{24,20},{28,0},{1,29},{... | collective-permute-start | bytes 368648 | tf_op jit(solution)/shard_map/ppermute | solution.py:639
  51.3 15.0 %collective-permute-start.12 = (bf16[4,448,128]{2,1,0:T(8,128)(2,1)S(1)}, bf16[4,448,128]{2,1,0:T(8,128)(2,1)S(1)}, u32[]{:S(2)}, u32[]{:S(2)}) collective-permute-start(bf16[4,448,128]{2,1,0:T(8,128)(2,1)S(1)} %pad_maximum_fusion.13), channel_id=1, source_target_pairs={{0,4},{1,5},{2,6},{3,7},{4,0},{5,1},{6,2},{7,3},{8,12},{9,13},{10,... | collective-permute-start | bytes 1376264 | tf_op jit(solution)/shard_map/ppermute | solution.py:572
  52.0 14.3 %collective-permute-start.11 = (bf16[8,192,128]{2,1,0:T(8,128)(2,1)S(1)}, bf16[8,192,128]{2,1,0:T(8,128)(2,1)S(1)}, u32[]{:S(2)}, u32[]{:S(2)}) collective-permute-start(bf16[8,192,128]{2,1,0:T(8,128)(2,1)S(1)} %slice.312), channel_id=1, source_target_pairs={{0,2},{1,3},{2,0},{3,1},{4,6},{5,7},{6,4},{7,5},{8,10},{9,11},{10,... | collective-permute-start | bytes 1179656 | tf_op jit(solution)/shard_map/ppermute | solution.py:572
  68.3 19.4 %collective-permute-start.13 = (bf16[8,256,128]{2,1,0:T(8,128)(2,1)S(1)}, bf16[8,256,128]{2,1,0:T(8,128)(2,1)S(1)}, u32[]{:S(2)}, u32[]{:S(2)}) collective-permute-start(bf16[8,256,128]{2,1,0:T(8,128)(2,1)S(1)} %slice.313), channel_id=1, source_target_pairs={{0,2},{1,3},{2,0},{3,1},{4,6},{5,7},{6,4},{7,5},{8,10},{9,11},{10,... | collective-permute-start | bytes 1572872 | tf_op jit(solution)/shard_map/ppermute | solution.py:572
  77.7 8.3 %collective-permute-start.16 = (bf16[3,40,512]{2,1,0:T(8,128)(2,1)S(1)}, bf16[3,40,512]{2,1,0:T(8,128)(2,1)S(1)}, u32[]{:S(2)}, u32[]{:S(2)}) collective-permute-start(bf16[3,40,512]{2,1,0:T(8,128)(2,1)S(1)} %get-tuple-element.389), channel_id=1, source_target_pairs={{0,4},{4,8},{8,12},{12,16},{16,20},{20,24},{24,28},{28,0},{1,5},{5... | collective-permute-start | bytes 368648 | tf_op jit(solution)/shard_map/ppermute | solution.py:627
  79.1 7.8 %collective-permute-start.17 = (bf16[3,40,512]{2,1,0:T(8,128)(2,1)S(1)}, bf16[3,40,512]{2,1,0:T(8,128)(2,1)S(1)}, u32[]{:S(2)}, u32[]{:S(2)}) collective-permute-start(bf16[3,40,512]{2,1,0:T(8,128)(2,1)S(1)} %get-tuple-element.390), channel_id=1, source_target_pairs={{4,0},{8,4},{12,8},{16,12},{20,16},{24,20},{28,24},{0,28},{5,1},{9... | collective-permute-start | bytes 368648 | tf_op jit(solution)/shard_map/ppermute | solution.py:628
  91.8 16.8 %collective-permute-start.20 = (bf16[40,3,512]{2,0,1:T(8,128)(2,1)S(1)}, bf16[40,3,512]{2,0,1:T(8,128)(2,1)S(1)}, u32[]{:S(2)}, u32[]{:S(2)}) collective-permute-start(bf16[40,3,512]{2,0,1:T(8,128)(2,1)S(1)} %constant_dynamic-slice_fusion), channel_id=1, source_target_pairs={{0,2},{1,3},{2,0},{3,1},{4,6},{5,7},{6,4},{7,5},{8,10},{9,11},{10,... | collective-permute-start | bytes 368648 | tf_op jit(solution)/shard_map/ppermute | solution.py:509
  92.4 16.2 %collective-permute-start.19 = (bf16[8,192,128]{2,1,0:T(8,128)(2,1)S(1)}, bf16[8,192,128]{2,1,0:T(8,128)(2,1)S(1)}, u32[]{:S(2)}, u32[]{:S(2)}) collective-permute-start(bf16[8,192,128]{2,1,0:T(8,128)(2,1)S(1)} %slice.314), channel_id=1, source_target_pairs={{0,2},{1,3},{2,0},{3,1},{4,6},{5,7},{6,4},{7,5},{8,10},{9,11},{10,... | collective-permute-start | bytes 1179656 | tf_op jit(solution)/shard_map/ppermute | solution.py:572
  124.2 17.7 %collective-permute-start.24 = (bf16[40,3,512]{2,0,1:T(8,128)(2,1)S(1)}, bf16[40,3,512]{2,0,1:T(8,128)(2,1)S(1)}, u32[]{:S(2)}, u32[]{:S(2)}) collective-permute-start(bf16[40,3,512]{2,0,1:T(8,128)(2,1)S(1)} %get-tuple-element.363), channel_id=1, source_target_pairs={{0,2},{1,3},{2,0},{3,1},{4,6},{5,7},{6,4},{7,5},{8,10},{9,11},{10,... | collective-permute-start | bytes 368648 | tf_op jit(solution)/shard_map/ppermute | solution.py:509
  138.4 13.3 %collective-permute-start.26 = (bf16[3,40,512]{2,1,0:T(8,128)(2,1)S(1)}, bf16[3,40,512]{2,1,0:T(8,128)(2,1)S(1)}, u32[]{:S(2)}, u32[]{:S(2)}) collective-permute-start(bf16[3,40,512]{2,1,0:T(8,128)(2,1)S(1)} %get-tuple-element.385), channel_id=1, source_target_pairs={{0,28},{4,8},{8,4},{12,16},{16,12},{20,24},{24,20},{28,0},{1,29},{... | collective-permute-start | bytes 368648 | tf_op jit(solution)/shard_map/ppermute | solution.py:639
  141.9 9.9 %collective-permute-start.25 = (bf16[3,40,512]{2,1,0:T(8,128)(2,1)S(1)}, bf16[3,40,512]{2,1,0:T(8,128)(2,1)S(1)}, u32[]{:S(2)}, u32[]{:S(2)}) collective-permute-start(bf16[3,40,512]{2,1,0:T(8,128)(2,1)S(1)} %get-tuple-element.386), channel_id=1, source_target_pairs={{0,4},{4,0},{8,12},{12,8},{16,20},{20,16},{24,28},{28,24},{1,5},{5... | collective-permute-start | bytes 368648 | tf_op jit(solution)/shard_map/ppermute | solution.py:638
  166.9 19.0 %collective-permute-start.30 = (bf16[16,192,128]{2,1,0:T(8,128)(2,1)}, bf16[16,192,128]{2,1,0:T(8,128)(2,1)S(1)}, u32[]{:S(2)}, u32[]{:S(2)}) collective-permute-start(bf16[16,192,128]{2,1,0:T(8,128)(2,1)} %get-tuple-element.219), channel_id=1, source_target_pairs={{0,1},{1,0},{2,3},{3,2},{4,5},{5,4},{6,7},{7,6},{8,9},{9,8},{10,11... | collective-permute-start | bytes 2359304 | tf_op jit(solution)/shard_map/ppermute | solution.py:572
  167.0 23.2 %collective-permute-start.29 = (bf16[8,448,128]{2,1,0:T(8,128)(2,1)S(1)}, bf16[8,448,128]{2,1,0:T(8,128)(2,1)S(1)}, u32[]{:S(2)}, u32[]{:S(2)}) collective-permute-start(bf16[8,448,128]{2,1,0:T(8,128)(2,1)S(1)} %slice.447), channel_id=1, source_target_pairs={{0,2},{1,3},{2,0},{3,1},{4,6},{5,7},{6,4},{7,5},{8,10},{9,11},{10,... | collective-permute-start | bytes 2752520 | tf_op jit(solution)/shard_map/ppermute | solution.py:572
  183.7 16.7 %collective-permute-start.34 = (bf16[3,40,512]{2,1,0:T(8,128)(2,1)S(1)}, bf16[3,40,512]{2,1,0:T(8,128)(2,1)S(1)}, u32[]{:S(2)}, u32[]{:S(2)}) collective-permute-start(bf16[3,40,512]{2,1,0:T(8,128)(2,1)S(1)} %get-tuple-element.381), channel_id=1, source_target_pairs={{0,28},{4,8},{8,4},{12,16},{16,12},{20,24},{24,20},{28,0},{1,29},{... | collective-permute-start | bytes 368648 | tf_op jit(solution)/shard_map/ppermute | solution.py:639
  185.0 15.3 %collective-permute-start.33 = (bf16[3,40,512]{2,1,0:T(8,128)(2,1)S(1)}, bf16[3,40,512]{2,1,0:T(8,128)(2,1)S(1)}, u32[]{:S(2)}, u32[]{:S(2)}) collective-permute-start(bf16[3,40,512]{2,1,0:T(8,128)(2,1)S(1)} %get-tuple-element.382), channel_id=1, source_target_pairs={{0,4},{4,0},{8,12},{12,8},{16,20},{20,16},{24,28},{28,24},{1,5},{5... | collective-permute-start | bytes 368648 | tf_op jit(solution)/shard_map/ppermute | solution.py:638
  186.1 14.3 %collective-permute-start.32 = (bf16[8,192,128]{2,1,0:T(8,128)(2,1)S(1)}, bf16[8,192,128]{2,1,0:T(8,128)(2,1)S(1)}, u32[]{:S(2)}, u32[]{:S(2)}) collective-permute-start(bf16[8,192,128]{2,1,0:T(8,128)(2,1)S(1)} %slice.450), channel_id=1, source_target_pairs={{0,2},{1,3},{2,0},{3,1},{4,6},{5,7},{6,4},{7,5},{8,10},{9,11},{10,... | collective-permute-start | bytes 1179656 | tf_op jit(solution)/shard_map/ppermute | solution.py:572
  190.5 12.0 %collective-permute-start.31 = (bf16[4,448,128]{2,1,0:T(8,128)(2,1)S(1)}, bf16[4,448,128]{2,1,0:T(8,128)(2,1)S(1)}, u32[]{:S(2)}, u32[]{:S(2)}) collective-permute-start(bf16[4,448,128]{2,1,0:T(8,128)(2,1)S(1)} %slice.449), channel_id=1, source_target_pairs={{0,4},{1,5},{2,6},{3,7},{4,0},{5,1},{6,2},{7,3},{8,12},{9,13},{10,... | collective-permute-start | bytes 1376264 | tf_op jit(solution)/shard_map/ppermute | solution.py:572
  205.8 7.4 %collective-permute-start.38 = (bf16[4,192,128]{2,1,0:T(8,128)(2,1)S(1)}, bf16[4,192,128]{2,1,0:T(8,128)(2,1)S(1)}, u32[]{:S(2)}, u32[]{:S(2)}) collective-permute-start(bf16[4,192,128]{2,1,0:T(8,128)(2,1)S(1)} %slice.452), channel_id=1, source_target_pairs={{0,4},{1,5},{2,6},{3,7},{4,0},{5,1},{6,2},{7,3},{8,12},{9,13},{10,... | collective-permute-start | bytes 589832 | tf_op jit(solution)/shard_map/ppermute | solution.py:572
  209.0 22.6 %collective-permute-start.36 = (bf16[8,256,128]{2,1,0:T(8,128)(2,1)S(1)}, bf16[8,256,128]{2,1,0:T(8,128)(2,1)S(1)}, u32[]{:S(2)}, u32[]{:S(2)}) collective-permute-start(bf16[8,256,128]{2,1,0:T(8,128)(2,1)S(1)} %slice.448), channel_id=1, source_target_pairs={{0,2},{1,3},{2,0},{3,1},{4,6},{5,7},{6,4},{7,5},{8,10},{9,11},{10,... | collective-permute-start | bytes 1572872 | tf_op jit(solution)/shard_map/ppermute | solution.py:572
  214.0 17.6 %collective-permute-start.37 = (bf16[3,160,512]{2,1,0:T(8,128)(2,1)S(1)}, bf16[3,160,512]{2,1,0:T(8,128)(2,1)S(1)}, u32[]{:S(2)}, u32[]{:S(2)}) collective-permute-start(bf16[3,160,512]{2,1,0:T(8,128)(2,1)S(1)} %get-tuple-element.354), channel_id=1, source_target_pairs={{0,1},{1,0},{2,3},{3,2},{4,5},{5,4},{6,7},{7,6},{8,9},{9,8},{10,11... | collective-permute-start | bytes 1474568 | tf_op jit(solution)/shard_map/ppermute | solution.py:509
  214.2 9.0 %collective-permute-start.41 = (bf16[1,640,128]{2,1,0:T(8,128)(2,1)S(1)}, bf16[1,640,128]{2,1,0:T(8,128)(2,1)S(1)}, u32[]{:S(2)}, u32[]{:S(2)}) collective-permute-start(bf16[1,640,128]{2,1,0:T(8,128)(2,1)S(1)} %get-tuple-element.358), channel_id=1, source_target_pairs={{0,24},{1,25},{2,26},{3,27},{4,28},{5,29},{6,30},{7,31},{8,16},{9,... | collective-permute-start | bytes 491528 | tf_op jit(solution)/shard_map/ppermute | solution.py:572
  216.1 11.6 %collective-permute-start.40 = (bf16[1,640,128]{2,1,0:T(8,128)(2,1)S(1)}, bf16[1,640,128]{2,1,0:T(8,128)(2,1)S(1)}, u32[]{:S(2)}, u32[]{:S(2)}) collective-permute-start(bf16[1,640,128]{2,1,0:T(8,128)(2,1)S(1)} %get-tuple-element.359), channel_id=1, source_target_pairs={{0,8},{1,9},{2,10},{3,11},{4,12},{5,13},{6,14},{7,15},{8,0},{9,1},... | collective-permute-start | bytes 491528 | tf_op jit(solution)/shard_map/ppermute | solution.py:572
  216.1 15.5 %collective-permute-start.39 = (bf16[1,640,128]{2,1,0:T(8,128)(2,1)S(1)}, bf16[1,640,128]{2,1,0:T(8,128)(2,1)S(1)}, u32[]{:S(2)}, u32[]{:S(2)}) collective-permute-start(bf16[1,640,128]{2,1,0:T(8,128)(2,1)S(1)} %get-tuple-element.360), channel_id=1, source_target_pairs={{0,16},{1,17},{2,18},{3,19},{4,20},{5,21},{6,22},{7,23},{8,24},{9,... | collective-permute-start | bytes 491528 | tf_op jit(solution)/shard_map/ppermute | solution.py:572
  231.9 7.9 %collective-permute-start.42 = (bf16[4,256,128]{2,1,0:T(8,128)(2,1)S(1)}, bf16[4,256,128]{2,1,0:T(8,128)(2,1)S(1)}, u32[]{:S(2)}, u32[]{:S(2)}) collective-permute-start(bf16[4,256,128]{2,1,0:T(8,128)(2,1)S(1)} %slice.451), channel_id=1, source_target_pairs={{0,4},{1,5},{2,6},{3,7},{4,0},{5,1},{6,2},{7,3},{8,12},{9,13},{10,... | collective-permute-start | bytes 786440 | tf_op jit(solution)/shard_map/ppermute | solution.py:572
  233.2 15.3 %collective-permute-start.46 = (bf16[320,512]{1,0:T(8,128)(2,1)S(1)}, bf16[320,512]{1,0:T(8,128)(2,1)S(1)}, u32[]{:S(2)}, u32[]{:S(2)}) collective-permute-start(bf16[320,512]{1,0:T(8,128)(2,1)S(1)} %fusion.7), channel_id=1, source_target_pairs={{0,2},{1,3},{2,0},{3,1},{4,6},{5,7},{6,4},{7,5},{8,10},{9,11},{10,... | collective-permute-start | bytes 983048 | tf_op jit(solution)/shard_map/ppermute | solution.py:509
  (97 other events, 833.3 us)

commit v7 on v6

--- a/solution.py
+++ b/solution.py
@@ -60,13 +60,18 @@
 
 
 def assemble(source, order, rows, offset, target):
-    width = source.shape[2]
+    own, arrived = source
+    half, _, width = own.shape
     nodes, hids = target.shape[0] // rows, target.shape[1] // width
     for i in range(nodes):
         for j in range(hids):
-            target[i * rows : (i + 1) * rows, j * width : (j + 1) * width] = source[
-                order[i * hids + j], offset : offset + rows, :
-            ]
+            place = order[i * hids + j]
+            index = jnp.where(place < half, place, place - half)
+            target[i * rows : (i + 1) * rows, j * width : (j + 1) * width] = jnp.where(
+                place < half,
+                own[index, offset : offset + rows, :],
+                arrived[index, offset : offset + rows, :],
+            )
 
 
 def store(target, begin, values):
@@ -104,9 +109,9 @@
     return pl.BlockSpec(array.shape, lambda s: (0,) * len(array.shape))
 
 
-def weight_block(array, rows, place):
-    blocks, _, width = array.shape
-    return pl.BlockSpec((blocks, rows, width), lambda s: (0, place, 0))
+def weight_blocks(halves, rows, place):
+    blocks, _, width = halves[0].shape
+    return [pl.BlockSpec((blocks, rows, width), lambda s: (0, place, 0)) for _ in halves]
 
 
 def in_scalars():
@@ -151,7 +156,7 @@
     edges = edge_low.shape[1]
     alike = edge_low.shape[0] == 1
 
-    def kernel(order, w1, w2, table, low, state, both, nodes, params, pre, act, normed, inverse, *rest):
+    def kernel(order, w1, w1x, w2, w2x, table, low, state, both, nodes, params, pre, act, normed, inverse, *rest):
         if last:
             pooled, w1s, w2s, projected = rest
         else:
@@ -159,8 +164,8 @@
 
         @pl.when(pl.program_id(0) == 0)
         def _():
-            assemble(w1, order, w1.shape[1], 0, w1s)
-            assemble(w2, order, w2.shape[1], 0, w2s)
+            assemble((w1, w1x), order, w1.shape[1], 0, w1s)
+            assemble((w2, w2x), order, w2.shape[1], 0, w2s)
 
         rows = table[0]
         projected[:table_total] = matmul(rows, w1s[latent : 2 * latent]).astype(BF16)
@@ -190,11 +195,11 @@
         kernel,
         "edge_forward",
         samples,
-        [order, first[0], second[0], table, edge_low, edge_state, at_both, at_nodes, params],
+        [order, *first[0], *second[0], table, edge_low, edge_state, at_both, at_nodes, params],
         [
             in_scalars(),
-            weight_block(*first),
-            weight_block(*second),
+            *weight_blocks(*first),
+            *weight_blocks(*second),
             per_sample(table),
             of_edges(edge_low),
             of_edges(edge_state),
@@ -217,7 +222,7 @@
     at_total = at_both_t.shape[0]
     table_total = at_total - node_total
 
-    def kernel(order, w1, w2, upstream, *rest):
+    def kernel(order, w1, w1x, w2, w2x, upstream, *rest):
         if not last:
             later, rest = rest[0], rest[1:]
         normed, inverse, pre, receiver, both_t, gain, low, hidden_low, at_rows, partial, returned, grad_out, minor = rest[:13]
@@ -229,8 +234,8 @@
 
         @pl.when(step == 0)
         def _():
-            assemble(w1, order, w1.shape[1], 0, w1s)
-            assemble(w2, order, w2.shape[1], 0, w2s)
+            assemble((w1, w1x), order, w1.shape[1], 0, w1s)
+            assemble((w2, w2x), order, w2.shape[1], 0, w2s)
             minor[...] = jnp.zeros_like(minor)
 
         grad = matmul(receiver[...], upstream[0])
@@ -283,8 +288,8 @@
         shared((4, latent), F32),
     ]
     scratch = [pltpu.VMEM((3 * latent, latent), BF16), pltpu.VMEM((latent, latent), BF16)]
-    inputs = [order, first[0], second[0], pooled_grad]
-    specs = [in_scalars(), weight_block(*first), weight_block(*second), per_sample(pooled_grad)]
+    inputs = [order, *first[0], *second[0], pooled_grad]
+    specs = [in_scalars(), *weight_blocks(*first), *weight_blocks(*second), per_sample(pooled_grad)]
     if not last:
         outputs.append(shared((edges, latent), BF16))
         scratch.append(pltpu.VMEM((edges, latent), F32))
@@ -363,8 +368,9 @@
 
 def node_pass(order, owners, weights, nodes, node_low, state, pooled_pair, params, at_halo, target, scaling, mask):
     samples, node_total, latent = node_low.shape
-    array, rows, place = weights
-    second_rows, hids = latent // nodes, latent // array.shape[2]
+    halves, rows, place = weights
+    width = halves[0].shape[2]
+    second_rows, hids = latent // nodes, latent // width
     first_rows = rows - second_rows
     count = samples * node_total
     last = target is not None
@@ -372,13 +378,13 @@
     def kernel(order, *rest):
         if last:
             owners, rest = rest[0], rest[1:]
-        w, node_low, state, pooled_own, pooled_other, params, *rest = rest
+        w, wx, node_low, state, pooled_own, pooled_other, params, *rest = rest
         if last:
             target, scaling, mask, new_low, upstream, input_grad, kept, sent, minor, w1s, w2s, first, second = rest
         else:
             at_halo, pooled_out, pre, act, normed, inverse, new_state, new_low, halo, w1s, w2s = rest
-        assemble(w, order, first_rows, 0, w1s)
-        assemble(w, order, second_rows, first_rows, w2s)
+        assemble((w, wx), order, first_rows, 0, w1s)
+        assemble((w, wx), order, second_rows, first_rows, w2s)
         rows_low = node_low[...].reshape(count, latent)
         pooled = (pooled_own[...].astype(F32) + pooled_other[...].astype(F32)).astype(BF16)
         pooled = pooled.reshape(count, latent)
@@ -406,11 +412,11 @@
             )
 
     shape = node_low.shape
-    inputs = [array, node_low, state, *pooled_pair, params]
+    inputs = [*halves, node_low, state, *pooled_pair, params]
     scratch = [pltpu.VMEM((2 * latent, latent), BF16), pltpu.VMEM((latent, latent), BF16)]
     if last:
         inputs += [target, scaling, mask]
-        outputs = [shared(shape, BF16), *gradient_outputs(shape, order.shape[0], rows, array.shape[2])]
+        outputs = [shared(shape, BF16), *gradient_outputs(shape, order.shape[0], rows, width)]
         scratch += [pltpu.VMEM((hids, 2 * latent, latent // hids), F32), pltpu.VMEM((hids, latent, latent // hids), F32)]
     else:
         inputs += [at_halo]
@@ -425,7 +431,7 @@
             shared((samples, at_halo.shape[0], latent), BF16),
         ]
     tables = [order, owners] if last else [order]
-    specs = [in_scalars() for _ in tables] + [weight_block(*weights)] + [constant(a) for a in inputs[1:]]
+    specs = [in_scalars() for _ in tables] + weight_blocks(*weights) + [constant(a) for a in inputs[2:]]
     inputs = tables + inputs
     return run_kernel(kernel, "node_pass", 1, inputs, specs, outputs, scratch, 6 * count * latent * latent * (3 if last else 1))
 
@@ -467,14 +473,15 @@
 
 def node_backward(order, owners, weights, nodes, grads, node_low, pooled, pre, act, normed, inverse, params, mask):
     samples, node_total, latent = node_low.shape
-    array, rows, place = weights
-    second_rows, hids = latent // nodes, latent // array.shape[2]
+    halves, rows, place = weights
+    width = halves[0].shape[2]
+    second_rows, hids = latent // nodes, latent // width
     first_rows = rows - second_rows
     count = samples * node_total
 
-    def kernel(order, owners, w, base, own, other, node_low, pooled, pre, act, normed, inverse, params, mask, upstream, input_grad, kept, sent, minor, w1s, w2s, first, second):
-        assemble(w, order, first_rows, 0, w1s)
-        assemble(w, order, second_rows, first_rows, w2s)
+    def kernel(order, owners, w, wx, base, own, other, node_low, pooled, pre, act, normed, inverse, params, mask, upstream, input_grad, kept, sent, minor, w1s, w2s, first, second):
+        assemble((w, wx), order, first_rows, 0, w1s)
+        assemble((w, wx), order, second_rows, first_rows, w2s)
         grad = (base[...] + (own[...] + other[...].astype(F32))).reshape(count, latent)
         node_gradients(
             grad, normed[...].astype(F32), inverse[...], pre[...].astype(F32), act[...],
@@ -482,15 +489,15 @@
             w1s, w2s, first, second, upstream, input_grad, kept, sent, minor, owners, first_rows, second_rows,
         )
 
-    inputs = [order, owners, array, *grads, node_low, pooled, pre, act, normed, inverse, params, mask]
-    specs = [in_scalars(), in_scalars(), weight_block(*weights)] + [constant(a) for a in inputs[3:]]
+    inputs = [order, owners, *halves, *grads, node_low, pooled, pre, act, normed, inverse, params, mask]
+    specs = [in_scalars(), in_scalars(), *weight_blocks(*weights)] + [constant(a) for a in inputs[4:]]
     return run_kernel(
         kernel,
         "node_backward",
         1,
         inputs,
         specs,
-        gradient_outputs(node_low.shape, order.shape[0], rows, array.shape[2]),
+        gradient_outputs(node_low.shape, order.shape[0], rows, width),
         [
             pltpu.VMEM((2 * latent, latent), BF16),
             pltpu.VMEM((latent, latent), BF16),
@@ -786,14 +793,16 @@
     halo_rows = neighbour_swaps(after(halo_rows, halo_gate), halo_width)
     begin, end = z_rounds[-1]
     arrived = [exchange(layer_one, begin, flips) for flips in range(1, 1 << (end - begin))]
-    edge_arrived, first, second, weight_local, *arrived = lax.optimization_barrier(
-        (exchange(edge_zero, steps - 2, 1), *halo_rows, weight_local, *arrived)
-    )
+    constants = (at_receiver, at_both, at_nodes, at_both_t, at_halo, mask, order, owners)
+    edge_arrived, first, second, weight_local, constants, *arrived = lax.optimization_barrier(
+        (exchange(edge_zero, steps - 2, 1), *halo_rows, weight_local, constants, *arrived)
+    )
+    at_receiver, at_both, at_nodes, at_both_t, at_halo, mask, order, owners = constants
     halo_rows = from_neighbours(first, second)
     edge_zero = jnp.concatenate([edge_zero, edge_arrived], axis=0)
     layer_one = jnp.concatenate([layer_one, *arrived], axis=0)
     node_zero = after(node_zero, edge_zero)
-    edge_zero = gather_round(edge_zero, steps - 1, steps)
+    edge_zero = (edge_zero, exchange(edge_zero, steps - 1, 1))
     table_zero = jnp.concatenate([node_low, halo_rows], axis=1)
     pre_zero, act_zero, normed_zero, inverse_zero, edge_state, edge_low, pooled = edge_forward(
         order,
@@ -811,7 +820,7 @@
         (pooled, exchange(node_zero, steps - 2, 1), exchange(layer_one, steps - 3, 1))
     )
     node_zero = jnp.concatenate([node_zero, arrived[0]], axis=0)
-    node_zero = gather_round(node_zero, steps - 1, steps)
+    node_zero = (node_zero, exchange(node_zero, steps - 1, 1))
     layer_one = jnp.concatenate([layer_one, arrived[1]], axis=0)
     node_one, edge_one = parted(layer_one)
     other = after(swap(pooled, "hid", 1), edge_one)
@@ -842,7 +851,7 @@
     arrived, halo_rows = lax.optimization_barrier((exchange(edge_one, steps - 2, 1), halo_rows))
     edge_one = jnp.concatenate([edge_one, arrived], axis=0)
     node_one = after(node_one, edge_one)
-    edge_one = gather_round(edge_one, steps - 1, steps)
+    edge_one = (edge_one, exchange(edge_one, steps - 1, 1))
 
     valid_mask = (ocean_mask[:, None] * present_mask).astype(BF16)
     masked = after(cotangent, pooled) * valid_mask[:, :, None]
@@ -872,7 +881,7 @@
     masked = jnp.stack(ordered(sample_half, own_samples(masked), cotangent_other), axis=0)
     masked = double_up(masked, "hid", 0, 1).reshape(node_total, samples, latent)
     target = jnp.transpose(masked, (1, 0, 2))
-    node_one = gather_round(node_one, steps - 1, steps)
+    node_one = (node_one, exchange(node_one, steps - 1, 1))
     node_low, pooled_grad, node_grad, kept, sent, node_minor_one = node_pass(
         order,
         owners,
@@ -988,28 +997,39 @@
     kept, sent = split(kept.astype(F32) + edge_arrived.astype(F32), 2)
     zero_arrived = after(exchange(chain_zero[1], steps - 3, 1), sent)
     returned = after(returned, sent)
-    chain_one = jnp.concatenate(
-        [chain_one, chain_zero[0].astype(F32) + zero_arrived.astype(F32)], axis=1
-    )
+    chain_zero = chain_zero[0].astype(F32) + zero_arrived.astype(F32)
     for begin, end in reversed(z_rounds[1:]):
         chain_one = scatter_round(split(chain_one, 1 << (end - begin)), begin)
+        chain_zero = scatter_round(split(chain_zero, 1 << (end - begin)), begin)
     begin, end = z_rounds[0]
     chain_one = split(chain_one, 1 << (end - begin))
+    chain_zero = split(chain_zero, 1 << (end - begin))
     partial = from_edges(partial, from_neighbours(*returned))
-    arrived, edge_input_grad, other, *others = lax.optimization_barrier(
+    arrived, edge_input_grad, other, chain_zero, *others = lax.optimization_barrier(
         (
             exchange(sent, steps - 2, 1),
             edge_input_grad,
             swap(partial.astype(BF16), "hid", 1),
+            chain_zero,
             *[exchange(chain_one[flips], begin, flips) for flips in range(1, len(chain_one))],
         )
     )
-    joined_grads = chain_one[0]
+    layer_one_grads = chain_one[0]
     for piece in others:
-        joined_grads = joined_grads + piece.astype(F32)
-    joined_grads = joined_grads[0]
+        layer_one_grads = layer_one_grads + piece.astype(F32)
+    layer_one_grads = layer_one_grads[0]
     chain_edge = split(kept + arrived.astype(F32), 2)
-    chain_edge = scatter_round(chain_edge, steps - 3)
+    arrived, *others = lax.optimization_barrier(
+        (
+            exchange(chain_edge[1], steps - 3, 1),
+            *[exchange(chain_zero[flips], begin, flips) for flips in range(1, len(chain_zero))],
+        )
+    )
+    node_zero_grads = chain_zero[0]
+    for piece in others:
+        node_zero_grads = node_zero_grads + piece.astype(F32)
+    node_zero_grads = node_zero_grads[0]
+    chain_edge = chain_edge[0] + arrived.astype(F32)
     halves = edge_input_grad.reshape(2, edge_part, latent)
     sent = lax.dynamic_index_in_dim(halves, 1 - sample_half, 0, keepdims=False).astype(BF16)
     kept = lax.dynamic_index_in_dim(halves, sample_half, 0, keepdims=False)
@@ -1022,9 +1042,6 @@
     edge_input_grad = kept + arrived.astype(F32)
     grad_node = all_samples(*grad_node)
 
-    edge_rows = first_rows + second_rows
-    layer_one_grads = joined_grads[: node_rows + edge_rows]
-    node_zero_grads = joined_grads[node_rows + edge_rows :]
     node_one_grads, edge_one_grads = layer_one_grads[:node_rows], layer_one_grads[node_rows:]
     node_first_rows = node_rows - second_rows
     grads = [

time: 273 us -> 265 us (0.971)
  waiting for transfers between devices: 59.6 us -> 50.2 us
  starting transfers between devices: 59.4 us -> 67 us
  other arithmetic: 32.4 us -> 26.4 us
    ppermute x38 -> x41, waiting for transfers between devices: 49.4 us -> 41.7 us  [exchange(): lax.ppermute(values, ('node', 'hid'), [(i, i ^ mask) for i in range(total)])]
    concatenate x4 -> x1, other arithmetic: 6.71 us -> 0.82 us  [gather_round(): return jnp.concatenate([held, *arrived], axis=0)]
    ppermute x38 -> x41, starting transfers between devices: 41.8 us -> 45.5 us  [exchange(): lax.ppermute(values, ('node', 'hid'), [(i, i ^ mask) for i in range(total)])]
    ppermute x9, starting transfers between devices: 2.79 us -> 6.53 us  [swap(): lax.ppermute(values, axis, [(i, i ^ offset) for i in range(lax.axis_size(...]
    unnamed x155 -> x171, local copies, waits for them, and re-layouts: 10.2 us -> 10.7 us
  transfers between devices with their start and end apart: 55 -> 58, of which waited for: 26 -> 28; matrix products, arithmetic and copies ran while one was open for 15% -> 11% of each run, Pallas kernels for 26% -> 27%
where the time goes in v7:
time: 265 us; the launch traced here: 264 us
  Pallas kernels  88.8 us (34%)
  starting transfers between devices  67 us (25%)
  waiting for transfers between devices  50.2 us (19%)
  local copies, waits for them, and re-layouts  27.7 us (10%)
  other arithmetic  26.4 us (10%)
  between operations  2.97 us (1%)
    pallas_call x9, Pallas kernels, run_kernel(): pl.pallas_call(kernel, name=name, grid=(samples,), in_specs=in_specs, out...  88.8 us
    ppermute x41, starting transfers between devices, exchange(): lax.ppermute(values, ('node', 'hid'), [(i, i ^ mask) for i in range(total)])  45.5 us
    ppermute x41, waiting for transfers between devices, exchange(): lax.ppermute(values, ('node', 'hid'), [(i, i ^ mask) for i in range(total)])  41.7 us
    unnamed x171, local copies, waits for them, and re-layouts  10.7 us
    ppermute x3, starting transfers between devices, neighbour_swaps(): second = lax.ppermute(jnp.where(even, to_previous, to_next), 'node', two)  8.82 us
    ppermute x9, starting transfers between devices, swap(): lax.ppermute(values, axis, [(i, i ^ offset) for i in range(lax.axis_size(...  6.53 us
  transfers between devices with their start and end apart: 58, of which 28 were waited for; matrix products, arithmetic and copies ran while one was open for 11% of the time, Pallas kernels for 27%

profile of v7, /device:TPU:0, one launch (start us, length us, event | category | flops | bytes accessed | tf_op | source)
XLA Modules:
  0.0 263.9 jit_solution(5783337257129717203)
XLA Ops:
  4.1 5.1 %collective-permute-start.2 = (bf16[1,448,128]{2,1,0:T(8,128)(2,1)S(1)}, bf16[1,448,128]{2,1,0:T(8,128)(2,1)S(1)}, u32[]{:S(2)}, u32[]{:S(2)}) collective-permute-start(bf16[1,448,128]{2,1,0:T(8,128)(2,1)S(1)} %maximum_bitcast_fusion), channel_id=1, source_target_pairs={{0,24},{1,25},{2,26},{3,27},{4,28},{5,29},{6,30},{7,31},{8,16},{9,... | collective-permute-start | bytes 344072 | tf_op jit(solution)/shard_map/ppermute | solution.py:579
  13.3 2.7 %collective-permute-done.1 = bf16[1,448,128]{2,1,0:T(8,128)(2,1)S(1)} collective-permute-done((bf16[1,448,128]{2,1,0:T(8,128)(2,1)S(1)}, bf16[1,448,128]{2,1,0:T(8,128)(2,1)S(1)}, u32[]{:S(2)}, u32[]{:S(2)}) %collective-permute-start.1) | collective-permute-done | bytes 114720 | tf_op jit(solution)/shard_map/ppermute | solution.py:579
  16.0 3.0 %collective-permute-done = bf16[1,448,128]{2,1,0:T(8,128)(2,1)S(1)} collective-permute-done((bf16[1,448,128]{2,1,0:T(8,128)(2,1)S(1)}, bf16[1,448,128]{2,1,0:T(8,128)(2,1)S(1)}, u32[]{:S(2)}, u32[]{:S(2)}) %collective-permute-start) | collective-permute-done | bytes 114720 | tf_op jit(solution)/shard_map/ppermute | solution.py:579
  25.6 7.0 %collective-permute-done.3 = bf16[4,448,128]{2,1,0:T(8,128)(2,1)} collective-permute-done((bf16[4,448,128]{2,1,0:T(8,128)(2,1)}, bf16[4,448,128]{2,1,0:T(8,128)(2,1)}, u32[]{:S(2)}, u32[]{:S(2)}) %collective-permute-start.3) | collective-permute-done | bytes 458784 | tf_op jit(solution)/shard_map/ppermute | solution.py:579
  35.4 3.0 %collective-permute-start.9 = (bf16[1,448,128]{2,1,0:T(8,128)(2,1)S(1)}, bf16[1,448,128]{2,1,0:T(8,128)(2,1)S(1)}, u32[]{:S(2)}, u32[]{:S(2)}) collective-permute-start(bf16[1,448,128]{2,1,0:T(8,128)(2,1)S(1)} %maximum_bitcast_fusion.1), channel_id=1, source_target_pairs={{0,24},{1,25},{2,26},{3,27},{4,28},{5,29},{6,30},{7,31},{8,16},{9,... | collective-permute-start | bytes 344072 | tf_op jit(solution)/shard_map/ppermute | solution.py:579
  39.8 4.0 %collective-permute-start.6 = (bf16[3,40,512]{2,1,0:T(8,128)(2,1)S(1)}, bf16[3,40,512]{2,1,0:T(8,128)(2,1)S(1)}, u32[]{:S(2)}, u32[]{:S(2)}) collective-permute-start(bf16[3,40,512]{2,1,0:T(8,128)(2,1)S(1)} %get-tuple-element.424), channel_id=1, source_target_pairs={{0,28},{4,8},{8,4},{12,16},{16,12},{20,24},{24,20},{28,0},{1,29},{... | collective-permute-start | bytes 368648 | tf_op jit(solution)/shard_map/ppermute | solution.py:646
  44.5 2.2 collective-permute-done.8
  46.7 2.7 %collective-permute-done.6 = bf16[3,40,512]{2,1,0:T(8,128)(2,1)S(1)} collective-permute-done((bf16[3,40,512]{2,1,0:T(8,128)(2,1)S(1)}, bf16[3,40,512]{2,1,0:T(8,128)(2,1)S(1)}, u32[]{:S(2)}, u32[]{:S(2)}) %collective-permute-start.6) | collective-permute-done | bytes 122912 | tf_op jit(solution)/shard_map/ppermute | solution.py:646
  55.2 11.6 %edge_forward.2 = (bf16[3,640,512]{2,1,0:T(8,128)(2,1)}, bf16[3,640,512]{2,1,0:T(8,128)(2,1)}, bf16[3,640,512]{2,1,0:T(8,128)(2,1)}, f32[3,640,1]{2,1,0:T(8,128)...) custom-call(s32[32]{0:T(128)} %add.290.order, ...), custom_call_target="tpu_custom_call" | custom-call | flops 15225323520 | bytes 19271296 | tf_op jit(solution)/shard_map/edge_forward/pallas_call | solution.py:129
  71.6 5.1 %node_pass.2 = (bf16[480,512]{1,0:T(8,128)(2,1)}, bf16[480,512]{1,0:T(8,128)(2,1)}, bf16[480,512]{1,0:T(8,128)(2,1)}, bf16[480,512]{1,0:T(8,128)(2,1)}, f32[480,...) custom-call(s32[32]{0:T(128)} %add.290.order, ...), custom_call_target="tpu_custom_call" | custom-call | flops 3019898880 | bytes 7269376 | tf_op jit(solution)/shard_map/node_pass/pallas_call | solution.py:129
  79.1 3.3 %collective-permute-start.17 = (bf16[3,40,512]{2,1,0:T(8,128)(2,1)S(1)}, bf16[3,40,512]{2,1,0:T(8,128)(2,1)S(1)}, u32[]{:S(2)}, u32[]{:S(2)}) collective-permute-start(bf16[3,40,512]{2,1,0:T(8,128)(2,1)S(1)} %get-tuple-element.421), channel_id=1, source_target_pairs={{4,0},{8,4},{12,8},{16,12},{20,16},{24,20},{28,24},{0,28},{5,1},{9... | collective-permute-start | bytes 368648 | tf_op jit(solution)/shard_map/ppermute | solution.py:635
  82.5 3.4 %collective-permute-done.16 = bf16[3,40,512]{2,1,0:T(8,128)(2,1)S(1)} collective-permute-done((bf16[3,40,512]{2,1,0:T(8,128)(2,1)S(1)}, bf16[3,40,512]{2,1,0:T(8,128)(2,1)S(1)}, u32[]{:S(2)}, u32[]{:S(2)}) %collective-permute-start.16) | collective-permute-done | bytes 122912 | tf_op jit(solution)/shard_map/ppermute | solution.py:634
  91.6 10.8 %edge_forward.3 = (bf16[3,640,512]{2,1,0:T(8,128)(2,1)}, bf16[3,640,512]{2,1,0:T(8,128)(2,1)}, bf16[3,640,512]{2,1,0:T(8,128)(2,1)}, f32[3,640,1]{2,1,0:T(8,128)}, bf16[3,160,512]{2,1,0:T(8,128)(2,1)}) custom-call(s32[32]{0:T(128)} %add.290.order, bf16[16,256,128]{2,1,0:T(8,128)(2,1)} %copy-done.11, bf16[16,256,128]{2,1,0:T(8,128)(2,1)} %collective-permute-done.18.w1x.w2x, ...), custom_call_target="tpu_custom_call" | custom-call | flops 15225323520 | bytes 17960576 | tf_op jit(solution)/shard_map/edge_forward/pallas_call | solution.py:129
  107.4 8.2 %node_pass.3 = (bf16[3,160,512]{2,1,0:T(8,128)(2,1)}, bf16[3,160,512]{2,1,0:T(8,128)(2,1)}, f32[3,160,512]{2,1,0:T(8,128)}, bf16[16,192,128]{2,1,0:T(8,128)(2,1)...) custom-call(s32[32]{0:T(128)} %add.290.order, s32[64]{0:T(128)} %reshape.341.rest_0_.owners, ...), custom_call_target="tpu_custom_call" | custom-call | flops 9059696640 | bytes 8087820 | tf_op jit(solution)/shard_map/node_pass/pallas_call | solution.py:129
  118.7 13.0 %edge_backward.2 = (bf16[3,640,512]{2,1,0:T(8,128)(2,1)}, bf16[3,640,512]{2,1,0:T(8,128)(2,1)}, bf16[3,400,512]{2,1,0:T(8,128)(2,1)}, f32[3,160,512]{2,1,0:T(8,1...) custom-call(s32[32]{0:T(128)} %add.290.order, bf16[16,256,128]{2,1,0:T(8,128)(2,1)} %copy-done.11, ...), custom_call_target="tpu_custom_call" | custom-call | flops 14344519680 | bytes 19674752 | tf_op jit(solution)/shard_map/edge_backward/pallas_call | solution.py:129
  132.7 3.5 %collective-permute-start.26 = (bf16[3,40,512]{2,1,0:T(8,128)(2,1)S(1)}, bf16[3,40,512]{2,1,0:T(8,128)(2,1)S(1)}, u32[]{:S(2)}, u32[]{:S(2)}) collective-permute-start(bf16[3,40,512]{2,1,0:T(8,128)(2,1)S(1)} %get-tuple-element.416), channel_id=1, source_target_pairs={{0,28},{4,8},{8,4},{12,16},{16,12},{20,24},{24,20},{28,0},{1,29},{... | collective-permute-start | bytes 368648 | tf_op jit(solution)/shard_map/ppermute | solution.py:646
  136.9 9.9 %edge_weight_grads.2 = (bf16[16,448,128]{2,1,0:T(8,128)(2,1)}, bf16[16,448,128]{2,1,0:T(8,128)(2,1)}) custom-call(s32[64]{0:T(128)} %reshape.341.rest_0_.owners, bf16[3,640,512]{2,1,0:T(8,128)(2,1)} %get-tuple-element.191.low.edge_low, bf16[3,240,512]{2,1,0:T(8,128)(2,1)} %copy-done.34, bf16[3,640,512]{2,1,0:T(8,128)(2,1)} %get-tuple-element.213.hidden_low, ...), custom_call_target="tpu_custom_call" | custom-call | flops 8053063680 | bytes 15073536 | tf_op jit(solution)/shard_map/edge_weight_grads/pallas_call | solution.py:129
  154.0 8.1 %node_backward.1 = (bf16[3,160,512]{2,1,0:T(8,128)(2,1)}, f32[3,160,512]{2,1,0:T(8,128)}, bf16[16,192,128]{2,1,0:T(8,128)(2,1)}, bf16[16,192,128]{2,1,0:T(8,128)(2,1)}, f32[4,512]{1,0:T(4,128)}) custom-call(s32[32]{0:T(128)} %add.290.order, s32[64]{0:T(128)} %reshape.341.rest_0_.owners, bf16[16,192,128]{2,1,0:T(8,128)(2,1)} %copy-done.43, ...), custom_call_target="tpu_custom_call" | custom-call | flops 6039797760 | bytes 9564288 | tf_op jit(solution)/shard_map/node_backward/pallas_call | solution.py:129
  162.8 14.4 %edge_backward.3 = (bf16[3,640,512]{2,1,0:T(8,128)(2,1)}, bf16[3,640,512]{2,1,0:T(8,128)(2,1)}, bf16[3,400,512]{2,1,0:T(8,128)(2,1)}, f32[3,160,512]{2,1,0:T(8,1...) custom-call(s32[32]{0:T(128)} %add.290.order, ...), custom_call_target="tpu_custom_call" | custom-call | flops 14344519680 | bytes 21640832 | tf_op jit(solution)/shard_map/edge_backward/pallas_call | solution.py:129
  182.2 3.3 %collective-permute-done.29 = bf16[8,448,128]{2,1,0:T(8,128)(2,1)S(1)} collective-permute-done((bf16[8,448,128]{2,1,0:T(8,128)(2,1)S(1)}, bf16[8,448,128]{2,1,0:T(8,128)(2,1)S(1)}, u32[]{:S(2)}, u32[]{:S(2)}) %collective-permute-start.29) | collective-permute-done | bytes 917536 | tf_op jit(solution)/shard_map/ppermute | solution.py:579
  185.8 2.1 collective-permute-start.31
  187.9 7.8 %edge_weight_grads.3 = (bf16[16,256,128]{2,1,0:T(8,128)(2,1)}, bf16[16,256,128]{2,1,0:T(8,128)(2,1)}) custom-call(s32[64]{0:T(128)} %reshape.341.rest_0_.owners, bf16[640,512]{1,0:T(8,128)(2,1)} %bitcast.164, bf16[3,240,512]{2,1,0:T(8,128)(2,1)} %pad_maximum_fusion.2.table, bf16[640,512]{1,0:T(8,128)(2,1)} %get-tuple-element.236.hidden_low, ...), custom_call_target="tpu_custom_call" | custom-call | flops 8053063680 | bytes 9306368 | tf_op jit(solution)/shard_map/edge_weight_grads/pallas_call | solution.py:129
  207.8 2.1 collective-permute-start.41
  210.0 2.3 collective-permute-start.39
  212.4 3.4 %collective-permute-done.41 = bf16[1,448,128]{2,1,0:T(8,128)(2,1)S(1)} collective-permute-done((bf16[1,448,128]{2,1,0:T(8,128)(2,1)S(1)}, bf16[1,448,128]{2,1,0:T(8,128)(2,1)S(1)}, u32[]{:S(2)}, u32[]{:S(2)}) %collective-permute-start.41) | collective-permute-done | bytes 114720 | tf_op jit(solution)/shard_map/ppermute | solution.py:579
  215.8 4.0 %collective-permute-done.40 = bf16[1,448,128]{2,1,0:T(8,128)(2,1)S(1)} collective-permute-done((bf16[1,448,128]{2,1,0:T(8,128)(2,1)S(1)}, bf16[1,448,128]{2,1,0:T(8,128)(2,1)S(1)}, u32[]{:S(2)}, u32[]{:S(2)}) %collective-permute-start.40) | collective-permute-done | bytes 114720 | tf_op jit(solution)/shard_map/ppermute | solution.py:579
  222.9 2.5 collective-permute-start.45
  228.8 3.6 %collective-permute-done.42 = bf16[4,256,128]{2,1,0:T(8,128)(2,1)S(1)} collective-permute-done((bf16[4,256,128]{2,1,0:T(8,128)(2,1)S(1)}, bf16[4,256,128]{2,1,0:T(8,128)(2,1)S(1)}, u32[]{:S(2)}, u32[]{:S(2)}) %collective-permute-start.42) | collective-permute-done | bytes 262176 | tf_op jit(solution)/shard_map/ppermute | solution.py:579
  233.4 2.2 collective-permute-start.48
  236.7 1.9 collective-permute-done.46
  251.2 2.1 collective-permute-start.57
  253.4 2.2 collective-permute-start.55
  (413 shorter events, 100.4 us)
Async XLA Ops:
  4.1 9.2 %collective-permute-start.2 = (bf16[1,448,128]{2,1,0:T(8,128)(2,1)S(1)}, bf16[1,448,128]{2,1,0:T(8,128)(2,1)S(1)}, u32[]{:S(2)}, u32[]{:S(2)}) collective-permute-start(bf16[1,448,128]{2,1,0:T(8,128)(2,1)S(1)} %maximum_bitcast_fusion), channel_id=1, source_target_pairs={{0,24},{1,25},{2,26},{3,27},{4,28},{5,29},{6,30},{7,31},{8,16},{9,... | collective-permute-start | bytes 344072 | tf_op jit(solution)/shard_map/ppermute | solution.py:579
  9.3 9.7 %collective-permute-start = (bf16[1,448,128]{2,1,0:T(8,128)(2,1)S(1)}, bf16[1,448,128]{2,1,0:T(8,128)(2,1)S(1)}, u32[]{:S(2)}, u32[]{:S(2)}) collective-permute-start(bf16[1,448,128]{2,1,0:T(8,128)(2,1)S(1)} %maximum_bitcast_fusion), channel_id=1, source_target_pairs={{0,16},{1,17},{2,18},{3,19},{4,20},{5,21},{6,22},{7,23},{8,24},{9,... | collective-permute-start | bytes 344072 | tf_op jit(solution)/shard_map/ppermute | solution.py:579
  20.6 12.0 %collective-permute-start.3 = (bf16[4,448,128]{2,1,0:T(8,128)(2,1)}, bf16[4,448,128]{2,1,0:T(8,128)(2,1)}, u32[]{:S(2)}, u32[]{:S(2)}) collective-permute-start(bf16[4,448,128]{2,1,0:T(8,128)(2,1)} %pad_maximum_fusion.6), channel_id=1, source_target_pairs={{0,4},{1,5},{2,6},{3,7},{4,0},{5,1},{6,2},{7,3},{8,12},{9,13},{10,... | collective-permute-start | bytes 1376264 | tf_op jit(solution)/shard_map/ppermute | solution.py:579
  33.7 16.3 %collective-permute-start.4 = (bf16[8,256,128]{2,1,0:T(8,128)(2,1)S(1)}, bf16[8,256,128]{2,1,0:T(8,128)(2,1)S(1)}, u32[]{:S(2)}, u32[]{:S(2)}) collective-permute-start(bf16[8,256,128]{2,1,0:T(8,128)(2,1)S(1)} %slice.322), channel_id=1, source_target_pairs={{0,2},{1,3},{2,0},{3,1},{4,6},{5,7},{6,4},{7,5},{8,10},{9,11},{10,... | collective-permute-start | bytes 1572872 | tf_op jit(solution)/shard_map/ppermute | solution.py:579
  35.4 8.4 %collective-permute-start.9 = (bf16[1,448,128]{2,1,0:T(8,128)(2,1)S(1)}, bf16[1,448,128]{2,1,0:T(8,128)(2,1)S(1)}, u32[]{:S(2)}, u32[]{:S(2)}) collective-permute-start(bf16[1,448,128]{2,1,0:T(8,128)(2,1)S(1)} %maximum_bitcast_fusion.1), channel_id=1, source_target_pairs={{0,24},{1,25},{2,26},{3,27},{4,28},{5,29},{6,30},{7,31},{8,16},{9,... | collective-permute-start | bytes 344072 | tf_op jit(solution)/shard_map/ppermute | solution.py:579
  38.4 8.3 %collective-permute-start.8 = (bf16[1,448,128]{2,1,0:T(8,128)(2,1)S(1)}, bf16[1,448,128]{2,1,0:T(8,128)(2,1)S(1)}, u32[]{:S(2)}, u32[]{:S(2)}) collective-permute-start(bf16[1,448,128]{2,1,0:T(8,128)(2,1)S(1)} %maximum_bitcast_fusion.1), channel_id=1, source_target_pairs={{0,8},{1,9},{2,10},{3,11},{4,12},{5,13},{6,14},{7,15},{8,0},{9,1},... | collective-permute-start | bytes 344072 | tf_op jit(solution)/shard_map/ppermute | solution.py:579
  38.4 8.3 %collective-permute-start.7 = (bf16[1,448,128]{2,1,0:T(8,128)(2,1)S(1)}, bf16[1,448,128]{2,1,0:T(8,128)(2,1)S(1)}, u32[]{:S(2)}, u32[]{:S(2)}) collective-permute-start(bf16[1,448,128]{2,1,0:T(8,128)(2,1)S(1)} %maximum_bitcast_fusion.1), channel_id=1, source_target_pairs={{0,16},{1,17},{2,18},{3,19},{4,20},{5,21},{6,22},{7,23},{8,24},{9,... | collective-permute-start | bytes 344072 | tf_op jit(solution)/shard_map/ppermute | solution.py:579
  39.8 9.6 %collective-permute-start.6 = (bf16[3,40,512]{2,1,0:T(8,128)(2,1)S(1)}, bf16[3,40,512]{2,1,0:T(8,128)(2,1)S(1)}, u32[]{:S(2)}, u32[]{:S(2)}) collective-permute-start(bf16[3,40,512]{2,1,0:T(8,128)(2,1)S(1)} %get-tuple-element.424), channel_id=1, source_target_pairs={{0,28},{4,8},{8,4},{12,16},{16,12},{20,24},{24,20},{28,0},{1,29},{... | collective-permute-start | bytes 368648 | tf_op jit(solution)/shard_map/ppermute | solution.py:646
  51.9 14.9 %collective-permute-start.11 = (bf16[8,192,128]{2,1,0:T(8,128)(2,1)S(1)}, bf16[8,192,128]{2,1,0:T(8,128)(2,1)S(1)}, u32[]{:S(2)}, u32[]{:S(2)}) collective-permute-start(bf16[8,192,128]{2,1,0:T(8,128)(2,1)S(1)} %slice.323), channel_id=1, source_target_pairs={{0,2},{1,3},{2,0},{3,1},{4,6},{5,7},{6,4},{7,5},{8,10},{9,11},{10,... | collective-permute-start | bytes 1179656 | tf_op jit(solution)/shard_map/ppermute | solution.py:579
  52.5 14.3 %collective-permute-start.12 = (bf16[4,448,128]{2,1,0:T(8,128)(2,1)S(1)}, bf16[4,448,128]{2,1,0:T(8,128)(2,1)S(1)}, u32[]{:S(2)}, u32[]{:S(2)}) collective-permute-start(bf16[4,448,128]{2,1,0:T(8,128)(2,1)S(1)} %pad_maximum_fusion.7), channel_id=1, source_target_pairs={{0,4},{1,5},{2,6},{3,7},{4,0},{5,1},{6,2},{7,3},{8,12},{9,13},{10,... | collective-permute-start | bytes 1376264 | tf_op jit(solution)/shard_map/ppermute | solution.py:579
  67.7 19.2 %collective-permute-start.13 = (bf16[8,256,128]{2,1,0:T(8,128)(2,1)S(1)}, bf16[8,256,128]{2,1,0:T(8,128)(2,1)S(1)}, u32[]{:S(2)}, u32[]{:S(2)}) collective-permute-start(bf16[8,256,128]{2,1,0:T(8,128)(2,1)S(1)} %slice.324), channel_id=1, source_target_pairs={{0,2},{1,3},{2,0},{3,1},{4,6},{5,7},{6,4},{7,5},{8,10},{9,11},{10,... | collective-permute-start | bytes 1572872 | tf_op jit(solution)/shard_map/ppermute | solution.py:579
  77.7 8.2 %collective-permute-start.16 = (bf16[3,40,512]{2,1,0:T(8,128)(2,1)S(1)}, bf16[3,40,512]{2,1,0:T(8,128)(2,1)S(1)}, u32[]{:S(2)}, u32[]{:S(2)}) collective-permute-start(bf16[3,40,512]{2,1,0:T(8,128)(2,1)S(1)} %get-tuple-element.420), channel_id=1, source_target_pairs={{0,4},{4,8},{8,12},{12,16},{16,20},{20,24},{24,28},{28,0},{1,5},{5... | collective-permute-start | bytes 368648 | tf_op jit(solution)/shard_map/ppermute | solution.py:634
  79.1 7.7 %collective-permute-start.17 = (bf16[3,40,512]{2,1,0:T(8,128)(2,1)S(1)}, bf16[3,40,512]{2,1,0:T(8,128)(2,1)S(1)}, u32[]{:S(2)}, u32[]{:S(2)}) collective-permute-start(bf16[3,40,512]{2,1,0:T(8,128)(2,1)S(1)} %get-tuple-element.421), channel_id=1, source_target_pairs={{4,0},{8,4},{12,8},{16,12},{20,16},{24,20},{28,24},{0,28},{5,1},{9... | collective-permute-start | bytes 368648 | tf_op jit(solution)/shard_map/ppermute | solution.py:635
  88.5 13.9 %collective-permute-start.20 = (bf16[40,3,512]{2,0,1:T(8,128)(2,1)S(1)}, bf16[40,3,512]{2,0,1:T(8,128)(2,1)S(1)}, u32[]{:S(2)}, u32[]{:S(2)}) collective-permute-start(bf16[40,3,512]{2,0,1:T(8,128)(2,1)S(1)} %constant_dynamic-slice_fusion), channel_id=1, source_target_pairs={{0,2},{1,3},{2,0},{3,1},{4,6},{5,7},{6,4},{7,5},{8,10},{9,11},{10,... | collective-permute-start | bytes 368648 | tf_op jit(solution)/shard_map/ppermute | solution.py:516
  90.1 12.4 %collective-permute-start.19 = (bf16[8,192,128]{2,1,0:T(8,128)(2,1)S(1)}, bf16[8,192,128]{2,1,0:T(8,128)(2,1)S(1)}, u32[]{:S(2)}, u32[]{:S(2)}) collective-permute-start(bf16[8,192,128]{2,1,0:T(8,128)(2,1)S(1)} %slice.325), channel_id=1, source_target_pairs={{0,2},{1,3},{2,0},{3,1},{4,6},{5,7},{6,4},{7,5},{8,10},{9,11},{10,... | collective-permute-start | bytes 1179656 | tf_op jit(solution)/shard_map/ppermute | solution.py:579
  117.2 19.0 %collective-permute-start.24 = (bf16[40,3,512]{2,0,1:T(8,128)(2,1)S(1)}, bf16[40,3,512]{2,0,1:T(8,128)(2,1)S(1)}, u32[]{:S(2)}, u32[]{:S(2)}) collective-permute-start(bf16[40,3,512]{2,0,1:T(8,128)(2,1)S(1)} %get-tuple-element.396), channel_id=1, source_target_pairs={{0,2},{1,3},{2,0},{3,1},{4,6},{5,7},{6,4},{7,5},{8,10},{9,11},{10,... | collective-permute-start | bytes 368648 | tf_op jit(solution)/shard_map/ppermute | solution.py:516
  132.7 14.0 %collective-permute-start.26 = (bf16[3,40,512]{2,1,0:T(8,128)(2,1)S(1)}, bf16[3,40,512]{2,1,0:T(8,128)(2,1)S(1)}, u32[]{:S(2)}, u32[]{:S(2)}) collective-permute-start(bf16[3,40,512]{2,1,0:T(8,128)(2,1)S(1)} %get-tuple-element.416), channel_id=1, source_target_pairs={{0,28},{4,8},{8,4},{12,16},{16,12},{20,24},{24,20},{28,0},{1,29},{... | collective-permute-start | bytes 368648 | tf_op jit(solution)/shard_map/ppermute | solution.py:646
  136.2 10.6 %collective-permute-start.25 = (bf16[3,40,512]{2,1,0:T(8,128)(2,1)S(1)}, bf16[3,40,512]{2,1,0:T(8,128)(2,1)S(1)}, u32[]{:S(2)}, u32[]{:S(2)}) collective-permute-start(bf16[3,40,512]{2,1,0:T(8,128)(2,1)S(1)} %get-tuple-element.417), channel_id=1, source_target_pairs={{0,4},{4,0},{8,12},{12,8},{16,20},{20,16},{24,28},{28,24},{1,5},{5... | collective-permute-start | bytes 368648 | tf_op jit(solution)/shard_map/ppermute | solution.py:645
  162.1 18.2 %collective-permute-start.30 = (bf16[16,192,128]{2,1,0:T(8,128)(2,1)}, bf16[16,192,128]{2,1,0:T(8,128)(2,1)S(1)}, u32[]{:S(2)}, u32[]{:S(2)}) collective-permute-start(bf16[16,192,128]{2,1,0:T(8,128)(2,1)} %get-tuple-element.243), channel_id=1, source_target_pairs={{0,1},{1,0},{2,3},{3,2},{4,5},{5,4},{6,7},{7,6},{8,9},{9,8},{10,11... | collective-permute-start | bytes 2359304 | tf_op jit(solution)/shard_map/ppermute | solution.py:579
  162.2 23.2 %collective-permute-start.29 = (bf16[8,448,128]{2,1,0:T(8,128)(2,1)S(1)}, bf16[8,448,128]{2,1,0:T(8,128)(2,1)S(1)}, u32[]{:S(2)}, u32[]{:S(2)}) collective-permute-start(bf16[8,448,128]{2,1,0:T(8,128)(2,1)S(1)} %slice.454), channel_id=1, source_target_pairs={{0,2},{1,3},{2,0},{3,1},{4,6},{5,7},{6,4},{7,5},{8,10},{9,11},{10,... | collective-permute-start | bytes 2752520 | tf_op jit(solution)/shard_map/ppermute | solution.py:579
  178.2 17.5 %collective-permute-start.34 = (bf16[3,40,512]{2,1,0:T(8,128)(2,1)S(1)}, bf16[3,40,512]{2,1,0:T(8,128)(2,1)S(1)}, u32[]{:S(2)}, u32[]{:S(2)}) collective-permute-start(bf16[3,40,512]{2,1,0:T(8,128)(2,1)S(1)} %get-tuple-element.412), channel_id=1, source_target_pairs={{0,28},{4,8},{8,4},{12,16},{16,12},{20,24},{24,20},{28,0},{1,29},{... | collective-permute-start | bytes 368648 | tf_op jit(solution)/shard_map/ppermute | solution.py:646
  179.5 16.1 %collective-permute-start.33 = (bf16[3,40,512]{2,1,0:T(8,128)(2,1)S(1)}, bf16[3,40,512]{2,1,0:T(8,128)(2,1)S(1)}, u32[]{:S(2)}, u32[]{:S(2)}) collective-permute-start(bf16[3,40,512]{2,1,0:T(8,128)(2,1)S(1)} %get-tuple-element.413), channel_id=1, source_target_pairs={{0,4},{4,0},{8,12},{12,8},{16,20},{20,16},{24,28},{28,24},{1,5},{5... | collective-permute-start | bytes 368648 | tf_op jit(solution)/shard_map/ppermute | solution.py:645
  180.6 15.1 %collective-permute-start.32 = (bf16[8,192,128]{2,1,0:T(8,128)(2,1)S(1)}, bf16[8,192,128]{2,1,0:T(8,128)(2,1)S(1)}, u32[]{:S(2)}, u32[]{:S(2)}) collective-permute-start(bf16[8,192,128]{2,1,0:T(8,128)(2,1)S(1)} %slice.457), channel_id=1, source_target_pairs={{0,2},{1,3},{2,0},{3,1},{4,6},{5,7},{6,4},{7,5},{8,10},{9,11},{10,... | collective-permute-start | bytes 1179656 | tf_op jit(solution)/shard_map/ppermute | solution.py:579
  185.8 11.7 %collective-permute-start.31 = (bf16[4,448,128]{2,1,0:T(8,128)(2,1)S(1)}, bf16[4,448,128]{2,1,0:T(8,128)(2,1)S(1)}, u32[]{:S(2)}, u32[]{:S(2)}) collective-permute-start(bf16[4,448,128]{2,1,0:T(8,128)(2,1)S(1)} %slice.456), channel_id=1, source_target_pairs={{0,4},{1,5},{2,6},{3,7},{4,0},{5,1},{6,2},{7,3},{8,12},{9,13},{10,... | collective-permute-start | bytes 1376264 | tf_op jit(solution)/shard_map/ppermute | solution.py:579
  202.5 7.4 %collective-permute-start.38 = (bf16[4,192,128]{2,1,0:T(8,128)(2,1)S(1)}, bf16[4,192,128]{2,1,0:T(8,128)(2,1)S(1)}, u32[]{:S(2)}, u32[]{:S(2)}) collective-permute-start(bf16[4,192,128]{2,1,0:T(8,128)(2,1)S(1)} %slice.459), channel_id=1, source_target_pairs={{0,4},{1,5},{2,6},{3,7},{4,0},{5,1},{6,2},{7,3},{8,12},{9,13},{10,... | collective-permute-start | bytes 589832 | tf_op jit(solution)/shard_map/ppermute | solution.py:579
  206.2 14.2 %collective-permute-start.36 = (bf16[8,256,128]{2,1,0:T(8,128)(2,1)S(1)}, bf16[8,256,128]{2,1,0:T(8,128)(2,1)S(1)}, u32[]{:S(2)}, u32[]{:S(2)}) collective-permute-start(bf16[8,256,128]{2,1,0:T(8,128)(2,1)S(1)} %slice.455), channel_id=1, source_target_pairs={{0,2},{1,3},{2,0},{3,1},{4,6},{5,7},{6,4},{7,5},{8,10},{9,11},{10,... | collective-permute-start | bytes 1572872 | tf_op jit(solution)/shard_map/ppermute | solution.py:579
  207.5 12.8 %collective-permute-start.37 = (bf16[3,160,512]{2,1,0:T(8,128)(2,1)S(1)}, bf16[3,160,512]{2,1,0:T(8,128)(2,1)S(1)}, u32[]{:S(2)}, u32[]{:S(2)}) collective-permute-start(bf16[3,160,512]{2,1,0:T(8,128)(2,1)S(1)} %get-tuple-element.390), channel_id=1, source_target_pairs={{0,1},{1,0},{2,3},{3,2},{4,5},{5,4},{6,7},{7,6},{8,9},{9,8},{10,11... | collective-permute-start | bytes 1474568 | tf_op jit(solution)/shard_map/ppermute | solution.py:516
  207.8 7.9 %collective-permute-start.41 = (bf16[1,448,128]{2,1,0:T(8,128)(2,1)S(1)}, bf16[1,448,128]{2,1,0:T(8,128)(2,1)S(1)}, u32[]{:S(2)}, u32[]{:S(2)}) collective-permute-start(bf16[1,448,128]{2,1,0:T(8,128)(2,1)S(1)} %get-tuple-element.400), channel_id=1, source_target_pairs={{0,24},{1,25},{2,26},{3,27},{4,28},{5,29},{6,30},{7,31},{8,16},{9,... | collective-permute-start | bytes 344072 | tf_op jit(solution)/shard_map/ppermute | solution.py:579
  209.9 9.9 %collective-permute-start.40 = (bf16[1,448,128]{2,1,0:T(8,128)(2,1)S(1)}, bf16[1,448,128]{2,1,0:T(8,128)(2,1)S(1)}, u32[]{:S(2)}, u32[]{:S(2)}) collective-permute-start(bf16[1,448,128]{2,1,0:T(8,128)(2,1)S(1)} %get-tuple-element.401), channel_id=1, source_target_pairs={{0,8},{1,9},{2,10},{3,11},{4,12},{5,13},{6,14},{7,15},{8,0},{9,1},... | collective-permute-start | bytes 344072 | tf_op jit(solution)/shard_map/ppermute | solution.py:579
  210.0 10.4 %collective-permute-start.39 = (bf16[1,448,128]{2,1,0:T(8,128)(2,1)S(1)}, bf16[1,448,128]{2,1,0:T(8,128)(2,1)S(1)}, u32[]{:S(2)}, u32[]{:S(2)}) collective-permute-start(bf16[1,448,128]{2,1,0:T(8,128)(2,1)S(1)} %get-tuple-element.402), channel_id=1, source_target_pairs={{0,16},{1,17},{2,18},{3,19},{4,20},{5,21},{6,22},{7,23},{8,24},{9,... | collective-permute-start | bytes 344072 | tf_op jit(solution)/shard_map/ppermute | solution.py:579
  225.3 14.8 %collective-permute-start.50 = (bf16[40,3,512]{2,0,1:T(8,128)(2,1)S(1)}, bf16[40,3,512]{2,0,1:T(8,128)(2,1)S(1)}, u32[]{:S(2)}, u32[]{:S(2)}) collective-permute-start(bf16[40,3,512]{2,0,1:T(8,128)(2,1)S(1)} %get-tuple-element.394), channel_id=1, source_target_pairs={{0,2},{1,3},{2,0},{3,1},{4,6},{5,7},{6,4},{7,5},{8,10},{9,11},{10,... | collective-permute-start | bytes 368648 | tf_op jit(solution)/shard_map/ppermute | solution.py:516
  227.2 13.0 %collective-permute-start.49 = (bf16[320,512]{1,0:T(8,128)(2,1)S(1)}, bf16[320,512]{1,0:T(8,128)(2,1)S(1)}, u32[]{:S(2)}, u32[]{:S(2)}) collective-permute-start(bf16[320,512]{1,0:T(8,128)(2,1)S(1)} %fusion.6), channel_id=1, source_target_pairs={{0,2},{1,3},{2,0},{3,1},{4,6},{5,7},{6,4},{7,5},{8,10},{9,11},{10,... | collective-permute-start | bytes 983048 | tf_op jit(solution)/shard_map/ppermute | solution.py:516
  (109 other events, 935.7 us)

commit v8 on v7

--- a/solution.py
+++ b/solution.py
@@ -934,7 +934,7 @@
     )
     returned, chain_one = from_neighbours(*returned), (kept, sent)
     partial = from_edges(partial, returned)
-    chain_one = split(scatter_round(chain_one, steps - 1), 2)
+    chain_one = split(scatter_round(chain_one, steps - 1).astype(BF16), 2)
     other, *chain_one = lax.optimization_barrier((swap(partial.astype(BF16), "hid", 1), *chain_one))
     pooled_grad, node_grad, kept, sent, node_minor_zero = node_backward(
         order,
@@ -994,7 +994,7 @@
     chain_one = chain_one[0].astype(F32) + one_arrived.astype(F32)
     chain_zero = split(chain_zero[0].astype(F32) + zero_arrived.astype(F32), 2)
     edge_arrived = exchange(sent, steps - 1, 1)
-    kept, sent = split(kept.astype(F32) + edge_arrived.astype(F32), 2)
+    kept, sent = split((kept.astype(F32) + edge_arrived.astype(F32)).astype(BF16), 2)
     zero_arrived = after(exchange(chain_zero[1], steps - 3, 1), sent)
     returned = after(returned, sent)
     chain_zero = chain_zero[0].astype(F32) + zero_arrived.astype(F32)
@@ -1019,6 +1019,7 @@
         layer_one_grads = layer_one_grads + piece.astype(F32)
     layer_one_grads = layer_one_grads[0]
     chain_edge = split(kept + arrived.astype(F32), 2)
+    chain_zero = after(chain_zero, chain_edge[1])
     arrived, *others = lax.optimization_barrier(
         (
             exchange(chain_edge[1], steps - 3, 1),

time: 265 us -> 261 us (0.985)
    unnamed x171 -> x165, local copies, waits for them, and re-layouts: 10.7 us -> 8.7 us
  transfers between devices with their start and end apart: 58 -> 58, of which waited for: 28 -> 28; matrix products, arithmetic and copies ran while one was open for 11% -> 11% of each run, Pallas kernels for 27% -> 28%
where the time goes in v8:
time: 261 us; the launch traced here: 260 us
  Pallas kernels  88.7 us (34%)
  starting transfers between devices  67.3 us (26%)
  waiting for transfers between devices  48.5 us (19%)
  other arithmetic  26.2 us (10%)
  local copies, waits for them, and re-layouts  25.6 us (10%)
  between operations  2.98 us (1%)
    pallas_call x9, Pallas kernels, run_kernel(): pl.pallas_call(kernel, name=name, grid=(samples,), in_specs=in_specs, out...  88.7 us
    ppermute x41, starting transfers between devices, exchange(): lax.ppermute(values, ('node', 'hid'), [(i, i ^ mask) for i in range(total)])  45.7 us
    ppermute x41, waiting for transfers between devices, exchange(): lax.ppermute(values, ('node', 'hid'), [(i, i ^ mask) for i in range(total)])  40 us
    ppermute x3, starting transfers between devices, neighbour_swaps(): second = lax.ppermute(jnp.where(even, to_previous, to_next), 'node', two)  8.76 us
    unnamed x165, local copies, waits for them, and re-layouts  8.7 us
    ppermute x9, starting transfers between devices, swap(): lax.ppermute(values, axis, [(i, i ^ offset) for i in range(lax.axis_size(...  6.83 us
  transfers between devices with their start and end apart: 58, of which 28 were waited for; matrix products, arithmetic and copies ran while one was open for 11% of the time, Pallas kernels for 28%

profile of v8, /device:TPU:0, one launch (start us, length us, event | category | flops | bytes accessed | tf_op | source)
XLA Modules:
  0.0 260.2 jit_solution(1825720035547228318)
XLA Ops:
  4.1 5.1 %collective-permute-start.2 = (bf16[1,448,128]{2,1,0:T(8,128)(2,1)S(1)}, bf16[1,448,128]{2,1,0:T(8,128)(2,1)S(1)}, u32[]{:S(2)}, u32[]{:S(2)}) collective-permute-start(bf16[1,448,128]{2,1,0:T(8,128)(2,1)S(1)} %maximum_bitcast_fusion), channel_id=1, source_target_pairs={{0,24},{1,25},{2,26},{3,27},{4,28},{5,29},{6,30},{7,31},{8,16},{9,... | collective-permute-start | bytes 344072 | tf_op jit(solution)/shard_map/ppermute | solution.py:579
  13.3 2.7 %collective-permute-done.1 = bf16[1,448,128]{2,1,0:T(8,128)(2,1)S(1)} collective-permute-done((bf16[1,448,128]{2,1,0:T(8,128)(2,1)S(1)}, bf16[1,448,128]{2,1,0:T(8,128)(2,1)S(1)}, u32[]{:S(2)}, u32[]{:S(2)}) %collective-permute-start.1) | collective-permute-done | bytes 114720 | tf_op jit(solution)/shard_map/ppermute | solution.py:579
  16.0 3.0 %collective-permute-done = bf16[1,448,128]{2,1,0:T(8,128)(2,1)S(1)} collective-permute-done((bf16[1,448,128]{2,1,0:T(8,128)(2,1)S(1)}, bf16[1,448,128]{2,1,0:T(8,128)(2,1)S(1)}, u32[]{:S(2)}, u32[]{:S(2)}) %collective-permute-start) | collective-permute-done | bytes 114720 | tf_op jit(solution)/shard_map/ppermute | solution.py:579
  25.6 7.0 %collective-permute-done.3 = bf16[4,448,128]{2,1,0:T(8,128)(2,1)} collective-permute-done((bf16[4,448,128]{2,1,0:T(8,128)(2,1)}, bf16[4,448,128]{2,1,0:T(8,128)(2,1)}, u32[]{:S(2)}, u32[]{:S(2)}) %collective-permute-start.3) | collective-permute-done | bytes 458784 | tf_op jit(solution)/shard_map/ppermute | solution.py:579
  35.4 3.0 %collective-permute-start.9 = (bf16[1,448,128]{2,1,0:T(8,128)(2,1)S(1)}, bf16[1,448,128]{2,1,0:T(8,128)(2,1)S(1)}, u32[]{:S(2)}, u32[]{:S(2)}) collective-permute-start(bf16[1,448,128]{2,1,0:T(8,128)(2,1)S(1)} %maximum_bitcast_fusion.1), channel_id=1, source_target_pairs={{0,24},{1,25},{2,26},{3,27},{4,28},{5,29},{6,30},{7,31},{8,16},{9,... | collective-permute-start | bytes 344072 | tf_op jit(solution)/shard_map/ppermute | solution.py:579
  39.8 4.0 %collective-permute-start.6 = (bf16[3,40,512]{2,1,0:T(8,128)(2,1)S(1)}, bf16[3,40,512]{2,1,0:T(8,128)(2,1)S(1)}, u32[]{:S(2)}, u32[]{:S(2)}) collective-permute-start(bf16[3,40,512]{2,1,0:T(8,128)(2,1)S(1)} %get-tuple-element.434), channel_id=1, source_target_pairs={{0,28},{4,8},{8,4},{12,16},{16,12},{20,24},{24,20},{28,0},{1,29},{... | collective-permute-start | bytes 368648 | tf_op jit(solution)/shard_map/ppermute | solution.py:646
  44.5 2.2 collective-permute-done.8
  46.7 2.7 %collective-permute-done.6 = bf16[3,40,512]{2,1,0:T(8,128)(2,1)S(1)} collective-permute-done((bf16[3,40,512]{2,1,0:T(8,128)(2,1)S(1)}, bf16[3,40,512]{2,1,0:T(8,128)(2,1)S(1)}, u32[]{:S(2)}, u32[]{:S(2)}) %collective-permute-start.6) | collective-permute-done | bytes 122912 | tf_op jit(solution)/shard_map/ppermute | solution.py:646
  55.3 11.5 %edge_forward.2 = (bf16[3,640,512]{2,1,0:T(8,128)(2,1)}, bf16[3,640,512]{2,1,0:T(8,128)(2,1)}, bf16[3,640,512]{2,1,0:T(8,128)(2,1)}, f32[3,640,1]{2,1,0:T(8,128)...) custom-call(s32[32]{0:T(128)} %add.290.order, ...), custom_call_target="tpu_custom_call" | custom-call | flops 15225323520 | bytes 19271296 | tf_op jit(solution)/shard_map/edge_forward/pallas_call | solution.py:129
  71.7 5.1 %node_pass.2 = (bf16[480,512]{1,0:T(8,128)(2,1)}, bf16[480,512]{1,0:T(8,128)(2,1)}, bf16[480,512]{1,0:T(8,128)(2,1)}, bf16[480,512]{1,0:T(8,128)(2,1)}, f32[480,...) custom-call(s32[32]{0:T(128)} %add.290.order, ...), custom_call_target="tpu_custom_call" | custom-call | flops 3019898880 | bytes 7269376 | tf_op jit(solution)/shard_map/node_pass/pallas_call | solution.py:129
  79.2 3.3 %collective-permute-start.17 = (bf16[3,40,512]{2,1,0:T(8,128)(2,1)S(1)}, bf16[3,40,512]{2,1,0:T(8,128)(2,1)S(1)}, u32[]{:S(2)}, u32[]{:S(2)}) collective-permute-start(bf16[3,40,512]{2,1,0:T(8,128)(2,1)S(1)} %get-tuple-element.431), channel_id=1, source_target_pairs={{4,0},{8,4},{12,8},{16,12},{20,16},{24,20},{28,24},{0,28},{5,1},{9... | collective-permute-start | bytes 368648 | tf_op jit(solution)/shard_map/ppermute | solution.py:635
  82.5 3.4 %collective-permute-done.16 = bf16[3,40,512]{2,1,0:T(8,128)(2,1)S(1)} collective-permute-done((bf16[3,40,512]{2,1,0:T(8,128)(2,1)S(1)}, bf16[3,40,512]{2,1,0:T(8,128)(2,1)S(1)}, u32[]{:S(2)}, u32[]{:S(2)}) %collective-permute-start.16) | collective-permute-done | bytes 122912 | tf_op jit(solution)/shard_map/ppermute | solution.py:634
  91.7 10.9 %edge_forward.3 = (bf16[3,640,512]{2,1,0:T(8,128)(2,1)}, bf16[3,640,512]{2,1,0:T(8,128)(2,1)}, bf16[3,640,512]{2,1,0:T(8,128)(2,1)}, f32[3,640,1]{2,1,0:T(8,128)}, bf16[3,160,512]{2,1,0:T(8,128)(2,1)}) custom-call(s32[32]{0:T(128)} %add.290.order, bf16[16,256,128]{2,1,0:T(8,128)(2,1)} %copy-done.11, bf16[16,256,128]{2,1,0:T(8,128)(2,1)} %collective-permute-done.18.w1x.w2x, ...), custom_call_target="tpu_custom_call" | custom-call | flops 15225323520 | bytes 17960576 | tf_op jit(solution)/shard_map/edge_forward/pallas_call | solution.py:129
  107.5 8.2 %node_pass.3 = (bf16[3,160,512]{2,1,0:T(8,128)(2,1)}, bf16[3,160,512]{2,1,0:T(8,128)(2,1)}, f32[3,160,512]{2,1,0:T(8,128)}, bf16[16,192,128]{2,1,0:T(8,128)(2,1)...) custom-call(s32[32]{0:T(128)} %add.290.order, s32[64]{0:T(128)} %reshape.341.rest_0_.owners, ...), custom_call_target="tpu_custom_call" | custom-call | flops 9059696640 | bytes 8087820 | tf_op jit(solution)/shard_map/node_pass/pallas_call | solution.py:129
  118.8 13.0 %edge_backward.2 = (bf16[3,640,512]{2,1,0:T(8,128)(2,1)}, bf16[3,640,512]{2,1,0:T(8,128)(2,1)}, bf16[3,400,512]{2,1,0:T(8,128)(2,1)}, f32[3,160,512]{2,1,0:T(8,1...) custom-call(s32[32]{0:T(128)} %add.290.order, bf16[16,256,128]{2,1,0:T(8,128)(2,1)} %copy-done.11, ...), custom_call_target="tpu_custom_call" | custom-call | flops 14344519680 | bytes 19674752 | tf_op jit(solution)/shard_map/edge_backward/pallas_call | solution.py:129
  132.8 3.5 %collective-permute-start.26 = (bf16[3,40,512]{2,1,0:T(8,128)(2,1)S(1)}, bf16[3,40,512]{2,1,0:T(8,128)(2,1)S(1)}, u32[]{:S(2)}, u32[]{:S(2)}) collective-permute-start(bf16[3,40,512]{2,1,0:T(8,128)(2,1)S(1)} %get-tuple-element.426), channel_id=1, source_target_pairs={{0,28},{4,8},{8,4},{12,16},{16,12},{20,24},{24,20},{28,0},{1,29},{... | collective-permute-start | bytes 368648 | tf_op jit(solution)/shard_map/ppermute | solution.py:646
  137.0 9.8 %edge_weight_grads.2 = (bf16[16,448,128]{2,1,0:T(8,128)(2,1)}, bf16[16,448,128]{2,1,0:T(8,128)(2,1)}) custom-call(s32[64]{0:T(128)} %reshape.341.rest_0_.owners, bf16[3,640,512]{2,1,0:T(8,128)(2,1)} %get-tuple-element.195.low.edge_low, bf16[3,240,512]{2,1,0:T(8,128)(2,1)} %copy-done.33, bf16[3,640,512]{2,1,0:T(8,128)(2,1)} %get-tuple-element.217.hidden_low, ...), custom_call_target="tpu_custom_call" | custom-call | flops 8053063680 | bytes 15073536 | tf_op jit(solution)/shard_map/edge_weight_grads/pallas_call | solution.py:129
  152.4 8.0 %node_backward.1 = (bf16[3,160,512]{2,1,0:T(8,128)(2,1)}, f32[3,160,512]{2,1,0:T(8,128)}, bf16[16,192,128]{2,1,0:T(8,128)(2,1)}, bf16[16,192,128]{2,1,0:T(8,128)(2,1)}, f32[4,512]{1,0:T(4,128)}) custom-call(s32[32]{0:T(128)} %add.290.order, s32[64]{0:T(128)} %reshape.341.rest_0_.owners, bf16[16,192,128]{2,1,0:T(8,128)(2,1)} %copy-done.41, ...), custom_call_target="tpu_custom_call" | custom-call | flops 6039797760 | bytes 9564288 | tf_op jit(solution)/shard_map/node_backward/pallas_call | solution.py:129
  161.0 14.4 %edge_backward.3 = (bf16[3,640,512]{2,1,0:T(8,128)(2,1)}, bf16[3,640,512]{2,1,0:T(8,128)(2,1)}, bf16[3,400,512]{2,1,0:T(8,128)(2,1)}, f32[3,160,512]{2,1,0:T(8,1...) custom-call(s32[32]{0:T(128)} %add.290.order, ...), custom_call_target="tpu_custom_call" | custom-call | flops 14344519680 | bytes 21640832 | tf_op jit(solution)/shard_map/edge_backward/pallas_call | solution.py:129
  181.0 2.8 %collective-permute-done.29 = bf16[8,448,128]{2,1,0:T(8,128)(2,1)S(1)} collective-permute-done((bf16[8,448,128]{2,1,0:T(8,128)(2,1)S(1)}, bf16[8,448,128]{2,1,0:T(8,128)(2,1)S(1)}, u32[]{:S(2)}, u32[]{:S(2)}) %collective-permute-start.29) | collective-permute-done | bytes 917536 | tf_op jit(solution)/shard_map/ppermute | solution.py:579
  184.0 2.1 collective-permute-start.31
  186.1 7.8 %edge_weight_grads.3 = (bf16[16,256,128]{2,1,0:T(8,128)(2,1)}, bf16[16,256,128]{2,1,0:T(8,128)(2,1)}) custom-call(s32[64]{0:T(128)} %reshape.341.rest_0_.owners, bf16[640,512]{1,0:T(8,128)(2,1)} %bitcast.164, bf16[3,240,512]{2,1,0:T(8,128)(2,1)} %pad_maximum_fusion.2.table, bf16[640,512]{1,0:T(8,128)(2,1)} %get-tuple-element.240.hidden_low, ...), custom_call_target="tpu_custom_call" | custom-call | flops 8053063680 | bytes 9306368 | tf_op jit(solution)/shard_map/edge_weight_grads/pallas_call | solution.py:129
  193.9 2.0 collective-permute-done.31
  206.2 2.8 %collective-permute-start.41 = (bf16[1,448,128]{2,1,0:T(8,128)(2,1)S(1)}, bf16[1,448,128]{2,1,0:T(8,128)(2,1)S(1)}, u32[]{:S(2)}, u32[]{:S(2)}) collective-permute-start(bf16[1,448,128]{2,1,0:T(8,128)(2,1)S(1)} %get-tuple-element.410), channel_id=1, source_target_pairs={{0,24},{1,25},{2,26},{3,27},{4,28},{5,29},{6,30},{7,31},{8,16},{9,... | collective-permute-start | bytes 344072 | tf_op jit(solution)/shard_map/ppermute | solution.py:579
  210.7 3.4 %collective-permute-done.41 = bf16[1,448,128]{2,1,0:T(8,128)(2,1)S(1)} collective-permute-done((bf16[1,448,128]{2,1,0:T(8,128)(2,1)S(1)}, bf16[1,448,128]{2,1,0:T(8,128)(2,1)S(1)}, u32[]{:S(2)}, u32[]{:S(2)}) %collective-permute-start.41) | collective-permute-done | bytes 114720 | tf_op jit(solution)/shard_map/ppermute | solution.py:579
  214.1 3.7 %collective-permute-done.40 = bf16[1,448,128]{2,1,0:T(8,128)(2,1)S(1)} collective-permute-done((bf16[1,448,128]{2,1,0:T(8,128)(2,1)S(1)}, bf16[1,448,128]{2,1,0:T(8,128)(2,1)S(1)}, u32[]{:S(2)}, u32[]{:S(2)}) %collective-permute-start.40) | collective-permute-done | bytes 114720 | tf_op jit(solution)/shard_map/ppermute | solution.py:579
  222.7 1.9 collective-permute-start.44
  224.6 1.8 collective-permute-start.45
  227.2 1.7 collective-permute-start.49
  230.8 1.8 collective-permute-start.48
  247.9 1.9 collective-permute-start.57
  249.7 2.6 collective-permute-start.55
  (405 shorter events, 100.2 us)
Async XLA Ops:
  4.1 9.2 %collective-permute-start.2 = (bf16[1,448,128]{2,1,0:T(8,128)(2,1)S(1)}, bf16[1,448,128]{2,1,0:T(8,128)(2,1)S(1)}, u32[]{:S(2)}, u32[]{:S(2)}) collective-permute-start(bf16[1,448,128]{2,1,0:T(8,128)(2,1)S(1)} %maximum_bitcast_fusion), channel_id=1, source_target_pairs={{0,24},{1,25},{2,26},{3,27},{4,28},{5,29},{6,30},{7,31},{8,16},{9,... | collective-permute-start | bytes 344072 | tf_op jit(solution)/shard_map/ppermute | solution.py:579
  9.3 9.7 %collective-permute-start = (bf16[1,448,128]{2,1,0:T(8,128)(2,1)S(1)}, bf16[1,448,128]{2,1,0:T(8,128)(2,1)S(1)}, u32[]{:S(2)}, u32[]{:S(2)}) collective-permute-start(bf16[1,448,128]{2,1,0:T(8,128)(2,1)S(1)} %maximum_bitcast_fusion), channel_id=1, source_target_pairs={{0,16},{1,17},{2,18},{3,19},{4,20},{5,21},{6,22},{7,23},{8,24},{9,... | collective-permute-start | bytes 344072 | tf_op jit(solution)/shard_map/ppermute | solution.py:579
  20.6 12.0 %collective-permute-start.3 = (bf16[4,448,128]{2,1,0:T(8,128)(2,1)}, bf16[4,448,128]{2,1,0:T(8,128)(2,1)}, u32[]{:S(2)}, u32[]{:S(2)}) collective-permute-start(bf16[4,448,128]{2,1,0:T(8,128)(2,1)} %pad_maximum_fusion.6), channel_id=1, source_target_pairs={{0,4},{1,5},{2,6},{3,7},{4,0},{5,1},{6,2},{7,3},{8,12},{9,13},{10,... | collective-permute-start | bytes 1376264 | tf_op jit(solution)/shard_map/ppermute | solution.py:579
  33.7 16.3 %collective-permute-start.4 = (bf16[8,256,128]{2,1,0:T(8,128)(2,1)S(1)}, bf16[8,256,128]{2,1,0:T(8,128)(2,1)S(1)}, u32[]{:S(2)}, u32[]{:S(2)}) collective-permute-start(bf16[8,256,128]{2,1,0:T(8,128)(2,1)S(1)} %slice.320), channel_id=1, source_target_pairs={{0,2},{1,3},{2,0},{3,1},{4,6},{5,7},{6,4},{7,5},{8,10},{9,11},{10,... | collective-permute-start | bytes 1572872 | tf_op jit(solution)/shard_map/ppermute | solution.py:579
  35.4 8.4 %collective-permute-start.9 = (bf16[1,448,128]{2,1,0:T(8,128)(2,1)S(1)}, bf16[1,448,128]{2,1,0:T(8,128)(2,1)S(1)}, u32[]{:S(2)}, u32[]{:S(2)}) collective-permute-start(bf16[1,448,128]{2,1,0:T(8,128)(2,1)S(1)} %maximum_bitcast_fusion.1), channel_id=1, source_target_pairs={{0,24},{1,25},{2,26},{3,27},{4,28},{5,29},{6,30},{7,31},{8,16},{9,... | collective-permute-start | bytes 344072 | tf_op jit(solution)/shard_map/ppermute | solution.py:579
  38.4 8.3 %collective-permute-start.8 = (bf16[1,448,128]{2,1,0:T(8,128)(2,1)S(1)}, bf16[1,448,128]{2,1,0:T(8,128)(2,1)S(1)}, u32[]{:S(2)}, u32[]{:S(2)}) collective-permute-start(bf16[1,448,128]{2,1,0:T(8,128)(2,1)S(1)} %maximum_bitcast_fusion.1), channel_id=1, source_target_pairs={{0,8},{1,9},{2,10},{3,11},{4,12},{5,13},{6,14},{7,15},{8,0},{9,1},... | collective-permute-start | bytes 344072 | tf_op jit(solution)/shard_map/ppermute | solution.py:579
  38.4 8.3 %collective-permute-start.7 = (bf16[1,448,128]{2,1,0:T(8,128)(2,1)S(1)}, bf16[1,448,128]{2,1,0:T(8,128)(2,1)S(1)}, u32[]{:S(2)}, u32[]{:S(2)}) collective-permute-start(bf16[1,448,128]{2,1,0:T(8,128)(2,1)S(1)} %maximum_bitcast_fusion.1), channel_id=1, source_target_pairs={{0,16},{1,17},{2,18},{3,19},{4,20},{5,21},{6,22},{7,23},{8,24},{9,... | collective-permute-start | bytes 344072 | tf_op jit(solution)/shard_map/ppermute | solution.py:579
  39.8 9.6 %collective-permute-start.6 = (bf16[3,40,512]{2,1,0:T(8,128)(2,1)S(1)}, bf16[3,40,512]{2,1,0:T(8,128)(2,1)S(1)}, u32[]{:S(2)}, u32[]{:S(2)}) collective-permute-start(bf16[3,40,512]{2,1,0:T(8,128)(2,1)S(1)} %get-tuple-element.434), channel_id=1, source_target_pairs={{0,28},{4,8},{8,4},{12,16},{16,12},{20,24},{24,20},{28,0},{1,29},{... | collective-permute-start | bytes 368648 | tf_op jit(solution)/shard_map/ppermute | solution.py:646
  51.9 14.9 %collective-permute-start.11 = (bf16[8,192,128]{2,1,0:T(8,128)(2,1)S(1)}, bf16[8,192,128]{2,1,0:T(8,128)(2,1)S(1)}, u32[]{:S(2)}, u32[]{:S(2)}) collective-permute-start(bf16[8,192,128]{2,1,0:T(8,128)(2,1)S(1)} %slice.321), channel_id=1, source_target_pairs={{0,2},{1,3},{2,0},{3,1},{4,6},{5,7},{6,4},{7,5},{8,10},{9,11},{10,... | collective-permute-start | bytes 1179656 | tf_op jit(solution)/shard_map/ppermute | solution.py:579
  52.6 14.2 %collective-permute-start.12 = (bf16[4,448,128]{2,1,0:T(8,128)(2,1)S(1)}, bf16[4,448,128]{2,1,0:T(8,128)(2,1)S(1)}, u32[]{:S(2)}, u32[]{:S(2)}) collective-permute-start(bf16[4,448,128]{2,1,0:T(8,128)(2,1)S(1)} %pad_maximum_fusion.7), channel_id=1, source_target_pairs={{0,4},{1,5},{2,6},{3,7},{4,0},{5,1},{6,2},{7,3},{8,12},{9,13},{10,... | collective-permute-start | bytes 1376264 | tf_op jit(solution)/shard_map/ppermute | solution.py:579
  67.7 19.3 %collective-permute-start.13 = (bf16[8,256,128]{2,1,0:T(8,128)(2,1)S(1)}, bf16[8,256,128]{2,1,0:T(8,128)(2,1)S(1)}, u32[]{:S(2)}, u32[]{:S(2)}) collective-permute-start(bf16[8,256,128]{2,1,0:T(8,128)(2,1)S(1)} %slice.322), channel_id=1, source_target_pairs={{0,2},{1,3},{2,0},{3,1},{4,6},{5,7},{6,4},{7,5},{8,10},{9,11},{10,... | collective-permute-start | bytes 1572872 | tf_op jit(solution)/shard_map/ppermute | solution.py:579
  77.8 8.2 %collective-permute-start.16 = (bf16[3,40,512]{2,1,0:T(8,128)(2,1)S(1)}, bf16[3,40,512]{2,1,0:T(8,128)(2,1)S(1)}, u32[]{:S(2)}, u32[]{:S(2)}) collective-permute-start(bf16[3,40,512]{2,1,0:T(8,128)(2,1)S(1)} %get-tuple-element.430), channel_id=1, source_target_pairs={{0,4},{4,8},{8,12},{12,16},{16,20},{20,24},{24,28},{28,0},{1,5},{5... | collective-permute-start | bytes 368648 | tf_op jit(solution)/shard_map/ppermute | solution.py:634
  88.5 14.0 %collective-permute-start.20 = (bf16[40,3,512]{2,0,1:T(8,128)(2,1)S(1)}, bf16[40,3,512]{2,0,1:T(8,128)(2,1)S(1)}, u32[]{:S(2)}, u32[]{:S(2)}) collective-permute-start(bf16[40,3,512]{2,0,1:T(8,128)(2,1)S(1)} %constant_dynamic-slice_fusion), channel_id=1, source_target_pairs={{0,2},{1,3},{2,0},{3,1},{4,6},{5,7},{6,4},{7,5},{8,10},{9,11},{10,... | collective-permute-start | bytes 368648 | tf_op jit(solution)/shard_map/ppermute | solution.py:516
  90.2 12.4 %collective-permute-start.19 = (bf16[8,192,128]{2,1,0:T(8,128)(2,1)S(1)}, bf16[8,192,128]{2,1,0:T(8,128)(2,1)S(1)}, u32[]{:S(2)}, u32[]{:S(2)}) collective-permute-start(bf16[8,192,128]{2,1,0:T(8,128)(2,1)S(1)} %slice.323), channel_id=1, source_target_pairs={{0,2},{1,3},{2,0},{3,1},{4,6},{5,7},{6,4},{7,5},{8,10},{9,11},{10,... | collective-permute-start | bytes 1179656 | tf_op jit(solution)/shard_map/ppermute | solution.py:579
  117.3 19.0 %collective-permute-start.24 = (bf16[40,3,512]{2,0,1:T(8,128)(2,1)S(1)}, bf16[40,3,512]{2,0,1:T(8,128)(2,1)S(1)}, u32[]{:S(2)}, u32[]{:S(2)}) collective-permute-start(bf16[40,3,512]{2,0,1:T(8,128)(2,1)S(1)} %get-tuple-element.406), channel_id=1, source_target_pairs={{0,2},{1,3},{2,0},{3,1},{4,6},{5,7},{6,4},{7,5},{8,10},{9,11},{10,... | collective-permute-start | bytes 368648 | tf_op jit(solution)/shard_map/ppermute | solution.py:516
  132.8 14.0 %collective-permute-start.26 = (bf16[3,40,512]{2,1,0:T(8,128)(2,1)S(1)}, bf16[3,40,512]{2,1,0:T(8,128)(2,1)S(1)}, u32[]{:S(2)}, u32[]{:S(2)}) collective-permute-start(bf16[3,40,512]{2,1,0:T(8,128)(2,1)S(1)} %get-tuple-element.426), channel_id=1, source_target_pairs={{0,28},{4,8},{8,4},{12,16},{16,12},{20,24},{24,20},{28,0},{1,29},{... | collective-permute-start | bytes 368648 | tf_op jit(solution)/shard_map/ppermute | solution.py:646
  136.3 10.5 %collective-permute-start.25 = (bf16[3,40,512]{2,1,0:T(8,128)(2,1)S(1)}, bf16[3,40,512]{2,1,0:T(8,128)(2,1)S(1)}, u32[]{:S(2)}, u32[]{:S(2)}) collective-permute-start(bf16[3,40,512]{2,1,0:T(8,128)(2,1)S(1)} %get-tuple-element.427), channel_id=1, source_target_pairs={{0,4},{4,0},{8,12},{12,8},{16,20},{20,16},{24,28},{28,24},{1,5},{5... | collective-permute-start | bytes 368648 | tf_op jit(solution)/shard_map/ppermute | solution.py:645
  160.4 18.7 %collective-permute-start.30 = (bf16[16,192,128]{2,1,0:T(8,128)(2,1)}, bf16[16,192,128]{2,1,0:T(8,128)(2,1)S(1)}, u32[]{:S(2)}, u32[]{:S(2)}) collective-permute-start(bf16[16,192,128]{2,1,0:T(8,128)(2,1)} %get-tuple-element.247), channel_id=1, source_target_pairs={{0,1},{1,0},{2,3},{3,2},{4,5},{5,4},{6,7},{7,6},{8,9},{9,8},{10,11... | collective-permute-start | bytes 2359304 | tf_op jit(solution)/shard_map/ppermute | solution.py:579
  160.5 23.2 %collective-permute-start.29 = (bf16[8,448,128]{2,1,0:T(8,128)(2,1)S(1)}, bf16[8,448,128]{2,1,0:T(8,128)(2,1)S(1)}, u32[]{:S(2)}, u32[]{:S(2)}) collective-permute-start(bf16[8,448,128]{2,1,0:T(8,128)(2,1)S(1)} %get-tuple-element.244), channel_id=1, source_target_pairs={{0,2},{1,3},{2,0},{3,1},{4,6},{5,7},{6,4},{7,5},{8,10},{9,11},{10,... | collective-permute-start | bytes 2752520 | tf_op jit(solution)/shard_map/ppermute | solution.py:579
  177.1 16.8 %collective-permute-start.34 = (bf16[3,40,512]{2,1,0:T(8,128)(2,1)}, bf16[3,40,512]{2,1,0:T(8,128)(2,1)S(1)}, u32[]{:S(2)}, u32[]{:S(2)}) collective-permute-start(bf16[3,40,512]{2,1,0:T(8,128)(2,1)} %get-tuple-element.422), channel_id=1, source_target_pairs={{0,28},{4,8},{8,4},{12,16},{16,12},{20,24},{24,20},{28,0},{1,29},{... | collective-permute-start | bytes 368648 | tf_op jit(solution)/shard_map/ppermute | solution.py:646
  178.4 15.5 %collective-permute-start.33 = (bf16[3,40,512]{2,1,0:T(8,128)(2,1)S(1)}, bf16[3,40,512]{2,1,0:T(8,128)(2,1)S(1)}, u32[]{:S(2)}, u32[]{:S(2)}) collective-permute-start(bf16[3,40,512]{2,1,0:T(8,128)(2,1)S(1)} %get-tuple-element.423), channel_id=1, source_target_pairs={{0,4},{4,0},{8,12},{12,8},{16,20},{20,16},{24,28},{28,24},{1,5},{5... | collective-permute-start | bytes 368648 | tf_op jit(solution)/shard_map/ppermute | solution.py:645
  179.4 14.5 %collective-permute-start.32 = (bf16[8,192,128]{2,1,0:T(8,128)(2,1)S(1)}, bf16[8,192,128]{2,1,0:T(8,128)(2,1)S(1)}, u32[]{:S(2)}, u32[]{:S(2)}) collective-permute-start(bf16[8,192,128]{2,1,0:T(8,128)(2,1)S(1)} %slice.451), channel_id=1, source_target_pairs={{0,2},{1,3},{2,0},{3,1},{4,6},{5,7},{6,4},{7,5},{8,10},{9,11},{10,... | collective-permute-start | bytes 1179656 | tf_op jit(solution)/shard_map/ppermute | solution.py:579
  184.0 11.9 %collective-permute-start.31 = (bf16[4,448,128]{2,1,0:T(8,128)(2,1)S(1)}, bf16[4,448,128]{2,1,0:T(8,128)(2,1)S(1)}, u32[]{:S(2)}, u32[]{:S(2)}) collective-permute-start(bf16[4,448,128]{2,1,0:T(8,128)(2,1)S(1)} %slice.450), channel_id=1, source_target_pairs={{0,4},{1,5},{2,6},{3,7},{4,0},{5,1},{6,2},{7,3},{8,12},{9,13},{10,... | collective-permute-start | bytes 1376264 | tf_op jit(solution)/shard_map/ppermute | solution.py:579
  200.9 8.1 %collective-permute-start.38 = (bf16[4,192,128]{2,1,0:T(8,128)(2,1)S(1)}, bf16[4,192,128]{2,1,0:T(8,128)(2,1)S(1)}, u32[]{:S(2)}, u32[]{:S(2)}) collective-permute-start(bf16[4,192,128]{2,1,0:T(8,128)(2,1)S(1)} %slice.453), channel_id=1, source_target_pairs={{0,4},{1,5},{2,6},{3,7},{4,0},{5,1},{6,2},{7,3},{8,12},{9,13},{10,... | collective-permute-start | bytes 589832 | tf_op jit(solution)/shard_map/ppermute | solution.py:579
  204.3 15.0 %collective-permute-start.36 = (bf16[8,256,128]{2,1,0:T(8,128)(2,1)S(1)}, bf16[8,256,128]{2,1,0:T(8,128)(2,1)S(1)}, u32[]{:S(2)}, u32[]{:S(2)}) collective-permute-start(bf16[8,256,128]{2,1,0:T(8,128)(2,1)S(1)} %slice.331), channel_id=1, source_target_pairs={{0,2},{1,3},{2,0},{3,1},{4,6},{5,7},{6,4},{7,5},{8,10},{9,11},{10,... | collective-permute-start | bytes 1572872 | tf_op jit(solution)/shard_map/ppermute | solution.py:579
  206.0 13.3 %collective-permute-start.37 = (bf16[3,160,512]{2,1,0:T(8,128)(2,1)S(1)}, bf16[3,160,512]{2,1,0:T(8,128)(2,1)S(1)}, u32[]{:S(2)}, u32[]{:S(2)}) collective-permute-start(bf16[3,160,512]{2,1,0:T(8,128)(2,1)S(1)} %get-tuple-element.398), channel_id=1, source_target_pairs={{0,1},{1,0},{2,3},{3,2},{4,5},{5,4},{6,7},{7,6},{8,9},{9,8},{10,11... | collective-permute-start | bytes 1474568 | tf_op jit(solution)/shard_map/ppermute | solution.py:516
  206.2 7.9 %collective-permute-start.41 = (bf16[1,448,128]{2,1,0:T(8,128)(2,1)S(1)}, bf16[1,448,128]{2,1,0:T(8,128)(2,1)S(1)}, u32[]{:S(2)}, u32[]{:S(2)}) collective-permute-start(bf16[1,448,128]{2,1,0:T(8,128)(2,1)S(1)} %get-tuple-element.410), channel_id=1, source_target_pairs={{0,24},{1,25},{2,26},{3,27},{4,28},{5,29},{6,30},{7,31},{8,16},{9,... | collective-permute-start | bytes 344072 | tf_op jit(solution)/shard_map/ppermute | solution.py:579
  209.0 8.9 %collective-permute-start.40 = (bf16[1,448,128]{2,1,0:T(8,128)(2,1)S(1)}, bf16[1,448,128]{2,1,0:T(8,128)(2,1)S(1)}, u32[]{:S(2)}, u32[]{:S(2)}) collective-permute-start(bf16[1,448,128]{2,1,0:T(8,128)(2,1)S(1)} %get-tuple-element.411), channel_id=1, source_target_pairs={{0,8},{1,9},{2,10},{3,11},{4,12},{5,13},{6,14},{7,15},{8,0},{9,1},... | collective-permute-start | bytes 344072 | tf_op jit(solution)/shard_map/ppermute | solution.py:579
  209.0 10.4 %collective-permute-start.39 = (bf16[1,448,128]{2,1,0:T(8,128)(2,1)S(1)}, bf16[1,448,128]{2,1,0:T(8,128)(2,1)S(1)}, u32[]{:S(2)}, u32[]{:S(2)}) collective-permute-start(bf16[1,448,128]{2,1,0:T(8,128)(2,1)S(1)} %get-tuple-element.412), channel_id=1, source_target_pairs={{0,16},{1,17},{2,18},{3,19},{4,20},{5,21},{6,22},{7,23},{8,24},{9,... | collective-permute-start | bytes 344072 | tf_op jit(solution)/shard_map/ppermute | solution.py:579
  219.9 17.8 %collective-permute-start.50 = (bf16[40,3,512]{2,0,1:T(8,128)(2,1)S(1)}, bf16[40,3,512]{2,0,1:T(8,128)(2,1)S(1)}, u32[]{:S(2)}, u32[]{:S(2)}) collective-permute-start(bf16[40,3,512]{2,0,1:T(8,128)(2,1)S(1)} %get-tuple-element.404), channel_id=1, source_target_pairs={{0,2},{1,3},{2,0},{3,1},{4,6},{5,7},{6,4},{7,5},{8,10},{9,11},{10,... | collective-permute-start | bytes 368648 | tf_op jit(solution)/shard_map/ppermute | solution.py:516
  220.8 9.7 %collective-permute-start.42 = (bf16[4,256,128]{2,1,0:T(8,128)(2,1)S(1)}, bf16[4,256,128]{2,1,0:T(8,128)(2,1)S(1)}, u32[]{:S(2)}, u32[]{:S(2)}) collective-permute-start(bf16[4,256,128]{2,1,0:T(8,128)(2,1)S(1)} %slice.452), channel_id=1, source_target_pairs={{0,4},{1,5},{2,6},{3,7},{4,0},{5,1},{6,2},{7,3},{8,12},{9,13},{10,... | collective-permute-start | bytes 786440 | tf_op jit(solution)/shard_map/ppermute | solution.py:579
  227.2 10.5 %collective-permute-start.49 = (bf16[320,512]{1,0:T(8,128)(2,1)S(1)}, bf16[320,512]{1,0:T(8,128)(2,1)S(1)}, u32[]{:S(2)}, u32[]{:S(2)}) collective-permute-start(bf16[320,512]{1,0:T(8,128)(2,1)S(1)} %fusion.6), channel_id=1, source_target_pairs={{0,2},{1,3},{2,0},{3,1},{4,6},{5,7},{6,4},{7,5},{8,10},{9,11},{10,... | collective-permute-start | bytes 983048 | tf_op jit(solution)/shard_map/ppermute | solution.py:516
  (105 other events, 900.9 us)

commit v9 on v8

--- a/solution.py
+++ b/solution.py
@@ -995,7 +995,7 @@
     chain_zero = split(chain_zero[0].astype(F32) + zero_arrived.astype(F32), 2)
     edge_arrived = exchange(sent, steps - 1, 1)
     kept, sent = split((kept.astype(F32) + edge_arrived.astype(F32)).astype(BF16), 2)
-    zero_arrived = after(exchange(chain_zero[1], steps - 3, 1), sent)
+    zero_arrived = exchange(after(chain_zero[1], sent), steps - 3, 1)
     returned = after(returned, sent)
     chain_zero = chain_zero[0].astype(F32) + zero_arrived.astype(F32)
     for begin, end in reversed(z_rounds[1:]):

time: 261 us -> 262 us (level)
  transfers between devices with their start and end apart: 58 -> 58, of which waited for: 28 -> 29; matrix products, arithmetic and copies ran while one was open for 11% -> 11% of each run, Pallas kernels for 28% -> 28%
where the time goes in v9:
time: 262 us; the launch traced here: 261 us
  Pallas kernels  88.7 us (34%)
  starting transfers between devices  66 us (25%)
  waiting for transfers between devices  49.9 us (19%)
  local copies, waits for them, and re-layouts  26.6 us (10%)
  other arithmetic  26.1 us (10%)
  between operations  2.99 us (1%)
    pallas_call x9, Pallas kernels, run_kernel(): pl.pallas_call(kernel, name=name, grid=(samples,), in_specs=in_specs, out...  88.7 us
    ppermute x41, starting transfers between devices, exchange(): lax.ppermute(values, ('node', 'hid'), [(i, i ^ mask) for i in range(total)])  44.9 us
    ppermute x41, waiting for transfers between devices, exchange(): lax.ppermute(values, ('node', 'hid'), [(i, i ^ mask) for i in range(total)])  41.4 us
    unnamed x165, local copies, waits for them, and re-layouts  9.69 us
    ppermute x3, starting transfers between devices, neighbour_swaps(): second = lax.ppermute(jnp.where(even, to_previous, to_next), 'node', two)  8.76 us
    ppermute x9, starting transfers between devices, swap(): lax.ppermute(values, axis, [(i, i ^ offset) for i in range(lax.axis_size(...  6.27 us
  transfers between devices with their start and end apart: 58, of which 29 were waited for; matrix products, arithmetic and copies ran while one was open for 11% of the time, Pallas kernels for 28%

profile of v9, /device:TPU:0, one launch (start us, length us, event | category | flops | bytes accessed | tf_op | source)
XLA Modules:
  0.0 261.2 jit_solution(9834210664822421613)
XLA Ops:
  4.1 5.1 %collective-permute-start.2 = (bf16[1,448,128]{2,1,0:T(8,128)(2,1)S(1)}, bf16[1,448,128]{2,1,0:T(8,128)(2,1)S(1)}, u32[]{:S(2)}, u32[]{:S(2)}) collective-permute-start(bf16[1,448,128]{2,1,0:T(8,128)(2,1)S(1)} %maximum_bitcast_fusion), channel_id=1, source_target_pairs={{0,24},{1,25},{2,26},{3,27},{4,28},{5,29},{6,30},{7,31},{8,16},{9,... | collective-permute-start | bytes 344072 | tf_op jit(solution)/shard_map/ppermute | solution.py:579
  13.3 2.7 %collective-permute-done.1 = bf16[1,448,128]{2,1,0:T(8,128)(2,1)S(1)} collective-permute-done((bf16[1,448,128]{2,1,0:T(8,128)(2,1)S(1)}, bf16[1,448,128]{2,1,0:T(8,128)(2,1)S(1)}, u32[]{:S(2)}, u32[]{:S(2)}) %collective-permute-start.1) | collective-permute-done | bytes 114720 | tf_op jit(solution)/shard_map/ppermute | solution.py:579
  16.0 3.0 %collective-permute-done = bf16[1,448,128]{2,1,0:T(8,128)(2,1)S(1)} collective-permute-done((bf16[1,448,128]{2,1,0:T(8,128)(2,1)S(1)}, bf16[1,448,128]{2,1,0:T(8,128)(2,1)S(1)}, u32[]{:S(2)}, u32[]{:S(2)}) %collective-permute-start) | collective-permute-done | bytes 114720 | tf_op jit(solution)/shard_map/ppermute | solution.py:579
  25.6 7.0 %collective-permute-done.3 = bf16[4,448,128]{2,1,0:T(8,128)(2,1)} collective-permute-done((bf16[4,448,128]{2,1,0:T(8,128)(2,1)}, bf16[4,448,128]{2,1,0:T(8,128)(2,1)}, u32[]{:S(2)}, u32[]{:S(2)}) %collective-permute-start.3) | collective-permute-done | bytes 458784 | tf_op jit(solution)/shard_map/ppermute | solution.py:579
  35.4 3.0 %collective-permute-start.9 = (bf16[1,448,128]{2,1,0:T(8,128)(2,1)S(1)}, bf16[1,448,128]{2,1,0:T(8,128)(2,1)S(1)}, u32[]{:S(2)}, u32[]{:S(2)}) collective-permute-start(bf16[1,448,128]{2,1,0:T(8,128)(2,1)S(1)} %maximum_bitcast_fusion.1), channel_id=1, source_target_pairs={{0,24},{1,25},{2,26},{3,27},{4,28},{5,29},{6,30},{7,31},{8,16},{9,... | collective-permute-start | bytes 344072 | tf_op jit(solution)/shard_map/ppermute | solution.py:579
  39.8 4.0 %collective-permute-start.6 = (bf16[3,40,512]{2,1,0:T(8,128)(2,1)S(1)}, bf16[3,40,512]{2,1,0:T(8,128)(2,1)S(1)}, u32[]{:S(2)}, u32[]{:S(2)}) collective-permute-start(bf16[3,40,512]{2,1,0:T(8,128)(2,1)S(1)} %get-tuple-element.434), channel_id=1, source_target_pairs={{0,28},{4,8},{8,4},{12,16},{16,12},{20,24},{24,20},{28,0},{1,29},{... | collective-permute-start | bytes 368648 | tf_op jit(solution)/shard_map/ppermute | solution.py:646
  44.5 2.2 collective-permute-done.8
  46.7 2.7 %collective-permute-done.6 = bf16[3,40,512]{2,1,0:T(8,128)(2,1)S(1)} collective-permute-done((bf16[3,40,512]{2,1,0:T(8,128)(2,1)S(1)}, bf16[3,40,512]{2,1,0:T(8,128)(2,1)S(1)}, u32[]{:S(2)}, u32[]{:S(2)}) %collective-permute-start.6) | collective-permute-done | bytes 122912 | tf_op jit(solution)/shard_map/ppermute | solution.py:646
  55.3 11.5 %edge_forward.2 = (bf16[3,640,512]{2,1,0:T(8,128)(2,1)}, bf16[3,640,512]{2,1,0:T(8,128)(2,1)}, bf16[3,640,512]{2,1,0:T(8,128)(2,1)}, f32[3,640,1]{2,1,0:T(8,128)...) custom-call(s32[32]{0:T(128)} %add.290.order, ...), custom_call_target="tpu_custom_call" | custom-call | flops 15225323520 | bytes 19271296 | tf_op jit(solution)/shard_map/edge_forward/pallas_call | solution.py:129
  71.7 5.1 %node_pass.2 = (bf16[480,512]{1,0:T(8,128)(2,1)}, bf16[480,512]{1,0:T(8,128)(2,1)}, bf16[480,512]{1,0:T(8,128)(2,1)}, bf16[480,512]{1,0:T(8,128)(2,1)}, f32[480,...) custom-call(s32[32]{0:T(128)} %add.290.order, ...), custom_call_target="tpu_custom_call" | custom-call | flops 3019898880 | bytes 7269376 | tf_op jit(solution)/shard_map/node_pass/pallas_call | solution.py:129
  79.2 3.3 %collective-permute-start.17 = (bf16[3,40,512]{2,1,0:T(8,128)(2,1)S(1)}, bf16[3,40,512]{2,1,0:T(8,128)(2,1)S(1)}, u32[]{:S(2)}, u32[]{:S(2)}) collective-permute-start(bf16[3,40,512]{2,1,0:T(8,128)(2,1)S(1)} %get-tuple-element.431), channel_id=1, source_target_pairs={{4,0},{8,4},{12,8},{16,12},{20,16},{24,20},{28,24},{0,28},{5,1},{9... | collective-permute-start | bytes 368648 | tf_op jit(solution)/shard_map/ppermute | solution.py:635
  82.5 3.4 %collective-permute-done.16 = bf16[3,40,512]{2,1,0:T(8,128)(2,1)S(1)} collective-permute-done((bf16[3,40,512]{2,1,0:T(8,128)(2,1)S(1)}, bf16[3,40,512]{2,1,0:T(8,128)(2,1)S(1)}, u32[]{:S(2)}, u32[]{:S(2)}) %collective-permute-start.16) | collective-permute-done | bytes 122912 | tf_op jit(solution)/shard_map/ppermute | solution.py:634
  91.7 10.9 %edge_forward.3 = (bf16[3,640,512]{2,1,0:T(8,128)(2,1)}, bf16[3,640,512]{2,1,0:T(8,128)(2,1)}, bf16[3,640,512]{2,1,0:T(8,128)(2,1)}, f32[3,640,1]{2,1,0:T(8,128)}, bf16[3,160,512]{2,1,0:T(8,128)(2,1)}) custom-call(s32[32]{0:T(128)} %add.290.order, bf16[16,256,128]{2,1,0:T(8,128)(2,1)} %copy-done.11, bf16[16,256,128]{2,1,0:T(8,128)(2,1)} %collective-permute-done.18.w1x.w2x, ...), custom_call_target="tpu_custom_call" | custom-call | flops 15225323520 | bytes 17960576 | tf_op jit(solution)/shard_map/edge_forward/pallas_call | solution.py:129
  107.5 8.2 %node_pass.3 = (bf16[3,160,512]{2,1,0:T(8,128)(2,1)}, bf16[3,160,512]{2,1,0:T(8,128)(2,1)}, f32[3,160,512]{2,1,0:T(8,128)}, bf16[16,192,128]{2,1,0:T(8,128)(2,1)...) custom-call(s32[32]{0:T(128)} %add.290.order, s32[64]{0:T(128)} %reshape.341.rest_0_.owners, ...), custom_call_target="tpu_custom_call" | custom-call | flops 9059696640 | bytes 8087820 | tf_op jit(solution)/shard_map/node_pass/pallas_call | solution.py:129
  118.8 13.0 %edge_backward.2 = (bf16[3,640,512]{2,1,0:T(8,128)(2,1)}, bf16[3,640,512]{2,1,0:T(8,128)(2,1)}, bf16[3,400,512]{2,1,0:T(8,128)(2,1)}, f32[3,160,512]{2,1,0:T(8,1...) custom-call(s32[32]{0:T(128)} %add.290.order, bf16[16,256,128]{2,1,0:T(8,128)(2,1)} %copy-done.11, ...), custom_call_target="tpu_custom_call" | custom-call | flops 14344519680 | bytes 19674752 | tf_op jit(solution)/shard_map/edge_backward/pallas_call | solution.py:129
  132.8 3.5 %collective-permute-start.26 = (bf16[3,40,512]{2,1,0:T(8,128)(2,1)S(1)}, bf16[3,40,512]{2,1,0:T(8,128)(2,1)S(1)}, u32[]{:S(2)}, u32[]{:S(2)}) collective-permute-start(bf16[3,40,512]{2,1,0:T(8,128)(2,1)S(1)} %get-tuple-element.426), channel_id=1, source_target_pairs={{0,28},{4,8},{8,4},{12,16},{16,12},{20,24},{24,20},{28,0},{1,29},{... | collective-permute-start | bytes 368648 | tf_op jit(solution)/shard_map/ppermute | solution.py:646
  137.0 9.8 %edge_weight_grads.2 = (bf16[16,448,128]{2,1,0:T(8,128)(2,1)}, bf16[16,448,128]{2,1,0:T(8,128)(2,1)}) custom-call(s32[64]{0:T(128)} %reshape.341.rest_0_.owners, bf16[3,640,512]{2,1,0:T(8,128)(2,1)} %get-tuple-element.195.low.edge_low, bf16[3,240,512]{2,1,0:T(8,128)(2,1)} %copy-done.33, bf16[3,640,512]{2,1,0:T(8,128)(2,1)} %get-tuple-element.217.hidden_low, ...), custom_call_target="tpu_custom_call" | custom-call | flops 8053063680 | bytes 15073536 | tf_op jit(solution)/shard_map/edge_weight_grads/pallas_call | solution.py:129
  149.2 1.7 collective-permute-done.28
  152.4 8.0 %node_backward.1 = (bf16[3,160,512]{2,1,0:T(8,128)(2,1)}, f32[3,160,512]{2,1,0:T(8,128)}, bf16[16,192,128]{2,1,0:T(8,128)(2,1)}, bf16[16,192,128]{2,1,0:T(8,128)(2,1)}, f32[4,512]{1,0:T(4,128)}) custom-call(s32[32]{0:T(128)} %add.290.order, s32[64]{0:T(128)} %reshape.341.rest_0_.owners, bf16[16,192,128]{2,1,0:T(8,128)(2,1)} %copy-done.41, ...), custom_call_target="tpu_custom_call" | custom-call | flops 6039797760 | bytes 9564288 | tf_op jit(solution)/shard_map/node_backward/pallas_call | solution.py:129
  161.0 14.4 %edge_backward.3 = (bf16[3,640,512]{2,1,0:T(8,128)(2,1)}, bf16[3,640,512]{2,1,0:T(8,128)(2,1)}, bf16[3,400,512]{2,1,0:T(8,128)(2,1)}, f32[3,160,512]{2,1,0:T(8,1...) custom-call(s32[32]{0:T(128)} %add.290.order, ...), custom_call_target="tpu_custom_call" | custom-call | flops 14344519680 | bytes 21640832 | tf_op jit(solution)/shard_map/edge_backward/pallas_call | solution.py:129
  181.0 2.8 %collective-permute-done.29 = bf16[8,448,128]{2,1,0:T(8,128)(2,1)S(1)} collective-permute-done((bf16[8,448,128]{2,1,0:T(8,128)(2,1)S(1)}, bf16[8,448,128]{2,1,0:T(8,128)(2,1)S(1)}, u32[]{:S(2)}, u32[]{:S(2)}) %collective-permute-start.29) | collective-permute-done | bytes 917536 | tf_op jit(solution)/shard_map/ppermute | solution.py:579
  184.0 2.1 collective-permute-start.31
  186.1 7.8 %edge_weight_grads.3 = (bf16[16,256,128]{2,1,0:T(8,128)(2,1)}, bf16[16,256,128]{2,1,0:T(8,128)(2,1)}) custom-call(s32[64]{0:T(128)} %reshape.341.rest_0_.owners, bf16[640,512]{1,0:T(8,128)(2,1)} %bitcast.164, bf16[3,240,512]{2,1,0:T(8,128)(2,1)} %pad_maximum_fusion.2.table, bf16[640,512]{1,0:T(8,128)(2,1)} %get-tuple-element.240.hidden_low, ...), custom_call_target="tpu_custom_call" | custom-call | flops 8053063680 | bytes 9306368 | tf_op jit(solution)/shard_map/edge_weight_grads/pallas_call | solution.py:129
  193.9 2.0 collective-permute-done.31
  207.0 2.8 %collective-permute-start.41 = (bf16[1,448,128]{2,1,0:T(8,128)(2,1)S(1)}, bf16[1,448,128]{2,1,0:T(8,128)(2,1)S(1)}, u32[]{:S(2)}, u32[]{:S(2)}) collective-permute-start(bf16[1,448,128]{2,1,0:T(8,128)(2,1)S(1)} %get-tuple-element.410), channel_id=1, source_target_pairs={{0,24},{1,25},{2,26},{3,27},{4,28},{5,29},{6,30},{7,31},{8,16},{9,... | collective-permute-start | bytes 344072 | tf_op jit(solution)/shard_map/ppermute | solution.py:579
  209.8 2.4 collective-permute-done.38
  214.9 3.7 %collective-permute-done.40 = bf16[1,448,128]{2,1,0:T(8,128)(2,1)S(1)} collective-permute-done((bf16[1,448,128]{2,1,0:T(8,128)(2,1)S(1)}, bf16[1,448,128]{2,1,0:T(8,128)(2,1)S(1)}, u32[]{:S(2)}, u32[]{:S(2)}) %collective-permute-start.40) | collective-permute-done | bytes 114720 | tf_op jit(solution)/shard_map/ppermute | solution.py:579
  222.8 2.8 %collective-permute-start.44 = (bf16[1,192,128]{2,1,0:T(8,128)(2,1)S(1)}, bf16[1,192,128]{2,1,0:T(8,128)(2,1)S(1)}, u32[]{:S(2)}, u32[]{:S(2)}) collective-permute-start(bf16[1,192,128]{2,1,0:T(8,128)(2,1)S(1)} %get-tuple-element.271), channel_id=1, source_target_pairs={{0,8},{1,9},{2,10},{3,11},{4,12},{5,13},{6,14},{7,15},{8,0},{9,1},... | collective-permute-start | bytes 147464 | tf_op jit(solution)/shard_map/ppermute | solution.py:579
  229.2 2.8 %collective-permute-done.45 = bf16[1,192,128]{2,1,0:T(8,128)(2,1)S(1)} collective-permute-done((bf16[1,192,128]{2,1,0:T(8,128)(2,1)S(1)}, bf16[1,192,128]{2,1,0:T(8,128)(2,1)S(1)}, u32[]{:S(2)}, u32[]{:S(2)}) %collective-permute-start.45) | collective-permute-done | bytes 49184 | tf_op jit(solution)/shard_map/ppermute | solution.py:579
  233.5 2.3 collective-permute-start.47
  248.7 1.9 collective-permute-start.57
  250.5 2.6 collective-permute-start.55
  (405 shorter events, 99.8 us)
Async XLA Ops:
  4.1 9.2 %collective-permute-start.2 = (bf16[1,448,128]{2,1,0:T(8,128)(2,1)S(1)}, bf16[1,448,128]{2,1,0:T(8,128)(2,1)S(1)}, u32[]{:S(2)}, u32[]{:S(2)}) collective-permute-start(bf16[1,448,128]{2,1,0:T(8,128)(2,1)S(1)} %maximum_bitcast_fusion), channel_id=1, source_target_pairs={{0,24},{1,25},{2,26},{3,27},{4,28},{5,29},{6,30},{7,31},{8,16},{9,... | collective-permute-start | bytes 344072 | tf_op jit(solution)/shard_map/ppermute | solution.py:579
  9.3 9.7 %collective-permute-start = (bf16[1,448,128]{2,1,0:T(8,128)(2,1)S(1)}, bf16[1,448,128]{2,1,0:T(8,128)(2,1)S(1)}, u32[]{:S(2)}, u32[]{:S(2)}) collective-permute-start(bf16[1,448,128]{2,1,0:T(8,128)(2,1)S(1)} %maximum_bitcast_fusion), channel_id=1, source_target_pairs={{0,16},{1,17},{2,18},{3,19},{4,20},{5,21},{6,22},{7,23},{8,24},{9,... | collective-permute-start | bytes 344072 | tf_op jit(solution)/shard_map/ppermute | solution.py:579
  20.6 12.0 %collective-permute-start.3 = (bf16[4,448,128]{2,1,0:T(8,128)(2,1)}, bf16[4,448,128]{2,1,0:T(8,128)(2,1)}, u32[]{:S(2)}, u32[]{:S(2)}) collective-permute-start(bf16[4,448,128]{2,1,0:T(8,128)(2,1)} %pad_maximum_fusion.6), channel_id=1, source_target_pairs={{0,4},{1,5},{2,6},{3,7},{4,0},{5,1},{6,2},{7,3},{8,12},{9,13},{10,... | collective-permute-start | bytes 1376264 | tf_op jit(solution)/shard_map/ppermute | solution.py:579
  33.7 16.3 %collective-permute-start.4 = (bf16[8,256,128]{2,1,0:T(8,128)(2,1)S(1)}, bf16[8,256,128]{2,1,0:T(8,128)(2,1)S(1)}, u32[]{:S(2)}, u32[]{:S(2)}) collective-permute-start(bf16[8,256,128]{2,1,0:T(8,128)(2,1)S(1)} %slice.320), channel_id=1, source_target_pairs={{0,2},{1,3},{2,0},{3,1},{4,6},{5,7},{6,4},{7,5},{8,10},{9,11},{10,... | collective-permute-start | bytes 1572872 | tf_op jit(solution)/shard_map/ppermute | solution.py:579
  35.4 8.4 %collective-permute-start.9 = (bf16[1,448,128]{2,1,0:T(8,128)(2,1)S(1)}, bf16[1,448,128]{2,1,0:T(8,128)(2,1)S(1)}, u32[]{:S(2)}, u32[]{:S(2)}) collective-permute-start(bf16[1,448,128]{2,1,0:T(8,128)(2,1)S(1)} %maximum_bitcast_fusion.1), channel_id=1, source_target_pairs={{0,24},{1,25},{2,26},{3,27},{4,28},{5,29},{6,30},{7,31},{8,16},{9,... | collective-permute-start | bytes 344072 | tf_op jit(solution)/shard_map/ppermute | solution.py:579
  38.4 8.3 %collective-permute-start.8 = (bf16[1,448,128]{2,1,0:T(8,128)(2,1)S(1)}, bf16[1,448,128]{2,1,0:T(8,128)(2,1)S(1)}, u32[]{:S(2)}, u32[]{:S(2)}) collective-permute-start(bf16[1,448,128]{2,1,0:T(8,128)(2,1)S(1)} %maximum_bitcast_fusion.1), channel_id=1, source_target_pairs={{0,8},{1,9},{2,10},{3,11},{4,12},{5,13},{6,14},{7,15},{8,0},{9,1},... | collective-permute-start | bytes 344072 | tf_op jit(solution)/shard_map/ppermute | solution.py:579
  38.4 8.3 %collective-permute-start.7 = (bf16[1,448,128]{2,1,0:T(8,128)(2,1)S(1)}, bf16[1,448,128]{2,1,0:T(8,128)(2,1)S(1)}, u32[]{:S(2)}, u32[]{:S(2)}) collective-permute-start(bf16[1,448,128]{2,1,0:T(8,128)(2,1)S(1)} %maximum_bitcast_fusion.1), channel_id=1, source_target_pairs={{0,16},{1,17},{2,18},{3,19},{4,20},{5,21},{6,22},{7,23},{8,24},{9,... | collective-permute-start | bytes 344072 | tf_op jit(solution)/shard_map/ppermute | solution.py:579
  39.8 9.6 %collective-permute-start.6 = (bf16[3,40,512]{2,1,0:T(8,128)(2,1)S(1)}, bf16[3,40,512]{2,1,0:T(8,128)(2,1)S(1)}, u32[]{:S(2)}, u32[]{:S(2)}) collective-permute-start(bf16[3,40,512]{2,1,0:T(8,128)(2,1)S(1)} %get-tuple-element.434), channel_id=1, source_target_pairs={{0,28},{4,8},{8,4},{12,16},{16,12},{20,24},{24,20},{28,0},{1,29},{... | collective-permute-start | bytes 368648 | tf_op jit(solution)/shard_map/ppermute | solution.py:646
  51.9 14.9 %collective-permute-start.11 = (bf16[8,192,128]{2,1,0:T(8,128)(2,1)S(1)}, bf16[8,192,128]{2,1,0:T(8,128)(2,1)S(1)}, u32[]{:S(2)}, u32[]{:S(2)}) collective-permute-start(bf16[8,192,128]{2,1,0:T(8,128)(2,1)S(1)} %slice.321), channel_id=1, source_target_pairs={{0,2},{1,3},{2,0},{3,1},{4,6},{5,7},{6,4},{7,5},{8,10},{9,11},{10,... | collective-permute-start | bytes 1179656 | tf_op jit(solution)/shard_map/ppermute | solution.py:579
  52.6 14.2 %collective-permute-start.12 = (bf16[4,448,128]{2,1,0:T(8,128)(2,1)S(1)}, bf16[4,448,128]{2,1,0:T(8,128)(2,1)S(1)}, u32[]{:S(2)}, u32[]{:S(2)}) collective-permute-start(bf16[4,448,128]{2,1,0:T(8,128)(2,1)S(1)} %pad_maximum_fusion.7), channel_id=1, source_target_pairs={{0,4},{1,5},{2,6},{3,7},{4,0},{5,1},{6,2},{7,3},{8,12},{9,13},{10,... | collective-permute-start | bytes 1376264 | tf_op jit(solution)/shard_map/ppermute | solution.py:579
  67.7 19.3 %collective-permute-start.13 = (bf16[8,256,128]{2,1,0:T(8,128)(2,1)S(1)}, bf16[8,256,128]{2,1,0:T(8,128)(2,1)S(1)}, u32[]{:S(2)}, u32[]{:S(2)}) collective-permute-start(bf16[8,256,128]{2,1,0:T(8,128)(2,1)S(1)} %slice.322), channel_id=1, source_target_pairs={{0,2},{1,3},{2,0},{3,1},{4,6},{5,7},{6,4},{7,5},{8,10},{9,11},{10,... | collective-permute-start | bytes 1572872 | tf_op jit(solution)/shard_map/ppermute | solution.py:579
  77.8 8.2 %collective-permute-start.16 = (bf16[3,40,512]{2,1,0:T(8,128)(2,1)S(1)}, bf16[3,40,512]{2,1,0:T(8,128)(2,1)S(1)}, u32[]{:S(2)}, u32[]{:S(2)}) collective-permute-start(bf16[3,40,512]{2,1,0:T(8,128)(2,1)S(1)} %get-tuple-element.430), channel_id=1, source_target_pairs={{0,4},{4,8},{8,12},{12,16},{16,20},{20,24},{24,28},{28,0},{1,5},{5... | collective-permute-start | bytes 368648 | tf_op jit(solution)/shard_map/ppermute | solution.py:634
  79.2 7.7 %collective-permute-start.17 = (bf16[3,40,512]{2,1,0:T(8,128)(2,1)S(1)}, bf16[3,40,512]{2,1,0:T(8,128)(2,1)S(1)}, u32[]{:S(2)}, u32[]{:S(2)}) collective-permute-start(bf16[3,40,512]{2,1,0:T(8,128)(2,1)S(1)} %get-tuple-element.431), channel_id=1, source_target_pairs={{4,0},{8,4},{12,8},{16,12},{20,16},{24,20},{28,24},{0,28},{5,1},{9... | collective-permute-start | bytes 368648 | tf_op jit(solution)/shard_map/ppermute | solution.py:635
  88.5 14.0 %collective-permute-start.20 = (bf16[40,3,512]{2,0,1:T(8,128)(2,1)S(1)}, bf16[40,3,512]{2,0,1:T(8,128)(2,1)S(1)}, u32[]{:S(2)}, u32[]{:S(2)}) collective-permute-start(bf16[40,3,512]{2,0,1:T(8,128)(2,1)S(1)} %constant_dynamic-slice_fusion), channel_id=1, source_target_pairs={{0,2},{1,3},{2,0},{3,1},{4,6},{5,7},{6,4},{7,5},{8,10},{9,11},{10,... | collective-permute-start | bytes 368648 | tf_op jit(solution)/shard_map/ppermute | solution.py:516
  90.2 12.4 %collective-permute-start.19 = (bf16[8,192,128]{2,1,0:T(8,128)(2,1)S(1)}, bf16[8,192,128]{2,1,0:T(8,128)(2,1)S(1)}, u32[]{:S(2)}, u32[]{:S(2)}) collective-permute-start(bf16[8,192,128]{2,1,0:T(8,128)(2,1)S(1)} %slice.323), channel_id=1, source_target_pairs={{0,2},{1,3},{2,0},{3,1},{4,6},{5,7},{6,4},{7,5},{8,10},{9,11},{10,... | collective-permute-start | bytes 1179656 | tf_op jit(solution)/shard_map/ppermute | solution.py:579
  117.3 19.0 %collective-permute-start.24 = (bf16[40,3,512]{2,0,1:T(8,128)(2,1)S(1)}, bf16[40,3,512]{2,0,1:T(8,128)(2,1)S(1)}, u32[]{:S(2)}, u32[]{:S(2)}) collective-permute-start(bf16[40,3,512]{2,0,1:T(8,128)(2,1)S(1)} %get-tuple-element.406), channel_id=1, source_target_pairs={{0,2},{1,3},{2,0},{3,1},{4,6},{5,7},{6,4},{7,5},{8,10},{9,11},{10,... | collective-permute-start | bytes 368648 | tf_op jit(solution)/shard_map/ppermute | solution.py:516
  132.8 14.0 %collective-permute-start.26 = (bf16[3,40,512]{2,1,0:T(8,128)(2,1)S(1)}, bf16[3,40,512]{2,1,0:T(8,128)(2,1)S(1)}, u32[]{:S(2)}, u32[]{:S(2)}) collective-permute-start(bf16[3,40,512]{2,1,0:T(8,128)(2,1)S(1)} %get-tuple-element.426), channel_id=1, source_target_pairs={{0,28},{4,8},{8,4},{12,16},{16,12},{20,24},{24,20},{28,0},{1,29},{... | collective-permute-start | bytes 368648 | tf_op jit(solution)/shard_map/ppermute | solution.py:646
  136.3 10.5 %collective-permute-start.25 = (bf16[3,40,512]{2,1,0:T(8,128)(2,1)S(1)}, bf16[3,40,512]{2,1,0:T(8,128)(2,1)S(1)}, u32[]{:S(2)}, u32[]{:S(2)}) collective-permute-start(bf16[3,40,512]{2,1,0:T(8,128)(2,1)S(1)} %get-tuple-element.427), channel_id=1, source_target_pairs={{0,4},{4,0},{8,12},{12,8},{16,20},{20,16},{24,28},{28,24},{1,5},{5... | collective-permute-start | bytes 368648 | tf_op jit(solution)/shard_map/ppermute | solution.py:645
  160.4 18.7 %collective-permute-start.30 = (bf16[16,192,128]{2,1,0:T(8,128)(2,1)}, bf16[16,192,128]{2,1,0:T(8,128)(2,1)S(1)}, u32[]{:S(2)}, u32[]{:S(2)}) collective-permute-start(bf16[16,192,128]{2,1,0:T(8,128)(2,1)} %get-tuple-element.247), channel_id=1, source_target_pairs={{0,1},{1,0},{2,3},{3,2},{4,5},{5,4},{6,7},{7,6},{8,9},{9,8},{10,11... | collective-permute-start | bytes 2359304 | tf_op jit(solution)/shard_map/ppermute | solution.py:579
  160.5 23.2 %collective-permute-start.29 = (bf16[8,448,128]{2,1,0:T(8,128)(2,1)S(1)}, bf16[8,448,128]{2,1,0:T(8,128)(2,1)S(1)}, u32[]{:S(2)}, u32[]{:S(2)}) collective-permute-start(bf16[8,448,128]{2,1,0:T(8,128)(2,1)S(1)} %get-tuple-element.244), channel_id=1, source_target_pairs={{0,2},{1,3},{2,0},{3,1},{4,6},{5,7},{6,4},{7,5},{8,10},{9,11},{10,... | collective-permute-start | bytes 2752520 | tf_op jit(solution)/shard_map/ppermute | solution.py:579
  177.1 16.8 %collective-permute-start.34 = (bf16[3,40,512]{2,1,0:T(8,128)(2,1)}, bf16[3,40,512]{2,1,0:T(8,128)(2,1)S(1)}, u32[]{:S(2)}, u32[]{:S(2)}) collective-permute-start(bf16[3,40,512]{2,1,0:T(8,128)(2,1)} %get-tuple-element.422), channel_id=1, source_target_pairs={{0,28},{4,8},{8,4},{12,16},{16,12},{20,24},{24,20},{28,0},{1,29},{... | collective-permute-start | bytes 368648 | tf_op jit(solution)/shard_map/ppermute | solution.py:646
  178.4 15.5 %collective-permute-start.33 = (bf16[3,40,512]{2,1,0:T(8,128)(2,1)S(1)}, bf16[3,40,512]{2,1,0:T(8,128)(2,1)S(1)}, u32[]{:S(2)}, u32[]{:S(2)}) collective-permute-start(bf16[3,40,512]{2,1,0:T(8,128)(2,1)S(1)} %get-tuple-element.423), channel_id=1, source_target_pairs={{0,4},{4,0},{8,12},{12,8},{16,20},{20,16},{24,28},{28,24},{1,5},{5... | collective-permute-start | bytes 368648 | tf_op jit(solution)/shard_map/ppermute | solution.py:645
  179.4 14.5 %collective-permute-start.32 = (bf16[8,192,128]{2,1,0:T(8,128)(2,1)S(1)}, bf16[8,192,128]{2,1,0:T(8,128)(2,1)S(1)}, u32[]{:S(2)}, u32[]{:S(2)}) collective-permute-start(bf16[8,192,128]{2,1,0:T(8,128)(2,1)S(1)} %slice.451), channel_id=1, source_target_pairs={{0,2},{1,3},{2,0},{3,1},{4,6},{5,7},{6,4},{7,5},{8,10},{9,11},{10,... | collective-permute-start | bytes 1179656 | tf_op jit(solution)/shard_map/ppermute | solution.py:579
  184.0 11.9 %collective-permute-start.31 = (bf16[4,448,128]{2,1,0:T(8,128)(2,1)S(1)}, bf16[4,448,128]{2,1,0:T(8,128)(2,1)S(1)}, u32[]{:S(2)}, u32[]{:S(2)}) collective-permute-start(bf16[4,448,128]{2,1,0:T(8,128)(2,1)S(1)} %slice.450), channel_id=1, source_target_pairs={{0,4},{1,5},{2,6},{3,7},{4,0},{5,1},{6,2},{7,3},{8,12},{9,13},{10,... | collective-permute-start | bytes 1376264 | tf_op jit(solution)/shard_map/ppermute | solution.py:579
  203.6 16.6 %collective-permute-start.36 = (bf16[8,256,128]{2,1,0:T(8,128)(2,1)S(1)}, bf16[8,256,128]{2,1,0:T(8,128)(2,1)S(1)}, u32[]{:S(2)}, u32[]{:S(2)}) collective-permute-start(bf16[8,256,128]{2,1,0:T(8,128)(2,1)S(1)} %slice.331), channel_id=1, source_target_pairs={{0,2},{1,3},{2,0},{3,1},{4,6},{5,7},{6,4},{7,5},{8,10},{9,11},{10,... | collective-permute-start | bytes 1572872 | tf_op jit(solution)/shard_map/ppermute | solution.py:579
  206.9 13.3 %collective-permute-start.37 = (bf16[3,160,512]{2,1,0:T(8,128)(2,1)S(1)}, bf16[3,160,512]{2,1,0:T(8,128)(2,1)S(1)}, u32[]{:S(2)}, u32[]{:S(2)}) collective-permute-start(bf16[3,160,512]{2,1,0:T(8,128)(2,1)S(1)} %get-tuple-element.398), channel_id=1, source_target_pairs={{0,1},{1,0},{2,3},{3,2},{4,5},{5,4},{6,7},{7,6},{8,9},{9,8},{10,11... | collective-permute-start | bytes 1474568 | tf_op jit(solution)/shard_map/ppermute | solution.py:516
  207.0 7.9 %collective-permute-start.41 = (bf16[1,448,128]{2,1,0:T(8,128)(2,1)S(1)}, bf16[1,448,128]{2,1,0:T(8,128)(2,1)S(1)}, u32[]{:S(2)}, u32[]{:S(2)}) collective-permute-start(bf16[1,448,128]{2,1,0:T(8,128)(2,1)S(1)} %get-tuple-element.410), channel_id=1, source_target_pairs={{0,24},{1,25},{2,26},{3,27},{4,28},{5,29},{6,30},{7,31},{8,16},{9,... | collective-permute-start | bytes 344072 | tf_op jit(solution)/shard_map/ppermute | solution.py:579
  209.8 8.7 %collective-permute-start.40 = (bf16[1,448,128]{2,1,0:T(8,128)(2,1)S(1)}, bf16[1,448,128]{2,1,0:T(8,128)(2,1)S(1)}, u32[]{:S(2)}, u32[]{:S(2)}) collective-permute-start(bf16[1,448,128]{2,1,0:T(8,128)(2,1)S(1)} %get-tuple-element.411), channel_id=1, source_target_pairs={{0,8},{1,9},{2,10},{3,11},{4,12},{5,13},{6,14},{7,15},{8,0},{9,1},... | collective-permute-start | bytes 344072 | tf_op jit(solution)/shard_map/ppermute | solution.py:579
  212.3 8.0 %collective-permute-start.39 = (bf16[1,448,128]{2,1,0:T(8,128)(2,1)S(1)}, bf16[1,448,128]{2,1,0:T(8,128)(2,1)S(1)}, u32[]{:S(2)}, u32[]{:S(2)}) collective-permute-start(bf16[1,448,128]{2,1,0:T(8,128)(2,1)S(1)} %get-tuple-element.412), channel_id=1, source_target_pairs={{0,16},{1,17},{2,18},{3,19},{4,20},{5,21},{6,22},{7,23},{8,24},{9,... | collective-permute-start | bytes 344072 | tf_op jit(solution)/shard_map/ppermute | solution.py:579
  220.8 18.1 %collective-permute-start.50 = (bf16[40,3,512]{2,0,1:T(8,128)(2,1)S(1)}, bf16[40,3,512]{2,0,1:T(8,128)(2,1)S(1)}, u32[]{:S(2)}, u32[]{:S(2)}) collective-permute-start(bf16[40,3,512]{2,0,1:T(8,128)(2,1)S(1)} %get-tuple-element.404), channel_id=1, source_target_pairs={{0,2},{1,3},{2,0},{3,1},{4,6},{5,7},{6,4},{7,5},{8,10},{9,11},{10,... | collective-permute-start | bytes 368648 | tf_op jit(solution)/shard_map/ppermute | solution.py:516
  221.6 10.4 %collective-permute-start.42 = (bf16[4,256,128]{2,1,0:T(8,128)(2,1)S(1)}, bf16[4,256,128]{2,1,0:T(8,128)(2,1)S(1)}, u32[]{:S(2)}, u32[]{:S(2)}) collective-permute-start(bf16[4,256,128]{2,1,0:T(8,128)(2,1)S(1)} %slice.452), channel_id=1, source_target_pairs={{0,4},{1,5},{2,6},{3,7},{4,0},{5,1},{6,2},{7,3},{8,12},{9,13},{10,... | collective-permute-start | bytes 786440 | tf_op jit(solution)/shard_map/ppermute | solution.py:579
  227.9 11.0 %collective-permute-start.49 = (bf16[320,512]{1,0:T(8,128)(2,1)S(1)}, bf16[320,512]{1,0:T(8,128)(2,1)S(1)}, u32[]{:S(2)}, u32[]{:S(2)}) collective-permute-start(bf16[320,512]{1,0:T(8,128)(2,1)S(1)} %fusion.6), channel_id=1, source_target_pairs={{0,2},{1,3},{2,0},{3,1},{4,6},{5,7},{6,4},{7,5},{8,10},{9,11},{10,... | collective-permute-start | bytes 983048 | tf_op jit(solution)/shard_map/ppermute | solution.py:516
  (105 other events, 902.9 us)
